TPU v7x, 32 devices: a whole 2x2x4 slice. The times are simulated.
32 devices in a mesh: wide: 16 (over z, y, x), narrow: 2 (over core).
Axes of the slice: x: 2, y: 2, z: 4, core: 2. Of those that a mesh axis runs over, the one named last changes fastest.
Arguments:
- patches: bfloat16 [192, 256, 768], P(('wide', 'narrow')), may hold values from -6 to 6
- timeloc: bfloat16 [192, 768], P(('wide', 'narrow')), may hold values from -6 to 6
- visible: int32 [192, 64], P(('wide', 'narrow')), may hold values from 0 to 255, as said below
- masked: int32 [192, 192], P(('wide', 'narrow')), may hold values from 0 to 255, as said below
- flags: int32 [192], P(('wide', 'narrow')), may hold values 0 or 1
- cotangent: bfloat16 [192, 256, 512], P(('wide', 'narrow')), may hold values from -6 to 6
- params: float32 [79104, 128], P('narrow')
- moment1: float32 [79104, 128], P('narrow'), may hold values from -1.5 to 1.5
- moment2: float32 [79104, 128], P('narrow'), may hold values from 0.01 to 10
Outputs:
- dec_out: bfloat16 [192, 256, 512], P(('wide', 'narrow'))
- patch_grad: bfloat16 [192, 256, 768], P(('wide', 'narrow'))
- grads: float32 [79104, 128], P('narrow')
- update: float32 [79104, 128], P('narrow')
- new_moment1: float32 [79104, 128], P('narrow')
- new_moment2: float32 [79104, 128], P('narrow')
Inputs may be any that keep to these rules, and one draw needn't show every extreme that they name: For every chip, its 64 visible and 192 masked indices are distinct and together name each patch 0 to 255 once. `masked`: the complement of the same chip's visible indices.
All inputs are finite; a program needn't handle non-finite values. No bound on the sum of `flags` on one device may be relied on, other than what follows from the above.
Results may differ from a plain program's by a relative error of at most 0.018.
Values may be sent and summed in bfloat16 or wider, within the bound.
No kernel may reach another device: no remote copies, remote signals or barrier semaphores. Data moves between devices by JAX's collectives and lax.ppermute only.
A program may use at most 384 MiB of HBM per device.

v0:
```python
import math

import jax
import jax.numpy as jnp
from jax import lax
from jax.experimental import pallas as pl
from jax.experimental.pallas import tpu as pltpu
from jax.sharding import PartitionSpec as P

DE = 768
HE = 12
HD = 64
FE = 3072
DD = 512
HDEC = 4
FD = 2048
PATCH = 256


highest = lax.Precision.HIGHEST
first_bias_fix = 0.9999734386011124
second_bias_fix = 0.994079470779666


def block_segments(prefix, width, inner, hidden):
    names = ("g1", "b1", "qkv", "o", "ob", "g2", "b2", "u", "ub", "v", "vb")
    dims = ((width,), (width,), (width, 3 * inner), (inner, width), (width,), (width,), (width,))
    dims = (*dims, (width, hidden), (hidden,), (hidden, width), (width,))
    return [(prefix + name, size) for name, size in zip(names, dims)]


def segment_list():
    ends = (("fg", (DE,)), ("fb", (DE,)), ("proj", (DE, DD)), ("pb", (DD,)), ("mask", (DD,)))
    return [
        ("cls", (DE,)),
        *block_segments("e", DE, HE * HD, FE),
        *ends,
        *block_segments("d", DD, HDEC * HD, FD),
    ]


MARGIN = 256


def flat_rows():
    table = {}
    offset = 0
    for label, dims_of in segment_list():
        rows = math.prod(dims_of) // 128
        table[label] = (offset, rows)
        offset = offset + rows
    return table, offset


def round_up(value, unit):
    return -(-value // unit) * unit


def group_list():
    firsts = ("cls", "eo", "eu", "ev", "proj", "dqkv", "du", "dv")
    groups = []
    for label, dims in segment_list():
        if label in firsts:
            groups.append([])
        if label == "dg1" or label == "db1" or groups:
            groups[-1].append(label)
    return groups


def unpack(sources, total):
    table, used = flat_rows()
    shapes = dict(segment_list())
    groups = group_list()
    spans = [(table[g[0]][0], sum(table[g[-1]])) for g in groups]
    edges = [0, *[min(round_up(high, 16), total) for low, high in spans]]
    half = total // 2
    copies = []
    for k, (low, high) in enumerate(zip(edges, edges[1:])):
        parts = [(low, high)]
        if len(sources) == 2 and low < half < high:
            parts = [(low, half), (half, high)]
        copies.append(parts)
    slots = [(k, p) for k, parts in enumerate(copies) for p in range(len(parts))]
    labels = [label for label, dims in segment_list()]
    deepest = max(round_up(high, 16) - low // 16 * 16 for low, high in spans)

    def kernel(*refs):
        ins, rest = refs[: len(sources)], refs[len(sources) :]
        outs = dict(zip(labels, rest))
        staged, wide_rows, sems = rest[len(labels) :]

        def copy(slot, source, shift):
            k, p = slot
            low, high = copies[k][p]
            return pltpu.make_async_copy(
                source.at[pl.ds(low - shift, high - low)],
                staged.at[pl.ds(low, high - low)],
                sems.at[slots.index(slot)],
            )

        if len(sources) == 2:
            mine = lax.axis_index("narrow")
            for slot in slots:
                place = 0 if copies[slot[0]][slot[1]][0] < half else 1

                @pl.when(mine == place)
                def own_part(slot=slot, place=place):
                    copy(slot, ins[0], place * half).start()

                @pl.when(mine != place)
                def other_part(slot=slot, place=place):
                    copy(slot, ins[1], place * half).start()
        else:
            for slot in slots:
                copy(slot, ins[0], 0).start()
        for k, group in enumerate(groups):
            for p in range(len(copies[k])):
                copy((k, p), ins[0], copies[k][p][0]).wait()
            low, high = spans[k]
            origin = low // 16 * 16
            length = round_up(high, 16) - origin

            def widen(i, carry, origin=origin):
                spot = pl.multiple_of(i * 128, 128)
                wide_rows[pl.ds(spot, 128), :] = staged[
                    pl.ds(pl.multiple_of(origin + spot, 16), 128), :
                ].astype(jnp.float32)
                return carry

            lax.fori_loop(0, length // 128, widen, 0)
            done = length // 128 * 128
            if done < length:
                wide_rows[done:length, :] = staged[origin + done : origin + length, :].astype(
                    jnp.float32
                )
            for label in group:
                base = table[label][0] - origin
                dims, ref = shapes[label], outs[label]
                tiles = dims[-1] // 128
                if len(dims) == 1:
                    for c in range(tiles):
                        ref[:, c * 128 : (c + 1) * 128] = wide_rows[base + c : base + c + 1, :]
                    continue

                def step(i, carry, base=base, tiles=tiles, ref=ref):
                    for c in range(tiles):
                        rows = wide_rows[pl.ds(base + i * 16 * tiles + c, 16, stride=tiles), :]
                        ref[pl.ds(pl.multiple_of(i * 16, 16), 16), c * 128 : (c + 1) * 128] = (
                            rows.astype(jnp.bfloat16)
                        )
                    return carry

                lax.fori_loop(0, dims[0] // 16, step, 0)

    out_shape = [
        jax.ShapeDtypeStruct(dims, jnp.bfloat16)
        if len(dims) == 2
        else jax.ShapeDtypeStruct((1, dims[0]), jnp.float32)
        for label, dims in segment_list()
    ]
    outs = pl.pallas_call(
        kernel,
        out_shape=out_shape,
        in_specs=[pl.BlockSpec(memory_space=pl.ANY)] * len(sources),
        scratch_shapes=[
            pltpu.VMEM((total, 128), jnp.bfloat16),
            pltpu.VMEM((deepest, 128), jnp.float32),
            pltpu.SemaphoreType.DMA((len(slots),)),
        ],
        compiler_params=pltpu.CompilerParams(vmem_limit_bytes=61 << 20),
        name="unpack",
    )(*sources)
    return dict(zip(labels, outs))


def cut_points(total, unit):
    table, used = flat_rows()
    inner = [round_up(table[label][0], unit) for label in ("eu", "ev", "proj")]
    return [0, *inner, round_up(total, unit)]


def pack_segment(pieces, low, high, first, last, held):
    table, used = flat_rows()
    labels = [k for k, (off, rows) in table.items() if off < high and off + rows > low]
    arrays = [
        pieces[k] if pieces[k].ndim == 2 else pieces[k].reshape(1, -1) for k in labels
    ]
    length = high - low
    middle = (first + last) // 2
    runs = [
        (max(low, start), min(high, end), place, start)
        for place, (start, end) in enumerate(((first, middle), (middle, last)))
        if max(low, start) < min(high, end)
    ]
    taken = len(held)

    def kernel(*refs):
        ins, rest = refs[: len(labels)], refs[len(labels) + taken :]
        kept, sent, flat, out, sems = rest
        if used < high:
            start = max(used, low) - low + MARGIN
            flat[start : MARGIN + length, :] = jnp.zeros((MARGIN + length - start, 128), jnp.float32)
        for k, ref in zip(labels, ins):
            off, rows = table[k]
            tiles = ref.shape[1] // 128
            base = off - low + MARGIN
            if ref.shape[0] == 1:
                for c in range(tiles):
                    spot = base + c
                    if 0 <= spot < length + 2 * MARGIN:
                        flat[spot : spot + 1, :] = ref[:, c * 128 : (c + 1) * 128]
                continue
            block = 8 * tiles
            begin = max(0, low - off) // block
            end = -(-min(rows, high - off) // block)

            def step(i, carry, ref=ref, tiles=tiles, base=base, block=block):
                for c in range(tiles):
                    flat[pl.ds(base + i * block + c, 8, stride=tiles), :] = ref[
                        pl.ds(pl.multiple_of(i * 8, 8), 8), c * 128 : (c + 1) * 128
                    ]
                return carry

            lax.fori_loop(begin, end, step, 0)

        def narrow_down(i, carry):
            spot = pl.multiple_of(i * 128, 128)
            out[pl.ds(spot, 128), :] = flat[pl.ds(MARGIN + spot, 128), :].astype(jnp.bfloat16)
            return carry

        lax.fori_loop(0, length // 128, narrow_down, 0)
        mine = lax.axis_index("narrow")

        def copy(n, target):
            start, end, place, origin = runs[n]
            return pltpu.make_async_copy(
                out.at[pl.ds(start - low, end - start)],
                target.at[pl.ds(start - origin, end - start)],
                sems.at[n],
            )

        for n, (start, end, place, origin) in enumerate(runs):

            @pl.when(mine == place)
            def keep(n=n):
                copy(n, kept).start()

            @pl.when(mine != place)
            def send(n=n):
                copy(n, sent).start()

        for n in range(len(runs)):
            copy(n, kept).wait()

    anywhere = pl.BlockSpec(memory_space=pl.ANY)
    whole = pl.BlockSpec(memory_space=pltpu.VMEM)
    return pl.pallas_call(
        kernel,
        out_shape=[jax.ShapeDtypeStruct((middle - first, 128), jnp.bfloat16)] * 2,
        in_specs=[whole] * len(arrays) + [anywhere] * taken,
        out_specs=[anywhere] * 2,
        input_output_aliases={len(arrays) + n: n for n in range(taken)},
        scratch_shapes=[
            pltpu.VMEM((length + 2 * MARGIN, 128), jnp.float32),
            pltpu.VMEM((length, 128), jnp.bfloat16),
            pltpu.SemaphoreType.DMA((len(runs),)),
        ],
        compiler_params=pltpu.CompilerParams(vmem_limit_bytes=61 << 20),
        name=f"pack{low}",
    )(*arrays, *held)


def pack_halves(pieces, cuts):
    if lax.axis_size("narrow") == 2:
        held = ()
        for low, high in zip(cuts, cuts[1:]):
            held = pack_segment(pieces, low, high, cuts[0], cuts[-1], held)
        return held
    flat = jnp.concatenate([pieces[k].reshape(-1) for k, dims in segment_list()])
    flat = jnp.concatenate([flat, jnp.zeros((cuts[-1] * 128 - flat.shape[0],), jnp.float32)])
    return (flat.reshape(-1, 128)[cuts[0] :].astype(jnp.bfloat16),)


def added(first, second):
    return (first.astype(jnp.float32) + second.astype(jnp.float32)).astype(jnp.bfloat16)


def piece(value, index, rows):
    return lax.dynamic_slice_in_dim(value, index * rows, rows, 0)


class Line:
    def __init__(self, stride, size):
        self.stride, self.size, self.wide = stride, size, lax.axis_size("wide")
        self.me = (lax.axis_index("wide") // stride) % size
        self.groups = [
            [i + k * stride for k in range(size)]
            for i in range(self.wide)
            if (i // stride) % size == 0
        ]

    def swap(self, value):
        pairs = [pair for a, b in self.groups for pair in ((a, b), (b, a))]
        return lax.ppermute(value, "wide", pairs)

    def exchange(self, value):
        return lax.all_to_all(value, "wide", 0, 0, axis_index_groups=self.groups)

    def scatter(self, value):
        rows = value.shape[0] // self.size
        if self.size == 2:
            got = self.swap(piece(value, 1 - self.me, rows))
            return added(piece(value, self.me, rows), got)
        got = self.exchange(value.reshape(self.size, -1, 128)).astype(jnp.float32)
        return jnp.sum(got, 0).astype(jnp.bfloat16).reshape(rows, -1, 128)

    def gather(self, value):
        if self.size == 2:
            got = self.swap(value)
            low = self.me == 0
            return jnp.concatenate([jnp.where(low, value, got), jnp.where(low, got, value)], 0)
        copies = jnp.broadcast_to(value[None], (self.size, *value.shape))
        return self.exchange(copies).reshape(-1, *value.shape[1:])


def narrow_swap(value, step):
    count = lax.axis_size("narrow")
    return lax.ppermute(value, "narrow", [(i, (i + step) % count) for i in range(count)])


def sum_everywhere(halves):
    count, wide = lax.axis_size("narrow"), lax.axis_size("wide")
    if len(halves) == 2:
        total = added(halves[0], narrow_swap(halves[1], 1))
    else:
        (value,) = halves
        mine = lax.axis_index("narrow")
        rows = value.shape[0] // count
        total = piece(value, mine, rows)
        for step in range(1, count):
            total = added(total, narrow_swap(piece(value, (mine + step) % count, rows), step))
    rows = total.shape[0]
    depth = wide // 4
    x, y, z = Line(1, 2), Line(2, 2), Line(4, depth)
    unit = wide * 8
    units = rows // unit
    most = units * 4 // 11
    first, second = most * unit, 2 * most * unit
    a = total[:first].reshape(2, 2, depth, -1, 128)
    b = total[first:second].reshape(2, 2, depth, -1, 128)
    c = total[second:].reshape(depth, 2, 2, -1, 128)
    flat3 = lambda v, n: v.reshape(n, -1, 128)
    c = z.scatter(flat3(c, depth))
    a = x.scatter(flat3(a, 2))
    b = y.scatter(flat3(b, 2))
    a = y.scatter(flat3(a, 2))
    b = x.scatter(flat3(b, 2))
    a, b, c = lax.optimization_barrier((a, b, c))
    ab = z.scatter(jnp.concatenate([flat3(a, depth), flat3(b, depth)], 1))
    c = x.scatter(flat3(c, 2))
    c = y.scatter(flat3(c, 2))
    ab, c = lax.optimization_barrier((ab, c))
    ab = z.gather(flat3(ab, 1))
    c = x.gather(y.gather(flat3(c, 1)))
    ab, c = lax.optimization_barrier((ab, c))
    half = ab.shape[1] // 2
    a, b = ab[:, :half], ab[:, half:]
    c = z.gather(flat3(c, 1))
    a = y.gather(flat3(a, 1))
    b = x.gather(flat3(b, 1))
    a = x.gather(flat3(a, 1))
    b = y.gather(flat3(b, 1))
    return jnp.concatenate([v.reshape(-1, 128) for v in (a, b, c)], 0)


def whole_params(params):
    low_params = params.astype(jnp.bfloat16)
    if lax.axis_size("narrow") == 2:
        return (low_params, narrow_swap(low_params, 1))
    return (lax.all_gather(low_params, "narrow", axis=0, tiled=True),)


def position_table():
    half_width = DD // 2
    places = jnp.arange(PATCH, dtype=jnp.float32)[:, None]
    rates = jnp.exp(jnp.arange(half_width, dtype=jnp.float32) * (-math.log(10000.0) / half_width))
    angles = places * rates[None, :]
    return jnp.concatenate([jnp.sin(angles), jnp.cos(angles)], 1)


def layer_norm(stream, gain_vec, bias_vec):
    average = jnp.mean(stream, -1, keepdims=True)
    centred = stream - average
    spread = jnp.mean(centred * centred, -1, keepdims=True)
    return centred * lax.rsqrt(spread + 1e-05) * gain_vec + bias_vec


def vector(weights_map, label):
    return weights_map[label].reshape(-1)


def adam_step(grads, moment1, moment2):
    new_first = 0.9 * moment1 + (1.0 - 0.9) * grads
    new_second = 0.95 * moment2 + (1.0 - 0.95) * grads * grads
    update = new_first / first_bias_fix / (jnp.sqrt(new_second / second_bias_fix) + 1e-08)
    return (update, new_first, new_second)


def gelu_and_slope(u):
    t = 1.0 / (1.0 + (0.3275911 * math.sqrt(0.5)) * jnp.abs(u))
    bell = jnp.exp(-0.5 * u * u)
    tail = 0.5 * 1.061405429
    for term in (-1.453152027, 1.421413741, -0.284496736, 0.254829592):
        tail = tail * t + 0.5 * term
    tail = tail * t * bell
    below = jnp.where(u < 0, tail, 1.0 - tail)
    slope = below + u * bell * (1.0 / math.sqrt(2.0 * math.pi))
    return (u * below).astype(jnp.bfloat16), slope.astype(jnp.bfloat16)


def block_forward(stream, weights_map, prefix, heads):
    chips, tokens, width = stream.shape
    inner = heads * HD
    normed1 = layer_norm(
        stream,
        vector(weights_map, prefix + "g1"),
        vector(weights_map, prefix + "b1"),
    )
    first_in = normed1.astype(jnp.bfloat16)
    triple = jnp.einsum(
        "ctd,de->cte", first_in, weights_map[prefix + "qkv"], preferred_element_type=jnp.float32
    ).astype(jnp.bfloat16)
    query_rows = triple[:, :, :inner].reshape(chips, tokens, heads, HD)
    key_rows = triple[:, :, inner : 2 * inner].reshape(chips, tokens, heads, HD)
    value_rows = triple[:, :, 2 * inner :].reshape(chips, tokens, heads, HD)
    scores = jnp.einsum(
        "cqhe,ckhe->chqk", query_rows, key_rows, preferred_element_type=jnp.float32
    ) * HD ** (-0.5)
    topmost = jnp.max(scores, -1, keepdims=True)
    expos = jnp.exp(scores - topmost)
    totals = jnp.sum(expos, -1, keepdims=True)
    logsum = topmost + jnp.log(totals)
    probs = (expos / totals).astype(jnp.bfloat16)
    mixed = jnp.einsum("chqk,ckhe->cqhe", probs, value_rows, preferred_element_type=jnp.float32)
    mixed = mixed.reshape(chips, tokens, inner).astype(jnp.bfloat16)
    middle = (
        stream
        + jnp.einsum(
            "cti,id->ctd", mixed, weights_map[prefix + "o"], preferred_element_type=jnp.float32
        )
        + vector(weights_map, prefix + "ob")
    )
    normed2 = layer_norm(
        middle,
        vector(weights_map, prefix + "g2"),
        vector(weights_map, prefix + "b2"),
    )
    second_in = normed2.astype(jnp.bfloat16)
    hidden_pre = jnp.einsum(
        "ctd,df->ctf", second_in, weights_map[prefix + "u"], preferred_element_type=jnp.float32
    ) + vector(weights_map, prefix + "ub")
    activ, slope = gelu_and_slope(hidden_pre)
    result = (
        middle
        + jnp.einsum(
            "ctf,fd->ctd", activ, weights_map[prefix + "v"], preferred_element_type=jnp.float32
        )
        + vector(weights_map, prefix + "vb")
    )
    kept = (
        stream,
        middle,
        first_in,
        query_rows,
        key_rows,
        value_rows,
        logsum,
        mixed,
        second_in,
        slope,
        activ,
    )
    return (result, kept)


def block_backward(upstream, kept, weights_map, prefix, heads):
    (
        stream,
        middle,
        first_in,
        query_rows,
        key_rows,
        value_rows,
        logsum,
        mixed,
        second_in,
        slope,
        activ,
    ) = kept
    chips, tokens, width = stream.shape
    inner = heads * HD
    grads = {}
    branch_two = upstream.astype(jnp.bfloat16)
    grads[prefix + "vb"] = jnp.sum(branch_two.astype(jnp.float32), (0, 1))
    grads[prefix + "v"] = jnp.einsum(
        "ctf,ctd->fd", activ, branch_two, preferred_element_type=jnp.float32
    )
    d_activ = jnp.einsum(
        "ctd,fd->ctf", branch_two, weights_map[prefix + "v"], preferred_element_type=jnp.float32
    )
    d_hidden = (d_activ * slope.astype(jnp.float32)).astype(jnp.bfloat16)
    grads[prefix + "ub"] = jnp.sum(d_hidden.astype(jnp.float32), (0, 1))
    grads[prefix + "u"] = jnp.einsum(
        "ctd,ctf->df", second_in, d_hidden, preferred_element_type=jnp.float32
    )
    d_second = jnp.einsum(
        "ctf,df->ctd", d_hidden, weights_map[prefix + "u"], preferred_element_type=jnp.float32
    )
    norm_pull = jax.vjp(
        layer_norm,
        middle,
        vector(weights_map, prefix + "g2"),
        vector(weights_map, prefix + "b2"),
    )[1]
    d_middle_part, grads[prefix + "g2"], grads[prefix + "b2"] = norm_pull(
        d_second
    )
    d_middle = upstream + d_middle_part
    branch_one = d_middle.astype(jnp.bfloat16)
    grads[prefix + "ob"] = jnp.sum(branch_one.astype(jnp.float32), (0, 1))
    grads[prefix + "o"] = jnp.einsum(
        "cti,ctd->id", mixed, branch_one, preferred_element_type=jnp.float32
    )
    d_mixed = jnp.einsum(
        "ctd,id->cti", branch_one, weights_map[prefix + "o"], preferred_element_type=jnp.float32
    )
    d_mixed = d_mixed.astype(jnp.bfloat16).reshape(chips, tokens, heads, HD)
    scores = jnp.einsum(
        "cqhe,ckhe->chqk", query_rows, key_rows, preferred_element_type=jnp.float32
    ) * HD ** (-0.5)
    probs_full = jnp.exp(scores - logsum)
    probs_low = probs_full.astype(jnp.bfloat16)
    d_value = jnp.einsum("chqk,cqhe->ckhe", probs_low, d_mixed, preferred_element_type=jnp.float32)
    d_probs = jnp.einsum("cqhe,ckhe->chqk", d_mixed, value_rows, preferred_element_type=jnp.float32)
    row_shift = jnp.sum(d_probs * probs_full, -1, keepdims=True)
    d_scores = (probs_full * (d_probs - row_shift)).astype(jnp.bfloat16)
    d_query = jnp.einsum(
        "chqk,ckhe->cqhe", d_scores, key_rows, preferred_element_type=jnp.float32
    ) * HD ** (-0.5)
    d_key = jnp.einsum(
        "chqk,cqhe->ckhe", d_scores, query_rows, preferred_element_type=jnp.float32
    ) * HD ** (-0.5)
    d_triple = jnp.concatenate(
        [
            d_query.reshape(chips, tokens, inner),
            d_key.reshape(chips, tokens, inner),
            d_value.reshape(chips, tokens, inner),
        ],
        -1,
    ).astype(jnp.bfloat16)
    grads[prefix + "qkv"] = jnp.einsum(
        "ctd,cte->de", first_in, d_triple, preferred_element_type=jnp.float32
    )
    d_first = jnp.einsum(
        "cte,de->ctd", d_triple, weights_map[prefix + "qkv"], preferred_element_type=jnp.float32
    )
    first_pull = jax.vjp(
        layer_norm,
        stream,
        vector(weights_map, prefix + "g1"),
        vector(weights_map, prefix + "b1"),
    )[1]
    d_stream_part, grads[prefix + "g1"], grads[prefix + "b1"] = first_pull(
        d_first
    )
    return (d_middle + d_stream_part, grads)


def per_device(patches, timeloc, visible, masked, flags, cotangent, params, moment1, moment2):
    total_rows = params.shape[0] * lax.axis_size("narrow")
    weights_map = unpack(whole_params(params), total_rows)
    chips = patches.shape[0]
    patch_ids = jnp.arange(PATCH, dtype=jnp.int32)
    chooser = visible[:, :, None] == patch_ids[None, None, :]
    choose_low = chooser.astype(jnp.bfloat16)
    choose_full = chooser.astype(jnp.float32)
    picked = jnp.einsum("cvp,cpd->cvd", choose_low, patches, preferred_element_type=jnp.float32)
    keep_meta = (1 - flags).astype(jnp.float32)
    meta_row = timeloc.astype(jnp.float32) * keep_meta[:, None]
    class_row = jnp.broadcast_to(vector(weights_map, "cls")[None, None, :], (chips, 1, DE))
    enc_in = jnp.concatenate([class_row, meta_row[:, None, :], picked], 1)
    enc_out, enc_kept = block_forward(enc_in, weights_map, "e", HE)
    patch_rows = enc_out[:, 2:, :]
    final_gain = vector(weights_map, "fg")
    final_bias = vector(weights_map, "fb")
    encoded_low = layer_norm(patch_rows, final_gain, final_bias).astype(jnp.bfloat16)
    projected = jnp.einsum(
        "cvd,de->cve", encoded_low, weights_map["proj"], preferred_element_type=jnp.float32
    ) + vector(weights_map, "pb")
    filled = jnp.einsum("cvp,cve->cpe", choose_full, projected, precision=highest)
    mask_rows = jnp.sum((masked[:, :, None] == patch_ids[None, None, :]).astype(jnp.float32), 1)
    dec_in = (
        filled
        + mask_rows[:, :, None] * vector(weights_map, "mask")[None, None, :]
        + position_table()[None]
    )
    dec_out, dec_kept = block_forward(dec_in, weights_map, "d", HDEC)
    d_dec_in, grads = block_backward(
        cotangent.astype(jnp.float32), dec_kept, weights_map, "d", HDEC
    )
    grads["mask"] = jnp.sum(mask_rows[:, :, None] * d_dec_in, (0, 1))
    d_projected = jnp.einsum("cvp,cpe->cve", choose_full, d_dec_in, precision=highest).astype(
        jnp.bfloat16
    )
    grads["pb"] = jnp.sum(d_projected.astype(jnp.float32), (0, 1))
    grads["proj"] = jnp.einsum(
        "cvd,cve->de", encoded_low, d_projected, preferred_element_type=jnp.float32
    )
    d_encoded = jnp.einsum(
        "cve,de->cvd", d_projected, weights_map["proj"], preferred_element_type=jnp.float32
    )
    final_pull = jax.vjp(layer_norm, patch_rows, final_gain, final_bias)[1]
    d_patch_rows, grads["fg"], grads["fb"] = final_pull(d_encoded)
    d_enc_out = jnp.concatenate([jnp.zeros((chips, 2, DE), jnp.float32), d_patch_rows], 1)
    d_enc_in, enc_grads = block_backward(d_enc_out, enc_kept, weights_map, "e", HE)
    grads.update(enc_grads)
    grads["cls"] = jnp.sum(d_enc_in[:, 0, :], 0)
    patch_grad = jnp.einsum(
        "cvp,cvd->cpd", choose_full, d_enc_in[:, 2:, :], precision=highest
    ).astype(jnp.bfloat16)
    narrow_count, wide_count = lax.axis_size("narrow"), lax.axis_size("wide")
    chips_all = float(chips * wide_count * narrow_count)
    cuts = cut_points(total_rows, narrow_count * wide_count * 8)
    mine = sum_everywhere(pack_halves(grads, cuts))[: params.shape[0]]
    grad_out = mine.astype(jnp.float32) / chips_all
    update, new_moment1, new_moment2 = adam_step(grad_out, moment1, moment2)
    return (dec_out.astype(jnp.bfloat16), patch_grad, grad_out, update, new_moment1, new_moment2)


def solution(mesh):
    placed = (
        P(("wide", "narrow"), None, None),
        P(("wide", "narrow"), None),
        P(("wide", "narrow"), None),
        P(("wide", "narrow"), None),
        P(("wide", "narrow")),
        P(("wide", "narrow"), None, None),
        P("narrow", None),
        P("narrow", None),
        P("narrow", None),
    )
    return jax.shard_map(
        per_device,
        mesh=mesh,
        in_specs=placed,
        out_specs=(
            P(("wide", "narrow"), None, None),
            P(("wide", "narrow"), None, None),
            P("narrow", None),
            P("narrow", None),
            P("narrow", None),
            P("narrow", None),
        ),
        check_vma=False,
    )
```

profile of v0, /device:TPU:1, one launch (start us, length us, event | category | flops | bytes accessed | tf_op | source)
XLA Modules:
  0.0 669.4 jit_solution(18066667291835710333)
XLA Ops:
  0.7 8.2 %convert_element_type.214.refs_0_ = bf16[39552,128]{1,0:T(8,128)(2,1)S(1)} convert(f32[39552,128]{1,0:T(8,128)} %param.15) | non-fusion elementwise | flops 5062656 | bytes 30375936 | tf_op jit(solution)/shard_map/convert_element_type | solution.py:377
  14.7 10.1 %collective-permute-done.refs_1_ = bf16[39552,128]{1,0:T(8,128)(2,1)} collective-permute-done((bf16[39552,128]{1,0:T(8,128)(2,1)S(1)}, bf16[39552,128]{1,0:T(8,128)(2,1)}, u32[]{:S(2)}, u32[]{:S(2)}) %collective-permute-start) | collective-permute-done | bytes 10125344 | tf_op jit(solution)/shard_map/ppermute | solution.py:328
  24.8 22.7 %unpack.1 = (f32[1,768]{1,0:T(1,128)}, f32[1,768]{1,0:T(1,128)}, f32[1,768]{1,0:T(1,128)}, bf16[768,2304]{1,0:T(8,128)(2,1)}, bf16[768,768]{1,0:T(8,128)(2,1)}, ...) custom-call(bf16[39552,128]{1,0:T(8,128)(2,1)} %copy-done.10, ...), custom_call_target="tpu_custom_call" | custom-call | tf_op jit(solution)/shard_map/unpack/pallas_call | solution.py:161
  51.5 4.0 convolution_convert_fusion
  59.4 2.6 copy.162
  67.7 5.5 fusion.55
  73.2 4.5 multiply_convert_fusion.3
  77.8 5.6 fusion.19
  85.2 2.2 fusion.113
  88.1 2.3 convolution_convert_fusion.2
  93.5 2.3 copy.122
  103.3 7.1 %fusion.35 = (u8[256,2048]{1,0:T(8,128)(4,1)S(1)}, f32[6,256,2048]{2,1,0:T(8,128)}) fusion(f32[2048]{0:T(1024)S(1)} %bitcast.294, bf16[512,2048]{1,0:T(8,128)(2,1)S(1)} %copy-done.148, f32[6,256,512]{2,1,0:T(8,128)S(1)} %get-tuple-element.165, f32[512]{0:T(512)S(1)} %bitcast.306, f32[512]{0:T(512)S(1)} %bitcast.302, f32[6,256]{1,0:T(8,128)S(1)} %fusion.84, ...), kind=kOutput, calls=%fused_computation.86 | convolution fusion | flops 3243507712 | bytes 18374656 | tf_op jit(solution)/shard_map/ctd,df->ctf/dot_general | solution.py:459
  110.4 14.1 %multiply_convert_fusion = bf16[6,256,2048]{2,1,0:T(8,128)(2,1)} fusion(f32[6,256,2048]{2,1,0:T(8,128)} %get-tuple-element.167, f32[2048]{0:T(1024)S(1)} %bitcast.295, u8[256,2048]{1,0:T(8,128)(4,1)S(1)} %get-tuple-element.166), kind=kLoop, calls=%fused_computation.21 | loop fusion | flops 78643200 | bytes 19406848 | tf_op jit(solution)/shard_map/convert_element_type | solution.py:418
  124.5 16.7 %convert_reduce_fusion = (f32[2048]{0:T(1024)}, bf16[6,256,2048]{2,1,0:T(8,128)(2,1)S(1)}) fusion(f32[6,256,2048]{2,1,0:T(8,128)} %get-tuple-element.167, f32[2048]{0:T(1024)S(1)} %bitcast.296, u8[256,2048]{1,0:T(8,128)(4,1)S(1)} %get-tuple-element.166, bf16[6,256,512]{2,1,0:T(8,128)(2,1)S(1)} %copy-done.34, bf16[2048,512]{1,0:T(8,128)(2,1)S(1)} %copy-done.147), kind=kOutput, calls=%fused_computation.20 | convolution fusion | flops 3321886720 | bytes 23085056 | tf_op jit(solution)/shard_map/ctd,fd->ctf/dot_general | solution.py:508
  141.2 9.9 %multiply_reduce_fusion.2 = (f32[512]{0:T(512)}, f32[6,256]{1,0:T(8,128)S(1)}, f32[512]{0:T(512)}, f32[6,256,512]{2,1,0:T(8,128)}) fusion(f32[6,256,512]{2,1,0:T(8,128)S(1)} %get-tuple-element.165, f32[6,256]{1,0:T(8,128)S(1)} %fusion.84, f32[6,256]{1,0:T(8,128)S(1)} %broadcast_multiply_fusion, f32[512]{0:T(512)S(1)} %bitcast.303, ...), kind=kOutput, calls=%fused_computation.70 | convolution fusion | flops 3227514368 | bytes 14704640 | tf_op jit(solution)/shard_map/ctf,df->ctd/dot_general | solution.py:516
  151.1 7.0 %fusion.105 = (f32[6,256]{1,0:T(8,128)S(1)}, f32[6,256,512]{2,1,0:T(8,128)S(1)}, bf16[6,256,512]{2,1,0:T(8,128)(2,1)}) fusion(f32[6,256]{1,0:T(8,128)S(1)} %multiply_multiply_fusion.3, f32[6,256,512]{2,1,0:T(8,128)S(1)} %get-tuple-element.165, f32[6,256]{1,0:T(8,128)S(1)} %broadcast_multiply_fusion, f32[6,256]{1,0:T(8,128)S(1)} %fusion.84, ...), kind=kOutput, calls=%fused_computation.254 | convolution fusion | flops 3229088256 | bytes 19427328 | tf_op jit(solution)/shard_map/ctf,fd->ctd/dot_general | solution.py:465
  161.6 4.3 multiply_reduce_fusion
  166.0 4.5 multiply_convert_fusion.1
  179.0 5.2 fusion.97
  186.6 2.9 multiply_reduce_fusion.4
  195.3 7.2 %convert_reduce_fusion.1 = (f32[3072]{0:T(1024)}, bf16[6,66,3072]{2,1,0:T(8,128)(2,1)S(1)}) fusion(f32[6,66,3072]{2,1,0:T(8,128)S(1)} %bitcast.259, f32[3072]{0:T(1024)S(1)} %bitcast.292, u8[66,3072]{1,0:T(8,128)(4,1)S(1)} %copy-done.86, bf16[3072,768]{1,0:T(8,128)(2,1)S(1)} %bitcast.322, f32[6,64,768]{2,1,0:T(8,128)S(1)} %broadcast_add_fusion), kind=kOutput, calls=%fused_computation.42 | convolution fusion | flops 1907487744 | bytes 13424640 | tf_op jit(solution)/shard_map/ctd,fd->ctf/dot_general | solution.py:508
  202.5 3.2 multiply_reduce_fusion.11
  207.2 2.3 convolution_bitcast_fusion.5.refs_4_
  213.6 3.6 multiply_reduce_fusion.9
  224.5 5.3 convolution_bitcast_fusion.1.refs_8_.refs_0_
  229.8 2.4 copy.141
  232.2 2.4 copy.142
  234.6 2.3 copy.143
  237.0 6.7 convolution_bitcast_fusion.refs_3_
  245.8 5.2 convolution_bitcast_fusion.2.refs_2_.refs_0_
  253.4 5.5 convolution_bitcast_fusion.4.refs_10_
  260.4 2.9 convolution_bitcast_fusion.7.refs_5_
  263.3 5.0 convolution_bitcast_fusion.3.refs_12_
  277.2 11.4 %pack0.1 = (bf16[39552,128]{1,0:T(8,128)(2,1)}, bf16[39552,128]{1,0:T(8,128)(2,1)}) custom-call(f32[1,768]{1,0:T(1,128)} %reshape.412.refs_0_, f32[1,768]{1,0:T(1,128)} %reshape.413.refs_1_, f32[1,768]{1,0:T(1,128)} %reshape.414.refs_2_, f32[768,2304]{1,0:T(8,128)} %convolution_bitcast_fusion.refs_3_, f32[768,768]{1,0:T(8,128)} %convolution_bitcast_fusion.5.refs_4_, ...), custom_call_target="tpu_custom_call" | custom-call | tf_op jit(solution)/shard_map/pack0/pallas_call | solution.py:257
  288.6 11.6 %pack18688.1 = (bf16[39552,128]{1,0:T(8,128)(2,1)}, bf16[39552,128]{1,0:T(8,128)(2,1)}) custom-call(f32[768,3072]{1,0:T(8,128)} %convolution_bitcast_fusion.1.refs_8_.refs_0_, f32[1,3072]{1,0:T(1,128)} %bitcast.293, f32[3072,768]{1,0:T(8,128)} %convolution_bitcast_fusion.2.refs_2_.refs_0_, ...), custom_call_target="tpu_custom_call", output_to_operand_aliasing={{0}: (3, {}), {1}: (4, {})} | custom-call | tf_op jit(solution)/shard_map/pack18688/pallas_call | solution.py:257
  300.3 9.8 %pack37120.1 = (bf16[39552,128]{1,0:T(8,128)(2,1)}, bf16[39552,128]{1,0:T(8,128)(2,1)}) custom-call(f32[3072,768]{1,0:T(8,128)} %convolution_bitcast_fusion.2.refs_2_.refs_0_, f32[1,768]{1,0:T(1,128)} %reshape.408.refs_1_, f32[1,768]{1,0:T(1,128)} %reshape.409.refs_2_, f32[1,768]{1,0:T(1,128)} %reshape.410.refs_3_, ...), custom_call_target="tpu_custom_call", output_to_operand_aliasing={{0}: (5, {}), {1}: (6, {})} | custom-call | tf_op jit(solution)/shard_map/pack37120/pallas_call | solution.py:257
  310.1 13.0 %pack55552.1 = (bf16[39552,128]{1,0:T(8,128)(2,1)}, bf16[39552,128]{1,0:T(8,128)(2,1)}) custom-call(f32[768,512]{1,0:T(8,128)} %convolution_bitcast_fusion.6.refs_4_.refs_0_, f32[1,512]{1,0:T(1,128)} %bitcast.312, f32[1,512]{1,0:T(1,128)} %bitcast.310, f32[1,512]{1,0:T(1,128)} %bitcast.309, ...), custom_call_target="tpu_custom_call", output_to_operand_aliasing={{0}: (14, {}), {1}: (15, {})} | custom-call | tf_op jit(solution)/shard_map/pack55552/pallas_call | solution.py:257
  323.2 15.9 %collective-permute-done.1 = bf16[39552,128]{1,0:T(8,128)(2,1)} collective-permute-done((bf16[39552,128]{1,0:T(8,128)(2,1)}, bf16[39552,128]{1,0:T(8,128)(2,1)}, u32[]{:S(2)}, u32[]{:S(2)}) %collective-permute-start.1) | collective-permute-done | bytes 10125344 | tf_op jit(solution)/shard_map/ppermute | solution.py:328
  339.1 8.4 %add_convert_fusion = bf16[39552,128]{1,0:T(8,128)(2,1)S(1)} fusion(bf16[39552,128]{1,0:T(8,128)(2,1)} %collective-permute-done.1, bf16[39552,128]{1,0:T(8,128)(2,1)} %get-tuple-element.83), kind=kLoop, calls=%fused_computation.7 | loop fusion | flops 20250624 | bytes 30375936 | tf_op jit(solution)/shard_map/convert_element_type | solution.py:285
  349.8 2.8 copy-done.11
  354.6 2.4 collective-permute-start.4
  357.0 3.1 slice.68
  363.3 4.6 all-to-all-start
  367.9 29.2 %collective-permute-done.4 = bf16[1,7168,128]{2,1,0:T(8,128)(2,1)} collective-permute-done((bf16[1,7168,128]{2,1,0:T(8,128)(2,1)S(1)}, bf16[1,7168,128]{2,1,0:T(8,128)(2,1)}, u32[]{:S(2)}, u32[]{:S(2)}) %collective-permute-start.4) | collective-permute-done | bytes 1835040 | tf_op jit(solution)/shard_map/ppermute | solution.py:304
  397.1 2.5 add_convert_fusion.1
  401.0 2.3 collective-permute-done.2
  405.7 17.3 %collective-permute-done.5 = bf16[1,3584,128]{2,1,0:T(8,128)(2,1)S(1)} collective-permute-done((bf16[1,3584,128]{2,1,0:T(8,128)(2,1)S(1)}, bf16[1,3584,128]{2,1,0:T(8,128)(2,1)S(1)}, u32[]{:S(2)}, u32[]{:S(2)}) %collective-permute-start.5) | collective-permute-done | bytes 917536 | tf_op jit(solution)/shard_map/ppermute | solution.py:304
  425.1 5.4 all-to-all-done
  430.5 3.2 reduce_sum.490
  435.0 4.0 all-to-all-start.1
  439.4 8.0 %collective-permute-done.6 = bf16[1,1360,128]{2,1,0:T(8,128)(2,1)S(1)} collective-permute-done((bf16[1,1360,128]{2,1,0:T(8,128)(2,1)S(1)}, bf16[1,1360,128]{2,1,0:T(8,128)(2,1)S(1)}, u32[]{:S(2)}, u32[]{:S(2)}) %collective-permute-start.6) | collective-permute-done | bytes 348192 | tf_op jit(solution)/shard_map/ppermute | solution.py:304
  447.9 4.3 collective-permute-done.7
  452.2 28.9 %all-to-all-done.1 = bf16[4,1792,128]{2,1,0:T(8,128)(2,1)S(1)} async-done(((bf16[4,1792,128]{2,1,0:T(8,128)(2,1)}), bf16[4,1792,128]{2,1,0:T(8,128)(2,1)S(1)}, u32[]{:S(2)}, u32[]{:S(2)}) %all-to-all-start.1) | async-done | bytes 1835040 | tf_op jit(solution)/shard_map/all_to_all | solution.py:307
  483.1 3.6 all-to-all-start.2
  487.0 4.4 collective-permute-done.8
  491.8 7.2 %collective-permute-done.9 = bf16[2,680,128]{2,1,0:T(8,128)(2,1)S(1)} collective-permute-done((bf16[2,680,128]{2,1,0:T(8,128)(2,1)S(1)}, bf16[2,680,128]{2,1,0:T(8,128)(2,1)S(1)}, u32[]{:S(2)}, u32[]{:S(2)}) %collective-permute-start.9) | collective-permute-done | bytes 348192 | tf_op jit(solution)/shard_map/ppermute | solution.py:304
  500.0 28.8 %all-to-all-done.2 = bf16[4,1,1792,128]{3,2,1,0:T(8,128)(2,1)S(1)} async-done(((bf16[4,1,1792,128]{3,2,1,0:T(8,128)(2,1)}), bf16[4,1,1792,128]{3,2,1,0:T(8,128)(2,1)S(1)}, u32[]{:S(2)}, u32[]{:S(2)}) %all-to-all-start.2) | async-done | bytes 1835040 | tf_op jit(solution)/shard_map/all_to_all | solution.py:307
  529.5 20.1 %collective-permute-done.10 = bf16[1,3584,128]{2,1,0:T(8,128)(2,1)S(1)} collective-permute-done((bf16[1,3584,128]{2,1,0:T(8,128)(2,1)S(1)}, bf16[1,3584,128]{2,1,0:T(8,128)(2,1)S(1)}, u32[]{:S(2)}, u32[]{:S(2)}) %collective-permute-start.10) | collective-permute-done | bytes 917536 | tf_op jit(solution)/shard_map/ppermute | solution.py:304
  551.0 3.6 convolution_convert_fusion.1
  556.4 4.6 all-to-all-start.3
  562.9 26.8 %collective-permute-done.11 = bf16[1,7168,128]{2,1,0:T(8,128)(2,1)} collective-permute-done((bf16[1,7168,128]{2,1,0:T(8,128)(2,1)S(1)}, bf16[1,7168,128]{2,1,0:T(8,128)(2,1)}, u32[]{:S(2)}, u32[]{:S(2)}) %collective-permute-start.11) | collective-permute-done | bytes 1835040 | tf_op jit(solution)/shard_map/ppermute | solution.py:304
  593.5 8.6 %collective-permute-done.13 = bf16[1,7168,128]{2,1,0:T(8,128)(2,1)S(1)} collective-permute-done((bf16[1,7168,128]{2,1,0:T(8,128)(2,1)S(1)}, bf16[1,7168,128]{2,1,0:T(8,128)(2,1)S(1)}, u32[]{:S(2)}, u32[]{:S(2)}) %collective-permute-start.13) | collective-permute-done | bytes 1835040 | tf_op jit(solution)/shard_map/ppermute | solution.py:304
  604.5 19.1 %all-to-all-done.3 = bf16[4,1,2720,128]{3,2,1,0:T(8,128)(2,1)} async-done(((bf16[4,1,2720,128]{3,2,1,0:T(8,128)(2,1)}), bf16[4,1,2720,128]{3,2,1,0:T(8,128)(2,1)}, u32[]{:S(2)}, u32[]{:S(2)}) %all-to-all-start.3) | async-done | bytes 2785312 | tf_op jit(solution)/shard_map/all_to_all | solution.py:307
  623.6 45.3 %add_divide_fusion = (f32[39552,128]{1,0:T(8,128)}, f32[39552,128]{1,0:T(8,128)}, f32[39552,128]{1,0:T(8,128)}, f32[39552,128]{1,0:T(8,128)}) fusion(bf16[10880,128]{1,0:T(8,128)(2,1)} %bitcast.81, bf16[14336,128]{1,0:T(8,128)(2,1)} %bitcast.231, bf16[14336,128]{1,0:T(8,128)(2,1)} %bitcast.230, f32[39552,128]{1,0:T(8,128)} %param.16, f32[39552,128]{1,0:T(8,128)} %param.17), kind=kLoop, calls=%fused_computation.6 | loop fusion | flops 91127808 | bytes 131629056 | tf_op jit(solution)/shard_map/div | solution.py:405
  (480 shorter events, 109.9 us)
Async XLA Ops:
  0.6 12.4 %copy-start = (bf16[6,256,768]{2,1,0:T(8,128)(2,1)S(1)}, bf16[6,256,768]{2,1,0:T(8,128)(2,1)}, u32[]{:S(2)}) copy-start(bf16[6,256,768]{2,1,0:T(8,128)(2,1)} %param.9) | copy-start | bytes 7077892
  0.7 8.4 %copy-start.154 = (s32[6]{0:T(128)S(1)}, s32[6]{0:T(128)}, u32[]{:S(2)}) copy-start(s32[6]{0:T(128)} %param.13) | copy-start | bytes 76
  0.7 8.4 %copy-start.123 = (bf16[6,768]{1,0:T(8,128)(2,1)S(1)}, bf16[6,768]{1,0:T(8,128)(2,1)}, u32[]{:S(2)}) copy-start(bf16[6,768]{1,0:T(8,128)(2,1)} %param.10) | copy-start | bytes 27652
  0.7 10.9 %copy-start.131 = (s32[6,192]{1,0:T(8,128)S(1)}, s32[6,192]{1,0:T(8,128)}, u32[]{:S(2)}) copy-start(s32[6,192]{1,0:T(8,128)} %param.12) | copy-start | bytes 13828
  0.7 12.4 %copy-start.101 = (s32[6,64]{1,0:T(8,128)S(1)}, s32[6,64]{1,0:T(8,128)}, u32[]{:S(2)}) copy-start(s32[6,64]{1,0:T(8,128)} %param.11) | copy-start | bytes 4612
  9.0 15.8 %collective-permute-start = (bf16[39552,128]{1,0:T(8,128)(2,1)S(1)}, bf16[39552,128]{1,0:T(8,128)(2,1)}, u32[]{:S(2)}, u32[]{:S(2)}) collective-permute-start(bf16[39552,128]{1,0:T(8,128)(2,1)S(1)} %convert_element_type.214.refs_0_), channel_id=1, source_target_pairs={{0,1},{1,0},{2,3},{3,2},{4,5},{5,4},{6,7},{7,6},{8,9},{9,8},{10,11... | collective-permute-start | bytes 30375944 | tf_op jit(solution)/shard_map/ppermute | solution.py:328
  9.2 41.8 %copy-start.61 = (f32[6,1,768]{2,1,0:T(1,128)}, f32[6,1,768]{2,1,0:T(1,128)S(1)}, u32[]{:S(2)}) copy-start(f32[6,1,768]{2,1,0:T(1,128)S(1)} %broadcast_in_dim.36) | copy-start | bytes 55300
  14.7 33.5 %copy-start.8 = (f32[6,64,768]{2,1,0:T(8,128)S(1)}, f32[6,64,768]{2,1,0:T(8,128)}, u32[]{:S(2)}) copy-start(f32[6,64,768]{2,1,0:T(8,128)} %fusion.69) | copy-start | bytes 3538948
  66.1 7.0 %copy-start.104 = (f32[6,66]{1,0:T(8,128)}, f32[6,66]{1,0:T(8,128)S(1)}, u32[]{:S(2)}) copy-start(f32[6,66]{1,0:T(8,128)S(1)} %broadcast_multiply_fusion.3) | copy-start | bytes 4756
  83.9 109.8 %copy-start.95 = (f32[6,64]{1,0:T(8,128)}, f32[6,64]{1,0:T(8,128)S(1)}, u32[]{:S(2)}) copy-start(f32[6,64]{1,0:T(8,128)S(1)} %broadcast_multiply_fusion.2) | copy-start | bytes 4612
  84.2 108.4 %copy-start.112 = (f32[6,64]{1,0:T(8,128)}, f32[6,64]{1,0:T(8,128)S(1)}, u32[]{:S(2)}) copy-start(f32[6,64]{1,0:T(8,128)S(1)} %fusion.87) | copy-start | bytes 4612
  84.2 109.5 %copy-start.99 = (f32[768]{0:T(1024)}, f32[768]{0:T(1024)S(1)}, u32[]{:S(2)}) copy-start(f32[768]{0:T(1024)S(1)} %reduce.10) | copy-start | bytes 9220
  87.5 98.8 %copy-start.93 = (f32[6,256]{1,0:T(8,128)}, f32[6,256]{1,0:T(8,128)S(1)}, u32[]{:S(2)}) copy-start(f32[6,256]{1,0:T(8,128)S(1)} %broadcast_multiply_fusion.1) | copy-start | bytes 18436
  88.1 98.2 %copy-start.97 = (f32[6,256]{1,0:T(8,128)}, f32[6,256]{1,0:T(8,128)S(1)}, u32[]{:S(2)}) copy-start(f32[6,256]{1,0:T(8,128)S(1)} %fusion.83) | copy-start | bytes 18436
  100.5 50.6 %copy-start.12 = (f32[6,256,512]{2,1,0:T(8,128)}, f32[6,256,512]{2,1,0:T(8,128)S(1)}, u32[]{:S(2)}) copy-start(f32[6,256,512]{2,1,0:T(8,128)S(1)} %get-tuple-element.165) | copy-start | bytes 9437188
  100.6 50.5 %copy-start.83 = (f32[6,256]{1,0:T(8,128)}, f32[6,256]{1,0:T(8,128)S(1)}, u32[]{:S(2)}) copy-start(f32[6,256]{1,0:T(8,128)S(1)} %broadcast_multiply_fusion) | copy-start | bytes 18436
  101.2 49.9 %copy-start.87 = (f32[6,256]{1,0:T(8,128)}, f32[6,256]{1,0:T(8,128)S(1)}, u32[]{:S(2)}) copy-start(f32[6,256]{1,0:T(8,128)S(1)} %fusion.84) | copy-start | bytes 18436
  110.4 14.1 %copy-start.34 = (bf16[6,256,512]{2,1,0:T(8,128)(2,1)S(1)}, bf16[6,256,512]{2,1,0:T(8,128)(2,1)}, u32[]{:S(2)}) copy-start(bf16[6,256,512]{2,1,0:T(8,128)(2,1)} %param.14) | copy-start | bytes 4718596
  110.4 14.1 %copy-start.147 = (bf16[2048,512]{1,0:T(8,128)(2,1)S(1)}, bf16[2048,512]{1,0:T(8,128)(2,1)}, u32[]{:S(2)}) copy-start(bf16[2048,512]{1,0:T(8,128)(2,1)} %get-tuple-element.75) | copy-start | bytes 6291460
  141.2 9.9 %copy-start.33 = (bf16[6,256,2048]{2,1,0:T(8,128)(2,1)}, bf16[6,256,2048]{2,1,0:T(8,128)(2,1)S(1)}, u32[]{:S(2)}) copy-start(bf16[6,256,2048]{2,1,0:T(8,128)(2,1)S(1)} %get-tuple-element.180) | copy-start | bytes 18874372
  141.2 9.9 %copy-start.37 = (bf16[6,256,2048]{2,1,0:T(8,128)(2,1)S(1)}, bf16[6,256,2048]{2,1,0:T(8,128)(2,1)}, u32[]{:S(2)}) copy-start(bf16[6,256,2048]{2,1,0:T(8,128)(2,1)} %multiply_convert_fusion) | copy-start | bytes 18874372
  141.2 9.9 %copy-start.152 = (f32[1,512]{1,0:T(1,128)S(1)}, f32[1,512]{1,0:T(1,128)}, u32[]{:S(2)}) copy-start(f32[1,512]{1,0:T(1,128)} %get-tuple-element.76) | copy-start | bytes 6148
  184.2 10.9 %slice-start.8 = ((s8[4718592]{0:T(1024)(128)(4,1)}), s8[4194304]{0:T(1024)(128)(4,1)S(1)}, s32[]{:S(2)}) async-start(s8[4718592]{0:T(1024)(128)(4,1)} %bitcast.321), calls=%async_computation.12 | async-start | bytes 8388608
  186.6 8.6 %slice-start.9 = ((s8[4718592]{0:T(1024)(128)(4,1)}), s8[524288]{0:T(1024)(128)(4,1)S(1)}, s32[]{:S(2)}) async-start(s8[4718592]{0:T(1024)(128)(4,1)} %bitcast.321), calls=%async_computation.13 | async-start | bytes 1048576
  192.6 9.8 %slice-start.6 = ((s8[4718592]{0:T(1024)(128)(4,1)}), s8[4194304]{0:T(1024)(128)(4,1)S(1)}, s32[]{:S(2)}) async-start(s8[4718592]{0:T(1024)(128)(4,1)} %bitcast.319), calls=%async_computation.10 | async-start | bytes 8388608
  195.2 7.2 %copy-start.16 = (f32[6,66,768]{2,1,0:T(8,128)S(1)}, f32[6,66,768]{2,1,0:T(8,128)}, u32[]{:S(2)}) copy-start(f32[6,66,768]{2,1,0:T(8,128)} %copy-done.14) | copy-start | bytes 3649540
  195.2 7.2 %copy-start.105 = (f32[6,66]{1,0:T(8,128)S(1)}, f32[6,66]{1,0:T(8,128)}, u32[]{:S(2)}) copy-start(f32[6,66]{1,0:T(8,128)} %copy-done.104) | copy-start | bytes 4756
  195.2 7.2 %copy-start.118 = (f32[6,66]{1,0:T(8,128)S(1)}, f32[6,66]{1,0:T(8,128)}, u32[]{:S(2)}) copy-start(f32[6,66]{1,0:T(8,128)} %copy-done.117) | copy-start | bytes 4756
  195.2 7.2 %copy-start.120 = (f32[768]{0:T(1024)S(1)}, f32[768]{0:T(1024)}, u32[]{:S(2)}) copy-start(f32[768]{0:T(1024)} %copy-done.119) | copy-start | bytes 9220
  195.2 7.2 %slice-start.7 = ((s8[4718592]{0:T(1024)(128)(4,1)}), s8[524288]{0:T(1024)(128)(4,1)S(1)}, s32[]{:S(2)}) async-start(s8[4718592]{0:T(1024)(128)(4,1)} %bitcast.319), calls=%async_computation.11 | async-start | bytes 1048576
  229.8 7.2 %copy-start.9 = (f32[6,64,768]{2,1,0:T(8,128)S(1)}, f32[6,64,768]{2,1,0:T(8,128)}, u32[]{:S(2)}) copy-start(f32[6,64,768]{2,1,0:T(8,128)} %fusion.69) | copy-start | bytes 3538948
  229.8 7.2 %copy-start.78 = (f32[6,66]{1,0:T(8,128)S(1)}, f32[6,66]{1,0:T(8,128)}, u32[]{:S(2)}) copy-start(f32[6,66]{1,0:T(8,128)} %copy-done.77) | copy-start | bytes 4756
  229.8 7.2 %copy-start.80 = (f32[6,66]{1,0:T(8,128)S(1)}, f32[6,66]{1,0:T(8,128)}, u32[]{:S(2)}) copy-start(f32[6,66]{1,0:T(8,128)} %copy-done.79) | copy-start | bytes 4756
  229.8 7.2 %copy-start.82 = (f32[768]{0:T(1024)S(1)}, f32[768]{0:T(1024)}, u32[]{:S(2)}) copy-start(f32[768]{0:T(1024)} %copy-done.81) | copy-start | bytes 9220
  229.8 7.2 %copy-start.90 = (f32[768]{0:T(1024)S(1)}, f32[768]{0:T(1024)}, u32[]{:S(2)}) copy-start(f32[768]{0:T(1024)} %copy-done.89) | copy-start | bytes 9220
  243.8 9.3 %slice-start = ((s8[6291456]{0:T(1024)(128)(4,1)}), s8[4194304]{0:T(1024)(128)(4,1)S(1)}, s32[]{:S(2)}) async-start(s8[6291456]{0:T(1024)(128)(4,1)} %bitcast.254), calls=%async_computation.4 | async-start | bytes 8388608
  245.8 7.3 %slice-start.1 = ((s8[6291456]{0:T(1024)(128)(4,1)}), s8[2097152]{0:T(1024)(128)(4,1)S(1)}, s32[]{:S(2)}) async-start(s8[6291456]{0:T(1024)(128)(4,1)} %bitcast.254), calls=%async_computation.5 | async-start | bytes 4194304
  253.3 7.0 %copy-start.5 = (f32[6,256,512]{2,1,0:T(8,128)S(1)}, f32[6,256,512]{2,1,0:T(8,128)}, u32[]{:S(2)}) copy-start(f32[6,256,512]{2,1,0:T(8,128)} %copy-done.2) | copy-start | bytes 9437188
  253.3 7.0 %copy-start.71 = (bf16[6,256,256]{2,1,0:T(8,128)(2,1)S(1)}, bf16[6,256,256]{2,1,0:T(8,128)(2,1)}, u32[]{:S(2)}) copy-start(bf16[6,256,256]{2,1,0:T(8,128)(2,1)} %copy.130) | copy-start | bytes 2359300
  253.3 7.0 %copy-start.72 = (bf16[6,256,256]{2,1,0:T(8,128)(2,1)S(1)}, bf16[6,256,256]{2,1,0:T(8,128)(2,1)}, u32[]{:S(2)}) copy-start(bf16[6,256,256]{2,1,0:T(8,128)(2,1)} %copy.131) | copy-start | bytes 2359300
  253.3 7.0 %copy-start.74 = (bf16[6,256,256]{2,1,0:T(8,128)(2,1)S(1)}, bf16[6,256,256]{2,1,0:T(8,128)(2,1)}, u32[]{:S(2)}) copy-start(bf16[6,256,256]{2,1,0:T(8,128)(2,1)} %copy-done.73) | copy-start | bytes 2359300
  253.3 7.0 %copy-start.94 = (f32[6,256]{1,0:T(8,128)S(1)}, f32[6,256]{1,0:T(8,128)}, u32[]{:S(2)}) copy-start(f32[6,256]{1,0:T(8,128)} %copy-done.93) | copy-start | bytes 18436
  253.3 7.0 %copy-start.98 = (f32[6,256]{1,0:T(8,128)S(1)}, f32[6,256]{1,0:T(8,128)}, u32[]{:S(2)}) copy-start(f32[6,256]{1,0:T(8,128)} %copy-done.97) | copy-start | bytes 18436
  253.4 7.0 %copy-start.126 = (f32[1,512]{1,0:T(1,128)S(1)}, f32[1,512]{1,0:T(1,128)}, u32[]{:S(2)}) copy-start(f32[1,512]{1,0:T(1,128)} %get-tuple-element.66) | copy-start | bytes 6148
  253.4 9.9 %slice-start.2 = ((s8[6291456]{0:T(1024)(128)(4,1)}), s8[2097152]{0:T(1024)(128)(4,1)S(1)}, s32[]{:S(2)}) async-start(s8[6291456]{0:T(1024)(128)(4,1)} %bitcast.256), calls=%async_computation.6 | async-start | bytes 4194304
  323.1 16.0 %collective-permute-start.1 = (bf16[39552,128]{1,0:T(8,128)(2,1)}, bf16[39552,128]{1,0:T(8,128)(2,1)}, u32[]{:S(2)}, u32[]{:S(2)}) collective-permute-start(bf16[39552,128]{1,0:T(8,128)(2,1)} %get-tuple-element.84), channel_id=1, source_target_pairs={{0,1},{1,0},{2,3},{3,2},{4,5},{5,4},{6,7},{7,6},{8,9},{9,8},{10,11... | collective-permute-start | bytes 30375944 | tf_op jit(solution)/shard_map/ppermute | solution.py:328
  354.6 42.5 %collective-permute-start.4 = (bf16[1,7168,128]{2,1,0:T(8,128)(2,1)S(1)}, bf16[1,7168,128]{2,1,0:T(8,128)(2,1)}, u32[]{:S(2)}, u32[]{:S(2)}) collective-permute-start(bf16[1,7168,128]{2,1,0:T(8,128)(2,1)S(1)} %constant_dynamic-slice_fusion.3), channel_id=1, source_target_pairs={{0,4},{4,0},{2,6},{6,2},{8,12},{12,8},{10,14},{14,10},{16,20},{20,... | collective-permute-start | bytes 5505032 | tf_op jit(solution)/shard_map/ppermute | solution.py:304
  362.1 41.2 %collective-permute-start.2 = (bf16[1,7168,128]{2,1,0:T(8,128)(2,1)}, bf16[1,7168,128]{2,1,0:T(8,128)(2,1)}, u32[]{:S(2)}, u32[]{:S(2)}) collective-permute-start(bf16[1,7168,128]{2,1,0:T(8,128)(2,1)} %constant_dynamic-slice_fusion.5), channel_id=1, source_target_pairs={{0,2},{2,0},{4,6},{6,4},{8,10},{10,8},{12,14},{14,12},{16,18},{18,... | collective-permute-start | bytes 5505032 | tf_op jit(solution)/shard_map/ppermute | solution.py:304
  363.3 67.2 %all-to-all-start = ((bf16[4,2720,128]{2,1,0:T(8,128)(2,1)}), bf16[4,2720,128]{2,1,0:T(8,128)(2,1)}, u32[]{:S(2)}, u32[]{:S(2)}) async-start(bf16[4,2720,128]{2,1,0:T(8,128)(2,1)} %bitcast.232), calls=%async_computation | async-start | bytes 5570560 | tf_op jit(solution)/shard_map/all_to_all | solution.py:307
  367.9 35.4 %copy-start.19 = (bf16[14336,128]{1,0:T(8,128)(2,1)S(1)}, bf16[14336,128]{1,0:T(8,128)(2,1)}, u32[]{:S(2)}) copy-start(bf16[14336,128]{1,0:T(8,128)(2,1)} %get-tuple-element.127) | copy-start | bytes 11010052
  399.7 23.2 %collective-permute-start.5 = (bf16[1,3584,128]{2,1,0:T(8,128)(2,1)S(1)}, bf16[1,3584,128]{2,1,0:T(8,128)(2,1)S(1)}, u32[]{:S(2)}, u32[]{:S(2)}) collective-permute-start(bf16[1,3584,128]{2,1,0:T(8,128)(2,1)S(1)} %constant_dynamic-slice_fusion.2), channel_id=1, source_target_pairs={{0,2},{2,0},{4,6},{6,4},{8,10},{10,8},{12,14},{14,12},{16,18},{18,... | collective-permute-start | bytes 2752520 | tf_op jit(solution)/shard_map/ppermute | solution.py:304
  405.4 19.5 %collective-permute-start.3 = (bf16[1,3584,128]{2,1,0:T(8,128)(2,1)S(1)}, bf16[1,3584,128]{2,1,0:T(8,128)(2,1)S(1)}, u32[]{:S(2)}, u32[]{:S(2)}) collective-permute-start(bf16[1,3584,128]{2,1,0:T(8,128)(2,1)S(1)} %constant_dynamic-slice_fusion.4), channel_id=1, source_target_pairs={{0,4},{4,0},{2,6},{6,2},{8,12},{12,8},{10,14},{14,10},{16,20},{20,... | collective-permute-start | bytes 2752520 | tf_op jit(solution)/shard_map/ppermute | solution.py:304
  435.0 46.1 %all-to-all-start.1 = ((bf16[4,1792,128]{2,1,0:T(8,128)(2,1)}), bf16[4,1792,128]{2,1,0:T(8,128)(2,1)S(1)}, u32[]{:S(2)}, u32[]{:S(2)}) async-start(bf16[4,1792,128]{2,1,0:T(8,128)(2,1)} %pad_maximum_fusion.5), calls=%async_computation.1 | async-start | bytes 3670016 | tf_op jit(solution)/shard_map/all_to_all | solution.py:307
  439.1 8.4 %collective-permute-start.6 = (bf16[1,1360,128]{2,1,0:T(8,128)(2,1)S(1)}, bf16[1,1360,128]{2,1,0:T(8,128)(2,1)S(1)}, u32[]{:S(2)}, u32[]{:S(2)}) collective-permute-start(bf16[1,1360,128]{2,1,0:T(8,128)(2,1)S(1)} %constant_dynamic-slice_fusion.1), channel_id=1, source_target_pairs={{0,2},{2,0},{4,6},{6,4},{8,10},{10,8},{12,14},{14,12},{16,18},{18,... | collective-permute-start | bytes 1044488 | tf_op jit(solution)/shard_map/ppermute | solution.py:304
  447.6 4.6 collective-permute-start.7
  483.1 45.7 %all-to-all-start.2 = ((bf16[4,1,1792,128]{3,2,1,0:T(8,128)(2,1)}), bf16[4,1,1792,128]{3,2,1,0:T(8,128)(2,1)S(1)}, u32[]{:S(2)}, u32[]{:S(2)}) async-start(bf16[4,1,1792,128]{3,2,1,0:T(8,128)(2,1)} %broadcast_in_dim.48), calls=%async_computation.2 | async-start | bytes 3670016 | tf_op jit(solution)/shard_map/all_to_all | solution.py:307
  486.7 4.7 collective-permute-start.8
  491.5 7.5 %collective-permute-start.9 = (bf16[2,680,128]{2,1,0:T(8,128)(2,1)S(1)}, bf16[2,680,128]{2,1,0:T(8,128)(2,1)S(1)}, u32[]{:S(2)}, u32[]{:S(2)}) collective-permute-start(bf16[2,680,128]{2,1,0:T(8,128)(2,1)S(1)} %pad_maximum_fusion.15), channel_id=1, source_target_pairs={{0,2},{2,0},{4,6},{6,4},{8,10},{10,8},{12,14},{14,12},{16,18},{18,... | collective-permute-start | bytes 1044488 | tf_op jit(solution)/shard_map/ppermute | solution.py:304
  529.0 20.7 %collective-permute-start.10 = (bf16[1,3584,128]{2,1,0:T(8,128)(2,1)S(1)}, bf16[1,3584,128]{2,1,0:T(8,128)(2,1)S(1)}, u32[]{:S(2)}, u32[]{:S(2)}) collective-permute-start(bf16[1,3584,128]{2,1,0:T(8,128)(2,1)S(1)} %bitcast.269), channel_id=1, source_target_pairs={{0,4},{4,0},{2,6},{6,2},{8,12},{12,8},{10,14},{14,10},{16,20},{20,... | collective-permute-start | bytes 2752520 | tf_op jit(solution)/shard_map/ppermute | solution.py:304
  529.3 31.8 %collective-permute-start.12 = (bf16[1,3584,128]{2,1,0:T(8,128)(2,1)S(1)}, bf16[1,3584,128]{2,1,0:T(8,128)(2,1)}, u32[]{:S(2)}, u32[]{:S(2)}) collective-permute-start(bf16[1,3584,128]{2,1,0:T(8,128)(2,1)S(1)} %bitcast.267), channel_id=1, source_target_pairs={{0,2},{2,0},{4,6},{6,4},{8,10},{10,8},{12,14},{14,12},{16,18},{18,... | collective-permute-start | bytes 2752520 | tf_op jit(solution)/shard_map/ppermute | solution.py:304
  550.1 39.6 %collective-permute-start.11 = (bf16[1,7168,128]{2,1,0:T(8,128)(2,1)S(1)}, bf16[1,7168,128]{2,1,0:T(8,128)(2,1)}, u32[]{:S(2)}, u32[]{:S(2)}) collective-permute-start(bf16[1,7168,128]{2,1,0:T(8,128)(2,1)S(1)} %bitcast.240), channel_id=1, source_target_pairs={{0,2},{2,0},{4,6},{6,4},{8,10},{10,8},{12,14},{14,12},{16,18},{18,... | collective-permute-start | bytes 5505032 | tf_op jit(solution)/shard_map/ppermute | solution.py:304
  556.4 67.2 %all-to-all-start.3 = ((bf16[4,1,2720,128]{3,2,1,0:T(8,128)(2,1)}), bf16[4,1,2720,128]{3,2,1,0:T(8,128)(2,1)}, u32[]{:S(2)}, u32[]{:S(2)}) async-start(bf16[4,1,2720,128]{3,2,1,0:T(8,128)(2,1)} %broadcast_in_dim.50), calls=%async_computation.3 | async-start | bytes 5570560 | tf_op jit(solution)/shard_map/all_to_all | solution.py:307
  562.6 39.6 %collective-permute-start.13 = (bf16[1,7168,128]{2,1,0:T(8,128)(2,1)S(1)}, bf16[1,7168,128]{2,1,0:T(8,128)(2,1)S(1)}, u32[]{:S(2)}, u32[]{:S(2)}) collective-permute-start(bf16[1,7168,128]{2,1,0:T(8,128)(2,1)S(1)} %bitcast.242), channel_id=1, source_target_pairs={{0,4},{4,0},{2,6},{6,2},{8,12},{12,8},{10,14},{14,10},{16,20},{20,... | collective-permute-start | bytes 5505032 | tf_op jit(solution)/shard_map/ppermute | solution.py:304
  623.6 45.3 %copy-start.1 = (bf16[6,256,768]{2,1,0:T(8,128)(2,1)S(1)}, bf16[6,256,768]{2,1,0:T(8,128)(2,1)}, u32[]{:S(2)}) copy-start(bf16[6,256,768]{2,1,0:T(8,128)(2,1)} %param.9) | copy-start | bytes 7077892
  (121 other events, 376.6 us)
where the time goes:
time: 680 us; the launch traced here: 669 us
  waiting for transfers between devices  238 us (35%)
  matrix products  149 us (22%)
  other arithmetic  128 us (19%)
  Pallas kernels  68.5 us (10%)
  local copies, waits for them, and re-layouts  58.4 us (9%)
  starting transfers between devices  24.7 us (4%)
    ppermute x12, waiting for transfers between devices, swap(): return lax.ppermute(value, 'wide', pairs)  130 us
    all_to_all x4, waiting for transfers between devices, exchange(): return lax.all_to_all(value, 'wide', 0, 0, axis_index_groups=self.groups)  82.2 us
    pallas_call x4, Pallas kernels, pack_segment(): pl.pallas_call(kernel, out_shape=[jax.ShapeDtypeStruct((middle - first, 1...  45.8 us
    div x1, other arithmetic, adam_step(): new_first / first_bias_fix  45.3 us
    ppermute x2, waiting for transfers between devices, narrow_swap(): lax.ppermute(value, 'narrow', [(i, (i + step) % count) for i in range(cou...  26 us
    dot_general x2, matrix products, block_backward(): jnp.einsum('ctd,fd->ctf', branch_two, weights_map[prefix + 'v'], preferre...  23.9 us
    pallas_call x1, Pallas kernels, unpack(): pl.pallas_call(kernel, out_shape=out_shape, in_specs=[pl.BlockSpec(memory...  22.7 us
    convert_element_type x2, other arithmetic, gelu_and_slope(): return ((u * below).astype(jnp.bfloat16), slope.astype(jnp.bfloat16))  18.6 us
  transfers between devices with their start and end apart: 18, of which 17 were waited for; matrix products, arithmetic and copies ran while one was open for 4% of the time, Pallas kernels for 0%

commit v1 on v0

--- a/solution.py
+++ b/solution.py
@@ -173,35 +173,33 @@
     return dict(zip(labels, outs))
 
 
-def cut_points(total, unit):
-    table, used = flat_rows()
-    inner = [round_up(table[label][0], unit) for label in ("eu", "ev", "proj")]
-    return [0, *inner, round_up(total, unit)]
-
-
-def pack_segment(pieces, low, high, first, last, held):
+def pack_chunk(pieces, low, high):
     table, used = flat_rows()
     labels = [k for k, (off, rows) in table.items() if off < high and off + rows > low]
-    arrays = [
-        pieces[k] if pieces[k].ndim == 2 else pieces[k].reshape(1, -1) for k in labels
-    ]
+    arrays, places = [], []
+    for k in labels:
+        value = pieces[k] if pieces[k].ndim == 2 else pieces[k].reshape(1, -1)
+        off, rows = table[k]
+        tiles = value.shape[1] // 128
+        begin, end = 0, 1
+        if value.shape[0] > 1:
+            begin = max(0, low - off) // (8 * tiles)
+            end = -(-min(rows, high - off) // (8 * tiles))
+            if 3 * (end - begin) * 8 < value.shape[0]:
+                value = value[begin * 8 : end * 8]
+                off, end, begin = off + begin * 8 * tiles, end - begin, 0
+        arrays.append(value)
+        places.append((off, begin, end))
     length = high - low
-    middle = (first + last) // 2
-    runs = [
-        (max(low, start), min(high, end), place, start)
-        for place, (start, end) in enumerate(((first, middle), (middle, last)))
-        if max(low, start) < min(high, end)
-    ]
-    taken = len(held)
+    middle = length // 2
 
     def kernel(*refs):
-        ins, rest = refs[: len(labels)], refs[len(labels) + taken :]
+        ins, rest = refs[: len(labels)], refs[len(labels) :]
         kept, sent, flat, out, sems = rest
         if used < high:
             start = max(used, low) - low + MARGIN
             flat[start : MARGIN + length, :] = jnp.zeros((MARGIN + length - start, 128), jnp.float32)
-        for k, ref in zip(labels, ins):
-            off, rows = table[k]
+        for (off, begin, end), ref in zip(places, ins):
             tiles = ref.shape[1] // 128
             base = off - low + MARGIN
             if ref.shape[0] == 1:
@@ -211,8 +209,6 @@
                         flat[spot : spot + 1, :] = ref[:, c * 128 : (c + 1) * 128]
                 continue
             block = 8 * tiles
-            begin = max(0, low - off) // block
-            end = -(-min(rows, high - off) // block)
 
             def step(i, carry, ref=ref, tiles=tiles, base=base, block=block):
                 for c in range(tiles):
@@ -231,54 +227,45 @@
         lax.fori_loop(0, length // 128, narrow_down, 0)
         mine = lax.axis_index("narrow")
 
-        def copy(n, target):
-            start, end, place, origin = runs[n]
-            return pltpu.make_async_copy(
-                out.at[pl.ds(start - low, end - start)],
-                target.at[pl.ds(start - origin, end - start)],
-                sems.at[n],
-            )
-
-        for n, (start, end, place, origin) in enumerate(runs):
+        def copy(place, target):
+            return pltpu.make_async_copy(out.at[pl.ds(place * middle, middle)], target, sems.at[place])
+
+        for place in range(2):
 
             @pl.when(mine == place)
-            def keep(n=n):
-                copy(n, kept).start()
+            def keep(place=place):
+                copy(place, kept).start()
 
             @pl.when(mine != place)
-            def send(n=n):
-                copy(n, sent).start()
-
-        for n in range(len(runs)):
-            copy(n, kept).wait()
+            def send(place=place):
+                copy(place, sent).start()
+
+        for place in range(2):
+            copy(place, kept).wait()
 
     anywhere = pl.BlockSpec(memory_space=pl.ANY)
     whole = pl.BlockSpec(memory_space=pltpu.VMEM)
     return pl.pallas_call(
         kernel,
-        out_shape=[jax.ShapeDtypeStruct((middle - first, 128), jnp.bfloat16)] * 2,
-        in_specs=[whole] * len(arrays) + [anywhere] * taken,
+        out_shape=[jax.ShapeDtypeStruct((middle, 128), jnp.bfloat16)] * 2,
+        in_specs=[whole] * len(arrays),
         out_specs=[anywhere] * 2,
-        input_output_aliases={len(arrays) + n: n for n in range(taken)},
         scratch_shapes=[
             pltpu.VMEM((length + 2 * MARGIN, 128), jnp.float32),
             pltpu.VMEM((length, 128), jnp.bfloat16),
-            pltpu.SemaphoreType.DMA((len(runs),)),
+            pltpu.SemaphoreType.DMA((2,)),
         ],
         compiler_params=pltpu.CompilerParams(vmem_limit_bytes=61 << 20),
         name=f"pack{low}",
-    )(*arrays, *held)
-
-
-def pack_halves(pieces, cuts):
-    if lax.axis_size("narrow") == 2:
-        held = ()
-        for low, high in zip(cuts, cuts[1:]):
-            held = pack_segment(pieces, low, high, cuts[0], cuts[-1], held)
-        return held
-    flat = jnp.concatenate([pieces[k].reshape(-1) for k, dims in segment_list()])
-    flat = jnp.concatenate([flat, jnp.zeros((cuts[-1] * 128 - flat.shape[0],), jnp.float32)])
-    return (flat.reshape(-1, 128)[cuts[0] :].astype(jnp.bfloat16),)
+    )(*arrays)
+
+
+def flat_gradient(grads, unit):
+    table, used = flat_rows()
+    flat = jnp.concatenate([grads[k].reshape(-1) for k, dims in segment_list()])
+    padding = (round_up(used, unit) - used) * 128
+    flat = jnp.concatenate([flat, jnp.zeros((padding,), jnp.float32)])
+    return flat.reshape(-1, 128).astype(jnp.bfloat16)
 
 
 def added(first, second):
@@ -328,49 +315,108 @@
     return lax.ppermute(value, "narrow", [(i, (i + step) % count) for i in range(count)])
 
 
-def sum_everywhere(halves):
-    count, wide = lax.axis_size("narrow"), lax.axis_size("wide")
-    if len(halves) == 2:
-        total = added(halves[0], narrow_swap(halves[1], 1))
-    else:
-        (value,) = halves
-        mine = lax.axis_index("narrow")
-        rows = value.shape[0] // count
-        total = piece(value, mine, rows)
-        for step in range(1, count):
-            total = added(total, narrow_swap(piece(value, (mine + step) % count, rows), step))
-    rows = total.shape[0]
-    depth = wide // 4
-    x, y, z = Line(1, 2), Line(2, 2), Line(4, depth)
-    unit = wide * 8
-    units = rows // unit
-    most = units * 4 // 11
-    first, second = most * unit, 2 * most * unit
-    a = total[:first].reshape(2, 2, depth, -1, 128)
-    b = total[first:second].reshape(2, 2, depth, -1, 128)
-    c = total[second:].reshape(depth, 2, 2, -1, 128)
-    flat3 = lambda v, n: v.reshape(n, -1, 128)
-    c = z.scatter(flat3(c, depth))
-    a = x.scatter(flat3(a, 2))
-    b = y.scatter(flat3(b, 2))
-    a = y.scatter(flat3(a, 2))
-    b = x.scatter(flat3(b, 2))
-    a, b, c = lax.optimization_barrier((a, b, c))
-    ab = z.scatter(jnp.concatenate([flat3(a, depth), flat3(b, depth)], 1))
-    c = x.scatter(flat3(c, 2))
-    c = y.scatter(flat3(c, 2))
-    ab, c = lax.optimization_barrier((ab, c))
-    ab = z.gather(flat3(ab, 1))
-    c = x.gather(y.gather(flat3(c, 1)))
-    ab, c = lax.optimization_barrier((ab, c))
-    half = ab.shape[1] // 2
-    a, b = ab[:, :half], ab[:, half:]
-    c = z.gather(flat3(c, 1))
-    a = y.gather(flat3(a, 1))
-    b = x.gather(flat3(b, 1))
-    a = x.gather(flat3(a, 1))
-    b = y.gather(flat3(b, 1))
-    return jnp.concatenate([v.reshape(-1, 128) for v in (a, b, c)], 0)
+def wide_lines():
+    return Line(1, 2), Line(2, 2), Line(4, lax.axis_size("wide") // 4)
+
+
+def scatter_first(value):
+    x, y, z = wide_lines()
+    half = value.shape[0] // 2
+    a, b = value[:half].reshape(2, -1, 128), value[half:].reshape(2, -1, 128)
+    return x.scatter(a), y.scatter(b)
+
+
+def scatter_second(pair):
+    x, y, z = wide_lines()
+    return y.scatter(pair[0].reshape(2, -1, 128)), x.scatter(pair[1].reshape(2, -1, 128))
+
+
+def scatter_last(pair):
+    z = wide_lines()[2]
+    return z.scatter(jnp.concatenate([v.reshape(z.size, -1, 128) for v in pair], 1))
+
+
+def gather_first(value):
+    z = wide_lines()[2]
+    value = z.gather(value)
+    half = value.shape[1] // 2
+    return value[:, :half].reshape(1, -1, 128), value[:, half:].reshape(1, -1, 128)
+
+
+def gather_second(pair):
+    x, y, z = wide_lines()
+    return y.gather(pair[0]).reshape(1, -1, 128), x.gather(pair[1]).reshape(1, -1, 128)
+
+
+def gather_last(pair):
+    x, y, z = wide_lines()
+    a, b = x.gather(pair[0]), y.gather(pair[1])
+    return jnp.concatenate([a.reshape(-1, 128), b.reshape(-1, 128)], 0)
+
+
+def narrow_sum(halves):
+    return added(halves[0], narrow_swap(halves[1], 1))
+
+
+def sum_everywhere(value, rows):
+    count = lax.axis_size("narrow")
+    mine = lax.axis_index("narrow")
+    total = lax.dynamic_slice_in_dim(value, mine * rows, rows, 0)
+    for step in range(1, count):
+        other = lax.dynamic_slice_in_dim(value, (mine + step) % count * rows, rows, 0)
+        total = added(total, narrow_swap(other, step))
+    unit = lax.axis_size("wide") * 16
+    total = jnp.pad(total, ((0, round_up(rows, unit) - rows), (0, 0)))
+    pair = scatter_second(scatter_first(total))
+    return gather_last(gather_second(gather_first(scatter_last(pair))))[:rows]
+
+
+BLOCK = 768
+
+
+def adam_rows(parts, moment1, moment2, start, rows, held, chips_all):
+    half = parts[0].shape[0] // BLOCK
+    shift = start // BLOCK
+    steps = -(-rows // BLOCK)
+
+    def kernel(core, own_low, got_low, own_high, got_high, first, second, *rest):
+        grad_out, update, new_first, new_second = rest[len(held) :]
+        early = pl.program_id(0) < half
+        low = jnp.where(early, own_low[...], got_low[...])
+        high = jnp.where(early, got_high[...], own_high[...])
+        grad = jnp.where(core[0] == 0, low, high).astype(jnp.float32) / chips_all
+        grad_out[...] = grad
+        update[...], new_first[...], new_second[...] = adam_step(grad, first[...], second[...])
+
+    def early_rows(place):
+        return lambda i, core: (jnp.where(core[0] == place, jnp.minimum(i, half - 1), 0), 0)
+
+    def late_rows(place):
+        return lambda i, core: (jnp.where(core[0] == place, jnp.maximum(i - half, 0), 0), 0)
+
+    def spec(index_map):
+        return pl.BlockSpec((BLOCK, 128), index_map)
+
+    here = spec(lambda i, core: (i + shift, 0))
+    maps = (early_rows(0), late_rows(0), late_rows(1), early_rows(1))
+    core = lax.axis_index("narrow").astype(jnp.int32).reshape(1)
+    return pl.pallas_call(
+        kernel,
+        out_shape=[jax.ShapeDtypeStruct(moment1.shape, jnp.float32)] * 4,
+        grid_spec=pltpu.PrefetchScalarGridSpec(
+            num_scalar_prefetch=1,
+            grid=(steps,),
+            in_specs=[*[spec(m) for m in maps], here, here]
+            + [pl.BlockSpec(memory_space=pl.ANY)] * len(held),
+            out_specs=[here] * 4,
+        ),
+        input_output_aliases={7 + n: n for n in range(len(held))},
+        name=f"adam{start}",
+    )(core, *parts, moment1, moment2, *held)
+
+
+def to_owner(value, source):
+    return lax.ppermute(value, "narrow", [(source, 1 - source)])
 
 
 def whole_params(params):
@@ -406,11 +452,24 @@
     return (update, new_first, new_second)
 
 
+tail_terms = (
+    0.05025708328,
+    -0.1828833063,
+    0.1690591746,
+    -0.005588040603,
+    0.141423544,
+    0.1685436795,
+    0.2078425222,
+    0.2256696051,
+    0.2256758619,
+)
+
+
 def gelu_and_slope(u):
-    t = 1.0 / (1.0 + (0.3275911 * math.sqrt(0.5)) * jnp.abs(u))
+    t = 1.0 / (1.0 + (0.4 * math.sqrt(0.5)) * jnp.abs(u))
     bell = jnp.exp(-0.5 * u * u)
-    tail = 0.5 * 1.061405429
-    for term in (-1.453152027, 1.421413741, -0.284496736, 0.254829592):
+    tail = 0.5 * tail_terms[0]
+    for term in tail_terms[1:]:
         tail = tail * t + 0.5 * term
     tail = tail * t * bell
     below = jnp.where(u < 0, tail, 1.0 - tail)
@@ -483,54 +542,46 @@
     return (result, kept)
 
 
-def block_backward(upstream, kept, weights_map, prefix, heads):
-    (
-        stream,
-        middle,
-        first_in,
-        query_rows,
-        key_rows,
-        value_rows,
-        logsum,
-        mixed,
-        second_in,
-        slope,
-        activ,
-    ) = kept
-    chips, tokens, width = stream.shape
-    inner = heads * HD
+def norm_backward(stream, weights_map, gain_label, bias_label, upstream):
+    pull = jax.vjp(
+        layer_norm, stream, vector(weights_map, gain_label), vector(weights_map, bias_label)
+    )[1]
+    return pull(upstream)
+
+
+def mlp_backward(upstream, kept, weights_map, prefix):
+    middle, second_in, slope = kept[1], kept[8], kept[9]
     grads = {}
     branch_two = upstream.astype(jnp.bfloat16)
     grads[prefix + "vb"] = jnp.sum(branch_two.astype(jnp.float32), (0, 1))
-    grads[prefix + "v"] = jnp.einsum(
-        "ctf,ctd->fd", activ, branch_two, preferred_element_type=jnp.float32
-    )
     d_activ = jnp.einsum(
         "ctd,fd->ctf", branch_two, weights_map[prefix + "v"], preferred_element_type=jnp.float32
     )
     d_hidden = (d_activ * slope.astype(jnp.float32)).astype(jnp.bfloat16)
     grads[prefix + "ub"] = jnp.sum(d_hidden.astype(jnp.float32), (0, 1))
-    grads[prefix + "u"] = jnp.einsum(
-        "ctd,ctf->df", second_in, d_hidden, preferred_element_type=jnp.float32
-    )
     d_second = jnp.einsum(
         "ctf,df->ctd", d_hidden, weights_map[prefix + "u"], preferred_element_type=jnp.float32
     )
-    norm_pull = jax.vjp(
-        layer_norm,
-        middle,
-        vector(weights_map, prefix + "g2"),
-        vector(weights_map, prefix + "b2"),
-    )[1]
-    d_middle_part, grads[prefix + "g2"], grads[prefix + "b2"] = norm_pull(
-        d_second
-    )
-    d_middle = upstream + d_middle_part
+    d_middle_part, grads[prefix + "g2"], grads[prefix + "b2"] = norm_backward(
+        middle, weights_map, prefix + "g2", prefix + "b2", d_second
+    )
+    return upstream + d_middle_part, d_hidden, grads
+
+
+def hidden_gradient(kept, d_hidden):
+    return jnp.einsum("ctd,ctf->df", kept[8], d_hidden, preferred_element_type=jnp.float32)
+
+
+def output_gradient(kept, upstream):
+    return jnp.einsum(
+        "ctf,ctd->fd", kept[10], upstream.astype(jnp.bfloat16), preferred_element_type=jnp.float32
+    )
+
+
+def scores_backward(d_middle, kept, weights_map, prefix, heads):
+    query_rows, key_rows, value_rows, logsum = kept[3:7]
+    chips, tokens, width = d_middle.shape
     branch_one = d_middle.astype(jnp.bfloat16)
-    grads[prefix + "ob"] = jnp.sum(branch_one.astype(jnp.float32), (0, 1))
-    grads[prefix + "o"] = jnp.einsum(
-        "cti,ctd->id", mixed, branch_one, preferred_element_type=jnp.float32
-    )
     d_mixed = jnp.einsum(
         "ctd,id->cti", branch_one, weights_map[prefix + "o"], preferred_element_type=jnp.float32
     )
@@ -544,6 +595,19 @@
     d_probs = jnp.einsum("cqhe,ckhe->chqk", d_mixed, value_rows, preferred_element_type=jnp.float32)
     row_shift = jnp.sum(d_probs * probs_full, -1, keepdims=True)
     d_scores = (probs_full * (d_probs - row_shift)).astype(jnp.bfloat16)
+    return d_scores, d_value.astype(jnp.bfloat16)
+
+
+def stream_backward(d_middle, d_scores, d_value, kept, weights_map, prefix, heads):
+    stream, first_in, query_rows, key_rows, mixed = kept[0], kept[2], kept[3], kept[4], kept[7]
+    chips, tokens, width = stream.shape
+    inner = heads * HD
+    grads = {}
+    branch_one = d_middle.astype(jnp.bfloat16)
+    grads[prefix + "ob"] = jnp.sum(branch_one.astype(jnp.float32), (0, 1))
+    grads[prefix + "o"] = jnp.einsum(
+        "cti,ctd->id", mixed, branch_one, preferred_element_type=jnp.float32
+    )
     d_query = jnp.einsum(
         "chqk,ckhe->cqhe", d_scores, key_rows, preferred_element_type=jnp.float32
     ) * HD ** (-0.5)
@@ -552,26 +616,20 @@
     ) * HD ** (-0.5)
     d_triple = jnp.concatenate(
         [
-            d_query.reshape(chips, tokens, inner),
-            d_key.reshape(chips, tokens, inner),
+            d_query.reshape(chips, tokens, inner).astype(jnp.bfloat16),
+            d_key.reshape(chips, tokens, inner).astype(jnp.bfloat16),
             d_value.reshape(chips, tokens, inner),
         ],
         -1,
-    ).astype(jnp.bfloat16)
+    )
     grads[prefix + "qkv"] = jnp.einsum(
         "ctd,cte->de", first_in, d_triple, preferred_element_type=jnp.float32
     )
     d_first = jnp.einsum(
         "cte,de->ctd", d_triple, weights_map[prefix + "qkv"], preferred_element_type=jnp.float32
     )
-    first_pull = jax.vjp(
-        layer_norm,
-        stream,
-        vector(weights_map, prefix + "g1"),
-        vector(weights_map, prefix + "b1"),
-    )[1]
-    d_stream_part, grads[prefix + "g1"], grads[prefix + "b1"] = first_pull(
-        d_first
+    d_stream_part, grads[prefix + "g1"], grads[prefix + "b1"] = norm_backward(
+        stream, weights_map, prefix + "g1", prefix + "b1", d_first
     )
     return (d_middle + d_stream_part, grads)
 
@@ -605,9 +663,25 @@
         + position_table()[None]
     )
     dec_out, dec_kept = block_forward(dec_in, weights_map, "d", HDEC)
-    d_dec_in, grads = block_backward(
-        cotangent.astype(jnp.float32), dec_kept, weights_map, "d", HDEC
-    )
+    tie = lax.optimization_barrier
+    chunked = lax.axis_size("narrow") == 2 and lax.axis_size("wide") == 16
+    half_rows = params.shape[0]
+    cut = round_up(flat_rows()[0]["du"][0] - half_rows, 2 * BLOCK)
+    top = round_up(half_rows - cut, 2 * BLOCK)
+    upstream = cotangent.astype(jnp.float32)
+    d_mid, d_hidden, grads = mlp_backward(upstream, dec_kept, weights_map, "d")
+    grads["du"] = hidden_gradient(dec_kept, d_hidden)
+    grads["dv"] = output_gradient(dec_kept, upstream)
+    if chunked:
+        packed = pack_chunk(grads, half_rows + cut, half_rows + cut + top)
+        d_mid, e1 = tie((d_mid, packed))
+        e1 = scatter_first(narrow_sum(e1))
+    attention = scores_backward(d_mid, dec_kept, weights_map, "d", HDEC)
+    if chunked:
+        attention, d_mid, e1 = tie((attention, d_mid, e1))
+        e1 = scatter_last(scatter_second(e1))
+    d_dec_in, more = stream_backward(d_mid, *attention, dec_kept, weights_map, "d", HDEC)
+    grads.update(more)
     grads["mask"] = jnp.sum(mask_rows[:, :, None] * d_dec_in, (0, 1))
     d_projected = jnp.einsum("cvp,cpe->cve", choose_full, d_dec_in, precision=highest).astype(
         jnp.bfloat16
@@ -622,18 +696,67 @@
     final_pull = jax.vjp(layer_norm, patch_rows, final_gain, final_bias)[1]
     d_patch_rows, grads["fg"], grads["fb"] = final_pull(d_encoded)
     d_enc_out = jnp.concatenate([jnp.zeros((chips, 2, DE), jnp.float32), d_patch_rows], 1)
-    d_enc_in, enc_grads = block_backward(d_enc_out, enc_kept, weights_map, "e", HE)
-    grads.update(enc_grads)
+    if chunked:
+        d_enc_out, e1 = tie((d_enc_out, e1))
+    grads["ev"] = output_gradient(enc_kept, d_enc_out)
+    grads["evb"] = jnp.sum(d_enc_out.astype(jnp.bfloat16).astype(jnp.float32), (0, 1))
+    if chunked:
+        e2 = pack_chunk(grads, half_rows, half_rows + cut)
+        e1 = gather_second(gather_first(e1))
+        d_enc_out, e1, e2 = tie((d_enc_out, e1, e2))
+        e1 = gather_last(e1)
+        e2 = narrow_sum(e2)
+    d_mid, d_hidden, more = mlp_backward(d_enc_out, enc_kept, weights_map, "e")
+    grads.update(more)
+    grads["eu"] = hidden_gradient(enc_kept, d_hidden)
+    if chunked:
+        d_mid, grads["eu"], e1, e2 = tie((d_mid, grads["eu"], e1, e2))
+        l1 = pack_chunk(grads, cut, cut + top)
+        e1 = (e1, to_owner(e1, 0))
+        e2 = scatter_first(e2)
+        d_mid, e1, e2, l1 = tie((d_mid, e1, e2, l1))
+        e2 = scatter_last(scatter_second(e2))
+        l1 = scatter_first(narrow_sum(l1))
+    attention = scores_backward(d_mid, enc_kept, weights_map, "e", HE)
+    if chunked:
+        attention, d_mid, e2, l1 = tie((attention, d_mid, e2, l1))
+        e2 = gather_first(e2)
+        l1 = scatter_last(scatter_second(l1))
+    d_enc_in, more = stream_backward(d_mid, *attention, enc_kept, weights_map, "e", HE)
+    grads.update(more)
     grads["cls"] = jnp.sum(d_enc_in[:, 0, :], 0)
+    chips_all = float(chips * lax.axis_size("wide") * lax.axis_size("narrow"))
+    if chunked:
+        d_enc_in, e2, l1 = tie((d_enc_in, e2, l1))
+        l2 = pack_chunk(grads, 0, cut)
+        e2 = gather_second(e2)
+        l1 = gather_first(l1)
+        d_enc_in, e2, l1, l2 = tie((d_enc_in, e2, l1, l2))
+        e2 = gather_last(e2)
+        l1 = gather_second(l1)
+        l2 = scatter_first(narrow_sum(l2))
     patch_grad = jnp.einsum(
         "cvp,cvd->cpd", choose_full, d_enc_in[:, 2:, :], precision=highest
     ).astype(jnp.bfloat16)
-    narrow_count, wide_count = lax.axis_size("narrow"), lax.axis_size("wide")
-    chips_all = float(chips * wide_count * narrow_count)
-    cuts = cut_points(total_rows, narrow_count * wide_count * 8)
-    mine = sum_everywhere(pack_halves(grads, cuts))[: params.shape[0]]
-    grad_out = mine.astype(jnp.float32) / chips_all
-    update, new_moment1, new_moment2 = adam_step(grad_out, moment1, moment2)
+    if chunked:
+        patch_grad, e2, l1, l2 = tie((patch_grad, e2, l1, l2))
+        e2 = (e2, to_owner(e2, 0))
+        l1 = gather_last(l1)
+        l2 = scatter_last(scatter_second(l2))
+        e2, l1, l2 = tie((e2, l1, l2))
+        l1 = (l1, to_owner(l1, 1))
+        l2 = gather_first(l2)
+        l1, l2 = tie((l1, l2))
+        results = adam_rows((*l1, *e1), moment1, moment2, cut, half_rows - cut, (), chips_all)
+        l2 = gather_last(gather_second(l2))
+        l2 = (l2, to_owner(l2, 1))
+        grad_out, update, new_moment1, new_moment2 = adam_rows(
+            (*l2, *e2), moment1, moment2, 0, cut, results, chips_all
+        )
+    else:
+        every = flat_gradient(grads, half_rows * lax.axis_size("narrow"))
+        grad_out = sum_everywhere(every, half_rows).astype(jnp.float32) / chips_all
+        update, new_moment1, new_moment2 = adam_step(grad_out, moment1, moment2)
     return (dec_out.astype(jnp.bfloat16), patch_grad, grad_out, update, new_moment1, new_moment2)
 
 

time: 680 us -> 750 us (1.10)
  waiting for transfers between devices: 238 us -> 145 us
  Pallas kernels: 68.5 us -> 134 us
  starting transfers between devices: 24.7 us -> 85.1 us
  blocking collectives: 0 us -> 21.9 us
  matrix products: 149 us -> 157 us
    pallas_call x4 -> x6, Pallas kernels: 45.8 us -> 111 us  [the longest x2 68.7 us: adam_rows(): pl.pallas_call(kernel, out_shape=[jax.ShapeDtypeStruct(moment1.shape, jnp...]
    ppermute x12 -> x32, waiting for transfers between devices: 130 us -> 82.9 us  [swap(): return lax.ppermute(value, 'wide', pairs)]
    div x1 -> x0, other arithmetic: 45.3 us -> none  [adam_step(): new_first / first_bias_fix]
    concatenate x1 -> x8, other arithmetic: 1.35 us -> 42.5 us  [the longest x4 39 us: gather_last(): return jnp.concatenate([a.reshape(-1, 128), b.reshape(-1, 128)], 0)]
    all_to_all x4 -> x7, waiting for transfers between devices: 82.2 us -> 51.8 us  [exchange(): return lax.all_to_all(value, 'wide', 0, 0, axis_index_groups=self.groups)]
    all_to_all x0 -> x1, blocking collectives: none -> 21.9 us  [exchange(): return lax.all_to_all(value, 'wide', 0, 0, axis_index_groups=self.groups)]
    ppermute x12 -> x32, starting transfers between devices: 7.63 us -> 26.1 us  [swap(): return lax.ppermute(value, 'wide', pairs)]
    ppermute x0 -> x4, starting transfers between devices: none -> 17.1 us  [to_owner(): return lax.ppermute(value, 'narrow', [(source, 1 - source)])]
  transfers between devices with their start and end apart: 18 -> 48, of which waited for: 17 -> 22; matrix products, arithmetic and copies ran while one was open for 4% -> 22% of each run, Pallas kernels for 0% -> 8%
where the time goes in v1:
time: 750 us; the launch traced here: 738 us
  matrix products  157 us (21%)
  waiting for transfers between devices  145 us (19%)
  Pallas kernels  134 us (18%)
  other arithmetic  130 us (17%)
  starting transfers between devices  85.1 us (11%)
  local copies, waits for them, and re-layouts  62.9 us (8%)
  blocking collectives  21.9 us (3%)
    ppermute x32, waiting for transfers between devices, swap(): return lax.ppermute(value, 'wide', pairs)  82.9 us
    pallas_call x2, Pallas kernels, adam_rows(): pl.pallas_call(kernel, out_shape=[jax.ShapeDtypeStruct(moment1.shape, jnp...  68.7 us
    all_to_all x7, waiting for transfers between devices, exchange(): return lax.all_to_all(value, 'wide', 0, 0, axis_index_groups=self.groups)  51.8 us
    pallas_call x4, Pallas kernels, pack_chunk(): pl.pallas_call(kernel, out_shape=[jax.ShapeDtypeStruct((middle, 128), jnp...  42.1 us
    concatenate x4, other arithmetic, gather_last(): return jnp.concatenate([a.reshape(-1, 128), b.reshape(-1, 128)], 0)  39 us
    all_to_all x7, starting transfers between devices, exchange(): return lax.all_to_all(value, 'wide', 0, 0, axis_index_groups=self.groups)  29.3 us
    dot_general x2, matrix products, mlp_backward(): jnp.einsum('ctd,fd->ctf', branch_two, weights_map[prefix + 'v'], preferre...  28.6 us
    ppermute x32, starting transfers between devices, swap(): return lax.ppermute(value, 'wide', pairs)  26.1 us
  transfers between devices with their start and end apart: 48, of which 22 were waited for; matrix products, arithmetic and copies ran while one was open for 22% of the time, Pallas kernels for 8%

profile of v1, /device:TPU:1, one launch (start us, length us, event | category | flops | bytes accessed | tf_op | source)
XLA Modules:
  0.0 738.5 jit_solution(9815920832473128160)
XLA Ops:
  0.7 8.3 %convert_element_type.389.refs_0_ = bf16[39552,128]{1,0:T(8,128)(2,1)S(1)} convert(f32[39552,128]{1,0:T(8,128)} %param.15) | non-fusion elementwise | flops 5062656 | bytes 30375936 | tf_op jit(solution)/shard_map/convert_element_type | solution.py:423
  14.7 10.1 %collective-permute-done.refs_1_ = bf16[39552,128]{1,0:T(8,128)(2,1)} collective-permute-done((bf16[39552,128]{1,0:T(8,128)(2,1)S(1)}, bf16[39552,128]{1,0:T(8,128)(2,1)}, u32[]{:S(2)}, u32[]{:S(2)}) %collective-permute-start) | collective-permute-done | bytes 10125344 | tf_op jit(solution)/shard_map/ppermute | solution.py:315
  24.8 22.7 %unpack.1 = (f32[1,768]{1,0:T(1,128)}, f32[1,768]{1,0:T(1,128)}, f32[1,768]{1,0:T(1,128)}, bf16[768,2304]{1,0:T(8,128)(2,1)}, bf16[768,768]{1,0:T(8,128)(2,1)}, ...) custom-call(bf16[39552,128]{1,0:T(8,128)(2,1)} %copy-done.11, ...), custom_call_target="tpu_custom_call" | custom-call | tf_op jit(solution)/shard_map/unpack/pallas_call | solution.py:161
  58.0 4.0 convolution_convert_fusion
  78.0 5.9 multiply_convert_fusion.3
  108.0 4.5 fusion.39
  112.5 13.5 %multiply_convert_fusion = bf16[6,256,2048]{2,1,0:T(8,128)(2,1)S(1)} fusion(f32[6,256,2048]{2,1,0:T(8,128)S(1)} %get-tuple-element.307, f32[2048]{0:T(1024)S(1)} %bitcast.384, u8[256,2048]{1,0:T(8,128)(4,1)S(1)} %get-tuple-element.306), kind=kLoop, calls=%fused_computation.15 | loop fusion | flops 103809024 | bytes 19406848 | tf_op jit(solution)/shard_map/convert_element_type | solution.py:477
  126.0 17.6 %convert_reduce_fusion = (f32[2048]{0:T(1024)}, bf16[6,256,2048]{2,1,0:T(8,128)(2,1)S(1)}) fusion(f32[6,256,2048]{2,1,0:T(8,128)S(1)} %get-tuple-element.307, f32[2048]{0:T(1024)S(1)} %bitcast.385, u8[256,2048]{1,0:T(8,128)(4,1)S(1)} %get-tuple-element.306, bf16[6,256,512]{2,1,0:T(8,128)(2,1)S(1)} %copy-done.121, bf16[2048,512]{1,0:T(8,128)(2,1)S(1)} %copy-done.118), kind=kOutput, calls=%fused_computation.14 | convolution fusion | flops 3347052544 | bytes 23085056 | tf_op jit(solution)/shard_map/ctd,fd->ctf/dot_general | solution.py:557
  143.6 6.4 fusion.123
  150.0 5.4 convolution_bitcast_fusion.4.refs_0_
  157.5 5.1 convolution_bitcast_fusion.3.refs_2_
  162.6 6.1 convert_add_fusion
  168.7 9.9 %pack62592.1 = (bf16[8448,128]{1,0:T(8,128)(2,1)}, bf16[8448,128]{1,0:T(8,128)(2,1)}) custom-call(f32[512,2048]{1,0:T(8,128)} %convolution_bitcast_fusion.4.refs_0_, f32[1,2048]{1,0:T(1,128)} %bitcast.388, f32[2048,512]{1,0:T(8,128)} %convolution_bitcast_fusion.3.refs_2_, f32[1,512]{1,0:T(1,128)} %bitcast.402), custom_call_target="tpu_custom_call" | custom-call | tf_op jit(solution)/shard_map/pack62592/pallas_call | solution.py:248
  181.4 10.0 %multiply_convert_fusion.1 = bf16[6,4,256,256]{2,3,1,0:T(8,128)(2,1)} fusion(f32[6,4,256,256]{2,3,1,0:T(8,128)} %copy-done.4, f32[6,4,256]{2,1,0:T(4,128)S(1)} %bitcast.372, bf16[6,256,4,64]{1,3,2,0:T(8,128)(2,1)S(1)} %bitcast.302, bf16[6,256,4,64]{1,3,2,0:T(8,128)(2,1)} %bitcast.368), kind=kOutput, calls=%fused_computation.18 | convolution fusion | flops 415242496 | bytes 11034624 | tf_op jit(solution)/shard_map/sub | solution.py:597
  196.7 4.9 fusion.70
  204.5 4.7 collective-permute-done.3
  210.2 6.5 collective-permute-done.2
  228.5 5.3 multiply_reduce_fusion.3
  241.4 4.6 all-to-all-start
  252.0 8.3 %all-to-all-done = bf16[4,528,128]{2,1,0:T(8,128)(2,1)S(1)} async-done(((bf16[4,528,128]{2,1,0:T(8,128)(2,1)}), bf16[4,528,128]{2,1,0:T(8,128)(2,1)S(1)}, u32[]{:S(2)}, u32[]{:S(2)}) %all-to-all-start) | async-done | bytes 540704 | tf_op jit(solution)/shard_map/all_to_all | solution.py:294
  261.3 3.5 all-to-all-start.1
  267.6 4.2 convolution_bitcast_fusion.7.refs_9_
  271.9 7.2 all-to-all-done.1
  280.5 8.2 %convolution_bitcast_fusion.2.refs_0_ = f32[3072,768]{1,0:T(8,128)} fusion(bf16[6,66,3072]{2,1,0:T(8,128)(2,1)} %copy-done.50, f32[6,66,768]{2,1,0:T(8,128)S(1)} %copy-done.20), kind=kOutput, calls=%fused_computation.28 | convolution fusion | flops 1868866560 | bytes 13086720 | tf_op jit(solution)/shard_map/ctf,ctd->fd/dot_general | solution.py:576
  289.3 12.3 %pack39552.1 = (bf16[11520,128]{1,0:T(8,128)(2,1)}, bf16[11520,128]{1,0:T(8,128)(2,1)}) custom-call(f32[3072,768]{1,0:T(8,128)} %convolution_bitcast_fusion.2.refs_0_, f32[1,768]{1,0:T(1,128)} %reshape.530.refs_1_, f32[1,768]{1,0:T(1,128)} %reshape.531.refs_2_, f32[1,768]{1,0:T(1,128)} %reshape.532.refs_3_, f32[768,512]{1,0:T(8,128)} %convolution_bitcast_fusion.6.refs_4_, ...), custom_call_target="tpu_custom_call" | custom-call | tf_op jit(solution)/shard_map/pack39552/pallas_call | solution.py:248
  302.1 5.9 collective-permute-done.7
  308.2 11.0 %convert_reduce_fusion.1 = (f32[3072]{0:T(1024)}, bf16[6,66,3072]{2,1,0:T(8,128)(2,1)S(1)}) fusion(f32[6,66,3072]{2,1,0:T(8,128)} %copy-done.32, f32[3072]{0:T(1024)S(1)} %bitcast.381, u8[66,3072]{1,0:T(8,128)(4,1)S(1)} %copy-done.85, bf16[3072,768]{1,0:T(8,128)(2,1)} %get-tuple-element.117, f32[6,66,768]{2,1,0:T(8,128)S(1)} %copy-done.21), kind=kOutput, calls=%fused_computation.38 | convolution fusion | flops 1917523968 | bytes 13461504 | tf_op jit(solution)/shard_map/ctd,fd->ctf/dot_general | solution.py:557
  325.5 3.2 collective-permute-start.10
  331.0 4.9 collective-permute-done.8
  336.3 8.5 %pad_maximum_fusion.3.own_high = bf16[8448,128]{1,0:T(8,128)(2,1)} fusion(bf16[4224,128]{1,0:T(8,128)(2,1)S(1)} %bitcast.300, bf16[4224,128]{1,0:T(8,128)(2,1)S(1)} %bitcast.298), kind=kLoop, calls=%fused_computation.97 | loop fusion | flops 4325376 | bytes 4325376 | tf_op jit(solution)/shard_map/concatenate | solution.py:354
  355.3 9.5 %pack23040.1 = (bf16[8448,128]{1,0:T(8,128)(2,1)}, bf16[8448,128]{1,0:T(8,128)(2,1)}) custom-call(f32[768,3072]{1,0:T(8,128)} %copy-done.18, f32[1,3072]{1,0:T(1,128)} %bitcast.382, f32[504,768]{1,0:T(8,128)} %slice.125.refs_2_), custom_call_target="tpu_custom_call" | custom-call | tf_op jit(solution)/shard_map/pack23040/pallas_call | solution.py:248
  368.0 5.6 collective-permute-start.16
  379.1 6.6 multiply_convert_fusion.4
  388.8 4.2 all-to-all-start.2
  399.4 12.2 %all-to-all-done.2 = bf16[4,720,128]{2,1,0:T(8,128)(2,1)} async-done(((bf16[4,720,128]{2,1,0:T(8,128)(2,1)}), bf16[4,720,128]{2,1,0:T(8,128)(2,1)}, u32[]{:S(2)}, u32[]{:S(2)}) %all-to-all-start.2) | async-done | bytes 737312 | tf_op jit(solution)/shard_map/all_to_all | solution.py:294
  416.3 9.8 %collective-permute-done.17 = bf16[1,2112,128]{2,1,0:T(8,128)(2,1)S(1)} collective-permute-done((bf16[1,2112,128]{2,1,0:T(8,128)(2,1)S(1)}, bf16[1,2112,128]{2,1,0:T(8,128)(2,1)S(1)}, u32[]{:S(2)}, u32[]{:S(2)}) %collective-permute-start.17) | collective-permute-done | bytes 540704 | tf_op jit(solution)/shard_map/ppermute | solution.py:291
  440.6 3.8 collective-permute-done.19
  446.3 4.2 all-to-all-start.4
  450.5 4.2 fusion.125
  456.5 5.1 all-to-all-done.4
  462.6 4.9 all-to-all-start.3
  467.5 3.8 convert_reduce_fusion.4
  471.4 5.2 convolution_bitcast_fusion.refs_3_
  477.7 7.7 %all-to-all-done.3 = bf16[4,1,720,128]{3,2,1,0:T(8,128)(2,1)S(1)} async-done(((bf16[4,1,720,128]{3,2,1,0:T(8,128)(2,1)}), bf16[4,1,720,128]{3,2,1,0:T(8,128)(2,1)S(1)}, u32[]{:S(2)}, u32[]{:S(2)}) %all-to-all-start.3) | async-done | bytes 737312 | tf_op jit(solution)/shard_map/all_to_all | solution.py:294
  489.2 4.0 convolution_bitcast_fusion.5.refs_4_
  493.2 10.4 %pack0.1 = (bf16[11520,128]{1,0:T(8,128)(2,1)}, bf16[11520,128]{1,0:T(8,128)(2,1)}) custom-call(f32[1,768]{1,0:T(1,128)} %reshape.567.refs_0_, f32[1,768]{1,0:T(1,128)} %reshape.568.refs_1_, f32[1,768]{1,0:T(1,128)} %reshape.569.refs_2_, f32[768,2304]{1,0:T(8,128)} %convolution_bitcast_fusion.refs_3_, f32[768,768]{1,0:T(8,128)} %convolution_bitcast_fusion.5.refs_4_, ...), custom_call_target="tpu_custom_call" | custom-call | tf_op jit(solution)/shard_map/pack0/pallas_call | solution.py:248
  505.0 4.3 all-to-all-start.5
  511.6 11.2 %all-to-all-done.5 = bf16[4,1,528,128]{3,2,1,0:T(8,128)(2,1)} async-done(((bf16[4,1,528,128]{3,2,1,0:T(8,128)(2,1)}), bf16[4,1,528,128]{3,2,1,0:T(8,128)(2,1)}, u32[]{:S(2)}, u32[]{:S(2)}) %all-to-all-start.5) | async-done | bytes 540704 | tf_op jit(solution)/shard_map/all_to_all | solution.py:294
  526.9 3.5 collective-permute-start.27
  530.4 3.6 convolution_convert_fusion.1
  535.7 10.3 %collective-permute-done.23 = bf16[1,2880,128]{2,1,0:T(8,128)(2,1)S(1)} collective-permute-done((bf16[1,2880,128]{2,1,0:T(8,128)(2,1)S(1)}, bf16[1,2880,128]{2,1,0:T(8,128)(2,1)S(1)}, u32[]{:S(2)}, u32[]{:S(2)}) %collective-permute-start.23) | collective-permute-done | bytes 737312 | tf_op jit(solution)/shard_map/ppermute | solution.py:291
  550.9 11.4 %pad_maximum_fusion.own_high = bf16[11520,128]{1,0:T(8,128)(2,1)} fusion(bf16[5760,128]{1,0:T(8,128)(2,1)S(1)} %bitcast.280, bf16[5760,128]{1,0:T(8,128)(2,1)S(1)} %bitcast.277), kind=kLoop, calls=%fused_computation.84 | loop fusion | flops 5898240 | bytes 5898240 | tf_op jit(solution)/shard_map/concatenate | solution.py:354
  568.8 3.3 collective-permute-done.34
  573.2 3.7 all-to-all-start.6
  576.9 6.0 collective-permute-done.31
  585.6 7.6 %pad_maximum_fusion.4.own_low = bf16[8448,128]{1,0:T(8,128)(2,1)S(1)} fusion(bf16[4224,128]{1,0:T(8,128)(2,1)S(1)} %bitcast.301, bf16[4224,128]{1,0:T(8,128)(2,1)S(1)} %bitcast.299), kind=kLoop, calls=%fused_computation.98 | loop fusion | flops 4325376 | bytes 4325376 | tf_op jit(solution)/shard_map/concatenate | solution.py:354
  593.3 8.6 %collective-permute-start.35 = (bf16[8448,128]{1,0:T(8,128)(2,1)S(1)}, bf16[8448,128]{1,0:T(8,128)(2,1)S(1)}, u32[]{:S(2)}, u32[]{:S(2)}) collective-permute-start(bf16[8448,128]{1,0:T(8,128)(2,1)S(1)} %pad_maximum_fusion.4.own_low), channel_id=1, source_target_pairs={{1,0},{3,2},{5,4},{7,6},{9,8},{11,10},{13,12},{15,14},{17,16},{19,... | collective-permute-start | bytes 6488072 | tf_op jit(solution)/shard_map/ppermute | solution.py:419
  602.0 21.9 %all_to_all.40 = bf16[4,1,720,128]{3,2,1,0:T(8,128)(2,1)S(1)} all-to-all(bf16[4,1,720,128]{3,2,1,0:T(8,128)(2,1)S(1)} %broadcast_in_dim.62), channel_id=1, replica_groups={{0,8,16,24},{2,10,18,26},{4,12,20,28},{6,14,22,30},{1,9,17,25},{3,11,19..., dimensions={0} | all-to-all | bytes 1474560 | tf_op jit(solution)/shard_map/all_to_all | solution.py:294
  625.6 8.2 %collective-permute-done.38 = bf16[1,1440,128]{2,1,0:T(8,128)(2,1)S(1)} collective-permute-done((bf16[1,1440,128]{2,1,0:T(8,128)(2,1)S(1)}, bf16[1,1440,128]{2,1,0:T(8,128)(2,1)S(1)}, u32[]{:S(2)}, u32[]{:S(2)}) %collective-permute-start.38) | collective-permute-done | bytes 368672 | tf_op jit(solution)/shard_map/ppermute | solution.py:291
  635.8 15.1 %collective-permute-done.39 = bf16[1,2880,128]{2,1,0:T(8,128)(2,1)S(1)} collective-permute-done((bf16[1,2880,128]{2,1,0:T(8,128)(2,1)S(1)}, bf16[1,2880,128]{2,1,0:T(8,128)(2,1)S(1)}, u32[]{:S(2)}, u32[]{:S(2)}) %collective-permute-start.39) | collective-permute-done | bytes 737312 | tf_op jit(solution)/shard_map/ppermute | solution.py:291
  652.0 11.5 %pad_maximum_fusion.1.own_low = bf16[11520,128]{1,0:T(8,128)(2,1)} fusion(bf16[5760,128]{1,0:T(8,128)(2,1)S(1)} %bitcast.283, bf16[5760,128]{1,0:T(8,128)(2,1)S(1)} %bitcast.284), kind=kLoop, calls=%fused_computation.85 | loop fusion | flops 5898240 | bytes 5898240 | tf_op jit(solution)/shard_map/concatenate | solution.py:354
  663.5 5.9 collective-permute-start.40
  669.4 29.0 %adam23040.1 = (f32[39552,128]{1,0:T(8,128)}, f32[39552,128]{1,0:T(8,128)}, f32[39552,128]{1,0:T(8,128)}, f32[39552,128]{1,0:T(8,128)}) custom-call(s32[1]{0:T(128)} %bitcast.106.core, bf16[8448,128]{1,0:T(8,128)(2,1)} %copy-done.27, bf16[8448,128]{1,0:T(8,128)(2,1)} %copy-done.55, bf16[8448,128]{1,0:T(8,128)(2,1)} %pad_maximum_fusion.3.own_high, ...), custom_call_target="tpu_custom_call" | custom-call | tf_op jit(solution)/shard_map/adam23040/pallas_call | solution.py:403
  698.4 39.7 %adam0.1 = (f32[39552,128]{1,0:T(8,128)}, f32[39552,128]{1,0:T(8,128)}, f32[39552,128]{1,0:T(8,128)}, f32[39552,128]{1,0:T(8,128)}) custom-call(s32[1]{0:T(128)} %bitcast.106.core, bf16[11520,128]{1,0:T(8,128)(2,1)} %pad_maximum_fusion.1.own_low, ...), custom_call_target="tpu_custom_call", output_to_operand_aliasing={{0}: (7, {}), {1}: (8, {}), {2}: (9, {}), {3}: (10, {})} | custom-call | tf_op jit(solution)/shard_map/adam0/pallas_call | solution.py:403
  (536 shorter events, 196.6 us)
Async XLA Ops:
  9.0 15.8 %collective-permute-start = (bf16[39552,128]{1,0:T(8,128)(2,1)S(1)}, bf16[39552,128]{1,0:T(8,128)(2,1)}, u32[]{:S(2)}, u32[]{:S(2)}) collective-permute-start(bf16[39552,128]{1,0:T(8,128)(2,1)S(1)} %convert_element_type.389.refs_0_), channel_id=1, source_target_pairs={{0,1},{1,0},{2,3},{3,2},{4,5},{5,4},{6,7},{7,6},{8,9},{9,8},{10,11... | collective-permute-start | bytes 30375944 | tf_op jit(solution)/shard_map/ppermute | solution.py:315
  9.2 48.3 %copy-start.63 = (f32[6,1,768]{2,1,0:T(1,128)}, f32[6,1,768]{2,1,0:T(1,128)S(1)}, u32[]{:S(2)}) copy-start(f32[6,1,768]{2,1,0:T(1,128)S(1)} %broadcast_in_dim.44) | copy-start | bytes 55300
  14.7 42.1 %copy-start.2 = (f32[6,64,768]{2,1,0:T(8,128)S(1)}, f32[6,64,768]{2,1,0:T(8,128)}, u32[]{:S(2)}) copy-start(f32[6,64,768]{2,1,0:T(8,128)} %fusion.90) | copy-start | bytes 3538948
  178.6 12.7 %collective-permute-start.1 = (bf16[8448,128]{1,0:T(8,128)(2,1)}, bf16[8448,128]{1,0:T(8,128)(2,1)}, u32[]{:S(2)}, u32[]{:S(2)}) collective-permute-start(bf16[8448,128]{1,0:T(8,128)(2,1)} %get-tuple-element.139), channel_id=1, source_target_pairs={{0,1},{1,0},{2,3},{3,2},{4,5},{5,4},{6,7},{7,6},{8,9},{9,8},{10,11... | collective-permute-start | bytes 6488072 | tf_op jit(solution)/shard_map/ppermute | solution.py:315
  194.1 15.2 %collective-permute-start.3 = (bf16[1,2112,128]{2,1,0:T(8,128)(2,1)S(1)}, bf16[1,2112,128]{2,1,0:T(8,128)(2,1)S(1)}, u32[]{:S(2)}, u32[]{:S(2)}) collective-permute-start(bf16[1,2112,128]{2,1,0:T(8,128)(2,1)S(1)} %constant_dynamic-slice_fusion.14), channel_id=1, source_target_pairs={{0,4},{4,0},{2,6},{6,2},{8,12},{12,8},{10,14},{14,10},{16,20},{20,... | collective-permute-start | bytes 1622024 | tf_op jit(solution)/shard_map/ppermute | solution.py:291
  201.6 16.1 %copy-start.19 = (bf16[6,4,256,256]{2,3,1,0:T(8,128)(2,1)S(1)}, bf16[6,4,256,256]{2,3,1,0:T(8,128)(2,1)}, u32[]{:S(2)}) copy-start(bf16[6,4,256,256]{2,3,1,0:T(8,128)(2,1)} %multiply_convert_fusion.1) | copy-start | bytes 9437188
  201.6 16.1 %copy-start.29 = (bf16[6,256,256]{1,2,0:T(8,128)(2,1)S(1)}, bf16[6,256,256]{1,2,0:T(8,128)(2,1)}, u32[]{:S(2)}) copy-start(bf16[6,256,256]{1,2,0:T(8,128)(2,1)} %copy-done.28) | copy-start | bytes 2359300
  203.3 13.5 %collective-permute-start.2 = (bf16[1,2112,128]{2,1,0:T(8,128)(2,1)S(1)}, bf16[1,2112,128]{2,1,0:T(8,128)(2,1)S(1)}, u32[]{:S(2)}, u32[]{:S(2)}) collective-permute-start(bf16[1,2112,128]{2,1,0:T(8,128)(2,1)S(1)} %constant_dynamic-slice_fusion.15), channel_id=1, source_target_pairs={{0,2},{2,0},{4,6},{6,4},{8,10},{10,8},{12,14},{14,12},{16,18},{18,... | collective-permute-start | bytes 1622024 | tf_op jit(solution)/shard_map/ppermute | solution.py:291
  227.0 13.4 %collective-permute-start.5 = (bf16[1,1056,128]{2,1,0:T(8,128)(2,1)S(1)}, bf16[1,1056,128]{2,1,0:T(8,128)(2,1)S(1)}, u32[]{:S(2)}, u32[]{:S(2)}) collective-permute-start(bf16[1,1056,128]{2,1,0:T(8,128)(2,1)S(1)} %constant_dynamic-slice_fusion.12), channel_id=1, source_target_pairs={{0,2},{2,0},{4,6},{6,4},{8,10},{10,8},{12,14},{14,12},{16,18},{18,... | collective-permute-start | bytes 811016 | tf_op jit(solution)/shard_map/ppermute | solution.py:291
  228.3 12.2 %collective-permute-start.4 = (bf16[1,1056,128]{2,1,0:T(8,128)(2,1)S(1)}, bf16[1,1056,128]{2,1,0:T(8,128)(2,1)S(1)}, u32[]{:S(2)}, u32[]{:S(2)}) collective-permute-start(bf16[1,1056,128]{2,1,0:T(8,128)(2,1)S(1)} %constant_dynamic-slice_fusion.13), channel_id=1, source_target_pairs={{0,4},{4,0},{2,6},{6,2},{8,12},{12,8},{10,14},{14,10},{16,20},{20,... | collective-permute-start | bytes 811016 | tf_op jit(solution)/shard_map/ppermute | solution.py:291
  241.4 18.9 %all-to-all-start = ((bf16[4,528,128]{2,1,0:T(8,128)(2,1)}), bf16[4,528,128]{2,1,0:T(8,128)(2,1)S(1)}, u32[]{:S(2)}, u32[]{:S(2)}) async-start(bf16[4,528,128]{2,1,0:T(8,128)(2,1)} %pad_maximum_fusion.25), calls=%async_computation | async-start | bytes 1081344 | tf_op jit(solution)/shard_map/all_to_all | solution.py:294
  250.7 14.1 %copy-start.113 = (f32[768]{0:T(1024)S(1)}, f32[768]{0:T(1024)}, u32[]{:S(2)}) copy-start(f32[768]{0:T(1024)} %reduce.13) | copy-start | bytes 9220
  261.3 17.8 %all-to-all-start.1 = ((bf16[4,1,528,128]{3,2,1,0:T(8,128)(2,1)}), bf16[4,1,528,128]{3,2,1,0:T(8,128)(2,1)S(1)}, u32[]{:S(2)}, u32[]{:S(2)}) async-start(bf16[4,1,528,128]{3,2,1,0:T(8,128)(2,1)} %broadcast_in_dim.52), calls=%async_computation.1 | async-start | bytes 1081344 | tf_op jit(solution)/shard_map/all_to_all | solution.py:294
  279.1 22.8 %collective-permute-start.6 = (bf16[1,1056,128]{2,1,0:T(8,128)(2,1)S(1)}, bf16[1,1056,128]{2,1,0:T(8,128)(2,1)S(1)}, u32[]{:S(2)}, u32[]{:S(2)}) collective-permute-start(bf16[1,1056,128]{2,1,0:T(8,128)(2,1)S(1)} %bitcast.358), channel_id=1, source_target_pairs={{0,4},{4,0},{2,6},{6,2},{8,12},{12,8},{10,14},{14,10},{16,20},{20,... | collective-permute-start | bytes 811016 | tf_op jit(solution)/shard_map/ppermute | solution.py:291
  301.6 6.3 collective-permute-start.7
  302.0 17.2 %slice-start.2 = ((s8[4718592]{0:T(1024)(128)(4,1)}), s8[4194304]{0:T(1024)(128)(4,1)S(1)}, s32[]{:S(2)}) async-start(s8[4718592]{0:T(1024)(128)(4,1)} %bitcast.405), calls=%async_computation.10 | async-start | bytes 8388608
  324.6 29.0 %copy-start.18 = (f32[768,3072]{1,0:T(8,128)}, f32[768,3072]{1,0:T(8,128)S(1)}, u32[]{:S(2)}) copy-start(f32[768,3072]{1,0:T(8,128)S(1)} %convolution_bitcast_fusion.1.refs_0_) | copy-start | bytes 28311556
  324.6 11.3 %collective-permute-start.8 = (bf16[1,2112,128]{2,1,0:T(8,128)(2,1)S(1)}, bf16[1,2112,128]{2,1,0:T(8,128)(2,1)S(1)}, u32[]{:S(2)}, u32[]{:S(2)}) collective-permute-start(bf16[1,2112,128]{2,1,0:T(8,128)(2,1)S(1)} %bitcast.335), channel_id=1, source_target_pairs={{0,2},{2,0},{4,6},{6,4},{8,10},{10,8},{12,14},{14,12},{16,18},{18,... | collective-permute-start | bytes 1622024 | tf_op jit(solution)/shard_map/ppermute | solution.py:291
  324.9 11.1 %collective-permute-start.9 = (bf16[1,2112,128]{2,1,0:T(8,128)(2,1)S(1)}, bf16[1,2112,128]{2,1,0:T(8,128)(2,1)S(1)}, u32[]{:S(2)}, u32[]{:S(2)}) collective-permute-start(bf16[1,2112,128]{2,1,0:T(8,128)(2,1)S(1)} %bitcast.337), channel_id=1, source_target_pairs={{0,4},{4,0},{2,6},{6,2},{8,12},{12,8},{10,14},{14,10},{16,20},{20,... | collective-permute-start | bytes 1622024 | tf_op jit(solution)/shard_map/ppermute | solution.py:291
  325.5 19.4 %collective-permute-start.10 = (bf16[11520,128]{1,0:T(8,128)(2,1)S(1)}, bf16[11520,128]{1,0:T(8,128)(2,1)S(1)}, u32[]{:S(2)}, u32[]{:S(2)}) collective-permute-start(bf16[11520,128]{1,0:T(8,128)(2,1)S(1)} %copy-done.117), channel_id=1, source_target_pairs={{0,1},{1,0},{2,3},{3,2},{4,5},{5,4},{6,7},{7,6},{8,9},{9,8},{10,11... | collective-permute-start | bytes 8847368 | tf_op jit(solution)/shard_map/ppermute | solution.py:315
  345.7 22.3 %collective-permute-start.11 = (bf16[8448,128]{1,0:T(8,128)(2,1)}, bf16[8448,128]{1,0:T(8,128)(2,1)}, u32[]{:S(2)}, u32[]{:S(2)}) collective-permute-start(bf16[8448,128]{1,0:T(8,128)(2,1)} %pad_maximum_fusion.3.own_high), channel_id=1, source_target_pairs={{0,1},{2,3},{4,5},{6,7},{8,9},{10,11},{12,13},{14,15},{16,17},{18,... | collective-permute-start | bytes 6488072 | tf_op jit(solution)/shard_map/ppermute | solution.py:419
  347.3 17.5 %collective-permute-start.13 = (bf16[1,2880,128]{2,1,0:T(8,128)(2,1)S(1)}, bf16[1,2880,128]{2,1,0:T(8,128)(2,1)}, u32[]{:S(2)}, u32[]{:S(2)}) collective-permute-start(bf16[1,2880,128]{2,1,0:T(8,128)(2,1)S(1)} %constant_dynamic-slice_fusion.10), channel_id=1, source_target_pairs={{0,4},{4,0},{2,6},{6,2},{8,12},{12,8},{10,14},{14,10},{16,20},{20,... | collective-permute-start | bytes 2211848 | tf_op jit(solution)/shard_map/ppermute | solution.py:291
  349.0 17.5 %collective-permute-start.12 = (bf16[1,2880,128]{2,1,0:T(8,128)(2,1)}, bf16[1,2880,128]{2,1,0:T(8,128)(2,1)}, u32[]{:S(2)}, u32[]{:S(2)}) collective-permute-start(bf16[1,2880,128]{2,1,0:T(8,128)(2,1)} %constant_dynamic-slice_fusion.11), channel_id=1, source_target_pairs={{0,2},{2,0},{4,6},{6,4},{8,10},{10,8},{12,14},{14,12},{16,18},{18,... | collective-permute-start | bytes 2211848 | tf_op jit(solution)/shard_map/ppermute | solution.py:291
  368.0 25.0 %collective-permute-start.16 = (bf16[8448,128]{1,0:T(8,128)(2,1)}, bf16[8448,128]{1,0:T(8,128)(2,1)}, u32[]{:S(2)}, u32[]{:S(2)}) collective-permute-start(bf16[8448,128]{1,0:T(8,128)(2,1)} %get-tuple-element.164), channel_id=1, source_target_pairs={{0,1},{1,0},{2,3},{3,2},{4,5},{5,4},{6,7},{7,6},{8,9},{9,8},{10,11... | collective-permute-start | bytes 6488072 | tf_op jit(solution)/shard_map/ppermute | solution.py:315
  374.4 11.3 %collective-permute-start.14 = (bf16[1,1440,128]{2,1,0:T(8,128)(2,1)}, bf16[1,1440,128]{2,1,0:T(8,128)(2,1)}, u32[]{:S(2)}, u32[]{:S(2)}) collective-permute-start(bf16[1,1440,128]{2,1,0:T(8,128)(2,1)} %constant_dynamic-slice_fusion.9), channel_id=1, source_target_pairs={{0,4},{4,0},{2,6},{6,2},{8,12},{12,8},{10,14},{14,10},{16,20},{20,... | collective-permute-start | bytes 1105928 | tf_op jit(solution)/shard_map/ppermute | solution.py:291
  375.5 11.2 %collective-permute-start.15 = (bf16[1,1440,128]{2,1,0:T(8,128)(2,1)S(1)}, bf16[1,1440,128]{2,1,0:T(8,128)(2,1)}, u32[]{:S(2)}, u32[]{:S(2)}) collective-permute-start(bf16[1,1440,128]{2,1,0:T(8,128)(2,1)S(1)} %constant_dynamic-slice_fusion.8), channel_id=1, source_target_pairs={{0,2},{2,0},{4,6},{6,4},{8,10},{10,8},{12,14},{14,12},{16,18},{18,... | collective-permute-start | bytes 1105928 | tf_op jit(solution)/shard_map/ppermute | solution.py:291
  388.8 22.9 %all-to-all-start.2 = ((bf16[4,720,128]{2,1,0:T(8,128)(2,1)}), bf16[4,720,128]{2,1,0:T(8,128)(2,1)}, u32[]{:S(2)}, u32[]{:S(2)}) async-start(bf16[4,720,128]{2,1,0:T(8,128)(2,1)} %pad_maximum_fusion.19), calls=%async_computation.2 | async-start | bytes 1474560 | tf_op jit(solution)/shard_map/all_to_all | solution.py:294
  397.8 15.8 %copy-start.42 = (bf16[4224,128]{1,0:T(8,128)(2,1)S(1)}, bf16[4224,128]{1,0:T(8,128)(2,1)}, u32[]{:S(2)}) copy-start(bf16[4224,128]{1,0:T(8,128)(2,1)} %get-tuple-element.243) | copy-start | bytes 3244036
  397.8 17.1 %collective-permute-start.18 = (bf16[1,2112,128]{2,1,0:T(8,128)(2,1)}, bf16[1,2112,128]{2,1,0:T(8,128)(2,1)}, u32[]{:S(2)}, u32[]{:S(2)}) collective-permute-start(bf16[1,2112,128]{2,1,0:T(8,128)(2,1)} %constant_dynamic-slice_fusion.6), channel_id=1, source_target_pairs={{0,4},{4,0},{2,6},{6,2},{8,12},{12,8},{10,14},{14,10},{16,20},{20,... | collective-permute-start | bytes 1622024 | tf_op jit(solution)/shard_map/ppermute | solution.py:291
  399.4 27.7 %copy-start.26 = (bf16[6,66,768]{1,2,0:T(8,128)(2,1)S(1)}, bf16[6,66,768]{1,2,0:T(8,128)(2,1)}, u32[]{:S(2)}) copy-start(bf16[6,66,768]{1,2,0:T(8,128)(2,1)} %copy-done.25) | copy-start | bytes 1824772
  413.7 12.5 %collective-permute-start.17 = (bf16[1,2112,128]{2,1,0:T(8,128)(2,1)S(1)}, bf16[1,2112,128]{2,1,0:T(8,128)(2,1)S(1)}, u32[]{:S(2)}, u32[]{:S(2)}) collective-permute-start(bf16[1,2112,128]{2,1,0:T(8,128)(2,1)S(1)} %constant_dynamic-slice_fusion.7), channel_id=1, source_target_pairs={{0,2},{2,0},{4,6},{6,4},{8,10},{10,8},{12,14},{14,12},{16,18},{18,... | collective-permute-start | bytes 1622024 | tf_op jit(solution)/shard_map/ppermute | solution.py:291
  416.3 14.0 %copy-start.58 = (bf16[1,2112,128]{2,1,0:T(8,128)(2,1)}, bf16[1,2112,128]{2,1,0:T(8,128)(2,1)S(1)}, u32[]{:S(2)}) copy-start(bf16[1,2112,128]{2,1,0:T(8,128)(2,1)S(1)} %add_convert_fusion.14) | copy-start | bytes 1622020
  416.3 15.9 %copy-start.24 = (bf16[6,66,768]{1,2,0:T(8,128)(2,1)S(1)}, bf16[6,66,768]{1,2,0:T(8,128)(2,1)}, u32[]{:S(2)}) copy-start(bf16[6,66,768]{1,2,0:T(8,128)(2,1)} %copy-done.23) | copy-start | bytes 1824772
  416.3 15.9 %copy-start.33 = (bf16[6,12,66,66]{2,3,1,0:T(8,128)(2,1)S(1)}, bf16[6,12,66,66]{2,3,1,0:T(8,128)(2,1)}, u32[]{:S(2)}) copy-start(bf16[6,12,66,66]{2,3,1,0:T(8,128)(2,1)} %multiply_convert_fusion.4) | copy-start | bytes 1881796
  431.0 8.5 %collective-permute-start.20 = (bf16[1,1056,128]{2,1,0:T(8,128)(2,1)}, bf16[1,1056,128]{2,1,0:T(8,128)(2,1)}, u32[]{:S(2)}, u32[]{:S(2)}) collective-permute-start(bf16[1,1056,128]{2,1,0:T(8,128)(2,1)} %constant_dynamic-slice_fusion.4), channel_id=1, source_target_pairs={{0,2},{2,0},{4,6},{6,4},{8,10},{10,8},{12,14},{14,12},{16,18},{18,... | collective-permute-start | bytes 811016 | tf_op jit(solution)/shard_map/ppermute | solution.py:291
  436.6 13.9 %copy-start.79 = (f32[6,66]{1,0:T(8,128)S(1)}, f32[6,66]{1,0:T(8,128)}, u32[]{:S(2)}) copy-start(f32[6,66]{1,0:T(8,128)} %copy-done.78) | copy-start | bytes 4756
  439.0 5.4 collective-permute-start.19
  446.3 15.4 %all-to-all-start.4 = ((bf16[4,528,128]{2,1,0:T(8,128)(2,1)}), bf16[4,528,128]{2,1,0:T(8,128)(2,1)}, u32[]{:S(2)}, u32[]{:S(2)}) async-start(bf16[4,528,128]{2,1,0:T(8,128)(2,1)} %pad_maximum_fusion.28), calls=%async_computation.4 | async-start | bytes 1081344 | tf_op jit(solution)/shard_map/all_to_all | solution.py:294
  462.6 22.8 %all-to-all-start.3 = ((bf16[4,1,720,128]{3,2,1,0:T(8,128)(2,1)}), bf16[4,1,720,128]{3,2,1,0:T(8,128)(2,1)S(1)}, u32[]{:S(2)}, u32[]{:S(2)}) async-start(bf16[4,1,720,128]{3,2,1,0:T(8,128)(2,1)} %broadcast_in_dim.58), calls=%async_computation.3 | async-start | bytes 1474560 | tf_op jit(solution)/shard_map/all_to_all | solution.py:294
  485.5 23.9 %collective-permute-start.21 = (bf16[1,1440,128]{2,1,0:T(8,128)(2,1)S(1)}, bf16[1,1440,128]{2,1,0:T(8,128)(2,1)S(1)}, u32[]{:S(2)}, u32[]{:S(2)}) collective-permute-start(bf16[1,1440,128]{2,1,0:T(8,128)(2,1)S(1)} %bitcast.342), channel_id=1, source_target_pairs={{0,4},{4,0},{2,6},{6,2},{8,12},{12,8},{10,14},{14,10},{16,20},{20,... | collective-permute-start | bytes 1105928 | tf_op jit(solution)/shard_map/ppermute | solution.py:291
  503.6 7.8 %collective-permute-start.22 = (bf16[1,1440,128]{2,1,0:T(8,128)(2,1)S(1)}, bf16[1,1440,128]{2,1,0:T(8,128)(2,1)S(1)}, u32[]{:S(2)}, u32[]{:S(2)}) collective-permute-start(bf16[1,1440,128]{2,1,0:T(8,128)(2,1)S(1)} %bitcast.340), channel_id=1, source_target_pairs={{0,2},{2,0},{4,6},{6,4},{8,10},{10,8},{12,14},{14,12},{16,18},{18,... | collective-permute-start | bytes 1105928 | tf_op jit(solution)/shard_map/ppermute | solution.py:291
  505.0 17.8 %all-to-all-start.5 = ((bf16[4,1,528,128]{3,2,1,0:T(8,128)(2,1)}), bf16[4,1,528,128]{3,2,1,0:T(8,128)(2,1)}, u32[]{:S(2)}, u32[]{:S(2)}) async-start(bf16[4,1,528,128]{3,2,1,0:T(8,128)(2,1)} %broadcast_in_dim.60), calls=%async_computation.5 | async-start | bytes 1081344 | tf_op jit(solution)/shard_map/all_to_all | solution.py:294
  509.4 20.9 %copy-start.35 = (f32[6,66,768]{2,1,0:T(8,128)S(1)}, f32[6,66,768]{2,1,0:T(8,128)}, u32[]{:S(2)}) copy-start(f32[6,66,768]{2,1,0:T(8,128)} %get-tuple-element.177) | copy-start | bytes 3649540
  523.9 10.0 %collective-permute-start.25 = (bf16[1,1056,128]{2,1,0:T(8,128)(2,1)S(1)}, bf16[1,1056,128]{2,1,0:T(8,128)(2,1)S(1)}, u32[]{:S(2)}, u32[]{:S(2)}) collective-permute-start(bf16[1,1056,128]{2,1,0:T(8,128)(2,1)S(1)} %bitcast.362), channel_id=1, source_target_pairs={{0,4},{4,0},{2,6},{6,2},{8,12},{12,8},{10,14},{14,10},{16,20},{20,... | collective-permute-start | bytes 811016 | tf_op jit(solution)/shard_map/ppermute | solution.py:291
  524.8 10.0 %collective-permute-start.26 = (bf16[1,1056,128]{2,1,0:T(8,128)(2,1)S(1)}, bf16[1,1056,128]{2,1,0:T(8,128)(2,1)S(1)}, u32[]{:S(2)}, u32[]{:S(2)}) collective-permute-start(bf16[1,1056,128]{2,1,0:T(8,128)(2,1)S(1)} %bitcast.360), channel_id=1, source_target_pairs={{0,2},{2,0},{4,6},{6,4},{8,10},{10,8},{12,14},{14,12},{16,18},{18,... | collective-permute-start | bytes 811016 | tf_op jit(solution)/shard_map/ppermute | solution.py:291
  526.0 20.0 %collective-permute-start.23 = (bf16[1,2880,128]{2,1,0:T(8,128)(2,1)S(1)}, bf16[1,2880,128]{2,1,0:T(8,128)(2,1)S(1)}, u32[]{:S(2)}, u32[]{:S(2)}) collective-permute-start(bf16[1,2880,128]{2,1,0:T(8,128)(2,1)S(1)} %bitcast.317), channel_id=1, source_target_pairs={{0,2},{2,0},{4,6},{6,4},{8,10},{10,8},{12,14},{14,12},{16,18},{18,... | collective-permute-start | bytes 2211848 | tf_op jit(solution)/shard_map/ppermute | solution.py:291
  526.3 20.0 %collective-permute-start.24 = (bf16[1,2880,128]{2,1,0:T(8,128)(2,1)S(1)}, bf16[1,2880,128]{2,1,0:T(8,128)(2,1)S(1)}, u32[]{:S(2)}, u32[]{:S(2)}) collective-permute-start(bf16[1,2880,128]{2,1,0:T(8,128)(2,1)S(1)} %bitcast.319), channel_id=1, source_target_pairs={{0,4},{4,0},{2,6},{6,2},{8,12},{12,8},{10,14},{14,10},{16,20},{20,... | collective-permute-start | bytes 2211848 | tf_op jit(solution)/shard_map/ppermute | solution.py:291
  526.9 19.7 %collective-permute-start.27 = (bf16[11520,128]{1,0:T(8,128)(2,1)}, bf16[11520,128]{1,0:T(8,128)(2,1)S(1)}, u32[]{:S(2)}, u32[]{:S(2)}) collective-permute-start(bf16[11520,128]{1,0:T(8,128)(2,1)} %get-tuple-element.183), channel_id=1, source_target_pairs={{0,1},{1,0},{2,3},{3,2},{4,5},{5,4},{6,7},{7,6},{8,9},{9,8},{10,11... | collective-permute-start | bytes 8847368 | tf_op jit(solution)/shard_map/ppermute | solution.py:315
  549.2 14.6 %collective-permute-start.29 = (bf16[1,2880,128]{2,1,0:T(8,128)(2,1)S(1)}, bf16[1,2880,128]{2,1,0:T(8,128)(2,1)S(1)}, u32[]{:S(2)}, u32[]{:S(2)}) collective-permute-start(bf16[1,2880,128]{2,1,0:T(8,128)(2,1)S(1)} %constant_dynamic-slice_fusion.2), channel_id=1, source_target_pairs={{0,4},{4,0},{2,6},{6,2},{8,12},{12,8},{10,14},{14,10},{16,20},{20,... | collective-permute-start | bytes 2211848 | tf_op jit(solution)/shard_map/ppermute | solution.py:291
  549.9 14.3 %collective-permute-start.28 = (bf16[1,2880,128]{2,1,0:T(8,128)(2,1)S(1)}, bf16[1,2880,128]{2,1,0:T(8,128)(2,1)S(1)}, u32[]{:S(2)}, u32[]{:S(2)}) collective-permute-start(bf16[1,2880,128]{2,1,0:T(8,128)(2,1)S(1)} %constant_dynamic-slice_fusion.3), channel_id=1, source_target_pairs={{0,2},{2,0},{4,6},{6,4},{8,10},{10,8},{12,14},{14,12},{16,18},{18,... | collective-permute-start | bytes 2211848 | tf_op jit(solution)/shard_map/ppermute | solution.py:291
  564.4 7.6 %collective-permute-start.34 = (bf16[1,1440,128]{2,1,0:T(8,128)(2,1)S(1)}, bf16[1,1440,128]{2,1,0:T(8,128)(2,1)S(1)}, u32[]{:S(2)}, u32[]{:S(2)}) collective-permute-start(bf16[1,1440,128]{2,1,0:T(8,128)(2,1)S(1)} %constant_dynamic-slice_fusion), channel_id=1, source_target_pairs={{0,2},{2,0},{4,6},{6,4},{8,10},{10,8},{12,14},{14,12},{16,18},{18,... | collective-permute-start | bytes 1105928 | tf_op jit(solution)/shard_map/ppermute | solution.py:291
  565.6 6.6 collective-permute-start.33
  566.6 16.3 %collective-permute-start.31 = (bf16[1,2112,128]{2,1,0:T(8,128)(2,1)}, bf16[1,2112,128]{2,1,0:T(8,128)(2,1)}, u32[]{:S(2)}, u32[]{:S(2)}) collective-permute-start(bf16[1,2112,128]{2,1,0:T(8,128)(2,1)} %bitcast.102), channel_id=1, source_target_pairs={{0,2},{2,0},{4,6},{6,4},{8,10},{10,8},{12,14},{14,12},{16,18},{18,... | collective-permute-start | bytes 1622024 | tf_op jit(solution)/shard_map/ppermute | solution.py:291
  566.9 17.4 %collective-permute-start.32 = (bf16[1,2112,128]{2,1,0:T(8,128)(2,1)}, bf16[1,2112,128]{2,1,0:T(8,128)(2,1)S(1)}, u32[]{:S(2)}, u32[]{:S(2)}) collective-permute-start(bf16[1,2112,128]{2,1,0:T(8,128)(2,1)} %bitcast.103), channel_id=1, source_target_pairs={{0,4},{4,0},{2,6},{6,2},{8,12},{12,8},{10,14},{14,10},{16,20},{20,... | collective-permute-start | bytes 1622024 | tf_op jit(solution)/shard_map/ppermute | solution.py:291
  567.5 25.8 %collective-permute-start.30 = (bf16[11520,128]{1,0:T(8,128)(2,1)}, bf16[11520,128]{1,0:T(8,128)(2,1)}, u32[]{:S(2)}, u32[]{:S(2)}) collective-permute-start(bf16[11520,128]{1,0:T(8,128)(2,1)} %pad_maximum_fusion.own_high), channel_id=1, source_target_pairs={{0,1},{2,3},{4,5},{6,7},{8,9},{10,11},{12,13},{14,15},{16,17},{18,... | collective-permute-start | bytes 8847368 | tf_op jit(solution)/shard_map/ppermute | solution.py:419
  573.2 19.9 %all-to-all-start.6 = ((bf16[4,720,128]{2,1,0:T(8,128)(2,1)}), bf16[4,720,128]{2,1,0:T(8,128)(2,1)S(1)}, u32[]{:S(2)}, u32[]{:S(2)}) async-start(bf16[4,720,128]{2,1,0:T(8,128)(2,1)} %pad_maximum_fusion.22), calls=%async_computation.6 | async-start | bytes 1474560 | tf_op jit(solution)/shard_map/all_to_all | solution.py:294
  593.1 40.8 %copy-start.27 = (bf16[8448,128]{1,0:T(8,128)(2,1)}, bf16[8448,128]{1,0:T(8,128)(2,1)S(1)}, u32[]{:S(2)}) copy-start(bf16[8448,128]{1,0:T(8,128)(2,1)S(1)} %pad_maximum_fusion.4.own_low) | copy-start | bytes 6488068
  593.3 30.7 %collective-permute-start.35 = (bf16[8448,128]{1,0:T(8,128)(2,1)S(1)}, bf16[8448,128]{1,0:T(8,128)(2,1)S(1)}, u32[]{:S(2)}, u32[]{:S(2)}) collective-permute-start(bf16[8448,128]{1,0:T(8,128)(2,1)S(1)} %pad_maximum_fusion.4.own_low), channel_id=1, source_target_pairs={{1,0},{3,2},{5,4},{7,6},{9,8},{11,10},{13,12},{15,14},{17,16},{19,... | collective-permute-start | bytes 6488072 | tf_op jit(solution)/shard_map/ppermute | solution.py:419
  624.0 9.8 %collective-permute-start.38 = (bf16[1,1440,128]{2,1,0:T(8,128)(2,1)S(1)}, bf16[1,1440,128]{2,1,0:T(8,128)(2,1)S(1)}, u32[]{:S(2)}, u32[]{:S(2)}) collective-permute-start(bf16[1,1440,128]{2,1,0:T(8,128)(2,1)S(1)} %bitcast.346), channel_id=1, source_target_pairs={{0,2},{2,0},{4,6},{6,4},{8,10},{10,8},{12,14},{14,12},{16,18},{18,... | collective-permute-start | bytes 1105928 | tf_op jit(solution)/shard_map/ppermute | solution.py:291
  624.7 10.3 %collective-permute-start.36 = (bf16[1,1440,128]{2,1,0:T(8,128)(2,1)S(1)}, bf16[1,1440,128]{2,1,0:T(8,128)(2,1)S(1)}, u32[]{:S(2)}, u32[]{:S(2)}) collective-permute-start(bf16[1,1440,128]{2,1,0:T(8,128)(2,1)S(1)} %bitcast.344), channel_id=1, source_target_pairs={{0,4},{4,0},{2,6},{6,2},{8,12},{12,8},{10,14},{14,10},{16,20},{20,... | collective-permute-start | bytes 1105928 | tf_op jit(solution)/shard_map/ppermute | solution.py:291
  634.0 16.9 %collective-permute-start.39 = (bf16[1,2880,128]{2,1,0:T(8,128)(2,1)S(1)}, bf16[1,2880,128]{2,1,0:T(8,128)(2,1)S(1)}, u32[]{:S(2)}, u32[]{:S(2)}) collective-permute-start(bf16[1,2880,128]{2,1,0:T(8,128)(2,1)S(1)} %bitcast.322), channel_id=1, source_target_pairs={{0,4},{4,0},{2,6},{6,2},{8,12},{12,8},{10,14},{14,10},{16,20},{20,... | collective-permute-start | bytes 2211848 | tf_op jit(solution)/shard_map/ppermute | solution.py:291
  635.2 16.6 %collective-permute-start.37 = (bf16[1,2880,128]{2,1,0:T(8,128)(2,1)S(1)}, bf16[1,2880,128]{2,1,0:T(8,128)(2,1)S(1)}, u32[]{:S(2)}, u32[]{:S(2)}) collective-permute-start(bf16[1,2880,128]{2,1,0:T(8,128)(2,1)S(1)} %bitcast.324), channel_id=1, source_target_pairs={{0,2},{2,0},{4,6},{6,4},{8,10},{10,8},{12,14},{14,12},{16,18},{18,... | collective-permute-start | bytes 2211848 | tf_op jit(solution)/shard_map/ppermute | solution.py:291
  663.5 34.9 %collective-permute-start.40 = (bf16[11520,128]{1,0:T(8,128)(2,1)}, bf16[11520,128]{1,0:T(8,128)(2,1)}, u32[]{:S(2)}, u32[]{:S(2)}) collective-permute-start(bf16[11520,128]{1,0:T(8,128)(2,1)} %pad_maximum_fusion.1.own_low), channel_id=1, source_target_pairs={{1,0},{3,2},{5,4},{7,6},{9,8},{11,10},{13,12},{15,14},{17,16},{19,... | collective-permute-start | bytes 8847368 | tf_op jit(solution)/shard_map/ppermute | solution.py:419
  698.4 39.7 %copy-start.1 = (bf16[6,256,768]{2,1,0:T(8,128)(2,1)S(1)}, bf16[6,256,768]{2,1,0:T(8,128)(2,1)}, u32[]{:S(2)}) copy-start(bf16[6,256,768]{2,1,0:T(8,128)(2,1)} %param.9) | copy-start | bytes 7077892
  (118 other events, 597.2 us)

commit v2 on v1

--- a/solution.py
+++ b/solution.py
@@ -173,7 +173,7 @@
     return dict(zip(labels, outs))
 
 
-def pack_chunk(pieces, low, high):
+def pack_part(pieces, low, high, first, last, held=()):
     table, used = flat_rows()
     labels = [k for k, (off, rows) in table.items() if off < high and off + rows > low]
     arrays, places = [], []
@@ -191,10 +191,15 @@
         arrays.append(value)
         places.append((off, begin, end))
     length = high - low
-    middle = length // 2
+    middle = (first + last) // 2
+    runs = [
+        (max(low, start), min(high, end), place, start)
+        for place, (start, end) in enumerate(((first, middle), (middle, last)))
+        if max(low, start) < min(high, end)
+    ]
 
     def kernel(*refs):
-        ins, rest = refs[: len(labels)], refs[len(labels) :]
+        ins, rest = refs[: len(labels)], refs[len(labels) + len(held) :]
         kept, sent, flat, out, sems = rest
         if used < high:
             start = max(used, low) - low + MARGIN
@@ -227,37 +232,43 @@
         lax.fori_loop(0, length // 128, narrow_down, 0)
         mine = lax.axis_index("narrow")
 
-        def copy(place, target):
-            return pltpu.make_async_copy(out.at[pl.ds(place * middle, middle)], target, sems.at[place])
-
-        for place in range(2):
+        def copy(n, target):
+            start, end, place, origin = runs[n]
+            return pltpu.make_async_copy(
+                out.at[pl.ds(start - low, end - start)],
+                target.at[pl.ds(start - origin, end - start)],
+                sems.at[n],
+            )
+
+        for n, (start, end, place, origin) in enumerate(runs):
 
             @pl.when(mine == place)
-            def keep(place=place):
-                copy(place, kept).start()
+            def keep(n=n):
+                copy(n, kept).start()
 
             @pl.when(mine != place)
-            def send(place=place):
-                copy(place, sent).start()
-
-        for place in range(2):
-            copy(place, kept).wait()
+            def send(n=n):
+                copy(n, sent).start()
+
+        for n in range(len(runs)):
+            copy(n, kept).wait()
 
     anywhere = pl.BlockSpec(memory_space=pl.ANY)
     whole = pl.BlockSpec(memory_space=pltpu.VMEM)
     return pl.pallas_call(
         kernel,
-        out_shape=[jax.ShapeDtypeStruct((middle, 128), jnp.bfloat16)] * 2,
-        in_specs=[whole] * len(arrays),
+        out_shape=[jax.ShapeDtypeStruct((middle - first, 128), jnp.bfloat16)] * 2,
+        in_specs=[whole] * len(arrays) + [anywhere] * len(held),
         out_specs=[anywhere] * 2,
+        input_output_aliases={len(arrays) + n: n for n in range(len(held))},
         scratch_shapes=[
             pltpu.VMEM((length + 2 * MARGIN, 128), jnp.float32),
             pltpu.VMEM((length, 128), jnp.bfloat16),
-            pltpu.SemaphoreType.DMA((2,)),
+            pltpu.SemaphoreType.DMA((len(runs),)),
         ],
         compiler_params=pltpu.CompilerParams(vmem_limit_bytes=61 << 20),
         name=f"pack{low}",
-    )(*arrays)
+    )(*arrays, *held)
 
 
 def flat_gradient(grads, unit):
@@ -315,43 +326,47 @@
     return lax.ppermute(value, "narrow", [(i, (i + step) % count) for i in range(count)])
 
 
+def flat3(value, places):
+    return value.reshape(places, -1, 128)
+
+
 def wide_lines():
     return Line(1, 2), Line(2, 2), Line(4, lax.axis_size("wide") // 4)
 
 
-def scatter_first(value):
+def staged_scatter(total):
     x, y, z = wide_lines()
-    half = value.shape[0] // 2
-    a, b = value[:half].reshape(2, -1, 128), value[half:].reshape(2, -1, 128)
-    return x.scatter(a), y.scatter(b)
-
-
-def scatter_second(pair):
+    unit = lax.axis_size("wide") * 8
+    most = total.shape[0] // unit * 4 // 11
+    first, second = most * unit, 2 * most * unit
+    a = total[:first].reshape(2, 2, z.size, -1, 128)
+    b = total[first:second].reshape(2, 2, z.size, -1, 128)
+    c = total[second:].reshape(z.size, 2, 2, -1, 128)
+    c = z.scatter(flat3(c, z.size))
+    a = x.scatter(flat3(a, 2))
+    b = y.scatter(flat3(b, 2))
+    a = y.scatter(flat3(a, 2))
+    b = x.scatter(flat3(b, 2))
+    a, b, c = lax.optimization_barrier((a, b, c))
+    ab = z.scatter(jnp.concatenate([flat3(a, z.size), flat3(b, z.size)], 1))
+    c = x.scatter(flat3(c, 2))
+    c = y.scatter(flat3(c, 2))
+    return lax.optimization_barrier((ab, c))
+
+
+def staged_gather(ab, c):
     x, y, z = wide_lines()
-    return y.scatter(pair[0].reshape(2, -1, 128)), x.scatter(pair[1].reshape(2, -1, 128))
-
-
-def scatter_last(pair):
-    z = wide_lines()[2]
-    return z.scatter(jnp.concatenate([v.reshape(z.size, -1, 128) for v in pair], 1))
-
-
-def gather_first(value):
-    z = wide_lines()[2]
-    value = z.gather(value)
-    half = value.shape[1] // 2
-    return value[:, :half].reshape(1, -1, 128), value[:, half:].reshape(1, -1, 128)
-
-
-def gather_second(pair):
-    x, y, z = wide_lines()
-    return y.gather(pair[0]).reshape(1, -1, 128), x.gather(pair[1]).reshape(1, -1, 128)
-
-
-def gather_last(pair):
-    x, y, z = wide_lines()
-    a, b = x.gather(pair[0]), y.gather(pair[1])
-    return jnp.concatenate([a.reshape(-1, 128), b.reshape(-1, 128)], 0)
+    ab = z.gather(flat3(ab, 1))
+    c = x.gather(y.gather(flat3(c, 1)))
+    ab, c = lax.optimization_barrier((ab, c))
+    half = ab.shape[1] // 2
+    a, b = ab[:, :half], ab[:, half:]
+    c = z.gather(flat3(c, 1))
+    a = y.gather(flat3(a, 1))
+    b = x.gather(flat3(b, 1))
+    a = x.gather(flat3(a, 1))
+    b = y.gather(flat3(b, 1))
+    return jnp.concatenate([v.reshape(-1, 128) for v in (a, b, c)], 0)
 
 
 def narrow_sum(halves):
@@ -367,11 +382,10 @@
         total = added(total, narrow_swap(other, step))
     unit = lax.axis_size("wide") * 16
     total = jnp.pad(total, ((0, round_up(rows, unit) - rows), (0, 0)))
-    pair = scatter_second(scatter_first(total))
-    return gather_last(gather_second(gather_first(scatter_last(pair))))[:rows]
-
-
-BLOCK = 768
+    return staged_gather(*staged_scatter(total))[:rows]
+
+
+BLOCK = 2496
 
 
 def adam_rows(parts, moment1, moment2, start, rows, held, chips_all):
@@ -656,7 +670,7 @@
         "cvd,de->cve", encoded_low, weights_map["proj"], preferred_element_type=jnp.float32
     ) + vector(weights_map, "pb")
     filled = jnp.einsum("cvp,cve->cpe", choose_full, projected, precision=highest)
-    mask_rows = jnp.sum((masked[:, :, None] == patch_ids[None, None, :]).astype(jnp.float32), 1)
+    mask_rows = 1.0 - jnp.sum(choose_full, 1)
     dec_in = (
         filled
         + mask_rows[:, :, None] * vector(weights_map, "mask")[None, None, :]
@@ -666,20 +680,17 @@
     tie = lax.optimization_barrier
     chunked = lax.axis_size("narrow") == 2 and lax.axis_size("wide") == 16
     half_rows = params.shape[0]
-    cut = round_up(flat_rows()[0]["du"][0] - half_rows, 2 * BLOCK)
-    top = round_up(half_rows - cut, 2 * BLOCK)
+    padded = round_up(half_rows, 512)
+    upper = (half_rows, half_rows + padded)
     upstream = cotangent.astype(jnp.float32)
     d_mid, d_hidden, grads = mlp_backward(upstream, dec_kept, weights_map, "d")
     grads["du"] = hidden_gradient(dec_kept, d_hidden)
     grads["dv"] = output_gradient(dec_kept, upstream)
     if chunked:
-        packed = pack_chunk(grads, half_rows + cut, half_rows + cut + top)
-        d_mid, e1 = tie((d_mid, packed))
-        e1 = scatter_first(narrow_sum(e1))
+        cut = round_up(flat_rows()[0]["du"][0], 128)
+        held = pack_part(grads, cut, upper[1], *upper)
+        d_mid, held = tie((d_mid, held))
     attention = scores_backward(d_mid, dec_kept, weights_map, "d", HDEC)
-    if chunked:
-        attention, d_mid, e1 = tie((attention, d_mid, e1))
-        e1 = scatter_last(scatter_second(e1))
     d_dec_in, more = stream_backward(d_mid, *attention, dec_kept, weights_map, "d", HDEC)
     grads.update(more)
     grads["mask"] = jnp.sum(mask_rows[:, :, None] * d_dec_in, (0, 1))
@@ -696,62 +707,36 @@
     final_pull = jax.vjp(layer_norm, patch_rows, final_gain, final_bias)[1]
     d_patch_rows, grads["fg"], grads["fb"] = final_pull(d_encoded)
     d_enc_out = jnp.concatenate([jnp.zeros((chips, 2, DE), jnp.float32), d_patch_rows], 1)
-    if chunked:
-        d_enc_out, e1 = tie((d_enc_out, e1))
     grads["ev"] = output_gradient(enc_kept, d_enc_out)
     grads["evb"] = jnp.sum(d_enc_out.astype(jnp.bfloat16).astype(jnp.float32), (0, 1))
     if chunked:
-        e2 = pack_chunk(grads, half_rows, half_rows + cut)
-        e1 = gather_second(gather_first(e1))
-        d_enc_out, e1, e2 = tie((d_enc_out, e1, e2))
-        e1 = gather_last(e1)
-        e2 = narrow_sum(e2)
+        high = pack_part(grads, half_rows, cut, *upper, held)
+        d_enc_out, high = tie((d_enc_out, high))
+        high = lax.psum_scatter(narrow_sum(high), "wide", scatter_dimension=0, tiled=True)
     d_mid, d_hidden, more = mlp_backward(d_enc_out, enc_kept, weights_map, "e")
     grads.update(more)
     grads["eu"] = hidden_gradient(enc_kept, d_hidden)
     if chunked:
-        d_mid, grads["eu"], e1, e2 = tie((d_mid, grads["eu"], e1, e2))
-        l1 = pack_chunk(grads, cut, cut + top)
-        e1 = (e1, to_owner(e1, 0))
-        e2 = scatter_first(e2)
-        d_mid, e1, e2, l1 = tie((d_mid, e1, e2, l1))
-        e2 = scatter_last(scatter_second(e2))
-        l1 = scatter_first(narrow_sum(l1))
+        cut = round_up(flat_rows()[0]["eu"][0], 128)
+        held = pack_part(grads, cut, padded, 0, padded)
+        d_mid, held = tie((d_mid, held))
     attention = scores_backward(d_mid, enc_kept, weights_map, "e", HE)
-    if chunked:
-        attention, d_mid, e2, l1 = tie((attention, d_mid, e2, l1))
-        e2 = gather_first(e2)
-        l1 = scatter_last(scatter_second(l1))
     d_enc_in, more = stream_backward(d_mid, *attention, enc_kept, weights_map, "e", HE)
     grads.update(more)
     grads["cls"] = jnp.sum(d_enc_in[:, 0, :], 0)
     chips_all = float(chips * lax.axis_size("wide") * lax.axis_size("narrow"))
     if chunked:
-        d_enc_in, e2, l1 = tie((d_enc_in, e2, l1))
-        l2 = pack_chunk(grads, 0, cut)
-        e2 = gather_second(e2)
-        l1 = gather_first(l1)
-        d_enc_in, e2, l1, l2 = tie((d_enc_in, e2, l1, l2))
-        e2 = gather_last(e2)
-        l1 = gather_second(l1)
-        l2 = scatter_first(narrow_sum(l2))
+        low = pack_part(grads, 0, cut, 0, padded, held)
+        d_enc_in, high, low = tie((d_enc_in, high, low))
+        high = lax.all_gather(high, "wide", axis=0, tiled=True)
     patch_grad = jnp.einsum(
         "cvp,cvd->cpd", choose_full, d_enc_in[:, 2:, :], precision=highest
     ).astype(jnp.bfloat16)
     if chunked:
-        patch_grad, e2, l1, l2 = tie((patch_grad, e2, l1, l2))
-        e2 = (e2, to_owner(e2, 0))
-        l1 = gather_last(l1)
-        l2 = scatter_last(scatter_second(l2))
-        e2, l1, l2 = tie((e2, l1, l2))
-        l1 = (l1, to_owner(l1, 1))
-        l2 = gather_first(l2)
-        l1, l2 = tie((l1, l2))
-        results = adam_rows((*l1, *e1), moment1, moment2, cut, half_rows - cut, (), chips_all)
-        l2 = gather_last(gather_second(l2))
-        l2 = (l2, to_owner(l2, 1))
+        low = staged_gather(*staged_scatter(narrow_sum(low)))
+        parts = (low, to_owner(low, 1), high, to_owner(high, 0))
         grad_out, update, new_moment1, new_moment2 = adam_rows(
-            (*l2, *e2), moment1, moment2, 0, cut, results, chips_all
+            parts, moment1, moment2, 0, half_rows, (), chips_all
         )
     else:
         every = flat_gradient(grads, half_rows * lax.axis_size("narrow"))

time: 750 us -> 708 us (0.944)
  waiting for transfers between devices: 145 us -> 220 us
  starting transfers between devices: 85.1 us -> 37.8 us
  other arithmetic: 130 us -> 91.8 us
  blocking collectives: 21.9 us -> 0 us
  Pallas kernels: 134 us -> 113 us
  between operations: 3.35 us -> 16 us
    reduce_scatter x0 -> x1, waiting for transfers between devices: none -> 52.1 us  [per_device(): lax.psum_scatter(narrow_sum(high), 'wide', scatter_dimension=0, tiled=True)]
    all_to_all x1 -> x0, blocking collectives: 21.9 us -> none  [exchange(): return lax.all_to_all(value, 'wide', 0, 0, axis_index_groups=self.groups)]
    concatenate x8 -> x2, other arithmetic: 42.5 us -> 21.9 us  [the longest x1 21 us: staged_gather(): return jnp.concatenate([v.reshape(-1, 128) for v in (a, b, c)], 0)]
    pallas_call x2 -> x1, Pallas kernels: 68.7 us -> 49.1 us  [adam_rows(): pl.pallas_call(kernel, out_shape=[jax.ShapeDtypeStruct(moment1.shape, jnp...]
    ppermute x5 -> x3, waiting for transfers between devices: 10.1 us -> 27.1 us  [narrow_swap(): lax.ppermute(value, 'narrow', [(i, (i + step) % count) for i in range(cou...]
    sub x2 -> x0, matrix products: 16.5 us -> none  [scores_backward(): d_scores = (probs_full * (d_probs - row_shift)).astype(jnp.bfloat16)]
    all_to_all x7 -> x4, starting transfers between devices: 29.3 us -> 14.5 us  [exchange(): return lax.all_to_all(value, 'wide', 0, 0, axis_index_groups=self.groups)]
    ppermute x32 -> x12, starting transfers between devices: 26.1 us -> 13.3 us  [swap(): return lax.ppermute(value, 'wide', pairs)]
  transfers between devices with their start and end apart: 48 -> 23, of which waited for: 22 -> 20; matrix products, arithmetic and copies ran while one was open for 22% -> 17% of each run, Pallas kernels for 8% -> 3%
where the time goes in v2:
time: 708 us; the launch traced here: 697 us
  waiting for transfers between devices  220 us (31%)
  matrix products  153 us (22%)
  Pallas kernels  113 us (16%)
  other arithmetic  91.8 us (13%)
  local copies, waits for them, and re-layouts  65.9 us (9%)
  starting transfers between devices  37.8 us (5%)
  between operations  16 us (2%)
    ppermute x12, waiting for transfers between devices, swap(): return lax.ppermute(value, 'wide', pairs)  75.7 us
    all_to_all x4, waiting for transfers between devices, exchange(): return lax.all_to_all(value, 'wide', 0, 0, axis_index_groups=self.groups)  63.6 us
    reduce_scatter x1, waiting for transfers between devices, per_device(): lax.psum_scatter(narrow_sum(high), 'wide', scatter_dimension=0, tiled=True)  52.1 us
    pallas_call x1, Pallas kernels, adam_rows(): pl.pallas_call(kernel, out_shape=[jax.ShapeDtypeStruct(moment1.shape, jnp...  49.1 us
    pallas_call x4, Pallas kernels, pack_part(): pl.pallas_call(kernel, out_shape=[jax.ShapeDtypeStruct((middle - first, 1...  41.6 us
    dot_general x2, matrix products, mlp_backward(): jnp.einsum('ctd,fd->ctf', branch_two, weights_map[prefix + 'v'], preferre...  28.4 us
    ppermute x3, waiting for transfers between devices, narrow_swap(): lax.ppermute(value, 'narrow', [(i, (i + step) % count) for i in range(cou...  27.1 us
    pallas_call x1, Pallas kernels, unpack(): pl.pallas_call(kernel, out_shape=out_shape, in_specs=[pl.BlockSpec(memory...  22.7 us
  transfers between devices with their start and end apart: 23, of which 20 were waited for; matrix products, arithmetic and copies ran while one was open for 17% of the time, Pallas kernels for 3%

profile of v2, /device:TPU:1, one launch (start us, length us, event | category | flops | bytes accessed | tf_op | source)
XLA Modules:
  0.0 697.4 jit_solution(14559869365146559473)
XLA Ops:
  7.3 7.8 %convert_element_type.272.refs_0_ = bf16[39552,128]{1,0:T(8,128)(2,1)S(1)} convert(f32[39552,128]{1,0:T(8,128)} %param.14) | non-fusion elementwise | flops 5062656 | bytes 30375936 | tf_op jit(solution)/shard_map/convert_element_type | solution.py:437
  20.8 10.1 %collective-permute-done.refs_1_ = bf16[39552,128]{1,0:T(8,128)(2,1)} collective-permute-done((bf16[39552,128]{1,0:T(8,128)(2,1)S(1)}, bf16[39552,128]{1,0:T(8,128)(2,1)}, u32[]{:S(2)}, u32[]{:S(2)}) %collective-permute-start) | collective-permute-done | bytes 10125344 | tf_op jit(solution)/shard_map/ppermute | solution.py:326
  30.9 22.7 %unpack.1 = (f32[1,768]{1,0:T(1,128)}, f32[1,768]{1,0:T(1,128)}, f32[1,768]{1,0:T(1,128)}, bf16[768,2304]{1,0:T(8,128)(2,1)}, bf16[768,768]{1,0:T(8,128)(2,1)}, ...) custom-call(bf16[39552,128]{1,0:T(8,128)(2,1)} %copy-done.11, ...), custom_call_target="tpu_custom_call" | custom-call | tf_op jit(solution)/shard_map/unpack/pallas_call | solution.py:161
  57.1 4.0 convolution_convert_fusion
  64.0 2.6 copy.130
  74.7 5.1 fusion.51
  79.9 6.0 multiply_convert_fusion.3
  85.9 5.6 fusion.16
  94.1 3.3 fusion.112
  108.7 2.4 multiply_reduce_fusion.1
  117.8 4.5 fusion.32
  122.3 13.5 %multiply_convert_fusion = bf16[6,256,2048]{2,1,0:T(8,128)(2,1)S(1)} fusion(f32[6,256,2048]{2,1,0:T(8,128)S(1)} %get-tuple-element.195, f32[2048]{0:T(1024)S(1)} %bitcast.292, u8[256,2048]{1,0:T(8,128)(4,1)S(1)} %get-tuple-element.194), kind=kLoop, calls=%fused_computation.13 | loop fusion | flops 103809024 | bytes 19406848 | tf_op jit(solution)/shard_map/convert_element_type | solution.py:491
  135.8 17.5 %convert_reduce_fusion = (f32[2048]{0:T(1024)}, bf16[6,256,2048]{2,1,0:T(8,128)(2,1)S(1)}) fusion(f32[6,256,2048]{2,1,0:T(8,128)S(1)} %get-tuple-element.195, f32[2048]{0:T(1024)S(1)} %bitcast.293, u8[256,2048]{1,0:T(8,128)(4,1)S(1)} %get-tuple-element.194, bf16[6,256,512]{2,1,0:T(8,128)(2,1)S(1)} %copy-done.96, bf16[2048,512]{1,0:T(8,128)(2,1)S(1)} %copy-done.93), kind=kOutput, calls=%fused_computation.12 | convolution fusion | flops 3347052544 | bytes 23085056 | tf_op jit(solution)/shard_map/ctd,fd->ctf/dot_general | solution.py:571
  153.3 5.3 convolution_bitcast_fusion.4.refs_0_
  158.7 4.6 fusion.100
  165.4 5.0 convolution_bitcast_fusion.3.refs_2_
  170.4 6.1 convert_add_fusion
  176.5 9.9 %pack62592.1 = (bf16[19968,128]{1,0:T(8,128)(2,1)}, bf16[19968,128]{1,0:T(8,128)(2,1)}) custom-call(f32[512,2048]{1,0:T(8,128)} %convolution_bitcast_fusion.4.refs_0_, f32[1,2048]{1,0:T(1,128)} %bitcast.300, f32[2048,512]{1,0:T(8,128)} %convolution_bitcast_fusion.3.refs_2_, f32[1,512]{1,0:T(1,128)} %bitcast.310), custom_call_target="tpu_custom_call" | custom-call | tf_op jit(solution)/shard_map/pack62592/pallas_call | solution.py:258
  186.4 3.4 convolution_bitcast_fusion.8.refs_10_
  200.8 2.4 copy.98
  207.9 4.6 convolution_bitcast_fusion.7.refs_9_
  212.5 2.8 multiply_reduce_fusion.3
  225.2 5.2 convolution_bitcast_fusion.2.refs_0_
  233.8 12.4 %pack39552.1 = (bf16[19968,128]{1,0:T(8,128)(2,1)}, bf16[19968,128]{1,0:T(8,128)(2,1)}) custom-call(f32[3072,768]{1,0:T(8,128)} %convolution_bitcast_fusion.2.refs_0_, f32[1,768]{1,0:T(1,128)} %reshape.389.refs_1_, f32[1,768]{1,0:T(1,128)} %reshape.390.refs_2_, f32[1,768]{1,0:T(1,128)} %reshape.391.refs_3_, ...), custom_call_target="tpu_custom_call", output_to_operand_aliasing={{0}: (15, {}), {1}: (16, {})} | custom-call | tf_op jit(solution)/shard_map/pack39552/pallas_call | solution.py:258
  246.3 8.6 %collective-permute-done.1 = bf16[19968,128]{1,0:T(8,128)(2,1)S(1)} collective-permute-done((bf16[19968,128]{1,0:T(8,128)(2,1)}, bf16[19968,128]{1,0:T(8,128)(2,1)S(1)}, u32[]{:S(2)}, u32[]{:S(2)}) %collective-permute-start.1) | collective-permute-done | bytes 5111840 | tf_op jit(solution)/shard_map/ppermute | solution.py:326
  254.9 6.2 add_convert_fusion.1
  261.2 2.7 slice.77.refs_2_
  263.9 11.0 %convert_reduce_fusion.1 = (f32[3072]{0:T(1024)}, bf16[6,66,3072]{2,1,0:T(8,128)(2,1)S(1)}) fusion(f32[6,66,3072]{2,1,0:T(8,128)} %copy-done.25, f32[3072]{0:T(1024)S(1)} %bitcast.289, u8[66,3072]{1,0:T(8,128)(4,1)S(1)} %copy-done.58, bf16[3072,768]{1,0:T(8,128)(2,1)} %get-tuple-element.76, f32[6,66,768]{2,1,0:T(8,128)S(1)} %get-tuple-element.101), kind=kOutput, calls=%fused_computation.35 | convolution fusion | flops 1917523968 | bytes 13461504 | tf_op jit(solution)/shard_map/ctd,fd->ctf/dot_general | solution.py:571
  274.9 2.8 convolution_bitcast_fusion.1.refs_0_
  277.7 3.7 copy-done.21
  282.1 10.4 %pack18560.1 = (bf16[19968,128]{1,0:T(8,128)(2,1)}, bf16[19968,128]{1,0:T(8,128)(2,1)}) custom-call(f32[768,3072]{1,0:T(8,128)} %copy-done.21, f32[1,3072]{1,0:T(1,128)} %bitcast.290, f32[504,768]{1,0:T(8,128)} %slice.77.refs_2_), custom_call_target="tpu_custom_call" | custom-call | tf_op jit(solution)/shard_map/pack18560/pallas_call | solution.py:258
  292.6 5.7 fusion.101
  303.0 2.7 multiply_reduce_fusion.9
  310.7 3.6 multiply_convert_fusion.5
  316.7 3.1 convolution_convert_fusion.3
  321.5 4.7 fusion.102
  335.1 5.2 convolution_bitcast_fusion.refs_3_
  340.3 8.9 %pack0.1 = (bf16[19968,128]{1,0:T(8,128)(2,1)}, bf16[19968,128]{1,0:T(8,128)(2,1)}) custom-call(f32[1,768]{1,0:T(1,128)} %reshape.402.refs_0_, f32[1,768]{1,0:T(1,128)} %reshape.403.refs_1_, f32[1,768]{1,0:T(1,128)} %reshape.404.refs_2_, f32[768,2304]{1,0:T(8,128)} %convolution_bitcast_fusion.refs_3_, ...), custom_call_target="tpu_custom_call", output_to_operand_aliasing={{0}: (9, {}), {1}: (10, {})} | custom-call | tf_op jit(solution)/shard_map/pack0/pallas_call | solution.py:258
  349.2 52.1 %reduce-scatter.2.cloned.1.call-done = bf16[1248,128]{1,0:T(8,128)(2,1)} async-done(((bf16[19968,128]{1,0:T(8,128)(2,1)}), bf16[1248,128]{1,0:T(8,128)(2,1)}) %reduce-scatter.2.cloned.1.call-update) | async-done | bytes 319504 | tf_op jit(solution)/shard_map/reduce_scatter | solution.py:715
  403.8 8.4 %collective-permute-done.2 = bf16[19968,128]{1,0:T(8,128)(2,1)} collective-permute-done((bf16[19968,128]{1,0:T(8,128)(2,1)}, bf16[19968,128]{1,0:T(8,128)(2,1)}, u32[]{:S(2)}, u32[]{:S(2)}) %collective-permute-start.2) | collective-permute-done | bytes 5111840 | tf_op jit(solution)/shard_map/ppermute | solution.py:326
  412.2 7.5 %add_convert_fusion = bf16[19968,128]{1,0:T(8,128)(2,1)} fusion(bf16[19968,128]{1,0:T(8,128)(2,1)} %collective-permute-done.2, bf16[19968,128]{1,0:T(8,128)(2,1)} %get-tuple-element.112), kind=kLoop, calls=%fused_computation.14 | loop fusion | flops 10223616 | bytes 15335424 | tf_op jit(solution)/shard_map/convert_element_type | solution.py:283
  425.5 2.6 slice.82
  429.6 4.0 all-to-all-start
  433.6 17.1 %collective-permute-done.5 = bf16[1,3584,128]{2,1,0:T(8,128)(2,1)} collective-permute-done((bf16[1,3584,128]{2,1,0:T(8,128)(2,1)}, bf16[1,3584,128]{2,1,0:T(8,128)(2,1)}, u32[]{:S(2)}, u32[]{:S(2)}) %collective-permute-start.5) | collective-permute-done | bytes 917536 | tf_op jit(solution)/shard_map/ppermute | solution.py:302
  453.8 6.0 collective-permute-done.3
  461.5 7.9 %collective-permute-done.6 = bf16[1,1792,128]{2,1,0:T(8,128)(2,1)S(1)} collective-permute-done((bf16[1,1792,128]{2,1,0:T(8,128)(2,1)S(1)}, bf16[1,1792,128]{2,1,0:T(8,128)(2,1)S(1)}, u32[]{:S(2)}, u32[]{:S(2)}) %collective-permute-start.6) | collective-permute-done | bytes 458784 | tf_op jit(solution)/shard_map/ppermute | solution.py:302
  470.9 8.7 %all-to-all-done = bf16[4,1408,128]{2,1,0:T(8,128)(2,1)S(1)} async-done(((bf16[4,1408,128]{2,1,0:T(8,128)(2,1)}), bf16[4,1408,128]{2,1,0:T(8,128)(2,1)S(1)}, u32[]{:S(2)}, u32[]{:S(2)}) %all-to-all-start) | async-done | bytes 1441824 | tf_op jit(solution)/shard_map/all_to_all | solution.py:305
  481.0 3.5 all-to-all-start.1
  485.8 9.2 %collective-permute-done.7 = bf16[1,704,128]{2,1,0:T(8,128)(2,1)S(1)} collective-permute-done((bf16[1,704,128]{2,1,0:T(8,128)(2,1)S(1)}, bf16[1,704,128]{2,1,0:T(8,128)(2,1)S(1)}, u32[]{:S(2)}, u32[]{:S(2)}) %collective-permute-start.7) | collective-permute-done | bytes 180256 | tf_op jit(solution)/shard_map/ppermute | solution.py:302
  496.3 4.9 collective-permute-done.8
  501.2 27.8 %all-to-all-done.1 = bf16[4,896,128]{2,1,0:T(8,128)(2,1)S(1)} async-done(((bf16[4,896,128]{2,1,0:T(8,128)(2,1)}), bf16[4,896,128]{2,1,0:T(8,128)(2,1)S(1)}, u32[]{:S(2)}, u32[]{:S(2)}) %all-to-all-start.1) | async-done | bytes 917536 | tf_op jit(solution)/shard_map/all_to_all | solution.py:305
  530.3 3.5 all-to-all-start.2
  535.1 2.6 collective-permute-done.9
  538.9 3.7 collective-permute-done.10
  542.6 13.7 %all-to-all-done.2 = bf16[4,1,896,128]{3,2,1,0:T(8,128)(2,1)S(1)} async-done(((bf16[4,1,896,128]{3,2,1,0:T(8,128)(2,1)}), bf16[4,1,896,128]{3,2,1,0:T(8,128)(2,1)S(1)}, u32[]{:S(2)}, u32[]{:S(2)}) %all-to-all-start.2) | async-done | bytes 917536 | tf_op jit(solution)/shard_map/all_to_all | solution.py:305
  558.8 8.5 %collective-permute-done.11 = bf16[1,1792,128]{2,1,0:T(8,128)(2,1)S(1)} collective-permute-done((bf16[1,1792,128]{2,1,0:T(8,128)(2,1)S(1)}, bf16[1,1792,128]{2,1,0:T(8,128)(2,1)S(1)}, u32[]{:S(2)}, u32[]{:S(2)}) %collective-permute-start.11) | collective-permute-done | bytes 458784 | tf_op jit(solution)/shard_map/ppermute | solution.py:302
  571.3 3.6 all-to-all-start.3
  577.4 10.2 %collective-permute-done.12 = bf16[1,3584,128]{2,1,0:T(8,128)(2,1)} collective-permute-done((bf16[1,3584,128]{2,1,0:T(8,128)(2,1)S(1)}, bf16[1,3584,128]{2,1,0:T(8,128)(2,1)}, u32[]{:S(2)}, u32[]{:S(2)}) %collective-permute-start.12) | collective-permute-done | bytes 917536 | tf_op jit(solution)/shard_map/ppermute | solution.py:302
  589.1 4.4 collective-permute-done.14
  595.0 13.4 %all-to-all-done.3 = bf16[4,1,1408,128]{3,2,1,0:T(8,128)(2,1)S(1)} async-done(((bf16[4,1,1408,128]{3,2,1,0:T(8,128)(2,1)}), bf16[4,1,1408,128]{3,2,1,0:T(8,128)(2,1)S(1)}, u32[]{:S(2)}, u32[]{:S(2)}) %all-to-all-start.3) | async-done | bytes 1441824 | tf_op jit(solution)/shard_map/all_to_all | solution.py:305
  608.4 21.0 %pad_maximum_fusion.own_low = bf16[19968,128]{1,0:T(8,128)(2,1)} fusion(bf16[5632,128]{1,0:T(8,128)(2,1)S(1)} %bitcast.242, bf16[7168,128]{1,0:T(8,128)(2,1)} %bitcast.231, bf16[7168,128]{1,0:T(8,128)(2,1)S(1)} %bitcast.230), kind=kLoop, calls=%fused_computation.39 | loop fusion | flops 15335424 | bytes 10223616 | tf_op jit(solution)/shard_map/concatenate | solution.py:369
  629.3 5.9 collective-permute-start.15
  635.2 4.9 convolution_convert_fusion.1
  641.3 49.1 %adam0.1 = (f32[39552,128]{1,0:T(8,128)}, f32[39552,128]{1,0:T(8,128)}, f32[39552,128]{1,0:T(8,128)}, f32[39552,128]{1,0:T(8,128)}) custom-call(s32[1]{0:T(128)} %bitcast.61.core, bf16[19968,128]{1,0:T(8,128)(2,1)} %pad_maximum_fusion.own_low, bf16[19968,128]{1,0:T(8,128)(2,1)} %collective-permute-done.15.got_low, ...), custom_call_target="tpu_custom_call" | custom-call | tf_op jit(solution)/shard_map/adam0/pallas_call | solution.py:417
  (375 shorter events, 130.9 us)
Async XLA Ops:
  7.2 12.1 %copy-start = (bf16[6,256,768]{2,1,0:T(8,128)(2,1)S(1)}, bf16[6,256,768]{2,1,0:T(8,128)(2,1)}, u32[]{:S(2)}) copy-start(bf16[6,256,768]{2,1,0:T(8,128)(2,1)} %param.9) | copy-start | bytes 7077892
  7.2 8.0 %copy-start.103 = (s32[6]{0:T(128)S(1)}, s32[6]{0:T(128)}, u32[]{:S(2)}) copy-start(s32[6]{0:T(128)} %param.12) | copy-start | bytes 76
  7.2 8.0 %copy-start.79 = (bf16[6,768]{1,0:T(8,128)(2,1)S(1)}, bf16[6,768]{1,0:T(8,128)(2,1)}, u32[]{:S(2)}) copy-start(bf16[6,768]{1,0:T(8,128)(2,1)} %param.10) | copy-start | bytes 27652
  7.2 8.1 %copy-start.63 = (s32[6,64]{1,0:T(8,128)S(1)}, s32[6,64]{1,0:T(8,128)}, u32[]{:S(2)}) copy-start(s32[6,64]{1,0:T(8,128)} %param.11) | copy-start | bytes 4612
  7.2 394.1 %reduce-scatter.2.cloned.1.call-start = ((), (), s32[]{:S(2)}) async-start(), calls=%async_computation.5 | async-start | bytes 5431296 | tf_op jit(solution)/shard_map/reduce_scatter | solution.py:715
  15.1 15.8 %collective-permute-start = (bf16[39552,128]{1,0:T(8,128)(2,1)S(1)}, bf16[39552,128]{1,0:T(8,128)(2,1)}, u32[]{:S(2)}, u32[]{:S(2)}) collective-permute-start(bf16[39552,128]{1,0:T(8,128)(2,1)S(1)} %convert_element_type.272.refs_0_), channel_id=1, source_target_pairs={{0,1},{1,0},{2,3},{3,2},{4,5},{5,4},{6,7},{7,6},{8,9},{9,8},{10,11... | collective-permute-start | bytes 30375944 | tf_op jit(solution)/shard_map/ppermute | solution.py:326
  15.3 56.8 %copy-start.41 = (f32[6,1,768]{2,1,0:T(1,128)}, f32[6,1,768]{2,1,0:T(1,128)S(1)}, u32[]{:S(2)}) copy-start(f32[6,1,768]{2,1,0:T(1,128)S(1)} %broadcast_in_dim.36) | copy-start | bytes 55300
  20.8 33.6 %copy-start.5 = (f32[6,64,768]{2,1,0:T(8,128)S(1)}, f32[6,64,768]{2,1,0:T(8,128)}, u32[]{:S(2)}) copy-start(f32[6,64,768]{2,1,0:T(8,128)} %fusion.65) | copy-start | bytes 3538948
  54.4 17.7 %copy-start.43 = (f32[6,1,768]{2,1,0:T(1,128)}, f32[6,1,768]{2,1,0:T(1,128)S(1)}, u32[]{:S(2)}) copy-start(f32[6,1,768]{2,1,0:T(1,128)S(1)} %broadcast_in_dim.35) | copy-start | bytes 55300
  54.7 6.4 copy-start.51
  55.7 5.5 copy-start.53
  62.4 5.8 copy-start.89
  64.0 6.4 copy-start.19
  73.6 18.0 %copy-start.12 = (f32[6,66,768]{2,1,0:T(8,128)}, f32[6,66,768]{2,1,0:T(8,128)S(1)}, u32[]{:S(2)}) copy-start(f32[6,66,768]{2,1,0:T(8,128)S(1)} %get-tuple-element.185) | copy-start | bytes 3649540
  73.6 6.2 copy-start.64
  74.6 5.2 copy-start.66
  74.6 5.2 copy-start.68
  74.7 5.2 copy-start.82
  79.9 6.0 copy-start.25
  79.9 6.0 copy-start.57
  85.9 5.6 copy-start.34
  92.3 5.1 copy-start.74
  97.4 17.9 %copy-start.7 = (f32[6,256,512]{2,1,0:T(8,128)}, f32[6,256,512]{2,1,0:T(8,128)S(1)}, u32[]{:S(2)}) copy-start(f32[6,256,512]{2,1,0:T(8,128)S(1)} %get-tuple-element.189) | copy-start | bytes 9437188
  122.3 13.5 %copy-start.93 = (bf16[2048,512]{1,0:T(8,128)(2,1)S(1)}, bf16[2048,512]{1,0:T(8,128)(2,1)}, u32[]{:S(2)}) copy-start(bf16[2048,512]{1,0:T(8,128)(2,1)} %get-tuple-element.92) | copy-start | bytes 6291460
  122.3 13.5 %copy-start.96 = (bf16[6,256,512]{2,1,0:T(8,128)(2,1)S(1)}, bf16[6,256,512]{2,1,0:T(8,128)(2,1)}, u32[]{:S(2)}) copy-start(bf16[6,256,512]{2,1,0:T(8,128)(2,1)} %param.13) | copy-start | bytes 4718596
  153.3 5.4 copy-start.95
  165.4 5.0 copy-start.101
  176.5 9.9 %copy-start.31 = (bf16[6,4,64,256]{3,2,1,0:T(8,128)(2,1)S(1)}, bf16[6,4,64,256]{3,2,1,0:T(8,128)(2,1)}, u32[]{:S(2)}) copy-start(bf16[6,4,64,256]{3,2,1,0:T(8,128)(2,1)} %copy-done.30) | copy-start | bytes 2359300
  176.5 14.0 %slice-start = ((s8[6291456]{0:T(1024)(128)(4,1)}), s8[2097152]{0:T(1024)(128)(4,1)S(1)}, s32[]{:S(2)}) async-start(s8[6291456]{0:T(1024)(128)(4,1)} %bitcast.222), calls=%async_computation.7 | async-start | bytes 4194304
  200.8 7.0 %copy-start.8 = (f32[6,256,512]{2,1,0:T(8,128)S(1)}, f32[6,256,512]{2,1,0:T(8,128)}, u32[]{:S(2)}) copy-start(f32[6,256,512]{2,1,0:T(8,128)} %copy-done.7) | copy-start | bytes 9437188
  246.1 8.7 %collective-permute-start.1 = (bf16[19968,128]{1,0:T(8,128)(2,1)}, bf16[19968,128]{1,0:T(8,128)(2,1)S(1)}, u32[]{:S(2)}, u32[]{:S(2)}) collective-permute-start(bf16[19968,128]{1,0:T(8,128)(2,1)} %get-tuple-element.106), channel_id=1, source_target_pairs={{0,1},{1,0},{2,3},{3,2},{4,5},{5,4},{6,7},{7,6},{8,9},{9,8},{10,11... | collective-permute-start | bytes 15335432 | tf_op jit(solution)/shard_map/ppermute | solution.py:326
  261.1 307.7 %all-gather.2.cloned.1.call-start = ((), (), s32[]{:S(2)}) async-start(), calls=%async_computation.6 | async-start | bytes 5431296 | tf_op jit(solution)/shard_map/all_gather | solution.py:731
  263.9 11.0 %copy-start.13 = (f32[6,66,768]{2,1,0:T(8,128)S(1)}, f32[6,66,768]{2,1,0:T(8,128)}, u32[]{:S(2)}) copy-start(f32[6,66,768]{2,1,0:T(8,128)} %copy-done.12) | copy-start | bytes 3649540
  263.9 11.0 %copy-start.65 = (f32[6,66]{1,0:T(8,128)S(1)}, f32[6,66]{1,0:T(8,128)}, u32[]{:S(2)}) copy-start(f32[6,66]{1,0:T(8,128)} %copy-done.64) | copy-start | bytes 4756
  263.9 11.0 %copy-start.67 = (f32[6,66]{1,0:T(8,128)S(1)}, f32[6,66]{1,0:T(8,128)}, u32[]{:S(2)}) copy-start(f32[6,66]{1,0:T(8,128)} %copy-done.66) | copy-start | bytes 4756
  263.9 11.0 %copy-start.69 = (f32[768]{0:T(1024)S(1)}, f32[768]{0:T(1024)}, u32[]{:S(2)}) copy-start(f32[768]{0:T(1024)} %copy-done.68) | copy-start | bytes 9220
  263.9 11.0 %copy-start.83 = (f32[768]{0:T(1024)S(1)}, f32[768]{0:T(1024)}, u32[]{:S(2)}) copy-start(f32[768]{0:T(1024)} %copy-done.82) | copy-start | bytes 9220
  292.5 5.8 copy-start.73
  316.7 4.8 copy-start.44
  316.7 4.8 copy-start.52
  316.7 4.8 copy-start.56
  327.1 5.7 copy-start.38
  328.2 6.9 copy-start.36
  328.2 6.9 copy-start.60
  401.4 10.8 %collective-permute-start.2 = (bf16[19968,128]{1,0:T(8,128)(2,1)}, bf16[19968,128]{1,0:T(8,128)(2,1)}, u32[]{:S(2)}, u32[]{:S(2)}) collective-permute-start(bf16[19968,128]{1,0:T(8,128)(2,1)} %get-tuple-element.113), channel_id=1, source_target_pairs={{0,1},{1,0},{2,3},{3,2},{4,5},{5,4},{6,7},{7,6},{8,9},{9,8},{10,11... | collective-permute-start | bytes 15335432 | tf_op jit(solution)/shard_map/ppermute | solution.py:326
  424.3 26.4 %collective-permute-start.5 = (bf16[1,3584,128]{2,1,0:T(8,128)(2,1)}, bf16[1,3584,128]{2,1,0:T(8,128)(2,1)}, u32[]{:S(2)}, u32[]{:S(2)}) collective-permute-start(bf16[1,3584,128]{2,1,0:T(8,128)(2,1)} %constant_dynamic-slice_fusion.3), channel_id=1, source_target_pairs={{0,4},{4,0},{2,6},{6,2},{8,12},{12,8},{10,14},{14,10},{16,20},{20,... | collective-permute-start | bytes 2752520 | tf_op jit(solution)/shard_map/ppermute | solution.py:302
  429.0 30.7 %collective-permute-start.3 = (bf16[1,3584,128]{2,1,0:T(8,128)(2,1)}, bf16[1,3584,128]{2,1,0:T(8,128)(2,1)}, u32[]{:S(2)}, u32[]{:S(2)}) collective-permute-start(bf16[1,3584,128]{2,1,0:T(8,128)(2,1)} %constant_dynamic-slice_fusion.5), channel_id=1, source_target_pairs={{0,2},{2,0},{4,6},{6,4},{8,10},{10,8},{12,14},{14,12},{16,18},{18,... | collective-permute-start | bytes 2752520 | tf_op jit(solution)/shard_map/ppermute | solution.py:302
  429.6 50.0 %all-to-all-start = ((bf16[4,1408,128]{2,1,0:T(8,128)(2,1)}), bf16[4,1408,128]{2,1,0:T(8,128)(2,1)S(1)}, u32[]{:S(2)}, u32[]{:S(2)}) async-start(bf16[4,1408,128]{2,1,0:T(8,128)(2,1)} %bitcast.66), calls=%async_computation.1 | async-start | bytes 2883584 | tf_op jit(solution)/shard_map/all_to_all | solution.py:305
  452.4 17.0 %collective-permute-start.6 = (bf16[1,1792,128]{2,1,0:T(8,128)(2,1)S(1)}, bf16[1,1792,128]{2,1,0:T(8,128)(2,1)S(1)}, u32[]{:S(2)}, u32[]{:S(2)}) collective-permute-start(bf16[1,1792,128]{2,1,0:T(8,128)(2,1)S(1)} %constant_dynamic-slice_fusion.2), channel_id=1, source_target_pairs={{0,2},{2,0},{4,6},{6,4},{8,10},{10,8},{12,14},{14,12},{16,18},{18,... | collective-permute-start | bytes 1376264 | tf_op jit(solution)/shard_map/ppermute | solution.py:302
  461.2 9.5 %collective-permute-start.4 = (bf16[1,1792,128]{2,1,0:T(8,128)(2,1)S(1)}, bf16[1,1792,128]{2,1,0:T(8,128)(2,1)S(1)}, u32[]{:S(2)}, u32[]{:S(2)}) collective-permute-start(bf16[1,1792,128]{2,1,0:T(8,128)(2,1)S(1)} %constant_dynamic-slice_fusion.4), channel_id=1, source_target_pairs={{0,4},{4,0},{2,6},{6,2},{8,12},{12,8},{10,14},{14,10},{16,20},{20,... | collective-permute-start | bytes 1376264 | tf_op jit(solution)/shard_map/ppermute | solution.py:302
  481.0 48.1 %all-to-all-start.1 = ((bf16[4,896,128]{2,1,0:T(8,128)(2,1)}), bf16[4,896,128]{2,1,0:T(8,128)(2,1)S(1)}, u32[]{:S(2)}, u32[]{:S(2)}) async-start(bf16[4,896,128]{2,1,0:T(8,128)(2,1)} %pad_maximum_fusion.8), calls=%async_computation.2 | async-start | bytes 1835008 | tf_op jit(solution)/shard_map/all_to_all | solution.py:305
  484.5 10.4 %collective-permute-start.7 = (bf16[1,704,128]{2,1,0:T(8,128)(2,1)S(1)}, bf16[1,704,128]{2,1,0:T(8,128)(2,1)S(1)}, u32[]{:S(2)}, u32[]{:S(2)}) collective-permute-start(bf16[1,704,128]{2,1,0:T(8,128)(2,1)S(1)} %constant_dynamic-slice_fusion.1), channel_id=1, source_target_pairs={{0,2},{2,0},{4,6},{6,4},{8,10},{10,8},{12,14},{14,12},{16,18},{18,... | collective-permute-start | bytes 540680 | tf_op jit(solution)/shard_map/ppermute | solution.py:302
  495.0 6.2 collective-permute-start.8
  530.3 26.1 %all-to-all-start.2 = ((bf16[4,1,896,128]{3,2,1,0:T(8,128)(2,1)}), bf16[4,1,896,128]{3,2,1,0:T(8,128)(2,1)S(1)}, u32[]{:S(2)}, u32[]{:S(2)}) async-start(bf16[4,1,896,128]{3,2,1,0:T(8,128)(2,1)} %broadcast_in_dim.48), calls=%async_computation.3 | async-start | bytes 1835008 | tf_op jit(solution)/shard_map/all_to_all | solution.py:305
  533.8 3.8 collective-permute-start.9
  537.7 4.9 collective-permute-start.10
  556.4 11.0 %collective-permute-start.11 = (bf16[1,1792,128]{2,1,0:T(8,128)(2,1)S(1)}, bf16[1,1792,128]{2,1,0:T(8,128)(2,1)S(1)}, u32[]{:S(2)}, u32[]{:S(2)}) collective-permute-start(bf16[1,1792,128]{2,1,0:T(8,128)(2,1)S(1)} %bitcast.268), channel_id=1, source_target_pairs={{0,4},{4,0},{2,6},{6,2},{8,12},{12,8},{10,14},{14,10},{16,20},{20,... | collective-permute-start | bytes 1376264 | tf_op jit(solution)/shard_map/ppermute | solution.py:302
  557.7 17.2 %collective-permute-start.13 = (bf16[1,1792,128]{2,1,0:T(8,128)(2,1)S(1)}, bf16[1,1792,128]{2,1,0:T(8,128)(2,1)}, u32[]{:S(2)}, u32[]{:S(2)}) collective-permute-start(bf16[1,1792,128]{2,1,0:T(8,128)(2,1)S(1)} %bitcast.266), channel_id=1, source_target_pairs={{0,2},{2,0},{4,6},{6,4},{8,10},{10,8},{12,14},{14,12},{16,18},{18,... | collective-permute-start | bytes 1376264 | tf_op jit(solution)/shard_map/ppermute | solution.py:302
  567.5 20.0 %collective-permute-start.12 = (bf16[1,3584,128]{2,1,0:T(8,128)(2,1)S(1)}, bf16[1,3584,128]{2,1,0:T(8,128)(2,1)}, u32[]{:S(2)}, u32[]{:S(2)}) collective-permute-start(bf16[1,3584,128]{2,1,0:T(8,128)(2,1)S(1)} %bitcast.253), channel_id=1, source_target_pairs={{0,2},{2,0},{4,6},{6,4},{8,10},{10,8},{12,14},{14,12},{16,18},{18,... | collective-permute-start | bytes 2752520 | tf_op jit(solution)/shard_map/ppermute | solution.py:302
  568.8 71.3 %collective-permute-start.16 = (bf16[19968,128]{1,0:T(8,128)(2,1)}, bf16[19968,128]{1,0:T(8,128)(2,1)}, u32[]{:S(2)}, u32[]{:S(2)}) collective-permute-start(bf16[19968,128]{1,0:T(8,128)(2,1)} %all-gather.2.cloned.1.call-done.own_high), channel_id=1, source_target_pairs={{0,1},{2,3},{4,5},{6,7},{8,9},{10,11},{12,13},{14,15},{16,17},{18,... | collective-permute-start | bytes 15335432 | tf_op jit(solution)/shard_map/ppermute | solution.py:433
  571.3 37.0 %all-to-all-start.3 = ((bf16[4,1,1408,128]{3,2,1,0:T(8,128)(2,1)}), bf16[4,1,1408,128]{3,2,1,0:T(8,128)(2,1)S(1)}, u32[]{:S(2)}, u32[]{:S(2)}) async-start(bf16[4,1,1408,128]{3,2,1,0:T(8,128)(2,1)} %broadcast_in_dim.50), calls=%async_computation.4 | async-start | bytes 2883584 | tf_op jit(solution)/shard_map/all_to_all | solution.py:305
  576.1 17.3 %collective-permute-start.14 = (bf16[1,3584,128]{2,1,0:T(8,128)(2,1)S(1)}, bf16[1,3584,128]{2,1,0:T(8,128)(2,1)S(1)}, u32[]{:S(2)}, u32[]{:S(2)}) collective-permute-start(bf16[1,3584,128]{2,1,0:T(8,128)(2,1)S(1)} %bitcast.255), channel_id=1, source_target_pairs={{0,4},{4,0},{2,6},{6,2},{8,12},{12,8},{10,14},{14,10},{16,20},{20,... | collective-permute-start | bytes 2752520 | tf_op jit(solution)/shard_map/ppermute | solution.py:302
  629.3 11.9 %collective-permute-start.15 = (bf16[19968,128]{1,0:T(8,128)(2,1)}, bf16[19968,128]{1,0:T(8,128)(2,1)}, u32[]{:S(2)}, u32[]{:S(2)}) collective-permute-start(bf16[19968,128]{1,0:T(8,128)(2,1)} %pad_maximum_fusion.own_low), channel_id=1, source_target_pairs={{1,0},{3,2},{5,4},{7,6},{9,8},{11,10},{13,12},{15,14},{17,16},{19,... | collective-permute-start | bytes 15335432 | tf_op jit(solution)/shard_map/ppermute | solution.py:433
  641.3 49.1 %copy-start.1 = (bf16[6,256,768]{2,1,0:T(8,128)(2,1)S(1)}, bf16[6,256,768]{2,1,0:T(8,128)(2,1)}, u32[]{:S(2)}) copy-start(bf16[6,256,768]{2,1,0:T(8,128)(2,1)} %param.9) | copy-start | bytes 7077892
  (66 other events, 162.5 us)
Sparse Core Ops, SparseCore 0:
  261.2 140.0 reduce-scatter.1
  404.2 125.5 all-gather.1

commit v3 on v2

--- a/solution.py
+++ b/solution.py
@@ -39,7 +39,7 @@
     ]
 
 
-MARGIN = 256
+MARGIN = 512
 
 
 def flat_rows():
@@ -82,12 +82,19 @@
         copies.append(parts)
     slots = [(k, p) for k, parts in enumerate(copies) for p in range(len(parts))]
     labels = [label for label, dims in segment_list()]
+    matrices = [label for label, dims in segment_list() if len(dims) == 2]
     deepest = max(round_up(high, 16) - low // 16 * 16 for low, high in spans)
 
     def kernel(*refs):
         ins, rest = refs[: len(sources)], refs[len(sources) :]
-        outs = dict(zip(labels, rest))
-        staged, wide_rows, sems = rest[len(labels) :]
+        finals = dict(zip(labels, rest))
+        staged, wide_rows, sems, *own, out_sems = rest[len(labels) :]
+        outs = {**finals, **dict(zip(matrices, own))}
+
+        def leave(label):
+            return pltpu.make_async_copy(
+                outs[label], finals[label], out_sems.at[matrices.index(label)]
+            )
 
         def copy(slot, source, shift):
             k, p = slot
@@ -151,6 +158,9 @@
                     return carry
 
                 lax.fori_loop(0, dims[0] // 16, step, 0)
+                leave(label).start()
+        for label in matrices:
+            leave(label).wait()
 
     out_shape = [
         jax.ShapeDtypeStruct(dims, jnp.bfloat16)
@@ -162,10 +172,16 @@
         kernel,
         out_shape=out_shape,
         in_specs=[pl.BlockSpec(memory_space=pl.ANY)] * len(sources),
+        out_specs=[
+            pl.BlockSpec(memory_space=pl.ANY if label in matrices else pltpu.VMEM)
+            for label in labels
+        ],
         scratch_shapes=[
             pltpu.VMEM((total, 128), jnp.bfloat16),
             pltpu.VMEM((deepest, 128), jnp.float32),
             pltpu.SemaphoreType.DMA((len(slots),)),
+            *[pltpu.VMEM(shapes[label], jnp.bfloat16) for label in matrices],
+            pltpu.SemaphoreType.DMA((len(matrices),)),
         ],
         compiler_params=pltpu.CompilerParams(vmem_limit_bytes=61 << 20),
         name="unpack",
@@ -183,11 +199,11 @@
         tiles = value.shape[1] // 128
         begin, end = 0, 1
         if value.shape[0] > 1:
-            begin = max(0, low - off) // (8 * tiles)
-            end = -(-min(rows, high - off) // (8 * tiles))
-            if 3 * (end - begin) * 8 < value.shape[0]:
-                value = value[begin * 8 : end * 8]
-                off, end, begin = off + begin * 8 * tiles, end - begin, 0
+            begin = max(0, low - off) // (16 * tiles)
+            end = -(-min(rows, high - off) // (16 * tiles))
+            if 3 * (end - begin) * 16 < value.shape[0]:
+                value = value[begin * 16 : end * 16]
+                off, end, begin = off + begin * 16 * tiles, end - begin, 0
         arrays.append(value)
         places.append((off, begin, end))
     length = high - low
@@ -213,13 +229,12 @@
                     if 0 <= spot < length + 2 * MARGIN:
                         flat[spot : spot + 1, :] = ref[:, c * 128 : (c + 1) * 128]
                 continue
-            block = 8 * tiles
+            block = 16 * tiles
 
             def step(i, carry, ref=ref, tiles=tiles, base=base, block=block):
                 for c in range(tiles):
-                    flat[pl.ds(base + i * block + c, 8, stride=tiles), :] = ref[
-                        pl.ds(pl.multiple_of(i * 8, 8), 8), c * 128 : (c + 1) * 128
-                    ]
+                    rows = ref[pl.ds(pl.multiple_of(i * 16, 16), 16), c * 128 : (c + 1) * 128]
+                    flat[pl.ds(base + i * block + c, 16, stride=tiles), :] = rows.astype(jnp.float32)
                 return carry
 
             lax.fori_loop(begin, end, step, 0)
@@ -273,10 +288,10 @@
 
 def flat_gradient(grads, unit):
     table, used = flat_rows()
-    flat = jnp.concatenate([grads[k].reshape(-1) for k, dims in segment_list()])
+    flat = jnp.concatenate([grads[k].astype(jnp.bfloat16).reshape(-1) for k, dims in segment_list()])
     padding = (round_up(used, unit) - used) * 128
-    flat = jnp.concatenate([flat, jnp.zeros((padding,), jnp.float32)])
-    return flat.reshape(-1, 128).astype(jnp.bfloat16)
+    flat = jnp.concatenate([flat, jnp.zeros((padding,), jnp.bfloat16)])
+    return flat.reshape(-1, 128)
 
 
 def added(first, second):
@@ -334,7 +349,7 @@
     return Line(1, 2), Line(2, 2), Line(4, lax.axis_size("wide") // 4)
 
 
-def staged_scatter(total):
+def staged_scatter(total, beside=()):
     x, y, z = wide_lines()
     unit = lax.axis_size("wide") * 8
     most = total.shape[0] // unit * 4 // 11
@@ -347,11 +362,11 @@
     b = y.scatter(flat3(b, 2))
     a = y.scatter(flat3(a, 2))
     b = x.scatter(flat3(b, 2))
-    a, b, c = lax.optimization_barrier((a, b, c))
+    a, b, c, beside = lax.optimization_barrier((a, b, c, beside))
     ab = z.scatter(jnp.concatenate([flat3(a, z.size), flat3(b, z.size)], 1))
     c = x.scatter(flat3(c, 2))
     c = y.scatter(flat3(c, 2))
-    return lax.optimization_barrier((ab, c))
+    return lax.optimization_barrier((ab, c)), beside
 
 
 def staged_gather(ab, c):
@@ -362,11 +377,43 @@
     half = ab.shape[1] // 2
     a, b = ab[:, :half], ab[:, half:]
     c = z.gather(flat3(c, 1))
-    a = y.gather(flat3(a, 1))
-    b = x.gather(flat3(b, 1))
-    a = x.gather(flat3(a, 1))
-    b = y.gather(flat3(b, 1))
-    return jnp.concatenate([v.reshape(-1, 128) for v in (a, b, c)], 0)
+    a = y.gather(flat3(a, 1)).reshape(-1, 128)
+    b = x.gather(flat3(b, 1)).reshape(-1, 128)
+    return join_pieces((x, a, x.swap(a)), (y, b, y.swap(b)), c.reshape(-1, 128))
+
+
+def join_pieces(first, second, third):
+    pairs = (first, second)
+    sizes = [2 * own.shape[0] for line, own, other in pairs]
+
+    def kernel(own1, other1, own2, other2, last, out, sems):
+        copies = []
+        start = 0
+        for (line, own, other), refs in zip(pairs, ((own1, other1), (own2, other2))):
+            rows = own.shape[0]
+            me = (lax.axis_index("wide") // line.stride) % 2
+            for ref, place in zip(refs, (me, 1 - me)):
+                copies.append((ref, pl.multiple_of(start + place * rows, 8), rows))
+            start += 2 * rows
+        copies.append((last, start, third.shape[0]))
+        copies = [
+            pltpu.make_async_copy(ref, out.at[pl.ds(spot, rows)], sems.at[n])
+            for n, (ref, spot, rows) in enumerate(copies)
+        ]
+        for copy in copies:
+            copy.start()
+        for copy in copies:
+            copy.wait()
+
+    anywhere = pl.BlockSpec(memory_space=pl.ANY)
+    return pl.pallas_call(
+        kernel,
+        out_shape=jax.ShapeDtypeStruct((sum(sizes) + third.shape[0], 128), third.dtype),
+        in_specs=[anywhere] * 5,
+        out_specs=anywhere,
+        scratch_shapes=[pltpu.SemaphoreType.DMA((5,))],
+        name="join",
+    )(first[1], first[2], second[1], second[2], third)
 
 
 def narrow_sum(halves):
@@ -382,37 +429,38 @@
         total = added(total, narrow_swap(other, step))
     unit = lax.axis_size("wide") * 16
     total = jnp.pad(total, ((0, round_up(rows, unit) - rows), (0, 0)))
-    return staged_gather(*staged_scatter(total))[:rows]
+    return staged_gather(*staged_scatter(total)[0])[:rows]
 
 
 BLOCK = 2496
 
 
-def adam_rows(parts, moment1, moment2, start, rows, held, chips_all):
-    half = parts[0].shape[0] // BLOCK
+def adam_rows(low, high, moment1, moment2, start, held, chips_all):
     shift = start // BLOCK
-    steps = -(-rows // BLOCK)
-
-    def kernel(core, own_low, got_low, own_high, got_high, first, second, *rest):
+    steps = -(-min(low.shape[0], moment1.shape[0] - start) // BLOCK)
+
+    def kernel(core, low_rows, high_rows, first, second, *rest):
         grad_out, update, new_first, new_second = rest[len(held) :]
-        early = pl.program_id(0) < half
-        low = jnp.where(early, own_low[...], got_low[...])
-        high = jnp.where(early, got_high[...], own_high[...])
-        grad = jnp.where(core[0] == 0, low, high).astype(jnp.float32) / chips_all
+        grad = jnp.where(core[0] == 0, low_rows[...], high_rows[...].reshape(BLOCK, 128))
+        grad = grad.astype(jnp.float32) / chips_all
         grad_out[...] = grad
         update[...], new_first[...], new_second[...] = adam_step(grad, first[...], second[...])
 
-    def early_rows(place):
-        return lambda i, core: (jnp.where(core[0] == place, jnp.minimum(i, half - 1), 0), 0)
-
-    def late_rows(place):
-        return lambda i, core: (jnp.where(core[0] == place, jnp.maximum(i - half, 0), 0), 0)
-
     def spec(index_map):
         return pl.BlockSpec((BLOCK, 128), index_map)
 
     here = spec(lambda i, core: (i + shift, 0))
-    maps = (early_rows(0), late_rows(0), late_rows(1), early_rows(1))
+    group = BLOCK // high.shape[2]
+    count = high.shape[0] // group
+
+    def high_place(i, core):
+        turn = jnp.where(core[0] == 1, i, 0)
+        return turn % count, turn // count, 0, 0
+
+    parts = (
+        spec(lambda i, core: (jnp.where(core[0] == 0, i, 0), 0)),
+        pl.BlockSpec((group, 1, high.shape[2], 128), high_place),
+    )
     core = lax.axis_index("narrow").astype(jnp.int32).reshape(1)
     return pl.pallas_call(
         kernel,
@@ -420,13 +468,17 @@
         grid_spec=pltpu.PrefetchScalarGridSpec(
             num_scalar_prefetch=1,
             grid=(steps,),
-            in_specs=[*[spec(m) for m in maps], here, here]
-            + [pl.BlockSpec(memory_space=pl.ANY)] * len(held),
+            in_specs=[*parts, here, here] + [pl.BlockSpec(memory_space=pl.ANY)] * len(held),
             out_specs=[here] * 4,
         ),
-        input_output_aliases={7 + n: n for n in range(len(held))},
+        input_output_aliases={5 + n: n for n in range(len(held))},
+        compiler_params=pltpu.CompilerParams(vmem_limit_bytes=40 << 20),
         name=f"adam{start}",
-    )(core, *parts, moment1, moment2, *held)
+    )(core, low, high, moment1, moment2, *held)
+
+
+def scatter_wide(value):
+    return lax.psum_scatter(value, "wide", scatter_dimension=0, tiled=True)
 
 
 def to_owner(value, source):
@@ -532,7 +584,7 @@
     hidden_pre = jnp.einsum(
         "ctd,df->ctf", second_in, weights_map[prefix + "u"], preferred_element_type=jnp.float32
     ) + vector(weights_map, prefix + "ub")
-    activ, slope = gelu_and_slope(hidden_pre)
+    activ, slope = lax.optimization_barrier(gelu_and_slope(hidden_pre))
     result = (
         middle
         + jnp.einsum(
@@ -583,13 +635,15 @@
 
 
 def hidden_gradient(kept, d_hidden):
-    return jnp.einsum("ctd,ctf->df", kept[8], d_hidden, preferred_element_type=jnp.float32)
+    return jnp.einsum(
+        "ctd,ctf->df", kept[8], d_hidden, preferred_element_type=jnp.float32
+    ).astype(jnp.bfloat16)
 
 
 def output_gradient(kept, upstream):
     return jnp.einsum(
         "ctf,ctd->fd", kept[10], upstream.astype(jnp.bfloat16), preferred_element_type=jnp.float32
-    )
+    ).astype(jnp.bfloat16)
 
 
 def scores_backward(d_middle, kept, weights_map, prefix, heads):
@@ -621,7 +675,7 @@
     grads[prefix + "ob"] = jnp.sum(branch_one.astype(jnp.float32), (0, 1))
     grads[prefix + "o"] = jnp.einsum(
         "cti,ctd->id", mixed, branch_one, preferred_element_type=jnp.float32
-    )
+    ).astype(jnp.bfloat16)
     d_query = jnp.einsum(
         "chqk,ckhe->cqhe", d_scores, key_rows, preferred_element_type=jnp.float32
     ) * HD ** (-0.5)
@@ -638,7 +692,7 @@
     )
     grads[prefix + "qkv"] = jnp.einsum(
         "ctd,cte->de", first_in, d_triple, preferred_element_type=jnp.float32
-    )
+    ).astype(jnp.bfloat16)
     d_first = jnp.einsum(
         "cte,de->ctd", d_triple, weights_map[prefix + "qkv"], preferred_element_type=jnp.float32
     )
@@ -700,7 +754,7 @@
     grads["pb"] = jnp.sum(d_projected.astype(jnp.float32), (0, 1))
     grads["proj"] = jnp.einsum(
         "cvd,cve->de", encoded_low, d_projected, preferred_element_type=jnp.float32
-    )
+    ).astype(jnp.bfloat16)
     d_encoded = jnp.einsum(
         "cve,de->cvd", d_projected, weights_map["proj"], preferred_element_type=jnp.float32
     )
@@ -712,7 +766,7 @@
     if chunked:
         high = pack_part(grads, half_rows, cut, *upper, held)
         d_enc_out, high = tie((d_enc_out, high))
-        high = lax.psum_scatter(narrow_sum(high), "wide", scatter_dimension=0, tiled=True)
+        high = [scatter_wide(part) for part in jnp.split(narrow_sum(high), 2)]
     d_mid, d_hidden, more = mlp_backward(d_enc_out, enc_kept, weights_map, "e")
     grads.update(more)
     grads["eu"] = hidden_gradient(enc_kept, d_hidden)
@@ -727,16 +781,18 @@
     chips_all = float(chips * lax.axis_size("wide") * lax.axis_size("narrow"))
     if chunked:
         low = pack_part(grads, 0, cut, 0, padded, held)
-        d_enc_in, high, low = tie((d_enc_in, high, low))
-        high = lax.all_gather(high, "wide", axis=0, tiled=True)
+        d_enc_in, low, high[0] = tie((d_enc_in, low, high[0]))
     patch_grad = jnp.einsum(
         "cvp,cvd->cpd", choose_full, d_enc_in[:, 2:, :], precision=highest
     ).astype(jnp.bfloat16)
     if chunked:
-        low = staged_gather(*staged_scatter(narrow_sum(low)))
-        parts = (low, to_owner(low, 1), high, to_owner(high, 0))
+        low, high = staged_scatter(narrow_sum(low), high)
+        high = lax.all_gather(jnp.stack(high), "wide")
+        low = staged_gather(*low)
+        start = low.shape[0]
+        held = adam_rows(low, to_owner(high, 0), moment1, moment2, 0, (), chips_all)
         grad_out, update, new_moment1, new_moment2 = adam_rows(
-            parts, moment1, moment2, 0, half_rows, (), chips_all
+            to_owner(low, 1), high, moment1, moment2, start, held, chips_all
         )
     else:
         every = flat_gradient(grads, half_rows * lax.axis_size("narrow"))

time: 708 us -> 887 us (1.25)
  Pallas kernels: 113 us -> 255 us
  waiting for transfers between devices: 220 us -> 311 us
  other arithmetic: 91.8 us -> 51.3 us
  local copies, waits for them, and re-layouts: 65.9 us -> 56.1 us
    pallas_call x0 -> x1, Pallas kernels: none -> 156 us  [join_pieces(): pl.pallas_call(kernel, out_shape=jax.ShapeDtypeStruct((sum(sizes) + third...]
    reduce_scatter x1 -> x2, waiting for transfers between devices: 52.1 us -> 147 us  [scatter_wide(): return lax.psum_scatter(value, 'wide', scatter_dimension=0, tiled=True)]
    all_gather x1, waiting for transfers between devices: 0.01 us -> 35.4 us  [per_device(): high = lax.all_gather(jnp.stack(high), 'wide')]
    concatenate x1 -> x0, other arithmetic: 21 us -> none  [staged_gather(): return jnp.concatenate([v.reshape(-1, 128) for v in (a, b, c)], 0)]
    dot_general x2, matrix products: 9.57 us -> 30.5 us  [block_forward(): jnp.einsum('ctd,df->ctf', second_in, weights_map[prefix + 'u'], preferred...]
    ppermute x12, waiting for transfers between devices: 75.7 us -> 56 us  [swap(): return lax.ppermute(value, 'wide', pairs)]
    convert_element_type x2 -> x0, other arithmetic: 19.5 us -> none  [gelu_and_slope(): return ((u * below).astype(jnp.bfloat16), slope.astype(jnp.bfloat16))]
    dot_general x2, matrix products: 28.4 us -> 10.8 us  [mlp_backward(): jnp.einsum('ctd,fd->ctf', branch_two, weights_map[prefix + 'v'], preferre...]
  transfers between devices with their start and end apart: 23 -> 24, of which waited for: 20 -> 17; matrix products, arithmetic and copies ran while one was open for 17% -> 10% of each run, Pallas kernels for 3% -> 22%
where the time goes in v3:
time: 887 us; the launch traced here: 879 us
  waiting for transfers between devices  311 us (35%)
  Pallas kernels  255 us (29%)
  matrix products  148 us (17%)
  local copies, waits for them, and re-layouts  56.1 us (6%)
  other arithmetic  51.3 us (6%)
  starting transfers between devices  41.3 us (5%)
  between operations  16.1 us (2%)
    pallas_call x1, Pallas kernels, join_pieces(): pl.pallas_call(kernel, out_shape=jax.ShapeDtypeStruct((sum(sizes) + third...  156 us
    reduce_scatter x2, waiting for transfers between devices, scatter_wide(): return lax.psum_scatter(value, 'wide', scatter_dimension=0, tiled=True)  147 us
    ppermute x12, waiting for transfers between devices, swap(): return lax.ppermute(value, 'wide', pairs)  56 us
    all_to_all x4, waiting for transfers between devices, exchange(): return lax.all_to_all(value, 'wide', 0, 0, axis_index_groups=self.groups)  54 us
    pallas_call x2, Pallas kernels, adam_rows(): pl.pallas_call(kernel, out_shape=[jax.ShapeDtypeStruct(moment1.shape, jnp...  48.5 us
    all_gather x1, waiting for transfers between devices, per_device(): high = lax.all_gather(jnp.stack(high), 'wide')  35.4 us
    pallas_call x4, Pallas kernels, pack_part(): pl.pallas_call(kernel, out_shape=[jax.ShapeDtypeStruct((middle - first, 1...  32.4 us
    dot_general x2, matrix products, block_forward(): jnp.einsum('ctd,df->ctf', second_in, weights_map[prefix + 'u'], preferred...  30.5 us
  transfers between devices with their start and end apart: 24, of which 17 were waited for; matrix products, arithmetic and copies ran while one was open for 10% of the time, Pallas kernels for 22%

profile of v3, /device:TPU:1, one launch (start us, length us, event | category | flops | bytes accessed | tf_op | source)
XLA Modules:
  0.0 879.3 jit_solution(14602253877865302903)
XLA Ops:
  7.3 7.8 convert_element_type.299.refs_0_
  20.8 10.1 %collective-permute-done.refs_1_ = bf16[39552,128]{1,0:T(8,128)(2,1)} collective-permute-done((bf16[39552,128]{1,0:T(8,128)(2,1)S(1)}, bf16[39552,128]{1,0:T(8,128)(2,1)}, u32[]{:S(2)}, u32[]{:S(2)}) %collective-permute-start) | collective-permute-done | bytes 10125344 | tf_op jit(solution)/shard_map/ppermute | solution.py:341
  30.9 18.1 %unpack.1 = (f32[1,768]{1,0:T(1,128)}, f32[1,768]{1,0:T(1,128)}, f32[1,768]{1,0:T(1,128)}, bf16[768,2304]{1,0:T(8,128)(2,1)}, bf16[768,768]{1,0:T(8,128)(2,1)}, ...) custom-call(bf16[39552,128]{1,0:T(8,128)(2,1)} %copy-done.13, ...), custom_call_target="tpu_custom_call" | custom-call | tf_op jit(solution)/shard_map/unpack/pallas_call | solution.py:171
  52.5 4.0 convolution_convert_fusion
  60.4 2.6 copy.132
  69.9 11.9 %fusion.13 = (bf16[6,66,3072]{2,1,0:T(8,128)(2,1)}, bf16[6,66,3072]{2,1,0:T(8,128)(2,1)}) fusion(f32[3072]{0:T(1024)S(1)} %bitcast.309, bf16[768,3072]{1,0:T(8,128)(2,1)} %get-tuple-element.84, f32[6,66,768]{2,1,0:T(8,128)} %copy-done.14, f32[768]{0:T(1024)S(1)} %reduce.8, f32[768]{0:T(1024)S(1)} %reduce.7, f32[6,66]{1,0:T(8,128)S(1)} %fusion.83, ...), kind=kOutput, calls=%fused_computation.30 | convolution fusion | flops 1911444480 | bytes 10822752 | tf_op jit(solution)/shard_map/ctd,df->ctf/dot_general | solution.py:584
  81.9 5.5 fusion.16
  104.4 18.5 %fusion.5 = (bf16[6,256,2048]{2,1,0:T(8,128)(2,1)S(1)}, bf16[6,256,2048]{2,1,0:T(8,128)(2,1)}) fusion(f32[2048]{0:T(1024)S(1)} %bitcast.310, bf16[512,2048]{1,0:T(8,128)(2,1)S(1)} %copy-done.103, f32[6,256,512]{2,1,0:T(8,128)S(1)} %get-tuple-element.213, f32[512]{0:T(512)S(1)} %bitcast.314, f32[512]{0:T(512)S(1)} %bitcast.292, f32[6,256]{1,0:T(8,128)S(1)} %fusion.81, ...), kind=kOutput, calls=%fused_computation.7 | convolution fusion | flops 3332112384 | bytes 17850368 | tf_op jit(solution)/shard_map/ctd,df->ctf/dot_general | solution.py:584
  123.0 4.3 convert_reduce_fusion
  127.3 5.1 bitcast_convert_fusion.4.refs_0_
  132.4 4.7 fusion.99
  139.3 4.6 bitcast_convert_fusion.3.refs_2_
  143.9 6.1 convert_add_fusion
  150.0 8.1 pack62592.1
  158.2 3.3 fusion.50.refs_10_
  162.6 7.2 multiply_reduce_fusion
  169.9 4.5 multiply_convert_fusion.1
  178.3 4.6 bitcast_convert_fusion.6.refs_9_
  182.9 2.6 multiply_reduce_fusion.3
  188.8 2.2 convert_reduce_fusion.6
  195.2 4.3 bitcast_convert_fusion.1.refs_0_
  203.9 9.0 %pack39552.1 = (bf16[19968,128]{1,0:T(8,128)(2,1)}, bf16[19968,128]{1,0:T(8,128)(2,1)}) custom-call(bf16[3072,768]{1,0:T(8,128)(2,1)} %bitcast_convert_fusion.1.refs_0_, f32[1,768]{1,0:T(1,128)} %reshape.384.refs_1_, f32[1,768]{1,0:T(1,128)} %reshape.385.refs_2_, f32[1,768]{1,0:T(1,128)} %reshape.386.refs_3_, ...), custom_call_target="tpu_custom_call", output_to_operand_aliasing={{0}: (15, {}), {1}: (16, {})} | custom-call | tf_op jit(solution)/shard_map/pack39552/pallas_call | solution.py:273
  213.2 6.6 convert_reduce_fusion.1
  219.8 3.0 fusion.100
  224.6 4.6 bitcast_convert_fusion.refs_0_
  230.6 2.5 fusion.106
  233.4 3.2 add_add_fusion.9
  240.2 8.4 pack18560.1
  251.6 3.3 multiply_reduce_fusion.9
  257.8 2.4 copy.114
  262.0 2.5 copy.115
  264.5 2.7 convolution_convert_fusion.3
  268.0 4.6 fusion.101
  281.1 4.0 bitcast_convert_fusion.2.refs_3_
  285.2 6.8 pack0.1
  292.0 72.4 %reduce-scatter.3.cloned.1.call-done = bf16[624,128]{1,0:T(8,128)(2,1)} async-done(((bf16[9984,128]{1,0:T(8,128)(2,1)}), bf16[624,128]{1,0:T(8,128)(2,1)}) %reduce-scatter.3.cloned.1.call-update) | async-done | bytes 159760 | tf_op jit(solution)/shard_map/reduce_scatter | solution.py:481
  364.4 2.3 collective-permute-start.2
  366.7 8.4 collective-permute-done.2
  375.2 5.3 add_convert_fusion
  380.5 2.3 copy-done.19
  386.4 2.6 slice.82
  390.6 4.3 all-to-all-start
  395.0 14.2 %collective-permute-done.5 = bf16[1,3584,128]{2,1,0:T(8,128)(2,1)S(1)} collective-permute-done((bf16[1,3584,128]{2,1,0:T(8,128)(2,1)}, bf16[1,3584,128]{2,1,0:T(8,128)(2,1)S(1)}, u32[]{:S(2)}, u32[]{:S(2)}) %collective-permute-start.5) | collective-permute-done | bytes 917536 | tf_op jit(solution)/shard_map/ppermute | solution.py:317
  415.7 8.7 collective-permute-done.6
  425.8 11.2 %all-to-all-done = bf16[4,1408,128]{2,1,0:T(8,128)(2,1)} async-done(((bf16[4,1408,128]{2,1,0:T(8,128)(2,1)}), bf16[4,1408,128]{2,1,0:T(8,128)(2,1)}, u32[]{:S(2)}, u32[]{:S(2)}) %all-to-all-start) | async-done | bytes 1441824 | tf_op jit(solution)/shard_map/all_to_all | solution.py:320
  438.8 74.8 %reduce-scatter.5.cloned.1.call-done = bf16[624,128]{1,0:T(8,128)(2,1)} async-done(((bf16[9984,128]{1,0:T(8,128)(2,1)}), bf16[624,128]{1,0:T(8,128)(2,1)}) %reduce-scatter.5.cloned.1.call-update) | async-done | bytes 159760 | tf_op jit(solution)/shard_map/reduce_scatter | solution.py:481
  516.2 3.5 all-to-all-start.1
  521.0 3.2 collective-permute-done.7
  525.5 2.5 collective-permute-done.8
  528.0 21.0 %all-to-all-done.1 = bf16[4,896,128]{2,1,0:T(8,128)(2,1)S(1)} async-done(((bf16[4,896,128]{2,1,0:T(8,128)(2,1)}), bf16[4,896,128]{2,1,0:T(8,128)(2,1)S(1)}, u32[]{:S(2)}, u32[]{:S(2)}) %all-to-all-start.1) | async-done | bytes 917536 | tf_op jit(solution)/shard_map/all_to_all | solution.py:320
  550.3 3.5 all-to-all-start.2
  555.0 4.9 collective-permute-done.9
  561.2 6.2 collective-permute-done.10
  567.5 21.7 %all-to-all-done.2 = bf16[4,1,896,128]{3,2,1,0:T(8,128)(2,1)S(1)} async-done(((bf16[4,1,896,128]{3,2,1,0:T(8,128)(2,1)}), bf16[4,1,896,128]{3,2,1,0:T(8,128)(2,1)S(1)}, u32[]{:S(2)}, u32[]{:S(2)}) %all-to-all-start.2) | async-done | bytes 917536 | tf_op jit(solution)/shard_map/all_to_all | solution.py:320
  593.0 3.6 all-to-all-start.3
  596.5 13.6 %collective-permute-done.13 = bf16[1,1792,128]{2,1,0:T(8,128)(2,1)} collective-permute-done((bf16[1,1792,128]{2,1,0:T(8,128)(2,1)S(1)}, bf16[1,1792,128]{2,1,0:T(8,128)(2,1)}, u32[]{:S(2)}, u32[]{:S(2)}) %collective-permute-start.13) | collective-permute-done | bytes 458784 | tf_op jit(solution)/shard_map/ppermute | solution.py:317
  612.7 2.4 collective-permute-start.12
  615.1 35.4 %all-gather.3.cloned.1.call-done = bf16[32,624,128]{2,1,0:T(8,128)(2,1)} async-done(((bf16[2,624,128]{2,1,0:T(8,128)(2,1)}), bf16[32,624,128]{2,1,0:T(8,128)(2,1)}) %all-gather.3.cloned.1.call-update) | async-done | bytes 5111824 | tf_op jit(solution)/shard_map/all_gather | solution.py:790
  652.9 156.0 %join.1.low_rows = bf16[19968,128]{1,0:T(8,128)(2,1)} custom-call(bf16[3584,128]{1,0:T(8,128)(2,1)} %bitcast.253, bf16[3584,128]{1,0:T(8,128)(2,1)} %collective-permute-done.12.other1, bf16[3584,128]{1,0:T(8,128)(2,1)} %bitcast.251, bf16[3584,128]{1,0:T(8,128)(2,1)} %collective-permute-done.14.other2, bf16[5632,128]{1,0:T(8,128)(2,1)} %bitcast.243), custom_call_target="tpu_custom_call" | custom-call | tf_op jit(solution)/shard_map/join/pallas_call | solution.py:409
  808.9 7.5 collective-permute-start.15
  816.4 5.0 convolution_convert_fusion.1
  821.4 2.4 copy-done.2
  823.9 25.2 %adam0.1 = (f32[39552,128]{1,0:T(8,128)}, f32[39552,128]{1,0:T(8,128)}, f32[39552,128]{1,0:T(8,128)}, f32[39552,128]{1,0:T(8,128)}) custom-call(s32[1]{0:T(128)} %bitcast.61.core, bf16[19968,128]{1,0:T(8,128)(2,1)S(1)} %copy-done.2, bf16[16,2,624,128]{3,2,1,0:T(8,128)(2,1)} %collective-permute-done.16.high_rows, f32[39552,128]{1,0:T(8,128)} %first.3, ...), custom_call_target="tpu_custom_call" | custom-call | tf_op jit(solution)/shard_map/adam0/pallas_call | solution.py:465
  849.0 23.3 %adam19968.1 = (f32[39552,128]{1,0:T(8,128)}, f32[39552,128]{1,0:T(8,128)}, f32[39552,128]{1,0:T(8,128)}, f32[39552,128]{1,0:T(8,128)}) custom-call(s32[1]{0:T(128)} %bitcast.61.core, bf16[19968,128]{1,0:T(8,128)(2,1)} %collective-permute-done.15.low_rows, ...), custom_call_target="tpu_custom_call", output_to_operand_aliasing={{0}: (5, {}), {1}: (6, {}), {2}: (7, {}), {3}: (8, {})} | custom-call | tf_op jit(solution)/shard_map/adam19968/pallas_call | solution.py:465
  (417 shorter events, 111.8 us)
Async XLA Ops:
  7.2 12.1 %copy-start = (bf16[6,256,768]{2,1,0:T(8,128)(2,1)S(1)}, bf16[6,256,768]{2,1,0:T(8,128)(2,1)}, u32[]{:S(2)}) copy-start(bf16[6,256,768]{2,1,0:T(8,128)(2,1)} %param.9) | copy-start | bytes 7077892
  7.2 8.0 copy-start.114
  7.2 8.0 copy-start.84
  7.2 8.1 copy-start.61
  7.2 357.2 %reduce-scatter.3.cloned.1.call-start = ((), (), s32[]{:S(2)}) async-start(), calls=%async_computation.6 | async-start | bytes 2715648 | tf_op jit(solution)/shard_map/reduce_scatter | solution.py:481
  15.1 15.8 %collective-permute-start = (bf16[39552,128]{1,0:T(8,128)(2,1)S(1)}, bf16[39552,128]{1,0:T(8,128)(2,1)}, u32[]{:S(2)}, u32[]{:S(2)}) collective-permute-start(bf16[39552,128]{1,0:T(8,128)(2,1)S(1)} %convert_element_type.299.refs_0_), channel_id=1, source_target_pairs={{0,1},{1,0},{2,3},{3,2},{4,5},{5,4},{6,7},{7,6},{8,9},{9,8},{10,11... | collective-permute-start | bytes 30375944 | tf_op jit(solution)/shard_map/ppermute | solution.py:341
  15.3 36.6 %copy-start.46 = (f32[6,1,768]{2,1,0:T(1,128)}, f32[6,1,768]{2,1,0:T(1,128)S(1)}, u32[]{:S(2)}) copy-start(f32[6,1,768]{2,1,0:T(1,128)S(1)} %broadcast_in_dim.36) | copy-start | bytes 55300
  20.8 29.0 %copy-start.11 = (f32[6,64,768]{2,1,0:T(8,128)S(1)}, f32[6,64,768]{2,1,0:T(8,128)}, u32[]{:S(2)}) copy-start(f32[6,64,768]{2,1,0:T(8,128)} %fusion.64) | copy-start | bytes 3538948
  58.5 6.1 copy-start.22
  67.8 14.1 %copy-start.62 = (f32[6,66]{1,0:T(8,128)}, f32[6,66]{1,0:T(8,128)S(1)}, u32[]{:S(2)}) copy-start(f32[6,66]{1,0:T(8,128)S(1)} %broadcast_multiply_fusion.3) | copy-start | bytes 4756
  69.8 12.0 %copy-start.68 = (f32[6,66]{1,0:T(8,128)}, f32[6,66]{1,0:T(8,128)S(1)}, u32[]{:S(2)}) copy-start(f32[6,66]{1,0:T(8,128)S(1)} %fusion.83) | copy-start | bytes 4756
  69.9 12.0 %copy-start.70 = (f32[768]{0:T(1024)}, f32[768]{0:T(1024)S(1)}, u32[]{:S(2)}) copy-start(f32[768]{0:T(1024)S(1)} %reduce.7) | copy-start | bytes 9220
  69.9 12.0 %copy-start.88 = (f32[768]{0:T(1024)}, f32[768]{0:T(1024)S(1)}, u32[]{:S(2)}) copy-start(f32[768]{0:T(1024)S(1)} %reduce.8) | copy-start | bytes 9220
  69.9 12.0 %copy-start.94 = (f32[1,768]{1,0:T(1,128)S(1)}, f32[1,768]{1,0:T(1,128)}, u32[]{:S(2)}) copy-start(f32[1,768]{1,0:T(1,128)} %get-tuple-element.88) | copy-start | bytes 9220
  81.9 5.5 copy-start.15
  104.4 18.5 %copy-start.102 = (bf16[2048,512]{1,0:T(8,128)(2,1)S(1)}, bf16[2048,512]{1,0:T(8,128)(2,1)}, u32[]{:S(2)}) copy-start(bf16[2048,512]{1,0:T(8,128)(2,1)} %get-tuple-element.104) | copy-start | bytes 6291460
  104.4 18.5 %copy-start.104 = (bf16[6,256,512]{2,1,0:T(8,128)(2,1)S(1)}, bf16[6,256,512]{2,1,0:T(8,128)(2,1)}, u32[]{:S(2)}) copy-start(bf16[6,256,512]{2,1,0:T(8,128)(2,1)} %param.13) | copy-start | bytes 4718596
  127.2 12.0 %slice-start.8 = ((s8[6291456]{0:T(1024)(128)(4,1)}), s8[4194304]{0:T(1024)(128)(4,1)S(1)}, s32[]{:S(2)}) async-start(s8[6291456]{0:T(1024)(128)(4,1)} %bitcast.317), calls=%async_computation.17 | async-start | bytes 8388608
  132.4 6.9 slice-start.9
  162.2 7.7 slice-start.2
  162.6 7.2 slice-start.3
  178.2 4.7 copy-start.8
  212.9 6.8 slice-start.6
  212.9 6.8 copy-start.16
  212.9 6.8 copy-start.63
  213.0 6.8 copy-start.71
  213.0 6.8 slice-start.7
  213.0 16.2 %collective-permute-start.1 = (bf16[19968,128]{1,0:T(8,128)(2,1)}, bf16[19968,128]{1,0:T(8,128)(2,1)S(1)}, u32[]{:S(2)}, u32[]{:S(2)}) collective-permute-start(bf16[19968,128]{1,0:T(8,128)(2,1)} %get-tuple-element.124), channel_id=1, source_target_pairs={{0,1},{1,0},{2,3},{3,2},{4,5},{5,4},{6,7},{7,6},{8,9},{9,8},{10,11... | collective-permute-start | bytes 15335432 | tf_op jit(solution)/shard_map/ppermute | solution.py:341
  223.8 5.3 slice-start.4
  233.1 280.5 %reduce-scatter.5.cloned.1.call-start = ((), (), s32[]{:S(2)}) async-start(), calls=%async_computation.7 | async-start | bytes 2715648 | tf_op jit(solution)/shard_map/reduce_scatter | solution.py:481
  240.2 8.5 copy-start.20
  267.9 4.7 copy-start.54
  267.9 4.7 copy-start.73
  267.9 4.7 copy-start.48
  267.9 4.7 copy-start.51
  268.0 4.7 copy-start.79
  273.5 5.1 copy-start.85
  273.5 5.7 copy-start.41
  364.4 10.8 %collective-permute-start.2 = (bf16[19968,128]{1,0:T(8,128)(2,1)}, bf16[19968,128]{1,0:T(8,128)(2,1)}, u32[]{:S(2)}, u32[]{:S(2)}) collective-permute-start(bf16[19968,128]{1,0:T(8,128)(2,1)} %get-tuple-element.127), channel_id=1, source_target_pairs={{0,1},{1,0},{2,3},{3,2},{4,5},{5,4},{6,7},{7,6},{8,9},{9,8},{10,11... | collective-permute-start | bytes 15335432 | tf_op jit(solution)/shard_map/ppermute | solution.py:341
  385.3 23.9 %collective-permute-start.5 = (bf16[1,3584,128]{2,1,0:T(8,128)(2,1)}, bf16[1,3584,128]{2,1,0:T(8,128)(2,1)S(1)}, u32[]{:S(2)}, u32[]{:S(2)}) collective-permute-start(bf16[1,3584,128]{2,1,0:T(8,128)(2,1)} %constant_dynamic-slice_fusion.3), channel_id=1, source_target_pairs={{0,4},{4,0},{2,6},{6,2},{8,12},{12,8},{10,14},{14,10},{16,20},{20,... | collective-permute-start | bytes 2752520 | tf_op jit(solution)/shard_map/ppermute | solution.py:317
  390.0 23.4 %collective-permute-start.3 = (bf16[1,3584,128]{2,1,0:T(8,128)(2,1)}, bf16[1,3584,128]{2,1,0:T(8,128)(2,1)}, u32[]{:S(2)}, u32[]{:S(2)}) collective-permute-start(bf16[1,3584,128]{2,1,0:T(8,128)(2,1)} %constant_dynamic-slice_fusion.5), channel_id=1, source_target_pairs={{0,2},{2,0},{4,6},{6,4},{8,10},{10,8},{12,14},{14,12},{16,18},{18,... | collective-permute-start | bytes 2752520 | tf_op jit(solution)/shard_map/ppermute | solution.py:317
  390.6 46.4 %all-to-all-start = ((bf16[4,1408,128]{2,1,0:T(8,128)(2,1)}), bf16[4,1408,128]{2,1,0:T(8,128)(2,1)}, u32[]{:S(2)}, u32[]{:S(2)}) async-start(bf16[4,1408,128]{2,1,0:T(8,128)(2,1)} %bitcast.244), calls=%async_computation.1 | async-start | bytes 2883584 | tf_op jit(solution)/shard_map/all_to_all | solution.py:320
  394.9 255.6 %all-gather.3.cloned.1.call-start = ((), (), s32[]{:S(2)}) async-start(), calls=%async_computation.8 | async-start | bytes 5431296 | tf_op jit(solution)/shard_map/all_gather | solution.py:790
  410.6 13.8 %collective-permute-start.6 = (bf16[1,1792,128]{2,1,0:T(8,128)(2,1)S(1)}, bf16[1,1792,128]{2,1,0:T(8,128)(2,1)S(1)}, u32[]{:S(2)}, u32[]{:S(2)}) collective-permute-start(bf16[1,1792,128]{2,1,0:T(8,128)(2,1)S(1)} %constant_dynamic-slice_fusion.2), channel_id=1, source_target_pairs={{0,2},{2,0},{4,6},{6,4},{8,10},{10,8},{12,14},{14,12},{16,18},{18,... | collective-permute-start | bytes 1376264 | tf_op jit(solution)/shard_map/ppermute | solution.py:317
  414.9 98.7 %copy-start.60 = (bf16[624,128]{1,0:T(8,128)(2,1)S(1)}, bf16[624,128]{1,0:T(8,128)(2,1)}, u32[]{:S(2)}) copy-start(bf16[624,128]{1,0:T(8,128)(2,1)} %reduce-scatter.3.cloned.1.call-done) | copy-start | bytes 479236
  414.9 10.8 %collective-permute-start.4 = (bf16[1,1792,128]{2,1,0:T(8,128)(2,1)S(1)}, bf16[1,1792,128]{2,1,0:T(8,128)(2,1)S(1)}, u32[]{:S(2)}, u32[]{:S(2)}) collective-permute-start(bf16[1,1792,128]{2,1,0:T(8,128)(2,1)S(1)} %constant_dynamic-slice_fusion.4), channel_id=1, source_target_pairs={{0,4},{4,0},{2,6},{6,2},{8,12},{12,8},{10,14},{14,10},{16,20},{20,... | collective-permute-start | bytes 1376264 | tf_op jit(solution)/shard_map/ppermute | solution.py:317
  516.2 32.8 %all-to-all-start.1 = ((bf16[4,896,128]{2,1,0:T(8,128)(2,1)}), bf16[4,896,128]{2,1,0:T(8,128)(2,1)S(1)}, u32[]{:S(2)}, u32[]{:S(2)}) async-start(bf16[4,896,128]{2,1,0:T(8,128)(2,1)} %pad_maximum_fusion.5), calls=%async_computation.3 | async-start | bytes 1835008 | tf_op jit(solution)/shard_map/all_to_all | solution.py:320
  519.8 4.4 collective-permute-start.7
  524.3 3.7 collective-permute-start.8
  550.3 38.9 %all-to-all-start.2 = ((bf16[4,1,896,128]{3,2,1,0:T(8,128)(2,1)}), bf16[4,1,896,128]{3,2,1,0:T(8,128)(2,1)S(1)}, u32[]{:S(2)}, u32[]{:S(2)}) async-start(bf16[4,1,896,128]{3,2,1,0:T(8,128)(2,1)} %broadcast_in_dim.48), calls=%async_computation.4 | async-start | bytes 1835008 | tf_op jit(solution)/shard_map/all_to_all | solution.py:320
  553.8 6.1 collective-permute-start.9
  560.0 7.4 collective-permute-start.10
  589.3 20.9 %collective-permute-start.13 = (bf16[1,1792,128]{2,1,0:T(8,128)(2,1)S(1)}, bf16[1,1792,128]{2,1,0:T(8,128)(2,1)}, u32[]{:S(2)}, u32[]{:S(2)}) collective-permute-start(bf16[1,1792,128]{2,1,0:T(8,128)(2,1)S(1)} %bitcast.270), channel_id=1, source_target_pairs={{0,2},{2,0},{4,6},{6,4},{8,10},{10,8},{12,14},{14,12},{16,18},{18,... | collective-permute-start | bytes 1376264 | tf_op jit(solution)/shard_map/ppermute | solution.py:317
  590.5 22.0 %collective-permute-start.11 = (bf16[1,1792,128]{2,1,0:T(8,128)(2,1)S(1)}, bf16[1,1792,128]{2,1,0:T(8,128)(2,1)S(1)}, u32[]{:S(2)}, u32[]{:S(2)}) collective-permute-start(bf16[1,1792,128]{2,1,0:T(8,128)(2,1)S(1)} %bitcast.268), channel_id=1, source_target_pairs={{0,4},{4,0},{2,6},{6,2},{8,12},{12,8},{10,14},{14,10},{16,20},{20,... | collective-permute-start | bytes 1376264 | tf_op jit(solution)/shard_map/ppermute | solution.py:317
  593.0 58.9 %all-to-all-start.3 = ((bf16[4,1,1408,128]{3,2,1,0:T(8,128)(2,1)}), bf16[4,1,1408,128]{3,2,1,0:T(8,128)(2,1)S(1)}, u32[]{:S(2)}, u32[]{:S(2)}) async-start(bf16[4,1,1408,128]{3,2,1,0:T(8,128)(2,1)} %broadcast_in_dim.50), calls=%async_computation.5 | async-start | bytes 2883584 | tf_op jit(solution)/shard_map/all_to_all | solution.py:320
  611.3 40.5 %copy-start.35 = (bf16[2,1792,128]{2,1,0:T(8,128)(2,1)}, bf16[2,1792,128]{2,1,0:T(8,128)(2,1)S(1)}, u32[]{:S(2)}) copy-start(bf16[2,1792,128]{2,1,0:T(8,128)(2,1)S(1)} %pad_maximum_fusion.7) | copy-start | bytes 2752516
  611.3 40.4 %collective-permute-start.14 = (bf16[3584,128]{1,0:T(8,128)(2,1)S(1)}, bf16[3584,128]{1,0:T(8,128)(2,1)}, u32[]{:S(2)}, u32[]{:S(2)}) collective-permute-start(bf16[3584,128]{1,0:T(8,128)(2,1)S(1)} %bitcast.250), channel_id=1, source_target_pairs={{0,4},{4,0},{2,6},{6,2},{8,12},{12,8},{10,14},{14,10},{16,20},{20,... | collective-permute-start | bytes 2752520 | tf_op jit(solution)/shard_map/ppermute | solution.py:317
  612.7 39.1 %copy-start.36 = (bf16[2,1792,128]{2,1,0:T(8,128)(2,1)}, bf16[2,1792,128]{2,1,0:T(8,128)(2,1)S(1)}, u32[]{:S(2)}) copy-start(bf16[2,1792,128]{2,1,0:T(8,128)(2,1)S(1)} %pad_maximum_fusion.6) | copy-start | bytes 2752516
  612.7 39.0 %collective-permute-start.12 = (bf16[3584,128]{1,0:T(8,128)(2,1)S(1)}, bf16[3584,128]{1,0:T(8,128)(2,1)}, u32[]{:S(2)}, u32[]{:S(2)}) collective-permute-start(bf16[3584,128]{1,0:T(8,128)(2,1)S(1)} %bitcast.252), channel_id=1, source_target_pairs={{0,2},{2,0},{4,6},{6,4},{8,10},{10,8},{12,14},{14,12},{16,18},{18,... | collective-permute-start | bytes 2752520 | tf_op jit(solution)/shard_map/ppermute | solution.py:317
  650.5 170.9 %collective-permute-start.16 = (bf16[16,2,624,128]{3,2,1,0:T(8,128)(2,1)}, bf16[16,2,624,128]{3,2,1,0:T(8,128)(2,1)}, u32[]{:S(2)}, u32[]{:S(2)}) collective-permute-start(bf16[16,2,624,128]{3,2,1,0:T(8,128)(2,1)} %bitcast.219), channel_id=1, source_target_pairs={{0,1},{2,3},{4,5},{6,7},{8,9},{10,11},{12,13},{14,15},{16,17},{18,... | collective-permute-start | bytes 15335432 | tf_op jit(solution)/shard_map/ppermute | solution.py:485
  808.9 40.1 %collective-permute-start.15 = (bf16[19968,128]{1,0:T(8,128)(2,1)}, bf16[19968,128]{1,0:T(8,128)(2,1)}, u32[]{:S(2)}, u32[]{:S(2)}) collective-permute-start(bf16[19968,128]{1,0:T(8,128)(2,1)} %join.1.low_rows), channel_id=1, source_target_pairs={{1,0},{3,2},{5,4},{7,6},{9,8},{11,10},{13,12},{15,14},{17,16},{19,... | collective-permute-start | bytes 15335432 | tf_op jit(solution)/shard_map/ppermute | solution.py:485
  816.4 32.6 %slice-start = ((s8[5111808]{0:T(1024)(128)(4,1)}), s8[917504]{0:T(1024)(128)(4,1)S(1)}, s32[]{:S(2)}) async-start(s8[5111808]{0:T(1024)(128)(4,1)} %bitcast.220), calls=%async_computation.9 | async-start | bytes 1835008
  823.9 25.2 %slice-start.1 = ((s8[5111808]{0:T(1024)(128)(4,1)}), s8[4194304]{0:T(1024)(128)(4,1)S(1)}, s32[]{:S(2)}) async-start(s8[5111808]{0:T(1024)(128)(4,1)} %bitcast.220), calls=%async_computation.10 | async-start | bytes 8388608
  849.0 23.3 %copy-start.1 = (bf16[6,256,768]{2,1,0:T(8,128)(2,1)S(1)}, bf16[6,256,768]{2,1,0:T(8,128)(2,1)}, u32[]{:S(2)}) copy-start(bf16[6,256,768]{2,1,0:T(8,128)(2,1)} %param.9) | copy-start | bytes 7077892
  (86 other events, 187.1 us)
Sparse Core Ops, SparseCore 0:
  233.2 131.1 reduce-scatter.2
  369.9 143.5 reduce-scatter.4
  516.9 133.4 all-gather.2

commit v4 on v3

--- a/solution.py
+++ b/solution.py
@@ -349,7 +349,7 @@
     return Line(1, 2), Line(2, 2), Line(4, lax.axis_size("wide") // 4)
 
 
-def staged_scatter(total, beside=()):
+def staged_scatter(total):
     x, y, z = wide_lines()
     unit = lax.axis_size("wide") * 8
     most = total.shape[0] // unit * 4 // 11
@@ -362,24 +362,24 @@
     b = y.scatter(flat3(b, 2))
     a = y.scatter(flat3(a, 2))
     b = x.scatter(flat3(b, 2))
-    a, b, c, beside = lax.optimization_barrier((a, b, c, beside))
+    a, b, c = lax.optimization_barrier((a, b, c))
     ab = z.scatter(jnp.concatenate([flat3(a, z.size), flat3(b, z.size)], 1))
     c = x.scatter(flat3(c, 2))
     c = y.scatter(flat3(c, 2))
-    return lax.optimization_barrier((ab, c)), beside
-
-
-def staged_gather(ab, c):
+    return lax.optimization_barrier((ab, c))
+
+
+def staged_gather(ab, c, beside=()):
     x, y, z = wide_lines()
     ab = z.gather(flat3(ab, 1))
     c = x.gather(y.gather(flat3(c, 1)))
-    ab, c = lax.optimization_barrier((ab, c))
+    ab, c, beside = lax.optimization_barrier((ab, c, beside))
     half = ab.shape[1] // 2
     a, b = ab[:, :half], ab[:, half:]
     c = z.gather(flat3(c, 1))
     a = y.gather(flat3(a, 1)).reshape(-1, 128)
     b = x.gather(flat3(b, 1)).reshape(-1, 128)
-    return join_pieces((x, a, x.swap(a)), (y, b, y.swap(b)), c.reshape(-1, 128))
+    return join_pieces((x, a, x.swap(a)), (y, b, y.swap(b)), c.reshape(-1, 128)), beside
 
 
 def join_pieces(first, second, third):
@@ -405,12 +405,11 @@
         for copy in copies:
             copy.wait()
 
-    anywhere = pl.BlockSpec(memory_space=pl.ANY)
     return pl.pallas_call(
         kernel,
         out_shape=jax.ShapeDtypeStruct((sum(sizes) + third.shape[0], 128), third.dtype),
-        in_specs=[anywhere] * 5,
-        out_specs=anywhere,
+        in_specs=[pl.BlockSpec(memory_space=pltpu.VMEM)] * 5,
+        out_specs=pl.BlockSpec(memory_space=pl.ANY),
         scratch_shapes=[pltpu.SemaphoreType.DMA((5,))],
         name="join",
     )(first[1], first[2], second[1], second[2], third)
@@ -429,7 +428,24 @@
         total = added(total, narrow_swap(other, step))
     unit = lax.axis_size("wide") * 16
     total = jnp.pad(total, ((0, round_up(rows, unit) - rows), (0, 0)))
-    return staged_gather(*staged_scatter(total)[0])[:rows]
+    return staged_gather(*staged_scatter(total))[0][:rows]
+
+
+def scatter_first(value):
+    x, y, z = wide_lines()
+    a, b = jnp.split(value, 2)
+    return x.scatter(flat3(a, 2)), y.scatter(flat3(b, 2))
+
+
+def scatter_second(pair):
+    x, y, z = wide_lines()
+    return y.scatter(flat3(pair[0], 2)), x.scatter(flat3(pair[1], 2))
+
+
+def scatter_last(pair):
+    z = wide_lines()[2]
+    both = jnp.concatenate([flat3(v, z.size) for v in pair], 1)
+    return z.scatter(both).reshape(-1, 128)
 
 
 BLOCK = 2496
@@ -450,16 +466,16 @@
         return pl.BlockSpec((BLOCK, 128), index_map)
 
     here = spec(lambda i, core: (i + shift, 0))
-    group = BLOCK // high.shape[2]
-    count = high.shape[0] // group
+    high = high.reshape(-1, 4, 2, BLOCK // 4, 128)
 
     def high_place(i, core):
         turn = jnp.where(core[0] == 1, i, 0)
-        return turn % count, turn // count, 0, 0
+        part, spot = turn // 4, turn % 4
+        return 0, jnp.where(part == 0, spot % 2 * 2 + spot // 2, spot), part, 0, 0
 
     parts = (
         spec(lambda i, core: (jnp.where(core[0] == 0, i, 0), 0)),
-        pl.BlockSpec((group, 1, high.shape[2], 128), high_place),
+        pl.BlockSpec((4, 1, 1, BLOCK // 4, 128), high_place),
     )
     core = lax.axis_index("narrow").astype(jnp.int32).reshape(1)
     return pl.pallas_call(
@@ -475,10 +491,6 @@
         compiler_params=pltpu.CompilerParams(vmem_limit_bytes=40 << 20),
         name=f"adam{start}",
     )(core, low, high, moment1, moment2, *held)
-
-
-def scatter_wide(value):
-    return lax.psum_scatter(value, "wide", scatter_dimension=0, tiled=True)
 
 
 def to_owner(value, source):
@@ -766,29 +778,32 @@
     if chunked:
         high = pack_part(grads, half_rows, cut, *upper, held)
         d_enc_out, high = tie((d_enc_out, high))
-        high = [scatter_wide(part) for part in jnp.split(narrow_sum(high), 2)]
+        high = scatter_first(narrow_sum(high))
     d_mid, d_hidden, more = mlp_backward(d_enc_out, enc_kept, weights_map, "e")
     grads.update(more)
     grads["eu"] = hidden_gradient(enc_kept, d_hidden)
     if chunked:
         cut = round_up(flat_rows()[0]["eu"][0], 128)
         held = pack_part(grads, cut, padded, 0, padded)
-        d_mid, held = tie((d_mid, held))
+        d_mid, held, high = tie((d_mid, held, high))
+        high = scatter_second(high)
     attention = scores_backward(d_mid, enc_kept, weights_map, "e", HE)
+    if chunked:
+        attention, d_mid, high = tie((attention, d_mid, high))
+        high = scatter_last(high)
     d_enc_in, more = stream_backward(d_mid, *attention, enc_kept, weights_map, "e", HE)
     grads.update(more)
     grads["cls"] = jnp.sum(d_enc_in[:, 0, :], 0)
     chips_all = float(chips * lax.axis_size("wide") * lax.axis_size("narrow"))
     if chunked:
         low = pack_part(grads, 0, cut, 0, padded, held)
-        d_enc_in, low, high[0] = tie((d_enc_in, low, high[0]))
+        d_enc_in, low, high = tie((d_enc_in, low, high))
+        high = lax.all_gather(high, "wide")
     patch_grad = jnp.einsum(
         "cvp,cvd->cpd", choose_full, d_enc_in[:, 2:, :], precision=highest
     ).astype(jnp.bfloat16)
     if chunked:
-        low, high = staged_scatter(narrow_sum(low), high)
-        high = lax.all_gather(jnp.stack(high), "wide")
-        low = staged_gather(*low)
+        low, high = staged_gather(*staged_scatter(narrow_sum(low)), high)
         start = low.shape[0]
         held = adam_rows(low, to_owner(high, 0), moment1, moment2, 0, (), chips_all)
         grad_out, update, new_moment1, new_moment2 = adam_rows(

time: 887 us -> 607 us (0.68)
  Pallas kernels: 255 us -> 105 us
  waiting for transfers between devices: 311 us -> 172 us
  other arithmetic: 51.3 us -> 60.6 us
    pallas_call x1, Pallas kernels: 156 us -> 4.85 us  [join_pieces(): pl.pallas_call(kernel, out_shape=jax.ShapeDtypeStruct((sum(sizes) + third...]
    reduce_scatter x2 -> x0, waiting for transfers between devices: 147 us -> none  [scatter_wide(): return lax.psum_scatter(value, 'wide', scatter_dimension=0, tiled=True)]
    all_gather x1, waiting for transfers between devices: 35.4 us -> 0.02 us  [per_device(): high = lax.all_gather(high, 'wide')]
    ppermute x12 -> x16, waiting for transfers between devices: 56 us -> 89.7 us  [swap(): return lax.ppermute(value, 'wide', pairs)]
    all_to_all x4 -> x5, waiting for transfers between devices: 54 us -> 63.6 us  [exchange(): return lax.all_to_all(value, 'wide', 0, 0, axis_index_groups=self.groups)]
    convert_element_type x8 -> x12, other arithmetic: 9.89 us -> 19.1 us  [added(): (first.astype(jnp.float32) + second.astype(jnp.float32)).astype(jnp.bfloa...]
    all_to_all x4 -> x5, starting transfers between devices: 14.9 us -> 19.7 us  [exchange(): return lax.all_to_all(value, 'wide', 0, 0, axis_index_groups=self.groups)]
    unnamed x252 -> x258, local copies, waits for them, and re-layouts: 21.4 us -> 18.5 us
  transfers between devices with their start and end apart: 24 -> 27, of which waited for: 17 -> 21; matrix products, arithmetic and copies ran while one was open for 10% -> 13% of each run, Pallas kernels for 22% -> 8%
where the time goes in v4:
time: 607 us; the launch traced here: 598 us
  waiting for transfers between devices  172 us (28%)
  matrix products  147 us (24%)
  Pallas kernels  105 us (17%)
  other arithmetic  60.6 us (10%)
  local copies, waits for them, and re-layouts  53.3 us (9%)
  starting transfers between devices  44 us (7%)
  between operations  16.2 us (3%)
    ppermute x16, waiting for transfers between devices, swap(): return lax.ppermute(value, 'wide', pairs)  89.7 us
    all_to_all x5, waiting for transfers between devices, exchange(): return lax.all_to_all(value, 'wide', 0, 0, axis_index_groups=self.groups)  63.6 us
    pallas_call x2, Pallas kernels, adam_rows(): pl.pallas_call(kernel, out_shape=[jax.ShapeDtypeStruct(moment1.shape, jnp...  50.2 us
    pallas_call x4, Pallas kernels, pack_part(): pl.pallas_call(kernel, out_shape=[jax.ShapeDtypeStruct((middle - first, 1...  32.1 us
    dot_general x2, matrix products, block_forward(): jnp.einsum('ctd,df->ctf', second_in, weights_map[prefix + 'u'], preferred...  30.2 us
    all_to_all x5, starting transfers between devices, exchange(): return lax.all_to_all(value, 'wide', 0, 0, axis_index_groups=self.groups)  19.7 us
    convert_element_type x12, other arithmetic, added(): (first.astype(jnp.float32) + second.astype(jnp.float32)).astype(jnp.bfloa...  19.1 us
    ppermute x3, waiting for transfers between devices, narrow_swap(): lax.ppermute(value, 'narrow', [(i, (i + step) % count) for i in range(cou...  18.5 us
  transfers between devices with their start and end apart: 27, of which 21 were waited for; matrix products, arithmetic and copies ran while one was open for 13% of the time, Pallas kernels for 8%

profile of v4, /device:TPU:1, one launch (start us, length us, event | category | flops | bytes accessed | tf_op | source)
XLA Modules:
  0.0 598.2 jit_solution(11838679853986570578)
XLA Ops:
  7.2 7.7 %convert_element_type.339.refs_0_ = bf16[39552,128]{1,0:T(8,128)(2,1)S(1)} convert(f32[39552,128]{1,0:T(8,128)} %param.14) | non-fusion elementwise | flops 5062656 | bytes 30375936 | tf_op jit(solution)/shard_map/convert_element_type | solution.py:501
  20.7 10.1 %collective-permute-done.refs_1_ = bf16[39552,128]{1,0:T(8,128)(2,1)} collective-permute-done((bf16[39552,128]{1,0:T(8,128)(2,1)S(1)}, bf16[39552,128]{1,0:T(8,128)(2,1)}, u32[]{:S(2)}, u32[]{:S(2)}) %collective-permute-start) | collective-permute-done | bytes 10125344 | tf_op jit(solution)/shard_map/ppermute | solution.py:341
  30.8 18.1 %unpack.1 = (f32[1,768]{1,0:T(1,128)}, f32[1,768]{1,0:T(1,128)}, f32[1,768]{1,0:T(1,128)}, bf16[768,2304]{1,0:T(8,128)(2,1)}, bf16[768,768]{1,0:T(8,128)(2,1)}, ...) custom-call(bf16[39552,128]{1,0:T(8,128)(2,1)} %copy-done.11, ...), custom_call_target="tpu_custom_call" | custom-call | tf_op jit(solution)/shard_map/unpack/pallas_call | solution.py:171
  52.4 4.0 convolution_convert_fusion
  60.2 2.6 copy.132
  71.1 11.7 %fusion.14 = (bf16[6,66,3072]{2,1,0:T(8,128)(2,1)}, bf16[6,66,3072]{2,1,0:T(8,128)(2,1)}) fusion(f32[3072]{0:T(1024)S(1)} %bitcast.321, bf16[768,3072]{1,0:T(8,128)(2,1)} %get-tuple-element.90, f32[6,66,768]{2,1,0:T(8,128)} %copy-done.12, f32[768]{0:T(1024)S(1)} %reduce.9, f32[768]{0:T(1024)S(1)} %reduce.8, f32[6,66]{1,0:T(8,128)S(1)} %fusion.92, ...), kind=kOutput, calls=%fused_computation.31 | convolution fusion | flops 1911444480 | bytes 10822752 | tf_op jit(solution)/shard_map/ctd,df->ctf/dot_general | solution.py:596
  82.8 5.5 fusion.17
  90.2 2.2 fusion.120
  105.3 18.5 %fusion.6 = (bf16[6,256,2048]{2,1,0:T(8,128)(2,1)S(1)}, bf16[6,256,2048]{2,1,0:T(8,128)(2,1)}) fusion(f32[2048]{0:T(1024)S(1)} %bitcast.322, bf16[512,2048]{1,0:T(8,128)(2,1)S(1)} %copy-done.108, f32[6,256,512]{2,1,0:T(8,128)S(1)} %get-tuple-element.225, f32[512]{0:T(512)S(1)} %bitcast.326, f32[512]{0:T(512)S(1)} %bitcast.304, f32[6,256]{1,0:T(8,128)S(1)} %fusion.90, ...), kind=kOutput, calls=%fused_computation.8 | convolution fusion | flops 3332112384 | bytes 17850368 | tf_op jit(solution)/shard_map/ctd,df->ctf/dot_general | solution.py:596
  123.9 4.3 convert_reduce_fusion
  128.1 5.3 bitcast_convert_fusion.4.refs_0_
  133.5 4.7 fusion.107
  140.4 4.7 bitcast_convert_fusion.3.refs_2_
  145.0 6.1 %convert_add_fusion = (f32[6,256,512]{2,1,0:T(8,128)}, bf16[6,256,512]{2,1,0:T(8,128)(2,1)}, f32[512]{0:T(512)}) fusion(bf16[6,256,512]{2,1,0:T(8,128)(2,1)S(1)} %copy-done.109, f32[6,256]{1,0:T(8,128)S(1)} %negate_multiply_fusion.1, f32[6,256]{1,0:T(8,128)S(1)} %multiply_multiply_fusion.3, f32[6,256,512]{2,1,0:T(8,128)S(1)} %get-tuple-element.225, ...), kind=kOutput, calls=%fused_computation.51 | convolution fusion | flops 3231448576 | bytes 21002240 | tf_op jit(solution)/shard_map/ctf,fd->ctd/dot_general | solution.py:602
  151.1 7.9 %pack62592.1 = (bf16[19968,128]{1,0:T(8,128)(2,1)}, bf16[19968,128]{1,0:T(8,128)(2,1)}) custom-call(bf16[512,2048]{1,0:T(8,128)(2,1)} %bitcast_convert_fusion.4.refs_0_, f32[1,2048]{1,0:T(1,128)} %bitcast.299, bf16[2048,512]{1,0:T(8,128)(2,1)} %bitcast_convert_fusion.3.refs_2_, f32[1,512]{1,0:T(1,128)} %bitcast.314), custom_call_target="tpu_custom_call" | custom-call | tf_op jit(solution)/shard_map/pack62592/pallas_call | solution.py:273
  159.0 3.3 fusion.57.refs_10_
  163.5 7.2 %multiply_reduce_fusion = (f32[6,4,256]{2,1,0:T(4,128)S(1)}, f32[6,4,256,256]{2,3,1,0:T(8,128)}) fusion(f32[6,4,256,256]{2,3,1,0:T(8,128)} %copy-done.3, f32[6,4,256]{2,1,0:T(4,128)S(1)} %bitcast.293, bf16[6,256,4,64]{1,3,2,0:T(8,128)(2,1)S(1)} %bitcast.247, bf16[6,256,4,64]{1,3,2,0:T(8,128)(2,1)S(1)} %bitcast.275), kind=kOutput, calls=%fused_computation.21 | convolution fusion | flops 207611904 | bytes 14204928 | tf_op jit(solution)/shard_map/cqhe,ckhe->chqk/dot_general | solution.py:675
  170.7 4.5 multiply_convert_fusion.1
  179.1 4.6 bitcast_convert_fusion.6.refs_9_
  183.8 2.7 multiply_reduce_fusion.3
  189.7 2.2 convert_reduce_fusion.6
  196.1 4.3 bitcast_convert_fusion.1.refs_0_
  204.8 9.0 %pack39552.1 = (bf16[19968,128]{1,0:T(8,128)(2,1)}, bf16[19968,128]{1,0:T(8,128)(2,1)}) custom-call(bf16[3072,768]{1,0:T(8,128)(2,1)} %bitcast_convert_fusion.1.refs_0_, f32[1,768]{1,0:T(1,128)} %reshape.408.refs_1_, f32[1,768]{1,0:T(1,128)} %reshape.409.refs_2_, f32[1,768]{1,0:T(1,128)} %reshape.410.refs_3_, ...), custom_call_target="tpu_custom_call", output_to_operand_aliasing={{0}: (15, {}), {1}: (16, {})} | custom-call | tf_op jit(solution)/shard_map/pack39552/pallas_call | solution.py:273
  214.1 6.6 %convert_reduce_fusion.1 = (f32[3072]{0:T(1024)}, bf16[6,66,3072]{2,1,0:T(8,128)(2,1)S(1)}) fusion(bf16[6,66,3072]{2,1,0:T(8,128)(2,1)} %get-tuple-element.121, bf16[3072,768]{1,0:T(8,128)(2,1)} %get-tuple-element.93, f32[6,66,768]{2,1,0:T(8,128)} %get-tuple-element.120), kind=kOutput, calls=%fused_computation.32 | convolution fusion | flops 1874946048 | bytes 10813440 | tf_op jit(solution)/shard_map/ctd,fd->ctf/dot_general | solution.py:635
  220.7 2.5 fusion.108
  224.0 3.2 bitcast_convert_fusion.refs_0_
  227.2 5.2 add_convert_fusion.1
  234.4 2.6 collective-permute-start.3
  245.4 8.3 %pack18560.1 = (bf16[19968,128]{1,0:T(8,128)(2,1)}, bf16[19968,128]{1,0:T(8,128)(2,1)}) custom-call(bf16[768,3072]{1,0:T(8,128)(2,1)} %copy-done.33, f32[1,3072]{1,0:T(1,128)} %bitcast.298, bf16[512,768]{1,0:T(8,128)(2,1)} %slice.77.refs_2_), custom_call_target="tpu_custom_call" | custom-call | tf_op jit(solution)/shard_map/pack18560/pallas_call | solution.py:273
  253.8 11.8 %collective-permute-done.3 = bf16[1,4992,128]{2,1,0:T(8,128)(2,1)} collective-permute-done((bf16[1,4992,128]{2,1,0:T(8,128)(2,1)}, bf16[1,4992,128]{2,1,0:T(8,128)(2,1)}, u32[]{:S(2)}, u32[]{:S(2)}) %collective-permute-start.3) | collective-permute-done | bytes 1277984 | tf_op jit(solution)/shard_map/ppermute | solution.py:317
  276.9 2.7 fusion.47
  279.6 5.5 multiply_convert_fusion.4
  294.7 4.6 all-to-all-start
  300.8 2.4 copy.115
  304.7 4.4 fusion.109
  316.5 4.0 bitcast_convert_fusion.2.refs_3_
  320.5 6.8 %pack0.1 = (bf16[19968,128]{1,0:T(8,128)(2,1)}, bf16[19968,128]{1,0:T(8,128)(2,1)}) custom-call(f32[1,768]{1,0:T(1,128)} %reshape.425.refs_0_, f32[1,768]{1,0:T(1,128)} %reshape.426.refs_1_, f32[1,768]{1,0:T(1,128)} %reshape.427.refs_2_, bf16[768,2304]{1,0:T(8,128)(2,1)} %bitcast_convert_fusion.2.refs_3_, ...), custom_call_target="tpu_custom_call", output_to_operand_aliasing={{0}: (9, {}), {1}: (10, {})} | custom-call | tf_op jit(solution)/shard_map/pack0/pallas_call | solution.py:273
  327.4 2.2 all-to-all-done
  329.6 2.3 reduce_sum.504
  333.3 8.4 %collective-permute-done.6 = bf16[19968,128]{1,0:T(8,128)(2,1)} collective-permute-done((bf16[19968,128]{1,0:T(8,128)(2,1)}, bf16[19968,128]{1,0:T(8,128)(2,1)}, u32[]{:S(2)}, u32[]{:S(2)}) %collective-permute-start.6) | collective-permute-done | bytes 5111840 | tf_op jit(solution)/shard_map/ppermute | solution.py:341
  341.7 5.1 add_convert_fusion
  353.0 4.3 all-to-all-start.1
  357.3 17.7 %collective-permute-done.9 = bf16[1,3584,128]{2,1,0:T(8,128)(2,1)} collective-permute-done((bf16[1,3584,128]{2,1,0:T(8,128)(2,1)}, bf16[1,3584,128]{2,1,0:T(8,128)(2,1)}, u32[]{:S(2)}, u32[]{:S(2)}) %collective-permute-start.9) | collective-permute-done | bytes 917536 | tf_op jit(solution)/shard_map/ppermute | solution.py:317
  377.8 4.9 collective-permute-done.7
  383.3 9.2 %collective-permute-done.10 = bf16[1,1792,128]{2,1,0:T(8,128)(2,1)S(1)} collective-permute-done((bf16[1,1792,128]{2,1,0:T(8,128)(2,1)S(1)}, bf16[1,1792,128]{2,1,0:T(8,128)(2,1)S(1)}, u32[]{:S(2)}, u32[]{:S(2)}) %collective-permute-start.10) | collective-permute-done | bytes 458784 | tf_op jit(solution)/shard_map/ppermute | solution.py:317
  392.9 11.9 %all-to-all-done.1 = bf16[4,1408,128]{2,1,0:T(8,128)(2,1)} async-done(((bf16[4,1408,128]{2,1,0:T(8,128)(2,1)}), bf16[4,1408,128]{2,1,0:T(8,128)(2,1)}, u32[]{:S(2)}, u32[]{:S(2)}) %all-to-all-start.1) | async-done | bytes 1441824 | tf_op jit(solution)/shard_map/all_to_all | solution.py:320
  407.6 3.5 all-to-all-start.2
  412.0 9.3 %collective-permute-done.11 = bf16[1,704,128]{2,1,0:T(8,128)(2,1)S(1)} collective-permute-done((bf16[1,704,128]{2,1,0:T(8,128)(2,1)S(1)}, bf16[1,704,128]{2,1,0:T(8,128)(2,1)S(1)}, u32[]{:S(2)}, u32[]{:S(2)}) %collective-permute-start.11) | collective-permute-done | bytes 180256 | tf_op jit(solution)/shard_map/ppermute | solution.py:317
  421.5 4.3 collective-permute-done.12
  425.8 28.6 %all-to-all-done.2 = bf16[4,896,128]{2,1,0:T(8,128)(2,1)S(1)} async-done(((bf16[4,896,128]{2,1,0:T(8,128)(2,1)}), bf16[4,896,128]{2,1,0:T(8,128)(2,1)S(1)}, u32[]{:S(2)}, u32[]{:S(2)}) %all-to-all-start.2) | async-done | bytes 917536 | tf_op jit(solution)/shard_map/all_to_all | solution.py:320
  455.6 3.5 all-to-all-start.3
  459.8 3.2 collective-permute-done.13
  463.7 4.2 collective-permute-done.14
  468.0 13.7 %all-to-all-done.3 = bf16[4,1,896,128]{3,2,1,0:T(8,128)(2,1)S(1)} async-done(((bf16[4,1,896,128]{3,2,1,0:T(8,128)(2,1)}), bf16[4,1,896,128]{3,2,1,0:T(8,128)(2,1)S(1)}, u32[]{:S(2)}, u32[]{:S(2)}) %all-to-all-start.3) | async-done | bytes 917536 | tf_op jit(solution)/shard_map/all_to_all | solution.py:320
  484.6 3.8 all-to-all-start.4
  488.3 4.4 collective-permute-done.17
  496.9 17.0 %collective-permute-done.18.other2 = bf16[3584,128]{1,0:T(8,128)(2,1)S(1)} collective-permute-done((bf16[3584,128]{1,0:T(8,128)(2,1)S(1)}, bf16[3584,128]{1,0:T(8,128)(2,1)S(1)}, u32[]{:S(2)}, u32[]{:S(2)}) %collective-permute-start.18) | collective-permute-done | bytes 917536 | tf_op jit(solution)/shard_map/ppermute | solution.py:317
  514.8 7.2 %all-to-all-done.4 = bf16[4,1,1408,128]{3,2,1,0:T(8,128)(2,1)S(1)} async-done(((bf16[4,1,1408,128]{3,2,1,0:T(8,128)(2,1)}), bf16[4,1,1408,128]{3,2,1,0:T(8,128)(2,1)S(1)}, u32[]{:S(2)}, u32[]{:S(2)}) %all-to-all-start.4) | async-done | bytes 1441824 | tf_op jit(solution)/shard_map/all_to_all | solution.py:320
  523.1 4.8 join.1.low_rows
  528.0 5.6 collective-permute-start.19
  533.6 4.9 convolution_convert_fusion.1
  538.5 2.4 copy-done.2
  540.9 25.1 %adam0.1 = (f32[39552,128]{1,0:T(8,128)}, f32[39552,128]{1,0:T(8,128)}, f32[39552,128]{1,0:T(8,128)}, f32[39552,128]{1,0:T(8,128)}) custom-call(s32[1]{0:T(128)} %bitcast.67.core, bf16[19968,128]{1,0:T(8,128)(2,1)S(1)} %copy-done.2, bf16[4,4,2,624,128]{4,3,2,1,0:T(8,128)(2,1)} %bitcast.89.high_rows, f32[39552,128]{1,0:T(8,128)} %first.3, f32[39552,128]{1,0:T(8,128)} %second.3), custom_call_target="tpu_custom_call" | custom-call | tf_op jit(solution)/shard_map/adam0/pallas_call | solution.py:481
  566.0 25.1 %adam19968.1 = (f32[39552,128]{1,0:T(8,128)}, f32[39552,128]{1,0:T(8,128)}, f32[39552,128]{1,0:T(8,128)}, f32[39552,128]{1,0:T(8,128)}) custom-call(s32[1]{0:T(128)} %bitcast.67.core, bf16[19968,128]{1,0:T(8,128)(2,1)} %collective-permute-done.19.low_rows, ...), custom_call_target="tpu_custom_call", output_to_operand_aliasing={{0}: (5, {}), {1}: (6, {}), {2}: (7, {}), {3}: (8, {})} | custom-call | tf_op jit(solution)/shard_map/adam19968/pallas_call | solution.py:481
  (434 shorter events, 123.4 us)
Async XLA Ops:
  7.2 11.9 %copy-start = (bf16[6,256,768]{2,1,0:T(8,128)(2,1)S(1)}, bf16[6,256,768]{2,1,0:T(8,128)(2,1)}, u32[]{:S(2)}) copy-start(bf16[6,256,768]{2,1,0:T(8,128)(2,1)} %param.9) | copy-start | bytes 7077892
  7.2 7.9 %copy-start.119 = (s32[6]{0:T(128)S(1)}, s32[6]{0:T(128)}, u32[]{:S(2)}) copy-start(s32[6]{0:T(128)} %param.12) | copy-start | bytes 76
  7.2 7.9 %copy-start.90 = (bf16[6,768]{1,0:T(8,128)(2,1)S(1)}, bf16[6,768]{1,0:T(8,128)(2,1)}, u32[]{:S(2)}) copy-start(bf16[6,768]{1,0:T(8,128)(2,1)} %param.10) | copy-start | bytes 27652
  7.2 8.0 %copy-start.67 = (s32[6,64]{1,0:T(8,128)S(1)}, s32[6,64]{1,0:T(8,128)}, u32[]{:S(2)}) copy-start(s32[6,64]{1,0:T(8,128)} %param.11) | copy-start | bytes 4612
  15.0 15.8 %collective-permute-start = (bf16[39552,128]{1,0:T(8,128)(2,1)S(1)}, bf16[39552,128]{1,0:T(8,128)(2,1)}, u32[]{:S(2)}, u32[]{:S(2)}) collective-permute-start(bf16[39552,128]{1,0:T(8,128)(2,1)S(1)} %convert_element_type.339.refs_0_), channel_id=1, source_target_pairs={{0,1},{1,0},{2,3},{3,2},{4,5},{5,4},{6,7},{7,6},{8,9},{9,8},{10,11... | collective-permute-start | bytes 30375944 | tf_op jit(solution)/shard_map/ppermute | solution.py:341
  15.2 36.6 %copy-start.51 = (f32[6,1,768]{2,1,0:T(1,128)}, f32[6,1,768]{2,1,0:T(1,128)S(1)}, u32[]{:S(2)}) copy-start(f32[6,1,768]{2,1,0:T(1,128)S(1)} %broadcast_in_dim.36) | copy-start | bytes 55300
  20.7 29.0 %copy-start.9 = (f32[6,64,768]{2,1,0:T(8,128)S(1)}, f32[6,64,768]{2,1,0:T(8,128)}, u32[]{:S(2)}) copy-start(f32[6,64,768]{2,1,0:T(8,128)} %fusion.72) | copy-start | bytes 3538948
  58.3 6.2 %copy-start.20 = (bf16[6,66,768]{1,2,0:T(8,128)(2,1)}, bf16[6,66,768]{1,2,0:T(8,128)(2,1)S(1)}, u32[]{:S(2)}) copy-start(bf16[6,66,768]{1,2,0:T(8,128)(2,1)S(1)} %copy.133) | copy-start | bytes 1824772
  68.9 13.8 %copy-start.68 = (f32[6,66]{1,0:T(8,128)}, f32[6,66]{1,0:T(8,128)S(1)}, u32[]{:S(2)}) copy-start(f32[6,66]{1,0:T(8,128)S(1)} %broadcast_multiply_fusion.3) | copy-start | bytes 4756
  71.0 11.8 %copy-start.74 = (f32[6,66]{1,0:T(8,128)}, f32[6,66]{1,0:T(8,128)S(1)}, u32[]{:S(2)}) copy-start(f32[6,66]{1,0:T(8,128)S(1)} %fusion.92) | copy-start | bytes 4756
  71.0 11.7 %copy-start.76 = (f32[768]{0:T(1024)}, f32[768]{0:T(1024)S(1)}, u32[]{:S(2)}) copy-start(f32[768]{0:T(1024)S(1)} %reduce.8) | copy-start | bytes 9220
  71.0 11.7 %copy-start.93 = (f32[768]{0:T(1024)}, f32[768]{0:T(1024)S(1)}, u32[]{:S(2)}) copy-start(f32[768]{0:T(1024)S(1)} %reduce.9) | copy-start | bytes 9220
  71.0 11.7 %copy-start.99 = (f32[1,768]{1,0:T(1,128)S(1)}, f32[1,768]{1,0:T(1,128)}, u32[]{:S(2)}) copy-start(f32[1,768]{1,0:T(1,128)} %get-tuple-element.94) | copy-start | bytes 9220
  82.8 5.5 copy-start.13
  105.3 18.5 %copy-start.107 = (bf16[2048,512]{1,0:T(8,128)(2,1)S(1)}, bf16[2048,512]{1,0:T(8,128)(2,1)}, u32[]{:S(2)}) copy-start(bf16[2048,512]{1,0:T(8,128)(2,1)} %get-tuple-element.110) | copy-start | bytes 6291460
  105.3 18.5 %copy-start.109 = (bf16[6,256,512]{2,1,0:T(8,128)(2,1)S(1)}, bf16[6,256,512]{2,1,0:T(8,128)(2,1)}, u32[]{:S(2)}) copy-start(bf16[6,256,512]{2,1,0:T(8,128)(2,1)} %param.13) | copy-start | bytes 4718596
  128.1 12.2 %slice-start.6 = ((s8[6291456]{0:T(1024)(128)(4,1)}), s8[4194304]{0:T(1024)(128)(4,1)S(1)}, s32[]{:S(2)}) async-start(s8[6291456]{0:T(1024)(128)(4,1)} %bitcast.329), calls=%async_computation.12 | async-start | bytes 8388608
  133.5 6.9 %slice-start.7 = ((s8[6291456]{0:T(1024)(128)(4,1)}), s8[2097152]{0:T(1024)(128)(4,1)S(1)}, s32[]{:S(2)}) async-start(s8[6291456]{0:T(1024)(128)(4,1)} %bitcast.329), calls=%async_computation.13 | async-start | bytes 4194304
  163.0 7.7 %slice-start = ((s8[6291456]{0:T(1024)(128)(4,1)}), s8[4194304]{0:T(1024)(128)(4,1)S(1)}, s32[]{:S(2)}) async-start(s8[6291456]{0:T(1024)(128)(4,1)} %bitcast.227), calls=%async_computation.6 | async-start | bytes 8388608
  163.5 7.2 %slice-start.1 = ((s8[6291456]{0:T(1024)(128)(4,1)}), s8[2097152]{0:T(1024)(128)(4,1)S(1)}, s32[]{:S(2)}) async-start(s8[6291456]{0:T(1024)(128)(4,1)} %bitcast.227), calls=%async_computation.7 | async-start | bytes 4194304
  204.8 15.8 %slice-start.4 = ((s8[4718592]{0:T(1024)(128)(4,1)}), s8[524288]{0:T(1024)(128)(4,1)S(1)}, s32[]{:S(2)}) async-start(s8[4718592]{0:T(1024)(128)(4,1)} %bitcast.319), calls=%async_computation.10 | async-start | bytes 1048576
  213.8 13.3 %collective-permute-start.1 = (bf16[19968,128]{1,0:T(8,128)(2,1)}, bf16[19968,128]{1,0:T(8,128)(2,1)}, u32[]{:S(2)}, u32[]{:S(2)}) collective-permute-start(bf16[19968,128]{1,0:T(8,128)(2,1)} %get-tuple-element.125), channel_id=1, source_target_pairs={{0,1},{1,0},{2,3},{3,2},{4,5},{5,4},{6,7},{7,6},{8,9},{9,8},{10,11... | collective-permute-start | bytes 15335432 | tf_op jit(solution)/shard_map/ppermute | solution.py:341
  214.1 6.6 %copy-start.14 = (f32[6,66,768]{2,1,0:T(8,128)S(1)}, f32[6,66,768]{2,1,0:T(8,128)}, u32[]{:S(2)}) copy-start(f32[6,66,768]{2,1,0:T(8,128)} %copy-done.12) | copy-start | bytes 3649540
  214.1 6.6 %copy-start.69 = (f32[6,66]{1,0:T(8,128)S(1)}, f32[6,66]{1,0:T(8,128)}, u32[]{:S(2)}) copy-start(f32[6,66]{1,0:T(8,128)} %copy-done.68) | copy-start | bytes 4756
  214.1 6.6 %copy-start.77 = (f32[768]{0:T(1024)S(1)}, f32[768]{0:T(1024)}, u32[]{:S(2)}) copy-start(f32[768]{0:T(1024)} %copy-done.76) | copy-start | bytes 9220
  214.1 6.6 %slice-start.5 = ((s8[4718592]{0:T(1024)(128)(4,1)}), s8[4194304]{0:T(1024)(128)(4,1)S(1)}, s32[]{:S(2)}) async-start(s8[4718592]{0:T(1024)(128)(4,1)} %bitcast.319), calls=%async_computation.11 | async-start | bytes 8388608
  227.1 16.5 %copy-start.33 = (bf16[768,3072]{1,0:T(8,128)(2,1)}, bf16[768,3072]{1,0:T(8,128)(2,1)S(1)}, u32[]{:S(2)}) copy-start(bf16[768,3072]{1,0:T(8,128)(2,1)S(1)} %bitcast_convert_fusion.refs_0_) | copy-start | bytes 14155780
  233.2 5.3 copy-start.26
  233.2 5.3 copy-start.24
  234.4 31.2 %collective-permute-start.3 = (bf16[1,4992,128]{2,1,0:T(8,128)(2,1)}, bf16[1,4992,128]{2,1,0:T(8,128)(2,1)}, u32[]{:S(2)}, u32[]{:S(2)}) collective-permute-start(bf16[1,4992,128]{2,1,0:T(8,128)(2,1)} %constant_dynamic-slice_fusion.8), channel_id=1, source_target_pairs={{0,4},{4,0},{2,6},{6,2},{8,12},{12,8},{10,14},{14,10},{16,20},{20,... | collective-permute-start | bytes 3833864 | tf_op jit(solution)/shard_map/ppermute | solution.py:317
  239.7 29.5 %collective-permute-start.2 = (bf16[1,4992,128]{2,1,0:T(8,128)(2,1)}, bf16[1,4992,128]{2,1,0:T(8,128)(2,1)}, u32[]{:S(2)}, u32[]{:S(2)}) collective-permute-start(bf16[1,4992,128]{2,1,0:T(8,128)(2,1)} %constant_dynamic-slice_fusion.9), channel_id=1, source_target_pairs={{0,2},{2,0},{4,6},{6,4},{8,10},{10,8},{12,14},{14,12},{16,18},{18,... | collective-permute-start | bytes 3833864 | tf_op jit(solution)/shard_map/ppermute | solution.py:317
  253.8 15.4 %copy-start.25 = (bf16[9984,128]{1,0:T(8,128)(2,1)S(1)}, bf16[9984,128]{1,0:T(8,128)(2,1)}, u32[]{:S(2)}) copy-start(bf16[9984,128]{1,0:T(8,128)(2,1)} %copy-done.24) | copy-start | bytes 7667716
  267.7 7.7 %copy-start.18 = (f32[6,66,768]{2,1,0:T(8,128)S(1)}, f32[6,66,768]{2,1,0:T(8,128)}, u32[]{:S(2)}) copy-start(f32[6,66,768]{2,1,0:T(8,128)} %add_add_fusion.9) | copy-start | bytes 3649540
  267.7 7.7 %copy-start.37 = (bf16[768,768]{1,0:T(8,128)(2,1)S(1)}, bf16[768,768]{1,0:T(8,128)(2,1)}, u32[]{:S(2)}) copy-start(bf16[768,768]{1,0:T(8,128)(2,1)} %get-tuple-element.86) | copy-start | bytes 3538948
  271.8 15.0 %collective-permute-start.5 = (bf16[1,2496,128]{2,1,0:T(8,128)(2,1)}, bf16[1,2496,128]{2,1,0:T(8,128)(2,1)}, u32[]{:S(2)}, u32[]{:S(2)}) collective-permute-start(bf16[1,2496,128]{2,1,0:T(8,128)(2,1)} %constant_dynamic-slice_fusion.6), channel_id=1, source_target_pairs={{0,2},{2,0},{4,6},{6,4},{8,10},{10,8},{12,14},{14,12},{16,18},{18,... | collective-permute-start | bytes 1916936 | tf_op jit(solution)/shard_map/ppermute | solution.py:317
  273.9 14.7 %collective-permute-start.4 = (bf16[1,2496,128]{2,1,0:T(8,128)(2,1)}, bf16[1,2496,128]{2,1,0:T(8,128)(2,1)}, u32[]{:S(2)}, u32[]{:S(2)}) collective-permute-start(bf16[1,2496,128]{2,1,0:T(8,128)(2,1)} %constant_dynamic-slice_fusion.7), channel_id=1, source_target_pairs={{0,4},{4,0},{2,6},{6,2},{8,12},{12,8},{10,14},{14,10},{16,20},{20,... | collective-permute-start | bytes 1916936 | tf_op jit(solution)/shard_map/ppermute | solution.py:317
  293.5 5.7 copy-start.35
  294.7 34.9 %all-to-all-start = ((bf16[4,1248,128]{2,1,0:T(8,128)(2,1)}), bf16[4,1248,128]{2,1,0:T(8,128)(2,1)}, u32[]{:S(2)}, u32[]{:S(2)}) async-start(bf16[4,1248,128]{2,1,0:T(8,128)(2,1)} %pad_maximum_fusion.3), calls=%async_computation | async-start | bytes 2555904 | tf_op jit(solution)/shard_map/all_to_all | solution.py:320
  299.2 168.7 %all-gather.3.cloned.1.call-start = ((), (), s32[]{:S(2)}) async-start(), calls=%async_computation.5 | async-start | bytes 5431296 | tf_op jit(solution)/shard_map/all_gather | solution.py:801
  299.3 5.4 copy-start.10
  299.3 5.4 copy-start.71
  299.3 5.4 copy-start.89
  331.9 9.8 %collective-permute-start.6 = (bf16[19968,128]{1,0:T(8,128)(2,1)}, bf16[19968,128]{1,0:T(8,128)(2,1)}, u32[]{:S(2)}, u32[]{:S(2)}) collective-permute-start(bf16[19968,128]{1,0:T(8,128)(2,1)} %get-tuple-element.140), channel_id=1, source_target_pairs={{0,1},{1,0},{2,3},{3,2},{4,5},{5,4},{6,7},{7,6},{8,9},{9,8},{10,11... | collective-permute-start | bytes 15335432 | tf_op jit(solution)/shard_map/ppermute | solution.py:341
  348.2 26.9 %collective-permute-start.9 = (bf16[1,3584,128]{2,1,0:T(8,128)(2,1)}, bf16[1,3584,128]{2,1,0:T(8,128)(2,1)}, u32[]{:S(2)}, u32[]{:S(2)}) collective-permute-start(bf16[1,3584,128]{2,1,0:T(8,128)(2,1)} %constant_dynamic-slice_fusion.3), channel_id=1, source_target_pairs={{0,4},{4,0},{2,6},{6,2},{8,12},{12,8},{10,14},{14,10},{16,20},{20,... | collective-permute-start | bytes 2752520 | tf_op jit(solution)/shard_map/ppermute | solution.py:317
  352.0 30.7 %collective-permute-start.7 = (bf16[1,3584,128]{2,1,0:T(8,128)(2,1)}, bf16[1,3584,128]{2,1,0:T(8,128)(2,1)S(1)}, u32[]{:S(2)}, u32[]{:S(2)}) collective-permute-start(bf16[1,3584,128]{2,1,0:T(8,128)(2,1)} %constant_dynamic-slice_fusion.5), channel_id=1, source_target_pairs={{0,2},{2,0},{4,6},{6,4},{8,10},{10,8},{12,14},{14,12},{16,18},{18,... | collective-permute-start | bytes 2752520 | tf_op jit(solution)/shard_map/ppermute | solution.py:317
  353.0 51.8 %all-to-all-start.1 = ((bf16[4,1408,128]{2,1,0:T(8,128)(2,1)}), bf16[4,1408,128]{2,1,0:T(8,128)(2,1)}, u32[]{:S(2)}, u32[]{:S(2)}) async-start(bf16[4,1408,128]{2,1,0:T(8,128)(2,1)} %bitcast.250), calls=%async_computation.1 | async-start | bytes 2883584 | tf_op jit(solution)/shard_map/all_to_all | solution.py:320
  376.8 15.8 %collective-permute-start.10 = (bf16[1,1792,128]{2,1,0:T(8,128)(2,1)S(1)}, bf16[1,1792,128]{2,1,0:T(8,128)(2,1)S(1)}, u32[]{:S(2)}, u32[]{:S(2)}) collective-permute-start(bf16[1,1792,128]{2,1,0:T(8,128)(2,1)S(1)} %constant_dynamic-slice_fusion.2), channel_id=1, source_target_pairs={{0,2},{2,0},{4,6},{6,4},{8,10},{10,8},{12,14},{14,12},{16,18},{18,... | collective-permute-start | bytes 1376264 | tf_op jit(solution)/shard_map/ppermute | solution.py:317
  383.0 9.7 %collective-permute-start.8 = (bf16[1,1792,128]{2,1,0:T(8,128)(2,1)S(1)}, bf16[1,1792,128]{2,1,0:T(8,128)(2,1)S(1)}, u32[]{:S(2)}, u32[]{:S(2)}) collective-permute-start(bf16[1,1792,128]{2,1,0:T(8,128)(2,1)S(1)} %constant_dynamic-slice_fusion.4), channel_id=1, source_target_pairs={{0,4},{4,0},{2,6},{6,2},{8,12},{12,8},{10,14},{14,10},{16,20},{20,... | collective-permute-start | bytes 1376264 | tf_op jit(solution)/shard_map/ppermute | solution.py:317
  407.6 46.7 %all-to-all-start.2 = ((bf16[4,896,128]{2,1,0:T(8,128)(2,1)}), bf16[4,896,128]{2,1,0:T(8,128)(2,1)S(1)}, u32[]{:S(2)}, u32[]{:S(2)}) async-start(bf16[4,896,128]{2,1,0:T(8,128)(2,1)} %pad_maximum_fusion.6), calls=%async_computation.2 | async-start | bytes 1835008 | tf_op jit(solution)/shard_map/all_to_all | solution.py:320
  411.1 10.2 %collective-permute-start.11 = (bf16[1,704,128]{2,1,0:T(8,128)(2,1)S(1)}, bf16[1,704,128]{2,1,0:T(8,128)(2,1)S(1)}, u32[]{:S(2)}, u32[]{:S(2)}) collective-permute-start(bf16[1,704,128]{2,1,0:T(8,128)(2,1)S(1)} %constant_dynamic-slice_fusion.1), channel_id=1, source_target_pairs={{0,2},{2,0},{4,6},{6,4},{8,10},{10,8},{12,14},{14,12},{16,18},{18,... | collective-permute-start | bytes 540680 | tf_op jit(solution)/shard_map/ppermute | solution.py:317
  421.4 4.3 collective-permute-start.12
  455.6 26.1 %all-to-all-start.3 = ((bf16[4,1,896,128]{3,2,1,0:T(8,128)(2,1)}), bf16[4,1,896,128]{3,2,1,0:T(8,128)(2,1)S(1)}, u32[]{:S(2)}, u32[]{:S(2)}) async-start(bf16[4,1,896,128]{3,2,1,0:T(8,128)(2,1)} %broadcast_in_dim.48), calls=%async_computation.3 | async-start | bytes 1835008 | tf_op jit(solution)/shard_map/all_to_all | solution.py:320
  459.1 3.8 collective-permute-start.13
  463.0 4.9 collective-permute-start.14
  481.7 11.0 %collective-permute-start.17 = (bf16[1,1792,128]{2,1,0:T(8,128)(2,1)S(1)}, bf16[1,1792,128]{2,1,0:T(8,128)(2,1)}, u32[]{:S(2)}, u32[]{:S(2)}) collective-permute-start(bf16[1,1792,128]{2,1,0:T(8,128)(2,1)S(1)} %bitcast.282), channel_id=1, source_target_pairs={{0,2},{2,0},{4,6},{6,4},{8,10},{10,8},{12,14},{14,12},{16,18},{18,... | collective-permute-start | bytes 1376264 | tf_op jit(solution)/shard_map/ppermute | solution.py:317
  482.7 11.6 %collective-permute-start.15 = (bf16[1,1792,128]{2,1,0:T(8,128)(2,1)S(1)}, bf16[1,1792,128]{2,1,0:T(8,128)(2,1)S(1)}, u32[]{:S(2)}, u32[]{:S(2)}) collective-permute-start(bf16[1,1792,128]{2,1,0:T(8,128)(2,1)S(1)} %bitcast.280), channel_id=1, source_target_pairs={{0,4},{4,0},{2,6},{6,2},{8,12},{12,8},{10,14},{14,10},{16,20},{20,... | collective-permute-start | bytes 1376264 | tf_op jit(solution)/shard_map/ppermute | solution.py:317
  484.6 37.4 %all-to-all-start.4 = ((bf16[4,1,1408,128]{3,2,1,0:T(8,128)(2,1)}), bf16[4,1,1408,128]{3,2,1,0:T(8,128)(2,1)S(1)}, u32[]{:S(2)}, u32[]{:S(2)}) async-start(bf16[4,1,1408,128]{3,2,1,0:T(8,128)(2,1)} %broadcast_in_dim.50), calls=%async_computation.4 | async-start | bytes 2883584 | tf_op jit(solution)/shard_map/all_to_all | solution.py:320
  493.9 28.1 %copy-start.38 = (bf16[2,1792,128]{2,1,0:T(8,128)(2,1)}, bf16[2,1792,128]{2,1,0:T(8,128)(2,1)S(1)}, u32[]{:S(2)}) copy-start(bf16[2,1792,128]{2,1,0:T(8,128)(2,1)S(1)} %pad_maximum_fusion.8) | copy-start | bytes 2752516
  493.9 19.9 %collective-permute-start.18 = (bf16[3584,128]{1,0:T(8,128)(2,1)S(1)}, bf16[3584,128]{1,0:T(8,128)(2,1)S(1)}, u32[]{:S(2)}, u32[]{:S(2)}) collective-permute-start(bf16[3584,128]{1,0:T(8,128)(2,1)S(1)} %bitcast.260), channel_id=1, source_target_pairs={{0,4},{4,0},{2,6},{6,2},{8,12},{12,8},{10,14},{14,10},{16,20},{20,... | collective-permute-start | bytes 2752520 | tf_op jit(solution)/shard_map/ppermute | solution.py:317
  494.5 27.6 %copy-start.39 = (bf16[2,1792,128]{2,1,0:T(8,128)(2,1)}, bf16[2,1792,128]{2,1,0:T(8,128)(2,1)S(1)}, u32[]{:S(2)}) copy-start(bf16[2,1792,128]{2,1,0:T(8,128)(2,1)S(1)} %pad_maximum_fusion.7) | copy-start | bytes 2752516
  494.5 20.3 %collective-permute-start.16 = (bf16[3584,128]{1,0:T(8,128)(2,1)S(1)}, bf16[3584,128]{1,0:T(8,128)(2,1)}, u32[]{:S(2)}, u32[]{:S(2)}) collective-permute-start(bf16[3584,128]{1,0:T(8,128)(2,1)S(1)} %bitcast.262), channel_id=1, source_target_pairs={{0,2},{2,0},{4,6},{6,4},{8,10},{10,8},{12,14},{14,12},{16,18},{18,... | collective-permute-start | bytes 2752520 | tf_op jit(solution)/shard_map/ppermute | solution.py:317
  495.6 42.9 %collective-permute-start.20 = (bf16[16,1248,128]{2,1,0:T(8,128)(2,1)}, bf16[16,1248,128]{2,1,0:T(8,128)(2,1)}, u32[]{:S(2)}, u32[]{:S(2)}) collective-permute-start(bf16[16,1248,128]{2,1,0:T(8,128)(2,1)} %bitcast.81), channel_id=1, source_target_pairs={{0,1},{2,3},{4,5},{6,7},{8,9},{10,11},{12,13},{14,15},{16,17},{18,... | collective-permute-start | bytes 15335432 | tf_op jit(solution)/shard_map/ppermute | solution.py:497
  528.0 38.0 %collective-permute-start.19 = (bf16[19968,128]{1,0:T(8,128)(2,1)}, bf16[19968,128]{1,0:T(8,128)(2,1)}, u32[]{:S(2)}, u32[]{:S(2)}) collective-permute-start(bf16[19968,128]{1,0:T(8,128)(2,1)} %join.1.low_rows), channel_id=1, source_target_pairs={{1,0},{3,2},{5,4},{7,6},{9,8},{11,10},{13,12},{15,14},{17,16},{19,... | collective-permute-start | bytes 15335432 | tf_op jit(solution)/shard_map/ppermute | solution.py:497
  566.0 25.1 %copy-start.1 = (bf16[6,256,768]{2,1,0:T(8,128)(2,1)S(1)}, bf16[6,256,768]{2,1,0:T(8,128)(2,1)}, u32[]{:S(2)}) copy-start(bf16[6,256,768]{2,1,0:T(8,128)(2,1)} %param.9) | copy-start | bytes 7077892
  (92 other events, 217.9 us)
Sparse Core Ops, SparseCore 0:
  333.4 120.2 all-gather.2

commit v5 on v4

--- a/solution.py
+++ b/solution.py
@@ -369,37 +369,36 @@
     return lax.optimization_barrier((ab, c))
 
 
-def staged_gather(ab, c, beside=()):
+def staged_gather(ab, c):
     x, y, z = wide_lines()
     ab = z.gather(flat3(ab, 1))
     c = x.gather(y.gather(flat3(c, 1)))
-    ab, c, beside = lax.optimization_barrier((ab, c, beside))
+    ab, c = lax.optimization_barrier((ab, c))
     half = ab.shape[1] // 2
     a, b = ab[:, :half], ab[:, half:]
     c = z.gather(flat3(c, 1))
     a = y.gather(flat3(a, 1)).reshape(-1, 128)
     b = x.gather(flat3(b, 1)).reshape(-1, 128)
-    return join_pieces((x, a, x.swap(a)), (y, b, y.swap(b)), c.reshape(-1, 128)), beside
-
-
-def join_pieces(first, second, third):
+    pieces = [x.gather(flat3(a, 1)), y.gather(flat3(b, 1)), c]
+    return jnp.concatenate([v.reshape(-1, 128) for v in pieces], 0)
+
+
+def join_pieces(first, second, after):
     pairs = (first, second)
-    sizes = [2 * own.shape[0] for line, own, other in pairs]
-
-    def kernel(own1, other1, own2, other2, last, out, sems):
+    total = sum(2 * own.shape[0] for line, own, other in pairs)
+
+    def kernel(own1, other1, own2, other2, *rest):
+        out, sems = rest[len(after) :]
         copies = []
         start = 0
         for (line, own, other), refs in zip(pairs, ((own1, other1), (own2, other2))):
             rows = own.shape[0]
             me = (lax.axis_index("wide") // line.stride) % 2
             for ref, place in zip(refs, (me, 1 - me)):
-                copies.append((ref, pl.multiple_of(start + place * rows, 8), rows))
+                spot = pl.multiple_of(start + place * rows, 8)
+                target = out.at[pl.ds(spot, rows)]
+                copies.append(pltpu.make_async_copy(ref, target, sems.at[len(copies)]))
             start += 2 * rows
-        copies.append((last, start, third.shape[0]))
-        copies = [
-            pltpu.make_async_copy(ref, out.at[pl.ds(spot, rows)], sems.at[n])
-            for n, (ref, spot, rows) in enumerate(copies)
-        ]
         for copy in copies:
             copy.start()
         for copy in copies:
@@ -407,12 +406,13 @@
 
     return pl.pallas_call(
         kernel,
-        out_shape=jax.ShapeDtypeStruct((sum(sizes) + third.shape[0], 128), third.dtype),
-        in_specs=[pl.BlockSpec(memory_space=pltpu.VMEM)] * 5,
+        out_shape=jax.ShapeDtypeStruct((total, 128), first[1].dtype),
+        in_specs=[pl.BlockSpec(memory_space=pltpu.VMEM)] * 4
+        + [pl.BlockSpec(memory_space=pl.ANY)] * len(after),
         out_specs=pl.BlockSpec(memory_space=pl.ANY),
-        scratch_shapes=[pltpu.SemaphoreType.DMA((5,))],
+        scratch_shapes=[pltpu.SemaphoreType.DMA((4,))],
         name="join",
-    )(first[1], first[2], second[1], second[2], third)
+    )(first[1], first[2], second[1], second[2], *after)
 
 
 def narrow_sum(halves):
@@ -428,7 +428,7 @@
         total = added(total, narrow_swap(other, step))
     unit = lax.axis_size("wide") * 16
     total = jnp.pad(total, ((0, round_up(rows, unit) - rows), (0, 0)))
-    return staged_gather(*staged_scatter(total))[0][:rows]
+    return staged_gather(*staged_scatter(total))[:rows]
 
 
 def scatter_first(value):
@@ -448,49 +448,94 @@
     return z.scatter(both).reshape(-1, 128)
 
 
-BLOCK = 2496
-
-
-def adam_rows(low, high, moment1, moment2, start, held, chips_all):
+def gather_first(value):
+    z = wide_lines()[2]
+    value = z.gather(flat3(value, 1))
+    half = value.shape[1] // 2
+    return flat3(value[:, :half], 1), flat3(value[:, half:], 1)
+
+
+def gather_second(pair):
+    x, y, z = wide_lines()
+    return y.gather(pair[0]).reshape(-1, 128), x.gather(pair[1]).reshape(-1, 128)
+
+
+def gather_last(pair):
+    x, y, z = wide_lines()
+    a, b = pair
+    return (a, x.swap(a)), (b, y.swap(b))
+
+
+def joined(pairs, after=()):
+    x, y, z = wide_lines()
+    return join_pieces((x, *pairs[0]), (y, *pairs[1]), after)
+
+
+BLOCK = 2368
+
+
+def adam_rows(low, high, moment1, moment2, start, stop, held, chips_all):
     shift = start // BLOCK
-    steps = -(-min(low.shape[0], moment1.shape[0] - start) // BLOCK)
-
-    def kernel(core, low_rows, high_rows, first, second, *rest):
-        grad_out, update, new_first, new_second = rest[len(held) :]
-        grad = jnp.where(core[0] == 0, low_rows[...], high_rows[...].reshape(BLOCK, 128))
-        grad = grad.astype(jnp.float32) / chips_all
+    steps = -(-min(stop - start, moment1.shape[0] - start) // BLOCK)
+    plans = []
+    for place, pieces in enumerate((low, high)):
+        for origin, piece_rows in pieces:
+            first, last = max(start, origin), min(stop, origin + piece_rows.shape[0])
+            if first < last:
+                plans.append((place, piece_rows, first - origin, first - start, last - first))
+
+    def kernel(*refs):
+        sources, rest = refs[: len(plans)], refs[len(plans) :]
+        first, second, *rest = rest
+        grad_out, update, new_first, new_second, token, fetched, sems = rest[len(held) :]
+        mine = lax.axis_index("narrow")
+        step = pl.program_id(0)
+
+        def copy(n):
+            place, piece_rows, source_row, row, count = plans[n]
+            return pltpu.make_async_copy(
+                sources[n].at[pl.ds(source_row, count)], fetched.at[pl.ds(row, count)], sems.at[n]
+            )
+
+        for place in range(2):
+
+            @pl.when(jnp.logical_and(step == 0, mine == place))
+            def fetch(place=place):
+                own = [n for n, plan in enumerate(plans) if plan[0] == place]
+                for n in own:
+                    copy(n).start()
+                for n in own:
+                    copy(n).wait()
+
+        token[...] = jnp.zeros((8, 128), jnp.float32)
+        spot = pl.multiple_of(step * BLOCK, 16)
+        grad = fetched[pl.ds(spot, BLOCK), :].astype(jnp.float32) / chips_all
         grad_out[...] = grad
         update[...], new_first[...], new_second[...] = adam_step(grad, first[...], second[...])
 
-    def spec(index_map):
-        return pl.BlockSpec((BLOCK, 128), index_map)
-
-    here = spec(lambda i, core: (i + shift, 0))
-    high = high.reshape(-1, 4, 2, BLOCK // 4, 128)
-
-    def high_place(i, core):
-        turn = jnp.where(core[0] == 1, i, 0)
-        part, spot = turn // 4, turn % 4
-        return 0, jnp.where(part == 0, spot % 2 * 2 + spot // 2, spot), part, 0, 0
-
-    parts = (
-        spec(lambda i, core: (jnp.where(core[0] == 0, i, 0), 0)),
-        pl.BlockSpec((4, 1, 1, BLOCK // 4, 128), high_place),
-    )
-    core = lax.axis_index("narrow").astype(jnp.int32).reshape(1)
+    here = pl.BlockSpec((BLOCK, 128), lambda i: (i + shift, 0))
+    anywhere = pl.BlockSpec(memory_space=pl.ANY)
+    base = len(plans) + 2
     return pl.pallas_call(
         kernel,
-        out_shape=[jax.ShapeDtypeStruct(moment1.shape, jnp.float32)] * 4,
-        grid_spec=pltpu.PrefetchScalarGridSpec(
-            num_scalar_prefetch=1,
-            grid=(steps,),
-            in_specs=[*parts, here, here] + [pl.BlockSpec(memory_space=pl.ANY)] * len(held),
-            out_specs=[here] * 4,
+        out_shape=[jax.ShapeDtypeStruct(moment1.shape, jnp.float32)] * 4
+        + [jax.ShapeDtypeStruct((8, 128), jnp.float32)],
+        grid=(steps,),
+        in_specs=[anywhere] * len(plans) + [here, here] + [anywhere] * len(held),
+        out_specs=[here] * 4 + [pl.BlockSpec((8, 128), lambda i: (0, 0))],
+        scratch_shapes=[
+            pltpu.VMEM((max(steps * BLOCK, stop - start), 128), jnp.bfloat16),
+            pltpu.SemaphoreType.DMA((len(plans),)),
+        ],
+        input_output_aliases={base + n: n for n in range(len(held))},
+        compiler_params=pltpu.CompilerParams(vmem_limit_bytes=40 << 20),
+        cost_estimate=pl.CostEstimate(
+            flops=(stop - start) * 128 * 16,
+            transcendentals=(stop - start) * 128 * 2,
+            bytes_accessed=(stop - start) * 128 * 26,
         ),
-        input_output_aliases={5 + n: n for n in range(len(held))},
-        compiler_params=pltpu.CompilerParams(vmem_limit_bytes=40 << 20),
         name=f"adam{start}",
-    )(core, low, high, moment1, moment2, *held)
+    )(*[plan[1] for plan in plans], moment1, moment2, *held)
 
 
 def to_owner(value, source):
@@ -783,31 +828,51 @@
     grads.update(more)
     grads["eu"] = hidden_gradient(enc_kept, d_hidden)
     if chunked:
-        cut = round_up(flat_rows()[0]["eu"][0], 128)
-        held = pack_part(grads, cut, padded, 0, padded)
-        d_mid, held, high = tie((d_mid, held, high))
+        cut = round_up(flat_rows()[0]["eu"][0], 512)
+        late = pack_part(grads, cut, padded, cut, padded)
+        d_mid, late, high = tie((d_mid, late, high))
         high = scatter_second(high)
+        late = scatter_first(narrow_sum(late))
     attention = scores_backward(d_mid, enc_kept, weights_map, "e", HE)
     if chunked:
-        attention, d_mid, high = tie((attention, d_mid, high))
+        attention, d_mid, high, late = tie((attention, d_mid, high, late))
         high = scatter_last(high)
+        late = scatter_second(late)
     d_enc_in, more = stream_backward(d_mid, *attention, enc_kept, weights_map, "e", HE)
     grads.update(more)
     grads["cls"] = jnp.sum(d_enc_in[:, 0, :], 0)
     chips_all = float(chips * lax.axis_size("wide") * lax.axis_size("narrow"))
     if chunked:
-        low = pack_part(grads, 0, cut, 0, padded, held)
-        d_enc_in, low, high = tie((d_enc_in, low, high))
-        high = lax.all_gather(high, "wide")
+        low = pack_part(grads, 0, cut, 0, cut)
+        d_enc_in, low, high, late = tie((d_enc_in, low, high, late))
+        high = gather_first(high)
+        late = scatter_last(late)
+        low = scatter_second(scatter_first(narrow_sum(low)))
     patch_grad = jnp.einsum(
         "cvp,cvd->cpd", choose_full, d_enc_in[:, 2:, :], precision=highest
     ).astype(jnp.bfloat16)
     if chunked:
-        low, high = staged_gather(*staged_scatter(narrow_sum(low)), high)
-        start = low.shape[0]
-        held = adam_rows(low, to_owner(high, 0), moment1, moment2, 0, (), chips_all)
-        grad_out, update, new_moment1, new_moment2 = adam_rows(
-            to_owner(low, 1), high, moment1, moment2, start, held, chips_all
+        patch_grad, low, high, late = tie((patch_grad, low, high, late))
+        high = gather_last(gather_second(high))
+        late = gather_first(late)
+        low = scatter_last(low)
+        low, high, late = tie((low, high, late))
+        high = joined(high)
+        late = gather_last(gather_second(late))
+        low = gather_first(low)
+        other_high = to_owner(high, 0)
+        low, high, other_high, late = tie((low, high, other_high, late))
+        late = joined(late)
+        other_late = to_owner(late, 1)
+        low = gather_second(low)
+        low, late, other_late = tie((low, late, other_late))
+        pieces = ((cut, late), (cut + late.shape[0], other_late))
+        uppers = ((0, other_high), (other_high.shape[0], high))
+        *held, token = adam_rows(pieces, uppers, moment1, moment2, cut, padded, (), chips_all)
+        low = joined(gather_last(low), (token,))
+        pieces = ((0, low), (low.shape[0], to_owner(low, 1)))
+        grad_out, update, new_moment1, new_moment2, token = adam_rows(
+            pieces, uppers, moment1, moment2, 0, cut, held, chips_all
         )
     else:
         every = flat_gradient(grads, half_rows * lax.axis_size("narrow"))

time: 607 us -> 631 us (1.040)
  starting transfers between devices: 44 us -> 62.5 us
  other arithmetic: 60.6 us -> 76.2 us
  between operations: 16.2 us -> 3.15 us
  waiting for transfers between devices: 172 us -> 160 us
  local copies, waits for them, and re-layouts: 53.3 us -> 62.2 us
  Pallas kernels: 105 us -> 112 us
    ppermute x3 -> x4, waiting for transfers between devices: 18.5 us -> 10.1 us  [narrow_swap(): lax.ppermute(value, 'narrow', [(i, (i + step) % count) for i in range(cou...]
    ppermute x2 -> x3, starting transfers between devices: 6.9 us -> 14.9 us  [to_owner(): return lax.ppermute(value, 'narrow', [(source, 1 - source)])]
    convert_element_type x12 -> x15, other arithmetic: 19.1 us -> 25.6 us  [added(): (first.astype(jnp.float32) + second.astype(jnp.float32)).astype(jnp.bfloa...]
    pallas_call x9, other arithmetic: 2.82 us -> 9.18 us  [unpack(): pl.pallas_call(kernel, out_shape=out_shape, in_specs=[pl.BlockSpec(memory...]
    ppermute x16 -> x24, waiting for transfers between devices: 89.7 us -> 83.3 us  [swap(): return lax.ppermute(value, 'wide', pairs)]
    all_to_all x5 -> x6, starting transfers between devices: 19.7 us -> 24.5 us  [exchange(): return lax.all_to_all(value, 'wide', 0, 0, axis_index_groups=self.groups)]
    ppermute x16 -> x24, starting transfers between devices: 15.7 us -> 20.4 us  [swap(): return lax.ppermute(value, 'wide', pairs)]
    all_to_all x5 -> x6, waiting for transfers between devices: 63.6 us -> 62.4 us  [exchange(): return lax.all_to_all(value, 'wide', 0, 0, axis_index_groups=self.groups)]
  transfers between devices with their start and end apart: 27 -> 37, of which waited for: 21 -> 21; matrix products, arithmetic and copies ran while one was open for 13% -> 14% of each run, Pallas kernels for 8% -> 7%
where the time goes in v5:
time: 631 us; the launch traced here: 620 us
  waiting for transfers between devices  160 us (25%)
  matrix products  145 us (23%)
  Pallas kernels  112 us (18%)
  other arithmetic  76.2 us (12%)
  starting transfers between devices  62.5 us (10%)
  local copies, waits for them, and re-layouts  62.2 us (10%)
    ppermute x24, waiting for transfers between devices, swap(): return lax.ppermute(value, 'wide', pairs)  83.3 us
    all_to_all x6, waiting for transfers between devices, exchange(): return lax.all_to_all(value, 'wide', 0, 0, axis_index_groups=self.groups)  62.4 us
    pallas_call x2, Pallas kernels, adam_rows(): pl.pallas_call(kernel, out_shape=[jax.ShapeDtypeStruct(moment1.shape, jnp...  50.7 us
    pallas_call x4, Pallas kernels, pack_part(): pl.pallas_call(kernel, out_shape=[jax.ShapeDtypeStruct((middle - first, 1...  31.7 us
    dot_general x2, matrix products, block_forward(): jnp.einsum('ctd,df->ctf', second_in, weights_map[prefix + 'u'], preferred...  28.2 us
    convert_element_type x15, other arithmetic, added(): (first.astype(jnp.float32) + second.astype(jnp.float32)).astype(jnp.bfloa...  25.6 us
    all_to_all x6, starting transfers between devices, exchange(): return lax.all_to_all(value, 'wide', 0, 0, axis_index_groups=self.groups)  24.5 us
    ppermute x24, starting transfers between devices, swap(): return lax.ppermute(value, 'wide', pairs)  20.4 us
  transfers between devices with their start and end apart: 37, of which 21 were waited for; matrix products, arithmetic and copies ran while one was open for 14% of the time, Pallas kernels for 7%

profile of v5, /device:TPU:1, one launch (start us, length us, event | category | flops | bytes accessed | tf_op | source)
XLA Modules:
  0.0 620.5 jit_solution(5537722313352270716)
XLA Ops:
  0.7 7.7 %convert_element_type.366.refs_0_ = bf16[39552,128]{1,0:T(8,128)(2,1)S(1)} convert(f32[39552,128]{1,0:T(8,128)} %param.14) | non-fusion elementwise | flops 5062656 | bytes 30375936 | tf_op jit(solution)/shard_map/convert_element_type | solution.py:546
  14.2 10.1 %collective-permute-done.refs_1_ = bf16[39552,128]{1,0:T(8,128)(2,1)} collective-permute-done((bf16[39552,128]{1,0:T(8,128)(2,1)S(1)}, bf16[39552,128]{1,0:T(8,128)(2,1)}, u32[]{:S(2)}, u32[]{:S(2)}) %collective-permute-start) | collective-permute-done | bytes 10125344 | tf_op jit(solution)/shard_map/ppermute | solution.py:341
  24.3 18.1 %unpack.1 = (f32[1,768]{1,0:T(1,128)}, f32[1,768]{1,0:T(1,128)}, f32[1,768]{1,0:T(1,128)}, bf16[768,2304]{1,0:T(8,128)(2,1)}, bf16[768,768]{1,0:T(8,128)(2,1)}, ...) custom-call(bf16[39552,128]{1,0:T(8,128)(2,1)} %copy-done.13, ...), custom_call_target="tpu_custom_call" | custom-call | tf_op jit(solution)/shard_map/unpack/pallas_call | solution.py:171
  53.0 4.0 convolution_convert_fusion
  60.9 2.6 copy.130
  69.7 9.5 %fusion.14 = (bf16[6,66,3072]{2,1,0:T(8,128)(2,1)}, bf16[6,66,3072]{2,1,0:T(8,128)(2,1)S(1)}) fusion(f32[3072]{0:T(1024)S(1)} %bitcast.342, bf16[768,3072]{1,0:T(8,128)(2,1)S(1)} %bitcast.337, f32[6,66,768]{2,1,0:T(8,128)S(1)} %get-tuple-element.273, f32[768]{0:T(1024)S(1)} %copy-done.104, f32[768]{0:T(1024)S(1)} %copy-done.89, f32[6,66]{1,0:T(8,128)S(1)} %fusion.92, ...), kind=kOutput, calls=%fused_computation.31 | convolution fusion | flops 1911444480 | bytes 10822752 | tf_op jit(solution)/shard_map/ctd,df->ctf/dot_general | solution.py:641
  92.4 2.6 copy.90
  102.9 18.7 %fusion.6 = (bf16[6,256,2048]{2,1,0:T(8,128)(2,1)S(1)}, bf16[6,256,2048]{2,1,0:T(8,128)(2,1)}) fusion(f32[2048]{0:T(1024)S(1)} %bitcast.343, bf16[512,2048]{1,0:T(8,128)(2,1)S(1)} %copy-done.112, f32[6,256,512]{2,1,0:T(8,128)S(1)} %get-tuple-element.279, f32[512]{0:T(512)S(1)} %bitcast.347, f32[512]{0:T(512)S(1)} %bitcast.321, f32[6,256]{1,0:T(8,128)S(1)} %fusion.90, ...), kind=kOutput, calls=%fused_computation.8 | convolution fusion | flops 3332112384 | bytes 17850368 | tf_op jit(solution)/shard_map/ctd,df->ctf/dot_general | solution.py:641
  121.7 4.3 convert_reduce_fusion
  125.9 4.7 fusion.107
  130.6 4.0 bitcast_convert_fusion.4.refs_0_
  138.2 4.6 bitcast_convert_fusion.3.refs_2_
  143.4 6.3 %convert_add_fusion = (f32[6,256,512]{2,1,0:T(8,128)}, bf16[6,256,512]{2,1,0:T(8,128)(2,1)}, f32[512]{0:T(512)}) fusion(bf16[6,256,512]{2,1,0:T(8,128)(2,1)S(1)} %copy-done.113, f32[6,256]{1,0:T(8,128)S(1)} %negate_multiply_fusion.1, f32[6,256]{1,0:T(8,128)S(1)} %multiply_multiply_fusion.3, f32[6,256,512]{2,1,0:T(8,128)S(1)} %get-tuple-element.279, ...), kind=kOutput, calls=%fused_computation.52 | convolution fusion | flops 3231448576 | bytes 21002240 | tf_op jit(solution)/shard_map/ctf,fd->ctd/dot_general | solution.py:647
  149.7 7.7 %pack62592.1 = (bf16[19968,128]{1,0:T(8,128)(2,1)}, bf16[19968,128]{1,0:T(8,128)(2,1)}) custom-call(bf16[512,2048]{1,0:T(8,128)(2,1)} %copy-done.54, f32[1,2048]{1,0:T(1,128)} %bitcast.316, bf16[2048,512]{1,0:T(8,128)(2,1)} %bitcast_convert_fusion.3.refs_2_, f32[1,512]{1,0:T(1,128)} %bitcast.331), custom_call_target="tpu_custom_call" | custom-call | tf_op jit(solution)/shard_map/pack62592/pallas_call | solution.py:273
  157.4 3.5 fusion.57.refs_10_
  161.7 4.3 fusion.49
  166.1 4.3 multiply_reduce_fusion
  170.4 4.6 multiply_convert_fusion.1
  183.2 5.1 bitcast_convert_fusion.6.refs_9_
  188.3 2.7 multiply_reduce_fusion.3
  201.6 4.3 bitcast_convert_fusion.1.refs_0_
  207.7 9.0 %pack39552.1 = (bf16[19968,128]{1,0:T(8,128)(2,1)}, bf16[19968,128]{1,0:T(8,128)(2,1)}) custom-call(bf16[3072,768]{1,0:T(8,128)(2,1)} %bitcast_convert_fusion.1.refs_0_, f32[1,768]{1,0:T(1,128)} %reshape.443.refs_1_, f32[1,768]{1,0:T(1,128)} %reshape.444.refs_2_, f32[1,768]{1,0:T(1,128)} %reshape.445.refs_3_, ...), custom_call_target="tpu_custom_call", output_to_operand_aliasing={{0}: (15, {}), {1}: (16, {})} | custom-call | tf_op jit(solution)/shard_map/pack39552/pallas_call | solution.py:273
  216.9 6.6 %convert_reduce_fusion.1 = (f32[3072]{0:T(1024)}, bf16[6,66,3072]{2,1,0:T(8,128)(2,1)S(1)}) fusion(bf16[6,66,3072]{2,1,0:T(8,128)(2,1)} %get-tuple-element.143, bf16[3072,768]{1,0:T(8,128)(2,1)} %get-tuple-element.115, f32[6,66,768]{2,1,0:T(8,128)} %get-tuple-element.142), kind=kOutput, calls=%fused_computation.32 | convolution fusion | flops 1874946048 | bytes 10813440 | tf_op jit(solution)/shard_map/ctd,fd->ctf/dot_general | solution.py:680
  226.1 4.6 bitcast_convert_fusion.refs_0_
  230.7 3.8 add_convert_fusion
  245.7 8.2 %pack18944.1 = (bf16[10496,128]{1,0:T(8,128)(2,1)}, bf16[10496,128]{1,0:T(8,128)(2,1)}) custom-call(bf16[768,3072]{1,0:T(8,128)(2,1)} %bitcast_convert_fusion.refs_0_, f32[1,3072]{1,0:T(1,128)} %bitcast.315, bf16[512,768]{1,0:T(8,128)(2,1)} %slice.81.refs_2_), custom_call_target="tpu_custom_call" | custom-call | tf_op jit(solution)/shard_map/pack18944/pallas_call | solution.py:273
  254.0 13.6 %collective-permute-done.3 = bf16[1,4992,128]{2,1,0:T(8,128)(2,1)} collective-permute-done((bf16[1,4992,128]{2,1,0:T(8,128)(2,1)}, bf16[1,4992,128]{2,1,0:T(8,128)(2,1)}, u32[]{:S(2)}, u32[]{:S(2)}) %collective-permute-start.3) | collective-permute-done | bytes 1277984 | tf_op jit(solution)/shard_map/ppermute | solution.py:317
  267.6 3.1 add_convert_fusion.6
  270.7 2.8 add_convert_fusion.7
  286.8 7.1 %multiply_convert_fusion.4 = bf16[6,12,66,66]{2,3,1,0:T(8,128)(2,1)} fusion(f32[6,12,66,66]{2,3,1,0:T(8,128)} %copy-done.16, f32[6,12,66]{2,1,0:T(8,128)S(1)} %log_add_fusion, bf16[6,66,12,64]{1,3,2,0:T(8,128)(2,1)} %bitcast.259, bf16[6,66,12,64]{1,3,2,0:T(8,128)(2,1)} %bitcast.306), kind=kOutput, calls=%fused_computation.74 | convolution fusion | flops 82803664 | bytes 3117312 | tf_op jit(solution)/shard_map/sub | solution.py:722
  293.9 4.0 collective-permute-done.4
  300.2 2.9 add_convert_fusion.1
  308.0 11.2 %collective-permute-done.8 = bf16[1,2624,128]{2,1,0:T(8,128)(2,1)S(1)} collective-permute-done((bf16[1,2624,128]{2,1,0:T(8,128)(2,1)S(1)}, bf16[1,2624,128]{2,1,0:T(8,128)(2,1)S(1)}, u32[]{:S(2)}, u32[]{:S(2)}) %collective-permute-start.8) | collective-permute-done | bytes 671776 | tf_op jit(solution)/shard_map/ppermute | solution.py:317
  332.2 4.4 fusion.109
  339.7 4.6 all-to-all-start
  346.4 2.7 convert_reduce_fusion.4
  349.2 4.0 bitcast_convert_fusion.2.refs_3_
  357.7 6.7 %pack0.1 = (bf16[9472,128]{1,0:T(8,128)(2,1)}, bf16[9472,128]{1,0:T(8,128)(2,1)}) custom-call(f32[1,768]{1,0:T(1,128)} %reshape.462.refs_0_, f32[1,768]{1,0:T(1,128)} %reshape.463.refs_1_, f32[1,768]{1,0:T(1,128)} %reshape.464.refs_2_, bf16[768,2304]{1,0:T(8,128)(2,1)} %bitcast_convert_fusion.2.refs_3_, bf16[768,768]{1,0:T(8,128)(2,1)} %bitcast_convert_fusion.5.refs_4_, ...), custom_call_target="tpu_custom_call" | custom-call | tf_op jit(solution)/shard_map/pack0/pallas_call | solution.py:273
  366.7 7.9 %all-to-all-done = bf16[4,1248,128]{2,1,0:T(8,128)(2,1)} async-done(((bf16[4,1248,128]{2,1,0:T(8,128)(2,1)}), bf16[4,1248,128]{2,1,0:T(8,128)(2,1)}, u32[]{:S(2)}, u32[]{:S(2)}) %all-to-all-start) | async-done | bytes 1277984 | tf_op jit(solution)/shard_map/all_to_all | solution.py:320
  378.5 3.5 all-to-all-start.2
  382.1 3.6 convolution_convert_fusion.1
  385.6 14.1 %all-to-all-done.2 = bf16[4,656,128]{2,1,0:T(8,128)(2,1)S(1)} async-done(((bf16[4,656,128]{2,1,0:T(8,128)(2,1)}), bf16[4,656,128]{2,1,0:T(8,128)(2,1)S(1)}, u32[]{:S(2)}, u32[]{:S(2)}) %all-to-all-start.2) | async-done | bytes 671776 | tf_op jit(solution)/shard_map/all_to_all | solution.py:320
  400.9 3.5 all-to-all-start.1
  404.6 2.7 add_convert_fusion.2
  410.0 24.6 %all-to-all-done.1 = bf16[4,1,1248,128]{3,2,1,0:T(8,128)(2,1)S(1)} async-done(((bf16[4,1,1248,128]{3,2,1,0:T(8,128)(2,1)}), bf16[4,1,1248,128]{3,2,1,0:T(8,128)(2,1)S(1)}, u32[]{:S(2)}, u32[]{:S(2)}) %all-to-all-start.1) | async-done | bytes 1277984 | tf_op jit(solution)/shard_map/all_to_all | solution.py:320
  438.9 11.0 %collective-permute-done.12 = bf16[1,2368,128]{2,1,0:T(8,128)(2,1)S(1)} collective-permute-done((bf16[1,2368,128]{2,1,0:T(8,128)(2,1)S(1)}, bf16[1,2368,128]{2,1,0:T(8,128)(2,1)S(1)}, u32[]{:S(2)}, u32[]{:S(2)}) %collective-permute-start.12) | collective-permute-done | bytes 606240 | tf_op jit(solution)/shard_map/ppermute | solution.py:317
  450.4 6.0 collective-permute-done.15
  458.7 4.4 all-to-all-start.3
  463.4 4.6 collective-permute-done.18
  468.5 5.8 collective-permute-done.16
  476.8 4.2 all-to-all-start.4
  482.2 9.5 %all-to-all-done.4 = bf16[4,1,656,128]{3,2,1,0:T(8,128)(2,1)S(1)} async-done(((bf16[4,1,656,128]{3,2,1,0:T(8,128)(2,1)}), bf16[4,1,656,128]{3,2,1,0:T(8,128)(2,1)S(1)}, u32[]{:S(2)}, u32[]{:S(2)}) %all-to-all-start.4) | async-done | bytes 671776 | tf_op jit(solution)/shard_map/all_to_all | solution.py:320
  491.8 10.0 %collective-permute-done.19.other2 = bf16[4992,128]{1,0:T(8,128)(2,1)} collective-permute-done((bf16[4992,128]{1,0:T(8,128)(2,1)S(1)}, bf16[4992,128]{1,0:T(8,128)(2,1)}, u32[]{:S(2)}, u32[]{:S(2)}) %collective-permute-start.19) | collective-permute-done | bytes 1277984 | tf_op jit(solution)/shard_map/ppermute | solution.py:317
  501.8 4.8 join.3.refs_3_
  509.3 4.2 all-to-all-start.5
  517.4 6.2 all-to-all-done.5
  523.6 4.0 collective-permute-done.24.other2
  529.5 3.2 join.4.refs_0_
  532.8 12.2 %collective-permute-start.27 = (bf16[10496,128]{1,0:T(8,128)(2,1)}, bf16[10496,128]{1,0:T(8,128)(2,1)S(1)}, u32[]{:S(2)}, u32[]{:S(2)}) collective-permute-start(bf16[10496,128]{1,0:T(8,128)(2,1)} %join.4.refs_0_), channel_id=1, source_target_pairs={{1,0},{3,2},{5,4},{7,6},{9,8},{11,10},{13,12},{15,14},{17,16},{19,... | collective-permute-start | bytes 8060936 | tf_op jit(solution)/shard_map/ppermute | solution.py:542
  546.5 7.4 %collective-permute-done.25 = bf16[1,1184,128]{2,1,0:T(8,128)(2,1)S(1)} collective-permute-done((bf16[1,1184,128]{2,1,0:T(8,128)(2,1)S(1)}, bf16[1,1184,128]{2,1,0:T(8,128)(2,1)S(1)}, u32[]{:S(2)}, u32[]{:S(2)}) %collective-permute-start.25) | collective-permute-done | bytes 303136 | tf_op jit(solution)/shard_map/ppermute | solution.py:317
  557.0 26.0 %adam18944.1 = (f32[39552,128]{1,0:T(8,128)}, f32[39552,128]{1,0:T(8,128)}, f32[39552,128]{1,0:T(8,128)}, f32[39552,128]{1,0:T(8,128)}, f32[8,128]{1,0:T(8,128)S(1)}) custom-call(bf16[10496,128]{1,0:T(8,128)(2,1)S(1)} %copy-done.2, bf16[10496,128]{1,0:T(8,128)(2,1)S(1)} %collective-permute-done.27.refs_1_, ...), custom_call_target="tpu_custom_call" | custom-call | flops 42991616 | bytes 69861376 | tf_op jit(solution)/shard_map/adam18944/pallas_call | solution.py:519
  584.8 3.1 join.5.refs_0_
  589.3 4.3 collective-permute-done.30.refs_1_
  595.3 24.7 %adam0.1 = (f32[39552,128]{1,0:T(8,128)}, f32[39552,128]{1,0:T(8,128)}, f32[39552,128]{1,0:T(8,128)}, f32[39552,128]{1,0:T(8,128)}, f32[8,128]{1,0:T(8,128)}) custom-call(bf16[9472,128]{1,0:T(8,128)(2,1)S(1)} %copy-done.3, ...), custom_call_target="tpu_custom_call", output_to_operand_aliasing={{0}: (5, {}), {1}: (6, {}), {2}: (7, {}), {3}: (8, {})} | custom-call | flops 38797312 | bytes 63045632 | tf_op jit(solution)/shard_map/adam0/pallas_call | solution.py:519
  (483 shorter events, 168.6 us)
Async XLA Ops:
  0.6 11.9 %copy-start = (bf16[6,256,768]{2,1,0:T(8,128)(2,1)S(1)}, bf16[6,256,768]{2,1,0:T(8,128)(2,1)}, u32[]{:S(2)}) copy-start(bf16[6,256,768]{2,1,0:T(8,128)(2,1)} %param.9) | copy-start | bytes 7077892
  0.7 7.9 %copy-start.122 = (s32[6]{0:T(128)S(1)}, s32[6]{0:T(128)}, u32[]{:S(2)}) copy-start(s32[6]{0:T(128)} %param.12) | copy-start | bytes 76
  0.7 7.9 %copy-start.101 = (bf16[6,768]{1,0:T(8,128)(2,1)S(1)}, bf16[6,768]{1,0:T(8,128)(2,1)}, u32[]{:S(2)}) copy-start(bf16[6,768]{1,0:T(8,128)(2,1)} %param.10) | copy-start | bytes 27652
  0.7 8.0 %copy-start.82 = (s32[6,64]{1,0:T(8,128)S(1)}, s32[6,64]{1,0:T(8,128)}, u32[]{:S(2)}) copy-start(s32[6,64]{1,0:T(8,128)} %param.11) | copy-start | bytes 4612
  8.4 15.8 %collective-permute-start = (bf16[39552,128]{1,0:T(8,128)(2,1)S(1)}, bf16[39552,128]{1,0:T(8,128)(2,1)}, u32[]{:S(2)}, u32[]{:S(2)}) collective-permute-start(bf16[39552,128]{1,0:T(8,128)(2,1)S(1)} %convert_element_type.366.refs_0_), channel_id=1, source_target_pairs={{0,1},{1,0},{2,3},{3,2},{4,5},{5,4},{6,7},{7,6},{8,9},{9,8},{10,11... | collective-permute-start | bytes 30375944 | tf_op jit(solution)/shard_map/ppermute | solution.py:341
  8.7 43.8 %copy-start.66 = (f32[6,1,768]{2,1,0:T(1,128)}, f32[6,1,768]{2,1,0:T(1,128)S(1)}, u32[]{:S(2)}) copy-start(f32[6,1,768]{2,1,0:T(1,128)S(1)} %broadcast_in_dim.34) | copy-start | bytes 55300
  14.2 37.5 %copy-start.11 = (f32[6,64,768]{2,1,0:T(8,128)S(1)}, f32[6,64,768]{2,1,0:T(8,128)}, u32[]{:S(2)}) copy-start(f32[6,64,768]{2,1,0:T(8,128)} %fusion.72) | copy-start | bytes 3538948
  43.8 8.6 %copy-start.97 = (f32[768]{0:T(1024)}, f32[768]{0:T(1024)S(1)}, u32[]{:S(2)}) copy-start(f32[768]{0:T(1024)S(1)} %reduce.5) | copy-start | bytes 9220
  69.3 12.4 %copy-start.14 = (f32[6,66,768]{2,1,0:T(8,128)}, f32[6,66,768]{2,1,0:T(8,128)S(1)}, u32[]{:S(2)}) copy-start(f32[6,66,768]{2,1,0:T(8,128)S(1)} %get-tuple-element.273) | copy-start | bytes 3649540
  69.3 9.9 %copy-start.83 = (f32[6,66]{1,0:T(8,128)}, f32[6,66]{1,0:T(8,128)S(1)}, u32[]{:S(2)}) copy-start(f32[6,66]{1,0:T(8,128)S(1)} %broadcast_multiply_fusion.3) | copy-start | bytes 4756
  69.3 10.0 %slice-start.8 = ((s8[4718592]{0:T(1024)(128)(4,1)}), s8[4194304]{0:T(1024)(128)(4,1)S(1)}, s32[]{:S(2)}) async-start(s8[4718592]{0:T(1024)(128)(4,1)} %bitcast.340), calls=%async_computation.14 | async-start | bytes 8388608
  69.6 9.6 %copy-start.93 = (f32[6,66]{1,0:T(8,128)}, f32[6,66]{1,0:T(8,128)S(1)}, u32[]{:S(2)}) copy-start(f32[6,66]{1,0:T(8,128)S(1)} %multiply_reduce_fusion.15) | copy-start | bytes 4756
  69.6 9.6 %copy-start.87 = (f32[6,66]{1,0:T(8,128)}, f32[6,66]{1,0:T(8,128)S(1)}, u32[]{:S(2)}) copy-start(f32[6,66]{1,0:T(8,128)S(1)} %fusion.92) | copy-start | bytes 4756
  69.7 9.6 %slice-start.9 = ((s8[4718592]{0:T(1024)(128)(4,1)}), s8[524288]{0:T(1024)(128)(4,1)S(1)}, s32[]{:S(2)}) async-start(s8[4718592]{0:T(1024)(128)(4,1)} %bitcast.340), calls=%async_computation.15 | async-start | bytes 1048576
  102.9 18.7 %copy-start.111 = (bf16[2048,512]{1,0:T(8,128)(2,1)S(1)}, bf16[2048,512]{1,0:T(8,128)(2,1)}, u32[]{:S(2)}) copy-start(bf16[2048,512]{1,0:T(8,128)(2,1)} %get-tuple-element.132) | copy-start | bytes 6291460
  102.9 18.7 %copy-start.113 = (bf16[6,256,512]{2,1,0:T(8,128)(2,1)S(1)}, bf16[6,256,512]{2,1,0:T(8,128)(2,1)}, u32[]{:S(2)}) copy-start(bf16[6,256,512]{2,1,0:T(8,128)(2,1)} %param.13) | copy-start | bytes 4718596
  134.6 8.2 %copy-start.54 = (bf16[512,2048]{1,0:T(8,128)(2,1)}, bf16[512,2048]{1,0:T(8,128)(2,1)S(1)}, u32[]{:S(2)}) copy-start(bf16[512,2048]{1,0:T(8,128)(2,1)S(1)} %bitcast_convert_fusion.4.refs_0_) | copy-start | bytes 6291460
  207.7 15.8 %slice-start.6 = ((s8[4718592]{0:T(1024)(128)(4,1)}), s8[524288]{0:T(1024)(128)(4,1)S(1)}, s32[]{:S(2)}) async-start(s8[4718592]{0:T(1024)(128)(4,1)} %bitcast.338), calls=%async_computation.12 | async-start | bytes 1048576
  216.7 14.0 %collective-permute-start.1 = (bf16[19968,128]{1,0:T(8,128)(2,1)}, bf16[19968,128]{1,0:T(8,128)(2,1)}, u32[]{:S(2)}, u32[]{:S(2)}) collective-permute-start(bf16[19968,128]{1,0:T(8,128)(2,1)} %get-tuple-element.147), channel_id=1, source_target_pairs={{0,1},{1,0},{2,3},{3,2},{4,5},{5,4},{6,7},{7,6},{8,9},{9,8},{10,11... | collective-permute-start | bytes 15335432 | tf_op jit(solution)/shard_map/ppermute | solution.py:341
  236.4 31.2 %collective-permute-start.3 = (bf16[1,4992,128]{2,1,0:T(8,128)(2,1)}, bf16[1,4992,128]{2,1,0:T(8,128)(2,1)}, u32[]{:S(2)}, u32[]{:S(2)}) collective-permute-start(bf16[1,4992,128]{2,1,0:T(8,128)(2,1)} %constant_dynamic-slice_fusion.10), channel_id=1, source_target_pairs={{0,4},{4,0},{2,6},{6,2},{8,12},{12,8},{10,14},{14,10},{16,20},{20,... | collective-permute-start | bytes 3833864 | tf_op jit(solution)/shard_map/ppermute | solution.py:317
  240.9 29.8 %collective-permute-start.2 = (bf16[1,4992,128]{2,1,0:T(8,128)(2,1)}, bf16[1,4992,128]{2,1,0:T(8,128)(2,1)}, u32[]{:S(2)}, u32[]{:S(2)}) collective-permute-start(bf16[1,4992,128]{2,1,0:T(8,128)(2,1)} %constant_dynamic-slice_fusion.11), channel_id=1, source_target_pairs={{0,2},{2,0},{4,6},{6,4},{8,10},{10,8},{12,14},{14,12},{16,18},{18,... | collective-permute-start | bytes 3833864 | tf_op jit(solution)/shard_map/ppermute | solution.py:317
  254.0 16.7 %copy-start.24 = (bf16[9984,128]{1,0:T(8,128)(2,1)S(1)}, bf16[9984,128]{1,0:T(8,128)(2,1)}, u32[]{:S(2)}) copy-start(bf16[9984,128]{1,0:T(8,128)(2,1)} %copy-done.23) | copy-start | bytes 7667716
  273.5 26.6 %collective-permute-start.6 = (bf16[10496,128]{1,0:T(8,128)(2,1)}, bf16[10496,128]{1,0:T(8,128)(2,1)}, u32[]{:S(2)}, u32[]{:S(2)}) collective-permute-start(bf16[10496,128]{1,0:T(8,128)(2,1)} %get-tuple-element.152), channel_id=1, source_target_pairs={{0,1},{1,0},{2,3},{3,2},{4,5},{5,4},{6,7},{7,6},{8,9},{9,8},{10,11... | collective-permute-start | bytes 8060936 | tf_op jit(solution)/shard_map/ppermute | solution.py:341
  281.6 16.2 %collective-permute-start.4 = (bf16[1,2496,128]{2,1,0:T(8,128)(2,1)}, bf16[1,2496,128]{2,1,0:T(8,128)(2,1)}, u32[]{:S(2)}, u32[]{:S(2)}) collective-permute-start(bf16[1,2496,128]{2,1,0:T(8,128)(2,1)} %constant_dynamic-slice_fusion.9), channel_id=1, source_target_pairs={{0,4},{4,0},{2,6},{6,2},{8,12},{12,8},{10,14},{14,10},{16,20},{20,... | collective-permute-start | bytes 1916936 | tf_op jit(solution)/shard_map/ppermute | solution.py:317
  282.9 21.7 %collective-permute-start.5 = (bf16[1,2496,128]{2,1,0:T(8,128)(2,1)S(1)}, bf16[1,2496,128]{2,1,0:T(8,128)(2,1)}, u32[]{:S(2)}, u32[]{:S(2)}) collective-permute-start(bf16[1,2496,128]{2,1,0:T(8,128)(2,1)S(1)} %constant_dynamic-slice_fusion.8), channel_id=1, source_target_pairs={{0,2},{2,0},{4,6},{6,4},{8,10},{10,8},{12,14},{14,12},{16,18},{18,... | collective-permute-start | bytes 1916936 | tf_op jit(solution)/shard_map/ppermute | solution.py:317
  303.3 15.8 %collective-permute-start.8 = (bf16[1,2624,128]{2,1,0:T(8,128)(2,1)S(1)}, bf16[1,2624,128]{2,1,0:T(8,128)(2,1)S(1)}, u32[]{:S(2)}, u32[]{:S(2)}) collective-permute-start(bf16[1,2624,128]{2,1,0:T(8,128)(2,1)S(1)} %constant_dynamic-slice_fusion.6), channel_id=1, source_target_pairs={{0,4},{4,0},{2,6},{6,2},{8,12},{12,8},{10,14},{14,10},{16,20},{20,... | collective-permute-start | bytes 2015240 | tf_op jit(solution)/shard_map/ppermute | solution.py:317
  306.7 16.6 %copy-start.22 = (bf16[6,66,768]{1,2,0:T(8,128)(2,1)S(1)}, bf16[6,66,768]{1,2,0:T(8,128)(2,1)}, u32[]{:S(2)}) copy-start(bf16[6,66,768]{1,2,0:T(8,128)(2,1)} %copy-done.21) | copy-start | bytes 1824772
  306.7 16.6 %copy-start.28 = (bf16[6,12,66,66]{2,3,1,0:T(8,128)(2,1)S(1)}, bf16[6,12,66,66]{2,3,1,0:T(8,128)(2,1)}, u32[]{:S(2)}) copy-start(bf16[6,12,66,66]{2,3,1,0:T(8,128)(2,1)} %multiply_convert_fusion.4) | copy-start | bytes 1881796
  306.7 15.6 %collective-permute-start.7 = (bf16[1,2624,128]{2,1,0:T(8,128)(2,1)S(1)}, bf16[1,2624,128]{2,1,0:T(8,128)(2,1)S(1)}, u32[]{:S(2)}, u32[]{:S(2)}) collective-permute-start(bf16[1,2624,128]{2,1,0:T(8,128)(2,1)S(1)} %constant_dynamic-slice_fusion.7), channel_id=1, source_target_pairs={{0,2},{2,0},{4,6},{6,4},{8,10},{10,8},{12,14},{14,12},{16,18},{18,... | collective-permute-start | bytes 2015240 | tf_op jit(solution)/shard_map/ppermute | solution.py:317
  339.7 34.9 %all-to-all-start = ((bf16[4,1248,128]{2,1,0:T(8,128)(2,1)}), bf16[4,1248,128]{2,1,0:T(8,128)(2,1)}, u32[]{:S(2)}, u32[]{:S(2)}) async-start(bf16[4,1248,128]{2,1,0:T(8,128)(2,1)} %pad_maximum_fusion.3), calls=%async_computation | async-start | bytes 2555904 | tf_op jit(solution)/shard_map/all_to_all | solution.py:320
  345.1 19.3 %collective-permute-start.10 = (bf16[1,1312,128]{2,1,0:T(8,128)(2,1)}, bf16[1,1312,128]{2,1,0:T(8,128)(2,1)}, u32[]{:S(2)}, u32[]{:S(2)}) collective-permute-start(bf16[1,1312,128]{2,1,0:T(8,128)(2,1)} %constant_dynamic-slice_fusion.4), channel_id=1, source_target_pairs={{0,2},{2,0},{4,6},{6,4},{8,10},{10,8},{12,14},{14,12},{16,18},{18,... | collective-permute-start | bytes 1007624 | tf_op jit(solution)/shard_map/ppermute | solution.py:317
  355.6 9.9 %collective-permute-start.9 = (bf16[1,1312,128]{2,1,0:T(8,128)(2,1)S(1)}, bf16[1,1312,128]{2,1,0:T(8,128)(2,1)}, u32[]{:S(2)}, u32[]{:S(2)}) collective-permute-start(bf16[1,1312,128]{2,1,0:T(8,128)(2,1)S(1)} %constant_dynamic-slice_fusion.5), channel_id=1, source_target_pairs={{0,4},{4,0},{2,6},{6,2},{8,12},{12,8},{10,14},{14,10},{16,20},{20,... | collective-permute-start | bytes 1007624 | tf_op jit(solution)/shard_map/ppermute | solution.py:317
  365.5 16.5 %copy-start.37 = (f32[6,66,768]{2,1,0:T(8,128)S(1)}, f32[6,66,768]{2,1,0:T(8,128)}, u32[]{:S(2)}) copy-start(f32[6,66,768]{2,1,0:T(8,128)} %copy-done.36) | copy-start | bytes 3649540
  376.2 28.4 %collective-permute-start.11 = (bf16[9472,128]{1,0:T(8,128)(2,1)}, bf16[9472,128]{1,0:T(8,128)(2,1)}, u32[]{:S(2)}, u32[]{:S(2)}) collective-permute-start(bf16[9472,128]{1,0:T(8,128)(2,1)} %get-tuple-element.164), channel_id=1, source_target_pairs={{0,1},{1,0},{2,3},{3,2},{4,5},{5,4},{6,7},{7,6},{8,9},{9,8},{10,11... | collective-permute-start | bytes 7274504 | tf_op jit(solution)/shard_map/ppermute | solution.py:341
  378.5 21.2 %all-to-all-start.2 = ((bf16[4,656,128]{2,1,0:T(8,128)(2,1)}), bf16[4,656,128]{2,1,0:T(8,128)(2,1)S(1)}, u32[]{:S(2)}, u32[]{:S(2)}) async-start(bf16[4,656,128]{2,1,0:T(8,128)(2,1)} %pad_maximum_fusion.10), calls=%async_computation.2 | async-start | bytes 1343488 | tf_op jit(solution)/shard_map/all_to_all | solution.py:320
  400.9 33.7 %all-to-all-start.1 = ((bf16[4,1,1248,128]{3,2,1,0:T(8,128)(2,1)}), bf16[4,1,1248,128]{3,2,1,0:T(8,128)(2,1)S(1)}, u32[]{:S(2)}, u32[]{:S(2)}) async-start(bf16[4,1,1248,128]{3,2,1,0:T(8,128)(2,1)} %broadcast_in_dim.45), calls=%async_computation.1 | async-start | bytes 2555904 | tf_op jit(solution)/shard_map/all_to_all | solution.py:320
  409.8 27.5 %collective-permute-start.14 = (bf16[1,2368,128]{2,1,0:T(8,128)(2,1)}, bf16[1,2368,128]{2,1,0:T(8,128)(2,1)}, u32[]{:S(2)}, u32[]{:S(2)}) collective-permute-start(bf16[1,2368,128]{2,1,0:T(8,128)(2,1)} %constant_dynamic-slice_fusion.1), channel_id=1, source_target_pairs={{0,4},{4,0},{2,6},{6,2},{8,12},{12,8},{10,14},{14,10},{16,20},{20,... | collective-permute-start | bytes 1818632 | tf_op jit(solution)/shard_map/ppermute | solution.py:317
  436.0 13.9 %collective-permute-start.12 = (bf16[1,2368,128]{2,1,0:T(8,128)(2,1)S(1)}, bf16[1,2368,128]{2,1,0:T(8,128)(2,1)S(1)}, u32[]{:S(2)}, u32[]{:S(2)}) collective-permute-start(bf16[1,2368,128]{2,1,0:T(8,128)(2,1)S(1)} %constant_dynamic-slice_fusion.3), channel_id=1, source_target_pairs={{0,2},{2,0},{4,6},{6,4},{8,10},{10,8},{12,14},{14,12},{16,18},{18,... | collective-permute-start | bytes 1818632 | tf_op jit(solution)/shard_map/ppermute | solution.py:317
  438.5 17.8 %collective-permute-start.15 = (bf16[1,1184,128]{2,1,0:T(8,128)(2,1)S(1)}, bf16[1,1184,128]{2,1,0:T(8,128)(2,1)S(1)}, u32[]{:S(2)}, u32[]{:S(2)}) collective-permute-start(bf16[1,1184,128]{2,1,0:T(8,128)(2,1)S(1)} %constant_dynamic-slice_fusion), channel_id=1, source_target_pairs={{0,2},{2,0},{4,6},{6,4},{8,10},{10,8},{12,14},{14,12},{16,18},{18,... | collective-permute-start | bytes 909320 | tf_op jit(solution)/shard_map/ppermute | solution.py:317
  450.1 6.4 %collective-permute-start.13 = (bf16[1,1184,128]{2,1,0:T(8,128)(2,1)S(1)}, bf16[1,1184,128]{2,1,0:T(8,128)(2,1)S(1)}, u32[]{:S(2)}, u32[]{:S(2)}) collective-permute-start(bf16[1,1184,128]{2,1,0:T(8,128)(2,1)S(1)} %constant_dynamic-slice_fusion.2), channel_id=1, source_target_pairs={{0,4},{4,0},{2,6},{6,2},{8,12},{12,8},{10,14},{14,10},{16,20},{20,... | collective-permute-start | bytes 909320 | tf_op jit(solution)/shard_map/ppermute | solution.py:317
  456.6 11.4 %collective-permute-start.18 = (bf16[1,2496,128]{2,1,0:T(8,128)(2,1)S(1)}, bf16[1,2496,128]{2,1,0:T(8,128)(2,1)S(1)}, u32[]{:S(2)}, u32[]{:S(2)}) collective-permute-start(bf16[1,2496,128]{2,1,0:T(8,128)(2,1)S(1)} %bitcast.281), channel_id=1, source_target_pairs={{0,2},{2,0},{4,6},{6,4},{8,10},{10,8},{12,14},{14,12},{16,18},{18,... | collective-permute-start | bytes 1916936 | tf_op jit(solution)/shard_map/ppermute | solution.py:317
  458.7 17.2 %all-to-all-start.3 = ((bf16[4,592,128]{2,1,0:T(8,128)(2,1)}), bf16[4,592,128]{2,1,0:T(8,128)(2,1)}, u32[]{:S(2)}, u32[]{:S(2)}) async-start(bf16[4,592,128]{2,1,0:T(8,128)(2,1)} %pad_maximum_fusion.13), calls=%async_computation.3 | async-start | bytes 1212416 | tf_op jit(solution)/shard_map/all_to_all | solution.py:320
  463.1 11.2 %collective-permute-start.16 = (bf16[1,2496,128]{2,1,0:T(8,128)(2,1)S(1)}, bf16[1,2496,128]{2,1,0:T(8,128)(2,1)S(1)}, u32[]{:S(2)}, u32[]{:S(2)}) collective-permute-start(bf16[1,2496,128]{2,1,0:T(8,128)(2,1)S(1)} %bitcast.279), channel_id=1, source_target_pairs={{0,4},{4,0},{2,6},{6,2},{8,12},{12,8},{10,14},{14,10},{16,20},{20,... | collective-permute-start | bytes 1916936 | tf_op jit(solution)/shard_map/ppermute | solution.py:317
  468.2 33.5 %collective-permute-start.19 = (bf16[4992,128]{1,0:T(8,128)(2,1)S(1)}, bf16[4992,128]{1,0:T(8,128)(2,1)}, u32[]{:S(2)}, u32[]{:S(2)}) collective-permute-start(bf16[4992,128]{1,0:T(8,128)(2,1)S(1)} %bitcast.247), channel_id=1, source_target_pairs={{0,4},{4,0},{2,6},{6,2},{8,12},{12,8},{10,14},{14,10},{16,20},{20,... | collective-permute-start | bytes 3833864 | tf_op jit(solution)/shard_map/ppermute | solution.py:317
  475.6 26.1 %collective-permute-start.17 = (bf16[4992,128]{1,0:T(8,128)(2,1)}, bf16[4992,128]{1,0:T(8,128)(2,1)}, u32[]{:S(2)}, u32[]{:S(2)}) collective-permute-start(bf16[4992,128]{1,0:T(8,128)(2,1)} %bitcast.82.own1), channel_id=1, source_target_pairs={{0,2},{2,0},{4,6},{6,4},{8,10},{10,8},{12,14},{14,12},{16,18},{18,... | collective-permute-start | bytes 3833864 | tf_op jit(solution)/shard_map/ppermute | solution.py:317
  476.8 14.9 %all-to-all-start.4 = ((bf16[4,1,656,128]{3,2,1,0:T(8,128)(2,1)}), bf16[4,1,656,128]{3,2,1,0:T(8,128)(2,1)S(1)}, u32[]{:S(2)}, u32[]{:S(2)}) async-start(bf16[4,1,656,128]{3,2,1,0:T(8,128)(2,1)} %broadcast_in_dim.46), calls=%async_computation.4 | async-start | bytes 1343488 | tf_op jit(solution)/shard_map/all_to_all | solution.py:320
  506.6 22.9 %collective-permute-start.20 = (bf16[19968,128]{1,0:T(8,128)(2,1)}, bf16[19968,128]{1,0:T(8,128)(2,1)}, u32[]{:S(2)}, u32[]{:S(2)}) collective-permute-start(bf16[19968,128]{1,0:T(8,128)(2,1)} %join.3.refs_3_), channel_id=1, source_target_pairs={{0,1},{2,3},{4,5},{6,7},{8,9},{10,11},{12,13},{14,15},{16,17},{18,... | collective-permute-start | bytes 15335432 | tf_op jit(solution)/shard_map/ppermute | solution.py:542
  507.9 6.1 collective-permute-start.23
  508.2 6.8 %collective-permute-start.21 = (bf16[1,1312,128]{2,1,0:T(8,128)(2,1)S(1)}, bf16[1,1312,128]{2,1,0:T(8,128)(2,1)}, u32[]{:S(2)}, u32[]{:S(2)}) collective-permute-start(bf16[1,1312,128]{2,1,0:T(8,128)(2,1)S(1)} %bitcast.296), channel_id=1, source_target_pairs={{0,4},{4,0},{2,6},{6,2},{8,12},{12,8},{10,14},{14,10},{16,20},{20,... | collective-permute-start | bytes 1007624 | tf_op jit(solution)/shard_map/ppermute | solution.py:317
  509.3 14.2 %all-to-all-start.5 = ((bf16[4,1,592,128]{3,2,1,0:T(8,128)(2,1)}), bf16[4,1,592,128]{3,2,1,0:T(8,128)(2,1)S(1)}, u32[]{:S(2)}, u32[]{:S(2)}) async-start(bf16[4,1,592,128]{3,2,1,0:T(8,128)(2,1)} %broadcast_in_dim.47), calls=%async_computation.5 | async-start | bytes 1212416 | tf_op jit(solution)/shard_map/all_to_all | solution.py:320
  514.1 15.4 %copy-start.48 = (bf16[2,1312,128]{2,1,0:T(8,128)(2,1)}, bf16[2,1312,128]{2,1,0:T(8,128)(2,1)S(1)}, u32[]{:S(2)}) copy-start(bf16[2,1312,128]{2,1,0:T(8,128)(2,1)S(1)} %pad_maximum_fusion.12) | copy-start | bytes 2015236
  514.1 13.5 %collective-permute-start.24 = (bf16[2624,128]{1,0:T(8,128)(2,1)S(1)}, bf16[2624,128]{1,0:T(8,128)(2,1)S(1)}, u32[]{:S(2)}, u32[]{:S(2)}) collective-permute-start(bf16[2624,128]{1,0:T(8,128)(2,1)S(1)} %bitcast.275), channel_id=1, source_target_pairs={{0,4},{4,0},{2,6},{6,2},{8,12},{12,8},{10,14},{14,10},{16,20},{20,... | collective-permute-start | bytes 2015240 | tf_op jit(solution)/shard_map/ppermute | solution.py:317
  516.1 13.4 %copy-start.49 = (bf16[2,1312,128]{2,1,0:T(8,128)(2,1)}, bf16[2,1312,128]{2,1,0:T(8,128)(2,1)S(1)}, u32[]{:S(2)}) copy-start(bf16[2,1312,128]{2,1,0:T(8,128)(2,1)S(1)} %pad_maximum_fusion.11) | copy-start | bytes 2015236
  516.1 13.4 %collective-permute-start.22 = (bf16[2624,128]{1,0:T(8,128)(2,1)S(1)}, bf16[2624,128]{1,0:T(8,128)(2,1)}, u32[]{:S(2)}, u32[]{:S(2)}) collective-permute-start(bf16[2624,128]{1,0:T(8,128)(2,1)S(1)} %bitcast.277), channel_id=1, source_target_pairs={{0,2},{2,0},{4,6},{6,4},{8,10},{10,8},{12,14},{14,12},{16,18},{18,... | collective-permute-start | bytes 2015240 | tf_op jit(solution)/shard_map/ppermute | solution.py:317
  532.8 24.3 %copy-start.2 = (bf16[10496,128]{1,0:T(8,128)(2,1)S(1)}, bf16[10496,128]{1,0:T(8,128)(2,1)}, u32[]{:S(2)}) copy-start(bf16[10496,128]{1,0:T(8,128)(2,1)} %join.4.refs_0_) | copy-start | bytes 8060932
  532.8 22.8 %collective-permute-start.27 = (bf16[10496,128]{1,0:T(8,128)(2,1)}, bf16[10496,128]{1,0:T(8,128)(2,1)S(1)}, u32[]{:S(2)}, u32[]{:S(2)}) collective-permute-start(bf16[10496,128]{1,0:T(8,128)(2,1)} %join.4.refs_0_), channel_id=1, source_target_pairs={{1,0},{3,2},{5,4},{7,6},{9,8},{11,10},{13,12},{15,14},{17,16},{19,... | collective-permute-start | bytes 8060936 | tf_op jit(solution)/shard_map/ppermute | solution.py:542
  545.0 8.9 %collective-permute-start.25 = (bf16[1,1184,128]{2,1,0:T(8,128)(2,1)S(1)}, bf16[1,1184,128]{2,1,0:T(8,128)(2,1)S(1)}, u32[]{:S(2)}, u32[]{:S(2)}) collective-permute-start(bf16[1,1184,128]{2,1,0:T(8,128)(2,1)S(1)} %bitcast.304), channel_id=1, source_target_pairs={{0,4},{4,0},{2,6},{6,2},{8,12},{12,8},{10,14},{14,10},{16,20},{20,... | collective-permute-start | bytes 909320 | tf_op jit(solution)/shard_map/ppermute | solution.py:317
  546.4 9.1 %collective-permute-start.26 = (bf16[1,1184,128]{2,1,0:T(8,128)(2,1)S(1)}, bf16[1,1184,128]{2,1,0:T(8,128)(2,1)S(1)}, u32[]{:S(2)}, u32[]{:S(2)}) collective-permute-start(bf16[1,1184,128]{2,1,0:T(8,128)(2,1)S(1)} %bitcast.302), channel_id=1, source_target_pairs={{0,2},{2,0},{4,6},{6,4},{8,10},{10,8},{12,14},{14,12},{16,18},{18,... | collective-permute-start | bytes 909320 | tf_op jit(solution)/shard_map/ppermute | solution.py:317
  554.0 29.0 %copy-start.52 = (bf16[2,1184,128]{2,1,0:T(8,128)(2,1)}, bf16[2,1184,128]{2,1,0:T(8,128)(2,1)S(1)}, u32[]{:S(2)}) copy-start(bf16[2,1184,128]{2,1,0:T(8,128)(2,1)S(1)} %pad_maximum_fusion.14) | copy-start | bytes 1818628
  555.6 27.4 %copy-start.53 = (bf16[2,1184,128]{2,1,0:T(8,128)(2,1)}, bf16[2,1184,128]{2,1,0:T(8,128)(2,1)S(1)}, u32[]{:S(2)}) copy-start(bf16[2,1184,128]{2,1,0:T(8,128)(2,1)S(1)} %pad_maximum_fusion.15) | copy-start | bytes 1818628
  555.6 28.0 %collective-permute-start.28 = (bf16[2368,128]{1,0:T(8,128)(2,1)S(1)}, bf16[2368,128]{1,0:T(8,128)(2,1)S(1)}, u32[]{:S(2)}, u32[]{:S(2)}) collective-permute-start(bf16[2368,128]{1,0:T(8,128)(2,1)S(1)} %bitcast.286), channel_id=1, source_target_pairs={{0,2},{2,0},{4,6},{6,4},{8,10},{10,8},{12,14},{14,12},{16,18},{18,... | collective-permute-start | bytes 1818632 | tf_op jit(solution)/shard_map/ppermute | solution.py:317
  555.8 27.8 %collective-permute-start.29 = (bf16[2368,128]{1,0:T(8,128)(2,1)S(1)}, bf16[2368,128]{1,0:T(8,128)(2,1)S(1)}, u32[]{:S(2)}, u32[]{:S(2)}) collective-permute-start(bf16[2368,128]{1,0:T(8,128)(2,1)S(1)} %bitcast.288), channel_id=1, source_target_pairs={{0,4},{4,0},{2,6},{6,2},{8,12},{12,8},{10,14},{14,10},{16,20},{20,... | collective-permute-start | bytes 1818632 | tf_op jit(solution)/shard_map/ppermute | solution.py:317
  587.8 5.7 collective-permute-start.30
  595.3 24.7 %copy-start.1 = (bf16[6,256,768]{2,1,0:T(8,128)(2,1)S(1)}, bf16[6,256,768]{2,1,0:T(8,128)(2,1)}, u32[]{:S(2)}) copy-start(bf16[6,256,768]{2,1,0:T(8,128)(2,1)} %param.9) | copy-start | bytes 7077892
  (109 other events, 363.7 us)

commit v6 on v4

--- a/solution.py
+++ b/solution.py
@@ -369,37 +369,35 @@
     return lax.optimization_barrier((ab, c))
 
 
-def staged_gather(ab, c, beside=()):
+def staged_gather(ab, c):
     x, y, z = wide_lines()
     ab = z.gather(flat3(ab, 1))
     c = x.gather(y.gather(flat3(c, 1)))
-    ab, c, beside = lax.optimization_barrier((ab, c, beside))
+    ab, c = lax.optimization_barrier((ab, c))
     half = ab.shape[1] // 2
     a, b = ab[:, :half], ab[:, half:]
     c = z.gather(flat3(c, 1))
     a = y.gather(flat3(a, 1)).reshape(-1, 128)
     b = x.gather(flat3(b, 1)).reshape(-1, 128)
-    return join_pieces((x, a, x.swap(a)), (y, b, y.swap(b)), c.reshape(-1, 128)), beside
-
-
-def join_pieces(first, second, third):
+    pieces = [x.gather(flat3(a, 1)), y.gather(flat3(b, 1)), c]
+    return jnp.concatenate([v.reshape(-1, 128) for v in pieces], 0)
+
+
+def join_pieces(first, second):
     pairs = (first, second)
-    sizes = [2 * own.shape[0] for line, own, other in pairs]
-
-    def kernel(own1, other1, own2, other2, last, out, sems):
+    total = sum(2 * own.shape[0] for line, own, other in pairs)
+
+    def kernel(own1, other1, own2, other2, out, sems):
         copies = []
         start = 0
         for (line, own, other), refs in zip(pairs, ((own1, other1), (own2, other2))):
             rows = own.shape[0]
             me = (lax.axis_index("wide") // line.stride) % 2
             for ref, place in zip(refs, (me, 1 - me)):
-                copies.append((ref, pl.multiple_of(start + place * rows, 8), rows))
+                spot = pl.multiple_of(start + place * rows, 8)
+                target = out.at[pl.ds(spot, rows)]
+                copies.append(pltpu.make_async_copy(ref, target, sems.at[len(copies)]))
             start += 2 * rows
-        copies.append((last, start, third.shape[0]))
-        copies = [
-            pltpu.make_async_copy(ref, out.at[pl.ds(spot, rows)], sems.at[n])
-            for n, (ref, spot, rows) in enumerate(copies)
-        ]
         for copy in copies:
             copy.start()
         for copy in copies:
@@ -407,12 +405,12 @@
 
     return pl.pallas_call(
         kernel,
-        out_shape=jax.ShapeDtypeStruct((sum(sizes) + third.shape[0], 128), third.dtype),
-        in_specs=[pl.BlockSpec(memory_space=pltpu.VMEM)] * 5,
+        out_shape=jax.ShapeDtypeStruct((total, 128), first[1].dtype),
+        in_specs=[pl.BlockSpec(memory_space=pltpu.VMEM)] * 4,
         out_specs=pl.BlockSpec(memory_space=pl.ANY),
-        scratch_shapes=[pltpu.SemaphoreType.DMA((5,))],
+        scratch_shapes=[pltpu.SemaphoreType.DMA((4,))],
         name="join",
-    )(first[1], first[2], second[1], second[2], third)
+    )(first[1], first[2], second[1], second[2])
 
 
 def narrow_sum(halves):
@@ -428,7 +426,7 @@
         total = added(total, narrow_swap(other, step))
     unit = lax.axis_size("wide") * 16
     total = jnp.pad(total, ((0, round_up(rows, unit) - rows), (0, 0)))
-    return staged_gather(*staged_scatter(total))[0][:rows]
+    return staged_gather(*staged_scatter(total))[:rows]
 
 
 def scatter_first(value):
@@ -448,49 +446,84 @@
     return z.scatter(both).reshape(-1, 128)
 
 
-BLOCK = 2496
-
-
-def adam_rows(low, high, moment1, moment2, start, held, chips_all):
-    shift = start // BLOCK
-    steps = -(-min(low.shape[0], moment1.shape[0] - start) // BLOCK)
-
-    def kernel(core, low_rows, high_rows, first, second, *rest):
-        grad_out, update, new_first, new_second = rest[len(held) :]
-        grad = jnp.where(core[0] == 0, low_rows[...], high_rows[...].reshape(BLOCK, 128))
-        grad = grad.astype(jnp.float32) / chips_all
+def gather_first(value):
+    z = wide_lines()[2]
+    value = z.gather(flat3(value, 1))
+    half = value.shape[1] // 2
+    return flat3(value[:, :half], 1), flat3(value[:, half:], 1)
+
+
+def gather_second(pair):
+    x, y, z = wide_lines()
+    return y.gather(pair[0]).reshape(-1, 128), x.gather(pair[1]).reshape(-1, 128)
+
+
+def gather_last(pair):
+    x, y, z = wide_lines()
+    a, b = pair
+    return (a, x.swap(a)), (b, y.swap(b))
+
+
+def joined(pairs):
+    x, y, z = wide_lines()
+    return join_pieces((x, *pairs[0]), (y, *pairs[1]))
+
+
+def adam_rows(low, high, moment1, moment2, flip, held, chips_all):
+    block = low[0].shape[0] // 2
+    x, y, z = wide_lines()
+
+    def kernel(places, low0, low1, low2, low3, high0, high1, first, second, *rest):
+        grad_out, update, new_first, new_second, token = rest[len(held) :]
+        i = pl.program_id(0)
+        early = jnp.where(i < 2, low0[...], low1[...])
+        lower = jnp.where(i < 4, early, jnp.where(i < 6, low2[...], low3[...]))
+        upper = jnp.where(i < 4, high0[...], high1[...])
+        grad = jnp.where(places[0] == 0, lower, upper).astype(jnp.float32) / chips_all
         grad_out[...] = grad
         update[...], new_first[...], new_second[...] = adam_step(grad, first[...], second[...])
-
-    def spec(index_map):
-        return pl.BlockSpec((BLOCK, 128), index_map)
-
-    here = spec(lambda i, core: (i + shift, 0))
-    high = high.reshape(-1, 4, 2, BLOCK // 4, 128)
-
-    def high_place(i, core):
-        turn = jnp.where(core[0] == 1, i, 0)
-        part, spot = turn // 4, turn % 4
-        return 0, jnp.where(part == 0, spot % 2 * 2 + spot // 2, spot), part, 0, 0
-
-    parts = (
-        spec(lambda i, core: (jnp.where(core[0] == 0, i, 0), 0)),
-        pl.BlockSpec((4, 1, 1, BLOCK // 4, 128), high_place),
-    )
-    core = lax.axis_index("narrow").astype(jnp.int32).reshape(1)
+        token[...] = jnp.zeros((8, 128), jnp.float32)
+
+    def spot(i, places):
+        part = i // 2 % 2
+        return part * 4 + jnp.where(part == 0, places[1], places[2]) * 2 + i % 2
+
+    def low_spec(n):
+        return pl.BlockSpec(
+            (block, 128),
+            lambda i, places: (jnp.where(places[0] == 0, jnp.clip(i - 2 * n, 0, 1), 0), 0),
+        )
+
+    def high_spec(n):
+        def place(i, places):
+            wanted = jnp.logical_and(places[0] == 1, i // 4 == n)
+            return jnp.where(wanted, spot(i, places), 0), 0
+
+        return pl.BlockSpec((block, 128), place)
+
+    here = pl.BlockSpec((block, 128), lambda i, places: (i // 4 * 8 + spot(i, places), 0))
+    mark = pl.BlockSpec((8, 128), lambda i, places: (0, 0))
+    rows = 8 * block
+    places = [lax.axis_index("narrow"), x.me ^ flip, y.me ^ flip]
+    places = jnp.stack([place.astype(jnp.int32) for place in places])
+    in_specs = [low_spec(n) for n in range(4)] + [high_spec(n) for n in range(2)] + [here, here]
     return pl.pallas_call(
         kernel,
-        out_shape=[jax.ShapeDtypeStruct(moment1.shape, jnp.float32)] * 4,
+        out_shape=[jax.ShapeDtypeStruct(moment1.shape, jnp.float32)] * 4
+        + [jax.ShapeDtypeStruct((8, 128), jnp.float32)],
         grid_spec=pltpu.PrefetchScalarGridSpec(
             num_scalar_prefetch=1,
-            grid=(steps,),
-            in_specs=[*parts, here, here] + [pl.BlockSpec(memory_space=pl.ANY)] * len(held),
-            out_specs=[here] * 4,
+            grid=(8,),
+            in_specs=in_specs + [pl.BlockSpec(memory_space=pl.ANY)] * len(held),
+            out_specs=[here] * 4 + [mark],
         ),
-        input_output_aliases={5 + n: n for n in range(len(held))},
+        input_output_aliases={9 + n: n for n in range(min(4, len(held)))},
         compiler_params=pltpu.CompilerParams(vmem_limit_bytes=40 << 20),
-        name=f"adam{start}",
-    )(core, low, high, moment1, moment2, *held)
+        cost_estimate=pl.CostEstimate(
+            flops=rows * 128 * 16, transcendentals=rows * 128 * 2, bytes_accessed=rows * 128 * 26
+        ),
+        name=f"adam{flip}",
+    )(places, *low, *high, moment1, moment2, *held)
 
 
 def to_owner(value, source):
@@ -798,16 +831,31 @@
     if chunked:
         low = pack_part(grads, 0, cut, 0, padded, held)
         d_enc_in, low, high = tie((d_enc_in, low, high))
-        high = lax.all_gather(high, "wide")
+        high = gather_first(high)
+        low = scatter_first(narrow_sum(low))
     patch_grad = jnp.einsum(
         "cvp,cvd->cpd", choose_full, d_enc_in[:, 2:, :], precision=highest
     ).astype(jnp.bfloat16)
     if chunked:
-        low, high = staged_gather(*staged_scatter(narrow_sum(low)), high)
-        start = low.shape[0]
-        held = adam_rows(low, to_owner(high, 0), moment1, moment2, 0, (), chips_all)
-        grad_out, update, new_moment1, new_moment2 = adam_rows(
-            to_owner(low, 1), high, moment1, moment2, start, held, chips_all
+        patch_grad, low, high = tie((patch_grad, low, high))
+        high = gather_second(high)
+        low = scatter_second(low)
+        low, high = tie((low, high))
+        high = gather_last(high)
+        low = scatter_last(low)
+        low, high = tie((low, high))
+        high = joined(high)
+        high = (to_owner(high, 0), high)
+        low = gather_first(low)
+        low, high = tie((low, high))
+        low = gather_second(low)
+        early = (*low, *[to_owner(v, 1) for v in low])
+        *held, token = adam_rows(early, high, moment1, moment2, 0, (), chips_all)
+        late = [pair[1] for pair in gather_last(low)]
+        late, token = tie((late, token))
+        late = (*late, *[to_owner(v, 1) for v in late])
+        grad_out, update, new_moment1, new_moment2, token = adam_rows(
+            late, high, moment1, moment2, 1, (*held, token), chips_all
         )
     else:
         every = flat_gradient(grads, half_rows * lax.axis_size("narrow"))

time: 607 us -> 601 us (level)
  waiting for transfers between devices: 172 us -> 132 us
  blocking collectives: 0 us -> 31.7 us
  local copies, waits for them, and re-layouts: 53.3 us -> 70.4 us
  between operations: 16.2 us -> 2.86 us
  matrix products: 147 us -> 137 us
    all_to_all x0 -> x1, blocking collectives: none -> 31.7 us  [exchange(): return lax.all_to_all(value, 'wide', 0, 0, axis_index_groups=self.groups)]
    ppermute x16, waiting for transfers between devices: 89.7 us -> 68.8 us  [swap(): return lax.ppermute(value, 'wide', pairs)]
    all_to_all x5 -> x3, waiting for transfers between devices: 63.6 us -> 48 us  [exchange(): return lax.all_to_all(value, 'wide', 0, 0, axis_index_groups=self.groups)]
    all_to_all x5 -> x3, starting transfers between devices: 19.7 us -> 13 us  [exchange(): return lax.all_to_all(value, 'wide', 0, 0, axis_index_groups=self.groups)]
    convert_element_type x12 -> x10, other arithmetic: 19.1 us -> 23 us  [added(): (first.astype(jnp.float32) + second.astype(jnp.float32)).astype(jnp.bfloa...]
    unnamed x258 -> x248, local copies, waits for them, and re-layouts: 18.5 us -> 21.9 us
  transfers between devices with their start and end apart: 27 -> 27, of which waited for: 21 -> 14; matrix products, arithmetic and copies ran while one was open for 13% -> 12% of each run, Pallas kernels for 8% -> 7%
where the time goes in v6:
time: 601 us; the launch traced here: 590 us
  matrix products  137 us (23%)
  waiting for transfers between devices  132 us (22%)
  Pallas kernels  108 us (18%)
  local copies, waits for them, and re-layouts  70.4 us (12%)
  other arithmetic  61.9 us (10%)
  starting transfers between devices  47.1 us (8%)
  blocking collectives  31.7 us (5%)
    ppermute x16, waiting for transfers between devices, swap(): return lax.ppermute(value, 'wide', pairs)  68.8 us
    pallas_call x2, Pallas kernels, adam_rows(): pl.pallas_call(kernel, out_shape=[jax.ShapeDtypeStruct(moment1.shape, jnp...  52.8 us
    all_to_all x3, waiting for transfers between devices, exchange(): return lax.all_to_all(value, 'wide', 0, 0, axis_index_groups=self.groups)  48 us
    pallas_call x4, Pallas kernels, pack_part(): pl.pallas_call(kernel, out_shape=[jax.ShapeDtypeStruct((middle - first, 1...  32.1 us
    all_to_all x1, blocking collectives, exchange(): return lax.all_to_all(value, 'wide', 0, 0, axis_index_groups=self.groups)  31.7 us
    dot_general x2, matrix products, block_forward(): jnp.einsum('ctd,df->ctf', second_in, weights_map[prefix + 'u'], preferred...  28.1 us
    convert_element_type x10, other arithmetic, added(): (first.astype(jnp.float32) + second.astype(jnp.float32)).astype(jnp.bfloa...  23 us
    unnamed x248, local copies, waits for them, and re-layouts  21.9 us
  transfers between devices with their start and end apart: 27, of which 14 were waited for; matrix products, arithmetic and copies ran while one was open for 12% of the time, Pallas kernels for 7%

profile of v6, /device:TPU:1, one launch (start us, length us, event | category | flops | bytes accessed | tf_op | source)
XLA Modules:
  0.0 590.2 jit_solution(14397843412129196070)
XLA Ops:
  0.7 7.7 %convert_element_type.319.refs_0_ = bf16[39552,128]{1,0:T(8,128)(2,1)S(1)} convert(f32[39552,128]{1,0:T(8,128)} %param.14) | non-fusion elementwise | flops 5062656 | bytes 30375936 | tf_op jit(solution)/shard_map/convert_element_type | solution.py:534
  14.2 10.1 %collective-permute-done.refs_1_ = bf16[39552,128]{1,0:T(8,128)(2,1)} collective-permute-done((bf16[39552,128]{1,0:T(8,128)(2,1)S(1)}, bf16[39552,128]{1,0:T(8,128)(2,1)}, u32[]{:S(2)}, u32[]{:S(2)}) %collective-permute-start) | collective-permute-done | bytes 10125344 | tf_op jit(solution)/shard_map/ppermute | solution.py:341
  24.3 18.1 %unpack.1 = (f32[1,768]{1,0:T(1,128)}, f32[1,768]{1,0:T(1,128)}, f32[1,768]{1,0:T(1,128)}, bf16[768,2304]{1,0:T(8,128)(2,1)}, bf16[768,768]{1,0:T(8,128)(2,1)}, ...) custom-call(bf16[39552,128]{1,0:T(8,128)(2,1)} %copy-done.16, ...), custom_call_target="tpu_custom_call" | custom-call | tf_op jit(solution)/shard_map/unpack/pallas_call | solution.py:171
  49.5 4.0 convolution_convert_fusion
  56.4 2.6 copy.133
  68.0 9.1 %fusion.14 = (bf16[6,66,3072]{2,1,0:T(8,128)(2,1)}, bf16[6,66,3072]{2,1,0:T(8,128)(2,1)S(1)}) fusion(f32[3072]{0:T(1024)S(1)} %bitcast.320, bf16[768,3072]{1,0:T(8,128)(2,1)S(1)} %bitcast.315, f32[6,66,768]{2,1,0:T(8,128)S(1)} %get-tuple-element.249, f32[768]{0:T(1024)S(1)} %reduce.8, f32[768]{0:T(1024)S(1)} %reduce.7, f32[6,66]{1,0:T(8,128)S(1)} %fusion.92, ...), kind=kOutput, calls=%fused_computation.31 | convolution fusion | flops 1911444480 | bytes 10822752 | tf_op jit(solution)/shard_map/ctd,df->ctf/dot_general | solution.py:629
  77.2 2.3 fusion.17
  88.7 2.3 copy.94
  91.0 2.3 copy.93
  93.3 2.3 copy.92
  95.6 2.4 multiply_reduce_fusion.1
  104.6 19.0 %fusion.6 = (bf16[6,256,2048]{2,1,0:T(8,128)(2,1)S(1)}, bf16[6,256,2048]{2,1,0:T(8,128)(2,1)}) fusion(f32[2048]{0:T(1024)S(1)} %bitcast.321, bf16[512,2048]{1,0:T(8,128)(2,1)S(1)} %copy-done.99, f32[6,256,512]{2,1,0:T(8,128)S(1)} %get-tuple-element.255, f32[512]{0:T(512)S(1)} %bitcast.325, f32[512]{0:T(512)S(1)} %bitcast.299, f32[6,256]{1,0:T(8,128)S(1)} %fusion.90, ...), kind=kOutput, calls=%fused_computation.8 | convolution fusion | flops 3332112384 | bytes 17850368 | tf_op jit(solution)/shard_map/ctd,df->ctf/dot_general | solution.py:629
  123.6 4.3 convert_reduce_fusion
  127.9 4.6 fusion.107
  132.5 4.0 bitcast_convert_fusion.4.refs_0_
  138.7 4.8 bitcast_convert_fusion.3.refs_2_
  144.1 6.2 %convert_add_fusion = (f32[6,256,512]{2,1,0:T(8,128)}, bf16[6,256,512]{2,1,0:T(8,128)(2,1)}, f32[512]{0:T(512)}) fusion(bf16[6,256,512]{2,1,0:T(8,128)(2,1)S(1)} %copy-done.100, f32[6,256]{1,0:T(8,128)S(1)} %negate_multiply_fusion.1, f32[6,256]{1,0:T(8,128)S(1)} %multiply_multiply_fusion.3, f32[6,256,512]{2,1,0:T(8,128)S(1)} %get-tuple-element.255, ...), kind=kOutput, calls=%fused_computation.51 | convolution fusion | flops 3231448576 | bytes 21002240 | tf_op jit(solution)/shard_map/ctf,fd->ctd/dot_general | solution.py:635
  150.3 7.9 %pack62592.1 = (bf16[19968,128]{1,0:T(8,128)(2,1)}, bf16[19968,128]{1,0:T(8,128)(2,1)}) custom-call(bf16[512,2048]{1,0:T(8,128)(2,1)} %copy-done.49, f32[1,2048]{1,0:T(1,128)} %bitcast.294, bf16[2048,512]{1,0:T(8,128)(2,1)} %bitcast_convert_fusion.3.refs_2_, f32[1,512]{1,0:T(1,128)} %bitcast.309), custom_call_target="tpu_custom_call" | custom-call | tf_op jit(solution)/shard_map/pack62592/pallas_call | solution.py:273
  158.3 3.3 fusion.57.refs_10_
  171.8 2.4 copy.104
  174.2 2.3 copy.102
  176.6 2.3 copy.103
  178.9 4.4 bitcast_convert_fusion.6.refs_9_
  183.3 2.8 multiply_reduce_fusion.3
  196.6 4.3 bitcast_convert_fusion.1.refs_0_
  202.7 9.0 %pack39552.1 = (bf16[19968,128]{1,0:T(8,128)(2,1)}, bf16[19968,128]{1,0:T(8,128)(2,1)}) custom-call(bf16[3072,768]{1,0:T(8,128)(2,1)} %bitcast_convert_fusion.1.refs_0_, f32[1,768]{1,0:T(1,128)} %reshape.407.refs_1_, f32[1,768]{1,0:T(1,128)} %reshape.408.refs_2_, f32[1,768]{1,0:T(1,128)} %reshape.409.refs_3_, ...), custom_call_target="tpu_custom_call", output_to_operand_aliasing={{0}: (15, {}), {1}: (16, {})} | custom-call | tf_op jit(solution)/shard_map/pack39552/pallas_call | solution.py:273
  212.0 6.2 %convert_reduce_fusion.1 = (f32[3072]{0:T(1024)}, bf16[6,66,3072]{2,1,0:T(8,128)(2,1)S(1)}) fusion(bf16[6,66,3072]{2,1,0:T(8,128)(2,1)} %get-tuple-element.135, bf16[3072,768]{1,0:T(8,128)(2,1)} %get-tuple-element.107, f32[6,66,768]{2,1,0:T(8,128)S(1)} %get-tuple-element.134), kind=kOutput, calls=%fused_computation.32 | convolution fusion | flops 1874946048 | bytes 10813440 | tf_op jit(solution)/shard_map/ctd,fd->ctf/dot_general | solution.py:668
  218.2 2.5 fusion.108
  221.5 3.2 bitcast_convert_fusion.refs_0_
  224.7 5.2 add_convert_fusion.1
  231.8 2.6 collective-permute-start.3
  241.2 8.3 %pack18560.1 = (bf16[19968,128]{1,0:T(8,128)(2,1)}, bf16[19968,128]{1,0:T(8,128)(2,1)}) custom-call(bf16[768,3072]{1,0:T(8,128)(2,1)} %copy-done.38, f32[1,3072]{1,0:T(1,128)} %bitcast.293, bf16[512,768]{1,0:T(8,128)(2,1)} %slice.73.refs_2_), custom_call_target="tpu_custom_call" | custom-call | tf_op jit(solution)/shard_map/pack18560/pallas_call | solution.py:273
  249.6 13.4 %collective-permute-done.3 = bf16[1,4992,128]{2,1,0:T(8,128)(2,1)} collective-permute-done((bf16[1,4992,128]{2,1,0:T(8,128)(2,1)}, bf16[1,4992,128]{2,1,0:T(8,128)(2,1)}, u32[]{:S(2)}, u32[]{:S(2)}) %collective-permute-start.3) | collective-permute-done | bytes 1277984 | tf_op jit(solution)/shard_map/ppermute | solution.py:317
  263.0 3.1 add_convert_fusion.7
  277.2 5.4 multiply_convert_fusion.4
  282.6 5.9 %collective-permute-done.4 = bf16[1,2496,128]{2,1,0:T(8,128)(2,1)} collective-permute-done((bf16[1,2496,128]{2,1,0:T(8,128)(2,1)}, bf16[1,2496,128]{2,1,0:T(8,128)(2,1)}, u32[]{:S(2)}, u32[]{:S(2)}) %collective-permute-start.4) | collective-permute-done | bytes 639008 | tf_op jit(solution)/shard_map/ppermute | solution.py:317
  288.5 2.3 add_convert_fusion.14
  290.8 2.4 add_convert_fusion.13
  298.8 2.4 pad_maximum_fusion.3
  301.1 4.2 all-to-all-start
  305.4 4.4 fusion.109
  316.1 4.0 bitcast_convert_fusion.2.refs_3_
  320.1 6.8 %pack0.1 = (bf16[19968,128]{1,0:T(8,128)(2,1)}, bf16[19968,128]{1,0:T(8,128)(2,1)}) custom-call(f32[1,768]{1,0:T(1,128)} %reshape.424.refs_0_, f32[1,768]{1,0:T(1,128)} %reshape.425.refs_1_, f32[1,768]{1,0:T(1,128)} %reshape.426.refs_2_, bf16[768,2304]{1,0:T(8,128)(2,1)} %bitcast_convert_fusion.2.refs_3_, ...), custom_call_target="tpu_custom_call", output_to_operand_aliasing={{0}: (9, {}), {1}: (10, {})} | custom-call | tf_op jit(solution)/shard_map/pack0/pallas_call | solution.py:273
  327.0 8.6 %all-to-all-done = bf16[4,1248,128]{2,1,0:T(8,128)(2,1)S(1)} async-done(((bf16[4,1248,128]{2,1,0:T(8,128)(2,1)}), bf16[4,1248,128]{2,1,0:T(8,128)(2,1)S(1)}, u32[]{:S(2)}, u32[]{:S(2)}) %all-to-all-start) | async-done | bytes 1277984 | tf_op jit(solution)/shard_map/all_to_all | solution.py:320
  338.6 4.5 all-to-all-start.1
  343.1 2.7 collective-permute-done.6
  345.8 5.0 add_convert_fusion
  355.0 4.9 convolution_convert_fusion.1
  362.3 11.6 %all-to-all-done.1 = bf16[4,1,1248,128]{3,2,1,0:T(8,128)(2,1)} async-done(((bf16[4,1,1248,128]{3,2,1,0:T(8,128)(2,1)}), bf16[4,1,1248,128]{3,2,1,0:T(8,128)(2,1)}, u32[]{:S(2)}, u32[]{:S(2)}) %all-to-all-start.1) | async-done | bytes 1277984 | tf_op jit(solution)/shard_map/all_to_all | solution.py:320
  375.4 8.0 %collective-permute-done.8 = bf16[1,4992,128]{2,1,0:T(8,128)(2,1)} collective-permute-done((bf16[1,4992,128]{2,1,0:T(8,128)(2,1)}, bf16[1,4992,128]{2,1,0:T(8,128)(2,1)}, u32[]{:S(2)}, u32[]{:S(2)}) %collective-permute-start.8) | collective-permute-done | bytes 1277984 | tf_op jit(solution)/shard_map/ppermute | solution.py:317
  385.0 5.3 collective-permute-done.7
  395.2 11.3 %collective-permute-done.11 = bf16[1,2496,128]{2,1,0:T(8,128)(2,1)S(1)} collective-permute-done((bf16[1,2496,128]{2,1,0:T(8,128)(2,1)S(1)}, bf16[1,2496,128]{2,1,0:T(8,128)(2,1)S(1)}, u32[]{:S(2)}, u32[]{:S(2)}) %collective-permute-start.11) | collective-permute-done | bytes 639008 | tf_op jit(solution)/shard_map/ppermute | solution.py:317
  406.6 13.6 %collective-permute-done.12 = bf16[1,2496,128]{2,1,0:T(8,128)(2,1)S(1)} collective-permute-done((bf16[1,2496,128]{2,1,0:T(8,128)(2,1)S(1)}, bf16[1,2496,128]{2,1,0:T(8,128)(2,1)S(1)}, u32[]{:S(2)}, u32[]{:S(2)}) %collective-permute-start.12) | collective-permute-done | bytes 639008 | tf_op jit(solution)/shard_map/ppermute | solution.py:317
  422.4 4.3 all-to-all-start.2
  429.2 27.7 %all-to-all-done.2 = bf16[4,1248,128]{2,1,0:T(8,128)(2,1)} async-done(((bf16[4,1248,128]{2,1,0:T(8,128)(2,1)}), bf16[4,1248,128]{2,1,0:T(8,128)(2,1)}, u32[]{:S(2)}, u32[]{:S(2)}) %all-to-all-start.2) | async-done | bytes 1277984 | tf_op jit(solution)/shard_map/all_to_all | solution.py:320
  458.6 4.8 join.1.high1
  464.9 31.7 %all_to_all.20 = bf16[4,1,1248,128]{3,2,1,0:T(8,128)(2,1)S(1)} all-to-all(bf16[4,1,1248,128]{3,2,1,0:T(8,128)(2,1)S(1)} %broadcast_in_dim.44), channel_id=1, replica_groups={{0,8,16,24},{2,10,18,26},{4,12,20,28},{6,14,22,30},{1,9,17,25},{3,11,19..., dimensions={0} | all-to-all | bytes 2555904 | tf_op jit(solution)/shard_map/all_to_all | solution.py:320
  499.9 11.3 %collective-permute-done.18 = bf16[1,2496,128]{2,1,0:T(8,128)(2,1)S(1)} collective-permute-done((bf16[1,2496,128]{2,1,0:T(8,128)(2,1)S(1)}, bf16[1,2496,128]{2,1,0:T(8,128)(2,1)S(1)}, u32[]{:S(2)}, u32[]{:S(2)}) %collective-permute-start.18) | collective-permute-done | bytes 639008 | tf_op jit(solution)/shard_map/ppermute | solution.py:317
  511.4 5.7 collective-permute-start.21
  517.4 2.3 collective-permute-start.20
  522.5 2.4 copy-done.3
  525.0 26.3 %adam0.1 = (f32[39552,128]{1,0:T(8,128)}, f32[39552,128]{1,0:T(8,128)}, f32[39552,128]{1,0:T(8,128)}, f32[39552,128]{1,0:T(8,128)}, f32[8,128]{1,0:T(8,128)S(1)}) custom-call(s32[3]{0:T(128)S(1)} %pad_add_fusion.1.places, bf16[4992,128]{1,0:T(8,128)(2,1)S(1)} %bitcast.224, bf16[4992,128]{1,0:T(8,128)(2,1)S(1)} %bitcast.221, ...), custom_call_target="tpu_custom_call" | custom-call | flops 40894464 | bytes 66453504 | tf_op jit(solution)/shard_map/adam0/pallas_call | solution.py:510
  558.2 2.4 copy-done.4
  563.3 26.5 %adam1.1 = (f32[39552,128]{1,0:T(8,128)}, f32[39552,128]{1,0:T(8,128)}, f32[39552,128]{1,0:T(8,128)}, f32[39552,128]{1,0:T(8,128)}, f32[8,128]{1,0:T(8,128)}) custom-call(s32[3]{0:T(128)S(1)} %pad_add_fusion.places, bf16[4992,128]{1,0:T(8,128)(2,1)} %collective-permute-done.17.low0, ...), custom_call_target="tpu_custom_call", output_to_operand_aliasing={{0}: (9, {}), {1}: (10, {}), {2}: (11, {}), {3}: (12, {})} | custom-call | flops 40894464 | bytes 66453504 | tf_op jit(solution)/shard_map/adam1/pallas_call | solution.py:510
  (423 shorter events, 139.0 us)
Async XLA Ops:
  0.6 11.9 %copy-start = (bf16[6,256,768]{2,1,0:T(8,128)(2,1)S(1)}, bf16[6,256,768]{2,1,0:T(8,128)(2,1)}, u32[]{:S(2)}) copy-start(bf16[6,256,768]{2,1,0:T(8,128)(2,1)} %param.9) | copy-start | bytes 7077892
  0.7 7.9 %copy-start.109 = (s32[6]{0:T(128)S(1)}, s32[6]{0:T(128)}, u32[]{:S(2)}) copy-start(s32[6]{0:T(128)} %param.12) | copy-start | bytes 76
  0.7 7.9 %copy-start.89 = (bf16[6,768]{1,0:T(8,128)(2,1)S(1)}, bf16[6,768]{1,0:T(8,128)(2,1)}, u32[]{:S(2)}) copy-start(bf16[6,768]{1,0:T(8,128)(2,1)} %param.10) | copy-start | bytes 27652
  0.7 8.0 %copy-start.72 = (s32[6,64]{1,0:T(8,128)S(1)}, s32[6,64]{1,0:T(8,128)}, u32[]{:S(2)}) copy-start(s32[6,64]{1,0:T(8,128)} %param.11) | copy-start | bytes 4612
  8.4 15.8 %collective-permute-start = (bf16[39552,128]{1,0:T(8,128)(2,1)S(1)}, bf16[39552,128]{1,0:T(8,128)(2,1)}, u32[]{:S(2)}, u32[]{:S(2)}) collective-permute-start(bf16[39552,128]{1,0:T(8,128)(2,1)S(1)} %convert_element_type.319.refs_0_), channel_id=1, source_target_pairs={{0,1},{1,0},{2,3},{3,2},{4,5},{5,4},{6,7},{7,6},{8,9},{9,8},{10,11... | collective-permute-start | bytes 30375944 | tf_op jit(solution)/shard_map/ppermute | solution.py:341
  8.7 57.1 %copy-start.61 = (f32[6,1,768]{2,1,0:T(1,128)}, f32[6,1,768]{2,1,0:T(1,128)S(1)}, u32[]{:S(2)}) copy-start(f32[6,1,768]{2,1,0:T(1,128)S(1)} %broadcast_in_dim.32) | copy-start | bytes 55300
  14.2 34.6 %copy-start.14 = (f32[6,64,768]{2,1,0:T(8,128)S(1)}, f32[6,64,768]{2,1,0:T(8,128)}, u32[]{:S(2)}) copy-start(f32[6,64,768]{2,1,0:T(8,128)} %fusion.72) | copy-start | bytes 3538948
  43.8 9.7 %copy-start.87 = (f32[768]{0:T(1024)}, f32[768]{0:T(1024)S(1)}, u32[]{:S(2)}) copy-start(f32[768]{0:T(1024)S(1)} %reduce.4) | copy-start | bytes 9220
  44.5 23.3 %copy-start.79 = (f32[768]{0:T(1024)}, f32[768]{0:T(1024)S(1)}, u32[]{:S(2)}) copy-start(f32[768]{0:T(1024)S(1)} %reduce.7) | copy-start | bytes 9220
  45.9 7.6 %copy-start.90 = (f32[768]{0:T(1024)}, f32[768]{0:T(1024)S(1)}, u32[]{:S(2)}) copy-start(f32[768]{0:T(1024)S(1)} %reduce.5) | copy-start | bytes 9220
  46.7 21.2 %copy-start.92 = (f32[768]{0:T(1024)}, f32[768]{0:T(1024)S(1)}, u32[]{:S(2)}) copy-start(f32[768]{0:T(1024)S(1)} %reduce.8) | copy-start | bytes 9220
  48.8 16.9 %copy-start.63 = (f32[6,1,768]{2,1,0:T(1,128)}, f32[6,1,768]{2,1,0:T(1,128)S(1)}, u32[]{:S(2)}) copy-start(f32[6,1,768]{2,1,0:T(1,128)S(1)} %broadcast_in_dim.31) | copy-start | bytes 55300
  67.5 12.0 %copy-start.17 = (f32[6,66,768]{2,1,0:T(8,128)}, f32[6,66,768]{2,1,0:T(8,128)S(1)}, u32[]{:S(2)}) copy-start(f32[6,66,768]{2,1,0:T(8,128)S(1)} %get-tuple-element.249) | copy-start | bytes 3649540
  67.5 9.6 %copy-start.73 = (f32[6,66]{1,0:T(8,128)}, f32[6,66]{1,0:T(8,128)S(1)}, u32[]{:S(2)}) copy-start(f32[6,66]{1,0:T(8,128)S(1)} %broadcast_multiply_fusion.3) | copy-start | bytes 4756
  67.5 9.6 %slice-start.8 = ((s8[4718592]{0:T(1024)(128)(4,1)}), s8[4194304]{0:T(1024)(128)(4,1)S(1)}, s32[]{:S(2)}) async-start(s8[4718592]{0:T(1024)(128)(4,1)} %bitcast.318), calls=%async_computation.12 | async-start | bytes 8388608
  67.9 9.2 %copy-start.83 = (f32[6,66]{1,0:T(8,128)}, f32[6,66]{1,0:T(8,128)S(1)}, u32[]{:S(2)}) copy-start(f32[6,66]{1,0:T(8,128)S(1)} %multiply_reduce_fusion.15) | copy-start | bytes 4756
  67.9 9.2 %copy-start.77 = (f32[6,66]{1,0:T(8,128)}, f32[6,66]{1,0:T(8,128)S(1)}, u32[]{:S(2)}) copy-start(f32[6,66]{1,0:T(8,128)S(1)} %fusion.92) | copy-start | bytes 4756
  67.9 9.2 %slice-start.9 = ((s8[4718592]{0:T(1024)(128)(4,1)}), s8[524288]{0:T(1024)(128)(4,1)S(1)}, s32[]{:S(2)}) async-start(s8[4718592]{0:T(1024)(128)(4,1)} %bitcast.318), calls=%async_computation.13 | async-start | bytes 1048576
  83.6 18.5 %copy-start.10 = (f32[6,256,512]{2,1,0:T(8,128)}, f32[6,256,512]{2,1,0:T(8,128)S(1)}, u32[]{:S(2)}) copy-start(f32[6,256,512]{2,1,0:T(8,128)S(1)} %get-tuple-element.251) | copy-start | bytes 9437188
  104.6 19.0 %copy-start.98 = (bf16[2048,512]{1,0:T(8,128)(2,1)S(1)}, bf16[2048,512]{1,0:T(8,128)(2,1)}, u32[]{:S(2)}) copy-start(bf16[2048,512]{1,0:T(8,128)(2,1)} %get-tuple-element.124) | copy-start | bytes 6291460
  104.6 19.0 %copy-start.100 = (bf16[6,256,512]{2,1,0:T(8,128)(2,1)S(1)}, bf16[6,256,512]{2,1,0:T(8,128)(2,1)}, u32[]{:S(2)}) copy-start(bf16[6,256,512]{2,1,0:T(8,128)(2,1)} %param.13) | copy-start | bytes 4718596
  123.6 15.1 %slice-start.10 = ((s8[6291456]{0:T(1024)(128)(4,1)}), s8[2097152]{0:T(1024)(128)(4,1)S(1)}, s32[]{:S(2)}) async-start(s8[6291456]{0:T(1024)(128)(4,1)} %bitcast.328), calls=%async_computation.14 | async-start | bytes 4194304
  127.9 10.8 %slice-start.11 = ((s8[6291456]{0:T(1024)(128)(4,1)}), s8[4194304]{0:T(1024)(128)(4,1)S(1)}, s32[]{:S(2)}) async-start(s8[6291456]{0:T(1024)(128)(4,1)} %bitcast.328), calls=%async_computation.15 | async-start | bytes 8388608
  136.5 7.0 %copy-start.49 = (bf16[512,2048]{1,0:T(8,128)(2,1)}, bf16[512,2048]{1,0:T(8,128)(2,1)S(1)}, u32[]{:S(2)}) copy-start(bf16[512,2048]{1,0:T(8,128)(2,1)S(1)} %bitcast_convert_fusion.4.refs_0_) | copy-start | bytes 6291460
  150.3 7.9 %copy-start.45 = (bf16[6,4,64,256]{3,2,1,0:T(8,128)(2,1)S(1)}, bf16[6,4,64,256]{3,2,1,0:T(8,128)(2,1)}, u32[]{:S(2)}) copy-start(bf16[6,4,64,256]{3,2,1,0:T(8,128)(2,1)} %copy-done.44) | copy-start | bytes 2359300
  150.3 11.9 %slice-start = ((s8[6291456]{0:T(1024)(128)(4,1)}), s8[2097152]{0:T(1024)(128)(4,1)S(1)}, s32[]{:S(2)}) async-start(s8[6291456]{0:T(1024)(128)(4,1)} %bitcast.225), calls=%async_computation.4 | async-start | bytes 4194304
  171.8 7.1 %copy-start.11 = (f32[6,256,512]{2,1,0:T(8,128)S(1)}, f32[6,256,512]{2,1,0:T(8,128)}, u32[]{:S(2)}) copy-start(f32[6,256,512]{2,1,0:T(8,128)} %copy-done.10) | copy-start | bytes 9437188
  202.7 15.4 %slice-start.6 = ((s8[4718592]{0:T(1024)(128)(4,1)}), s8[524288]{0:T(1024)(128)(4,1)S(1)}, s32[]{:S(2)}) async-start(s8[4718592]{0:T(1024)(128)(4,1)} %bitcast.316), calls=%async_computation.10 | async-start | bytes 1048576
  211.7 12.9 %collective-permute-start.1 = (bf16[19968,128]{1,0:T(8,128)(2,1)}, bf16[19968,128]{1,0:T(8,128)(2,1)}, u32[]{:S(2)}, u32[]{:S(2)}) collective-permute-start(bf16[19968,128]{1,0:T(8,128)(2,1)} %get-tuple-element.139), channel_id=1, source_target_pairs={{0,1},{1,0},{2,3},{3,2},{4,5},{5,4},{6,7},{7,6},{8,9},{9,8},{10,11... | collective-permute-start | bytes 15335432 | tf_op jit(solution)/shard_map/ppermute | solution.py:341
  224.6 16.0 %copy-start.38 = (bf16[768,3072]{1,0:T(8,128)(2,1)}, bf16[768,3072]{1,0:T(8,128)(2,1)S(1)}, u32[]{:S(2)}) copy-start(bf16[768,3072]{1,0:T(8,128)(2,1)S(1)} %bitcast_convert_fusion.refs_0_) | copy-start | bytes 14155780
  231.8 31.2 %collective-permute-start.3 = (bf16[1,4992,128]{2,1,0:T(8,128)(2,1)}, bf16[1,4992,128]{2,1,0:T(8,128)(2,1)}, u32[]{:S(2)}, u32[]{:S(2)}) collective-permute-start(bf16[1,4992,128]{2,1,0:T(8,128)(2,1)} %constant_dynamic-slice_fusion.6), channel_id=1, source_target_pairs={{0,4},{4,0},{2,6},{6,2},{8,12},{12,8},{10,14},{14,10},{16,20},{20,... | collective-permute-start | bytes 3833864 | tf_op jit(solution)/shard_map/ppermute | solution.py:317
  234.9 32.6 %copy-start.23 = (f32[6,66,768]{2,1,0:T(8,128)}, f32[6,66,768]{2,1,0:T(8,128)S(1)}, u32[]{:S(2)}) copy-start(f32[6,66,768]{2,1,0:T(8,128)S(1)} %add_add_fusion.9) | copy-start | bytes 3649540
  236.1 30.0 %collective-permute-start.2 = (bf16[1,4992,128]{2,1,0:T(8,128)(2,1)}, bf16[1,4992,128]{2,1,0:T(8,128)(2,1)S(1)}, u32[]{:S(2)}, u32[]{:S(2)}) collective-permute-start(bf16[1,4992,128]{2,1,0:T(8,128)(2,1)} %constant_dynamic-slice_fusion.7), channel_id=1, source_target_pairs={{0,2},{2,0},{4,6},{6,4},{8,10},{10,8},{12,14},{14,12},{16,18},{18,... | collective-permute-start | bytes 3833864 | tf_op jit(solution)/shard_map/ppermute | solution.py:317
  249.6 16.5 %copy-start.29 = (bf16[9984,128]{1,0:T(8,128)(2,1)S(1)}, bf16[9984,128]{1,0:T(8,128)(2,1)}, u32[]{:S(2)}) copy-start(bf16[9984,128]{1,0:T(8,128)(2,1)} %copy-done.28) | copy-start | bytes 7667716
  268.3 7.0 %copy-start.22 = (f32[6,12,66,66]{2,3,1,0:T(8,128)S(1)}, f32[6,12,66,66]{2,3,1,0:T(8,128)}, u32[]{:S(2)}) copy-start(f32[6,12,66,66]{2,3,1,0:T(8,128)} %copy-done.21) | copy-start | bytes 3763588
  272.9 15.5 %collective-permute-start.4 = (bf16[1,2496,128]{2,1,0:T(8,128)(2,1)}, bf16[1,2496,128]{2,1,0:T(8,128)(2,1)}, u32[]{:S(2)}, u32[]{:S(2)}) collective-permute-start(bf16[1,2496,128]{2,1,0:T(8,128)(2,1)} %constant_dynamic-slice_fusion.5), channel_id=1, source_target_pairs={{0,4},{4,0},{2,6},{6,2},{8,12},{12,8},{10,14},{14,10},{16,20},{20,... | collective-permute-start | bytes 1916936 | tf_op jit(solution)/shard_map/ppermute | solution.py:317
  274.1 16.7 %collective-permute-start.5 = (bf16[1,2496,128]{2,1,0:T(8,128)(2,1)S(1)}, bf16[1,2496,128]{2,1,0:T(8,128)(2,1)}, u32[]{:S(2)}, u32[]{:S(2)}) collective-permute-start(bf16[1,2496,128]{2,1,0:T(8,128)(2,1)S(1)} %constant_dynamic-slice_fusion.4), channel_id=1, source_target_pairs={{0,2},{2,0},{4,6},{6,4},{8,10},{10,8},{12,14},{14,12},{16,18},{18,... | collective-permute-start | bytes 1916936 | tf_op jit(solution)/shard_map/ppermute | solution.py:317
  282.6 10.6 %copy-start.27 = (bf16[6,66,768]{1,2,0:T(8,128)(2,1)S(1)}, bf16[6,66,768]{1,2,0:T(8,128)(2,1)}, u32[]{:S(2)}) copy-start(bf16[6,66,768]{1,2,0:T(8,128)(2,1)} %copy.133) | copy-start | bytes 1824772
  282.6 10.6 %copy-start.35 = (bf16[6,12,66,66]{2,3,1,0:T(8,128)(2,1)S(1)}, bf16[6,12,66,66]{2,3,1,0:T(8,128)(2,1)}, u32[]{:S(2)}) copy-start(bf16[6,12,66,66]{2,3,1,0:T(8,128)(2,1)} %multiply_convert_fusion.4) | copy-start | bytes 1881796
  301.1 34.4 %all-to-all-start = ((bf16[4,1248,128]{2,1,0:T(8,128)(2,1)}), bf16[4,1248,128]{2,1,0:T(8,128)(2,1)S(1)}, u32[]{:S(2)}, u32[]{:S(2)}) async-start(bf16[4,1248,128]{2,1,0:T(8,128)(2,1)} %pad_maximum_fusion.3), calls=%async_computation | async-start | bytes 2555904 | tf_op jit(solution)/shard_map/all_to_all | solution.py:320
  335.9 9.9 %collective-permute-start.6 = (bf16[19968,128]{1,0:T(8,128)(2,1)}, bf16[19968,128]{1,0:T(8,128)(2,1)}, u32[]{:S(2)}, u32[]{:S(2)}) collective-permute-start(bf16[19968,128]{1,0:T(8,128)(2,1)} %get-tuple-element.154), channel_id=1, source_target_pairs={{0,1},{1,0},{2,3},{3,2},{4,5},{5,4},{6,7},{7,6},{8,9},{9,8},{10,11... | collective-permute-start | bytes 15335432 | tf_op jit(solution)/shard_map/ppermute | solution.py:341
  338.6 35.3 %all-to-all-start.1 = ((bf16[4,1,1248,128]{3,2,1,0:T(8,128)(2,1)}), bf16[4,1,1248,128]{3,2,1,0:T(8,128)(2,1)}, u32[]{:S(2)}, u32[]{:S(2)}) async-start(bf16[4,1,1248,128]{3,2,1,0:T(8,128)(2,1)} %broadcast_in_dim.43), calls=%async_computation.1 | async-start | bytes 2555904 | tf_op jit(solution)/shard_map/all_to_all | solution.py:320
  353.8 29.6 %collective-permute-start.8 = (bf16[1,4992,128]{2,1,0:T(8,128)(2,1)}, bf16[1,4992,128]{2,1,0:T(8,128)(2,1)}, u32[]{:S(2)}, u32[]{:S(2)}) collective-permute-start(bf16[1,4992,128]{2,1,0:T(8,128)(2,1)} %constant_dynamic-slice_fusion.2), channel_id=1, source_target_pairs={{0,4},{4,0},{2,6},{6,2},{8,12},{12,8},{10,14},{14,10},{16,20},{20,... | collective-permute-start | bytes 3833864 | tf_op jit(solution)/shard_map/ppermute | solution.py:317
  361.0 29.3 %collective-permute-start.7 = (bf16[1,4992,128]{2,1,0:T(8,128)(2,1)}, bf16[1,4992,128]{2,1,0:T(8,128)(2,1)}, u32[]{:S(2)}, u32[]{:S(2)}) collective-permute-start(bf16[1,4992,128]{2,1,0:T(8,128)(2,1)} %constant_dynamic-slice_fusion.3), channel_id=1, source_target_pairs={{0,2},{2,0},{4,6},{6,4},{8,10},{10,8},{12,14},{14,12},{16,18},{18,... | collective-permute-start | bytes 3833864 | tf_op jit(solution)/shard_map/ppermute | solution.py:317
  373.9 9.5 %copy-start.32 = (bf16[9984,128]{1,0:T(8,128)(2,1)S(1)}, bf16[9984,128]{1,0:T(8,128)(2,1)}, u32[]{:S(2)}) copy-start(bf16[9984,128]{1,0:T(8,128)(2,1)} %copy-done.31) | copy-start | bytes 7667716
  392.0 14.5 %collective-permute-start.11 = (bf16[1,2496,128]{2,1,0:T(8,128)(2,1)S(1)}, bf16[1,2496,128]{2,1,0:T(8,128)(2,1)S(1)}, u32[]{:S(2)}, u32[]{:S(2)}) collective-permute-start(bf16[1,2496,128]{2,1,0:T(8,128)(2,1)S(1)} %bitcast.274), channel_id=1, source_target_pairs={{0,4},{4,0},{2,6},{6,2},{8,12},{12,8},{10,14},{14,10},{16,20},{20,... | collective-permute-start | bytes 1916936 | tf_op jit(solution)/shard_map/ppermute | solution.py:317
  392.3 28.4 %collective-permute-start.10 = (bf16[1,2496,128]{2,1,0:T(8,128)(2,1)S(1)}, bf16[1,2496,128]{2,1,0:T(8,128)(2,1)S(1)}, u32[]{:S(2)}, u32[]{:S(2)}) collective-permute-start(bf16[1,2496,128]{2,1,0:T(8,128)(2,1)S(1)} %constant_dynamic-slice_fusion), channel_id=1, source_target_pairs={{0,2},{2,0},{4,6},{6,4},{8,10},{10,8},{12,14},{14,12},{16,18},{18,... | collective-permute-start | bytes 1916936 | tf_op jit(solution)/shard_map/ppermute | solution.py:317
  393.6 27.2 %collective-permute-start.9 = (bf16[1,2496,128]{2,1,0:T(8,128)(2,1)S(1)}, bf16[1,2496,128]{2,1,0:T(8,128)(2,1)S(1)}, u32[]{:S(2)}, u32[]{:S(2)}) collective-permute-start(bf16[1,2496,128]{2,1,0:T(8,128)(2,1)S(1)} %constant_dynamic-slice_fusion.1), channel_id=1, source_target_pairs={{0,4},{4,0},{2,6},{6,2},{8,12},{12,8},{10,14},{14,10},{16,20},{20,... | collective-permute-start | bytes 1916936 | tf_op jit(solution)/shard_map/ppermute | solution.py:317
  395.0 25.3 %collective-permute-start.12 = (bf16[1,2496,128]{2,1,0:T(8,128)(2,1)S(1)}, bf16[1,2496,128]{2,1,0:T(8,128)(2,1)S(1)}, u32[]{:S(2)}, u32[]{:S(2)}) collective-permute-start(bf16[1,2496,128]{2,1,0:T(8,128)(2,1)S(1)} %bitcast.272), channel_id=1, source_target_pairs={{0,2},{2,0},{4,6},{6,4},{8,10},{10,8},{12,14},{14,12},{16,18},{18,... | collective-permute-start | bytes 1916936 | tf_op jit(solution)/shard_map/ppermute | solution.py:317
  420.6 7.3 %copy-start.37 = (bf16[2,2496,128]{2,1,0:T(8,128)(2,1)}, bf16[2,2496,128]{2,1,0:T(8,128)(2,1)S(1)}, u32[]{:S(2)}) copy-start(bf16[2,2496,128]{2,1,0:T(8,128)(2,1)S(1)} %pad_maximum_fusion.5) | copy-start | bytes 3833860
  422.4 34.6 %all-to-all-start.2 = ((bf16[4,1248,128]{2,1,0:T(8,128)(2,1)}), bf16[4,1248,128]{2,1,0:T(8,128)(2,1)}, u32[]{:S(2)}, u32[]{:S(2)}) async-start(bf16[4,1248,128]{2,1,0:T(8,128)(2,1)} %pad_maximum_fusion.6), calls=%async_computation.2 | async-start | bytes 2555904 | tf_op jit(solution)/shard_map/all_to_all | solution.py:320
  426.7 31.9 %collective-permute-start.13 = (bf16[4992,128]{1,0:T(8,128)(2,1)S(1)}, bf16[4992,128]{1,0:T(8,128)(2,1)}, u32[]{:S(2)}, u32[]{:S(2)}) collective-permute-start(bf16[4992,128]{1,0:T(8,128)(2,1)S(1)} %bitcast.247), channel_id=1, source_target_pairs={{0,2},{2,0},{4,6},{6,4},{8,10},{10,8},{12,14},{14,12},{16,18},{18,... | collective-permute-start | bytes 3833864 | tf_op jit(solution)/shard_map/ppermute | solution.py:317
  428.0 30.6 %collective-permute-start.14 = (bf16[4992,128]{1,0:T(8,128)(2,1)S(1)}, bf16[4992,128]{1,0:T(8,128)(2,1)}, u32[]{:S(2)}, u32[]{:S(2)}) collective-permute-start(bf16[4992,128]{1,0:T(8,128)(2,1)S(1)} %bitcast.249), channel_id=1, source_target_pairs={{0,4},{4,0},{2,6},{6,2},{8,12},{12,8},{10,14},{14,10},{16,20},{20,... | collective-permute-start | bytes 3833864 | tf_op jit(solution)/shard_map/ppermute | solution.py:317
  463.4 33.3 %collective-permute-start.15 = (bf16[19968,128]{1,0:T(8,128)(2,1)}, bf16[19968,128]{1,0:T(8,128)(2,1)S(1)}, u32[]{:S(2)}, u32[]{:S(2)}) collective-permute-start(bf16[19968,128]{1,0:T(8,128)(2,1)} %join.1.high1), channel_id=1, source_target_pairs={{0,1},{2,3},{4,5},{6,7},{8,9},{10,11},{12,13},{14,15},{16,17},{18,... | collective-permute-start | bytes 15335432 | tf_op jit(solution)/shard_map/ppermute | solution.py:530
  496.7 14.7 %copy-start.2 = (bf16[19968,128]{1,0:T(8,128)(2,1)}, bf16[19968,128]{1,0:T(8,128)(2,1)S(1)}, u32[]{:S(2)}) copy-start(bf16[19968,128]{1,0:T(8,128)(2,1)S(1)} %collective-permute-done.15.high0) | copy-start | bytes 15335428
  496.7 14.5 %collective-permute-start.18 = (bf16[1,2496,128]{2,1,0:T(8,128)(2,1)S(1)}, bf16[1,2496,128]{2,1,0:T(8,128)(2,1)S(1)}, u32[]{:S(2)}, u32[]{:S(2)}) collective-permute-start(bf16[1,2496,128]{2,1,0:T(8,128)(2,1)S(1)} %bitcast.278), channel_id=1, source_target_pairs={{0,2},{2,0},{4,6},{6,4},{8,10},{10,8},{12,14},{14,12},{16,18},{18,... | collective-permute-start | bytes 1916936 | tf_op jit(solution)/shard_map/ppermute | solution.py:317
  498.6 18.5 %collective-permute-start.16 = (bf16[1,2496,128]{2,1,0:T(8,128)(2,1)S(1)}, bf16[1,2496,128]{2,1,0:T(8,128)(2,1)S(1)}, u32[]{:S(2)}, u32[]{:S(2)}) collective-permute-start(bf16[1,2496,128]{2,1,0:T(8,128)(2,1)S(1)} %bitcast.276), channel_id=1, source_target_pairs={{0,4},{4,0},{2,6},{6,2},{8,12},{12,8},{10,14},{14,10},{16,20},{20,... | collective-permute-start | bytes 1916936 | tf_op jit(solution)/shard_map/ppermute | solution.py:317
  511.4 11.1 %collective-permute-start.21 = (bf16[4992,128]{1,0:T(8,128)(2,1)S(1)}, bf16[4992,128]{1,0:T(8,128)(2,1)}, u32[]{:S(2)}, u32[]{:S(2)}) collective-permute-start(bf16[4992,128]{1,0:T(8,128)(2,1)S(1)} %bitcast.219), channel_id=1, source_target_pairs={{1,0},{3,2},{5,4},{7,6},{9,8},{11,10},{13,12},{15,14},{17,16},{19,... | collective-permute-start | bytes 3833864 | tf_op jit(solution)/shard_map/ppermute | solution.py:530
  517.4 5.1 collective-permute-start.20
  519.7 31.5 %collective-permute-start.19 = (bf16[4992,128]{1,0:T(8,128)(2,1)S(1)}, bf16[4992,128]{1,0:T(8,128)(2,1)}, u32[]{:S(2)}, u32[]{:S(2)}) collective-permute-start(bf16[4992,128]{1,0:T(8,128)(2,1)S(1)} %bitcast.220), channel_id=1, source_target_pairs={{0,4},{4,0},{2,6},{6,2},{8,12},{12,8},{10,14},{14,10},{16,20},{20,... | collective-permute-start | bytes 3833864 | tf_op jit(solution)/shard_map/ppermute | solution.py:317
  521.0 30.3 %collective-permute-start.17 = (bf16[4992,128]{1,0:T(8,128)(2,1)S(1)}, bf16[4992,128]{1,0:T(8,128)(2,1)}, u32[]{:S(2)}, u32[]{:S(2)}) collective-permute-start(bf16[4992,128]{1,0:T(8,128)(2,1)S(1)} %bitcast.223), channel_id=1, source_target_pairs={{0,2},{2,0},{4,6},{6,4},{8,10},{10,8},{12,14},{14,12},{16,18},{18,... | collective-permute-start | bytes 3833864 | tf_op jit(solution)/shard_map/ppermute | solution.py:317
  551.3 4.1 collective-permute-start.22
  552.6 4.6 collective-permute-start.23
  563.3 26.5 %copy-start.1 = (bf16[6,256,768]{2,1,0:T(8,128)(2,1)S(1)}, bf16[6,256,768]{2,1,0:T(8,128)(2,1)}, u32[]{:S(2)}) copy-start(bf16[6,256,768]{2,1,0:T(8,128)(2,1)} %param.9) | copy-start | bytes 7077892
  (87 other events, 267.3 us)

commit v7 on v6

--- a/solution.py
+++ b/solution.py
@@ -409,6 +409,7 @@
         in_specs=[pl.BlockSpec(memory_space=pltpu.VMEM)] * 4,
         out_specs=pl.BlockSpec(memory_space=pl.ANY),
         scratch_shapes=[pltpu.SemaphoreType.DMA((4,))],
+        cost_estimate=pl.CostEstimate(flops=0, transcendentals=0, bytes_accessed=total * 512),
         name="join",
     )(first[1], first[2], second[1], second[2])
 
@@ -838,16 +839,16 @@
     ).astype(jnp.bfloat16)
     if chunked:
         patch_grad, low, high = tie((patch_grad, low, high))
-        high = gather_second(high)
         low = scatter_second(low)
         low, high = tie((low, high))
+        high = gather_second(high)
+        low = scatter_last(low)
+        low, high = tie((low, high))
         high = gather_last(high)
-        low = scatter_last(low)
+        low = gather_first(low)
         low, high = tie((low, high))
         high = joined(high)
         high = (to_owner(high, 0), high)
-        low = gather_first(low)
-        low, high = tie((low, high))
         low = gather_second(low)
         early = (*low, *[to_owner(v, 1) for v in low])
         *held, token = adam_rows(early, high, moment1, moment2, 0, (), chips_all)

time: 601 us -> 589 us (0.980)
  blocking collectives: 31.7 us -> 0 us
  waiting for transfers between devices: 132 us -> 151 us
    all_to_all x1 -> x0, blocking collectives: 31.7 us -> none  [exchange(): return lax.all_to_all(value, 'wide', 0, 0, axis_index_groups=self.groups)]
    all_to_all x3 -> x4, waiting for transfers between devices: 48 us -> 69.1 us  [exchange(): return lax.all_to_all(value, 'wide', 0, 0, axis_index_groups=self.groups)]
    unnamed x248 -> x246, local copies, waits for them, and re-layouts: 21.9 us -> 15.6 us
    all_to_all x3 -> x4, starting transfers between devices: 13 us -> 17.6 us  [exchange(): return lax.all_to_all(value, 'wide', 0, 0, axis_index_groups=self.groups)]
  transfers between devices with their start and end apart: 27 -> 28, of which waited for: 14 -> 18; matrix products, arithmetic and copies ran while one was open for 12% -> 12% of each run, Pallas kernels for 7% -> 7%
where the time goes in v7:
time: 589 us; the launch traced here: 579 us
  waiting for transfers between devices  151 us (26%)
  matrix products  136 us (23%)
  Pallas kernels  111 us (19%)
  local copies, waits for them, and re-layouts  68 us (12%)
  other arithmetic  62.7 us (11%)
  starting transfers between devices  48.1 us (8%)
    all_to_all x4, waiting for transfers between devices, exchange(): return lax.all_to_all(value, 'wide', 0, 0, axis_index_groups=self.groups)  69.1 us
    ppermute x16, waiting for transfers between devices, swap(): return lax.ppermute(value, 'wide', pairs)  65.3 us
    pallas_call x2, Pallas kernels, adam_rows(): pl.pallas_call(kernel, out_shape=[jax.ShapeDtypeStruct(moment1.shape, jnp...  55.5 us
    pallas_call x4, Pallas kernels, pack_part(): pl.pallas_call(kernel, out_shape=[jax.ShapeDtypeStruct((middle - first, 1...  32.1 us
    dot_general x2, matrix products, block_forward(): jnp.einsum('ctd,df->ctf', second_in, weights_map[prefix + 'u'], preferred...  28.1 us
    convert_element_type x10, other arithmetic, added(): (first.astype(jnp.float32) + second.astype(jnp.float32)).astype(jnp.bfloa...  22.9 us
    pallas_call x1, Pallas kernels, unpack(): pl.pallas_call(kernel, out_shape=out_shape, in_specs=[pl.BlockSpec(memory...  18.1 us
    all_to_all x4, starting transfers between devices, exchange(): return lax.all_to_all(value, 'wide', 0, 0, axis_index_groups=self.groups)  17.6 us
  transfers between devices with their start and end apart: 28, of which 18 were waited for; matrix products, arithmetic and copies ran while one was open for 12% of the time, Pallas kernels for 7%

profile of v7, /device:TPU:1, one launch (start us, length us, event | category | flops | bytes accessed | tf_op | source)
XLA Modules:
  0.0 578.5 jit_solution(753895347526670330)
XLA Ops:
  0.7 7.7 %convert_element_type.319.refs_0_ = bf16[39552,128]{1,0:T(8,128)(2,1)S(1)} convert(f32[39552,128]{1,0:T(8,128)} %param.14) | non-fusion elementwise | flops 5062656 | bytes 30375936 | tf_op jit(solution)/shard_map/convert_element_type | solution.py:535
  14.2 10.1 %collective-permute-done.refs_1_ = bf16[39552,128]{1,0:T(8,128)(2,1)} collective-permute-done((bf16[39552,128]{1,0:T(8,128)(2,1)S(1)}, bf16[39552,128]{1,0:T(8,128)(2,1)}, u32[]{:S(2)}, u32[]{:S(2)}) %collective-permute-start) | collective-permute-done | bytes 10125344 | tf_op jit(solution)/shard_map/ppermute | solution.py:341
  24.3 18.1 %unpack.1 = (f32[1,768]{1,0:T(1,128)}, f32[1,768]{1,0:T(1,128)}, f32[1,768]{1,0:T(1,128)}, bf16[768,2304]{1,0:T(8,128)(2,1)}, bf16[768,768]{1,0:T(8,128)(2,1)}, ...) custom-call(bf16[39552,128]{1,0:T(8,128)(2,1)} %copy-done.13, ...), custom_call_target="tpu_custom_call" | custom-call | tf_op jit(solution)/shard_map/unpack/pallas_call | solution.py:171
  49.5 4.0 convolution_convert_fusion
  56.4 2.6 copy.133
  67.9 9.4 %fusion.14 = (bf16[6,66,3072]{2,1,0:T(8,128)(2,1)}, bf16[6,66,3072]{2,1,0:T(8,128)(2,1)S(1)}) fusion(f32[3072]{0:T(1024)S(1)} %bitcast.317, bf16[768,3072]{1,0:T(8,128)(2,1)S(1)} %bitcast.312, f32[6,66,768]{2,1,0:T(8,128)S(1)} %get-tuple-element.249, f32[768]{0:T(1024)S(1)} %reduce.8, f32[768]{0:T(1024)S(1)} %reduce.7, f32[6,66]{1,0:T(8,128)S(1)} %fusion.92, ...), kind=kOutput, calls=%fused_computation.31 | convolution fusion | flops 1911444480 | bytes 10822752 | tf_op jit(solution)/shard_map/ctd,df->ctf/dot_general | solution.py:630
  77.4 2.3 fusion.17
  88.9 2.3 copy.94
  91.2 2.3 copy.93
  93.5 2.3 copy.92
  95.8 2.4 multiply_reduce_fusion.1
  104.8 18.7 %fusion.6 = (bf16[6,256,2048]{2,1,0:T(8,128)(2,1)S(1)}, bf16[6,256,2048]{2,1,0:T(8,128)(2,1)}) fusion(f32[2048]{0:T(1024)S(1)} %bitcast.318, bf16[512,2048]{1,0:T(8,128)(2,1)S(1)} %copy-done.98, f32[6,256,512]{2,1,0:T(8,128)S(1)} %get-tuple-element.255, f32[512]{0:T(512)S(1)} %bitcast.322, f32[512]{0:T(512)S(1)} %bitcast.296, f32[6,256]{1,0:T(8,128)S(1)} %fusion.90, ...), kind=kOutput, calls=%fused_computation.8 | convolution fusion | flops 3332112384 | bytes 17850368 | tf_op jit(solution)/shard_map/ctd,df->ctf/dot_general | solution.py:630
  123.6 4.3 convert_reduce_fusion
  127.8 4.7 fusion.107
  132.5 4.0 bitcast_convert_fusion.4.refs_0_
  138.7 4.8 bitcast_convert_fusion.3.refs_2_
  144.1 6.2 %convert_add_fusion = (f32[6,256,512]{2,1,0:T(8,128)}, bf16[6,256,512]{2,1,0:T(8,128)(2,1)}, f32[512]{0:T(512)}) fusion(bf16[6,256,512]{2,1,0:T(8,128)(2,1)S(1)} %copy-done.99, f32[6,256]{1,0:T(8,128)S(1)} %negate_multiply_fusion.1, f32[6,256]{1,0:T(8,128)S(1)} %multiply_multiply_fusion.3, f32[6,256,512]{2,1,0:T(8,128)S(1)} %get-tuple-element.255, ...), kind=kOutput, calls=%fused_computation.51 | convolution fusion | flops 3231448576 | bytes 21002240 | tf_op jit(solution)/shard_map/ctf,fd->ctd/dot_general | solution.py:636
  150.3 7.9 %pack62592.1 = (bf16[19968,128]{1,0:T(8,128)(2,1)}, bf16[19968,128]{1,0:T(8,128)(2,1)}) custom-call(bf16[512,2048]{1,0:T(8,128)(2,1)} %copy-done.48, f32[1,2048]{1,0:T(1,128)} %bitcast.291, bf16[2048,512]{1,0:T(8,128)(2,1)} %bitcast_convert_fusion.3.refs_2_, f32[1,512]{1,0:T(1,128)} %bitcast.306), custom_call_target="tpu_custom_call" | custom-call | tf_op jit(solution)/shard_map/pack62592/pallas_call | solution.py:273
  158.3 3.4 fusion.57.refs_10_
  171.8 2.4 copy.104
  174.2 2.3 copy.102
  178.9 4.4 bitcast_convert_fusion.6.refs_9_
  183.3 2.8 multiply_reduce_fusion.3
  196.7 4.3 bitcast_convert_fusion.1.refs_0_
  202.7 9.0 %pack39552.1 = (bf16[19968,128]{1,0:T(8,128)(2,1)}, bf16[19968,128]{1,0:T(8,128)(2,1)}) custom-call(bf16[3072,768]{1,0:T(8,128)(2,1)} %bitcast_convert_fusion.1.refs_0_, f32[1,768]{1,0:T(1,128)} %reshape.407.refs_1_, f32[1,768]{1,0:T(1,128)} %reshape.408.refs_2_, f32[1,768]{1,0:T(1,128)} %reshape.409.refs_3_, ...), custom_call_target="tpu_custom_call", output_to_operand_aliasing={{0}: (15, {}), {1}: (16, {})} | custom-call | tf_op jit(solution)/shard_map/pack39552/pallas_call | solution.py:273
  212.0 6.2 %convert_reduce_fusion.1 = (f32[3072]{0:T(1024)}, bf16[6,66,3072]{2,1,0:T(8,128)(2,1)S(1)}) fusion(bf16[6,66,3072]{2,1,0:T(8,128)(2,1)} %get-tuple-element.135, bf16[3072,768]{1,0:T(8,128)(2,1)} %get-tuple-element.107, f32[6,66,768]{2,1,0:T(8,128)S(1)} %get-tuple-element.134), kind=kOutput, calls=%fused_computation.32 | convolution fusion | flops 1874946048 | bytes 10813440 | tf_op jit(solution)/shard_map/ctd,fd->ctf/dot_general | solution.py:669
  218.2 2.5 fusion.108
  221.5 3.2 bitcast_convert_fusion.refs_0_
  224.7 5.2 add_convert_fusion.1
  231.8 2.6 collective-permute-start.3
  241.3 8.3 %pack18560.1 = (bf16[19968,128]{1,0:T(8,128)(2,1)}, bf16[19968,128]{1,0:T(8,128)(2,1)}) custom-call(bf16[768,3072]{1,0:T(8,128)(2,1)} %copy-done.35, f32[1,3072]{1,0:T(1,128)} %bitcast.290, bf16[512,768]{1,0:T(8,128)(2,1)} %slice.73.refs_2_), custom_call_target="tpu_custom_call" | custom-call | tf_op jit(solution)/shard_map/pack18560/pallas_call | solution.py:273
  249.6 13.4 %collective-permute-done.3 = bf16[1,4992,128]{2,1,0:T(8,128)(2,1)} collective-permute-done((bf16[1,4992,128]{2,1,0:T(8,128)(2,1)}, bf16[1,4992,128]{2,1,0:T(8,128)(2,1)}, u32[]{:S(2)}, u32[]{:S(2)}) %collective-permute-start.3) | collective-permute-done | bytes 1277984 | tf_op jit(solution)/shard_map/ppermute | solution.py:317
  263.0 3.1 add_convert_fusion.7
  277.2 5.3 multiply_convert_fusion.4
  282.5 5.9 %collective-permute-done.4 = bf16[1,2496,128]{2,1,0:T(8,128)(2,1)} collective-permute-done((bf16[1,2496,128]{2,1,0:T(8,128)(2,1)}, bf16[1,2496,128]{2,1,0:T(8,128)(2,1)}, u32[]{:S(2)}, u32[]{:S(2)}) %collective-permute-start.4) | collective-permute-done | bytes 639008 | tf_op jit(solution)/shard_map/ppermute | solution.py:317
  288.4 2.3 add_convert_fusion.14
  290.7 2.4 add_convert_fusion.13
  298.7 2.3 pad_maximum_fusion.3
  301.1 4.5 all-to-all-start
  305.6 4.4 fusion.109
  316.3 4.0 bitcast_convert_fusion.2.refs_3_
  320.3 6.8 %pack0.1 = (bf16[19968,128]{1,0:T(8,128)(2,1)}, bf16[19968,128]{1,0:T(8,128)(2,1)}) custom-call(f32[1,768]{1,0:T(1,128)} %reshape.424.refs_0_, f32[1,768]{1,0:T(1,128)} %reshape.425.refs_1_, f32[1,768]{1,0:T(1,128)} %reshape.426.refs_2_, bf16[768,2304]{1,0:T(8,128)(2,1)} %bitcast_convert_fusion.2.refs_3_, ...), custom_call_target="tpu_custom_call", output_to_operand_aliasing={{0}: (9, {}), {1}: (10, {})} | custom-call | tf_op jit(solution)/shard_map/pack0/pallas_call | solution.py:273
  327.2 8.6 %all-to-all-done = bf16[4,1248,128]{2,1,0:T(8,128)(2,1)S(1)} async-done(((bf16[4,1248,128]{2,1,0:T(8,128)(2,1)}), bf16[4,1248,128]{2,1,0:T(8,128)(2,1)S(1)}, u32[]{:S(2)}, u32[]{:S(2)}) %all-to-all-start) | async-done | bytes 1277984 | tf_op jit(solution)/shard_map/all_to_all | solution.py:320
  338.8 4.3 all-to-all-start.1
  343.1 2.9 collective-permute-done.6
  346.0 5.0 add_convert_fusion
  353.8 3.6 convolution_convert_fusion.1
  359.7 14.2 %all-to-all-done.1 = bf16[4,1,1248,128]{3,2,1,0:T(8,128)(2,1)} async-done(((bf16[4,1,1248,128]{3,2,1,0:T(8,128)(2,1)}), bf16[4,1,1248,128]{3,2,1,0:T(8,128)(2,1)}, u32[]{:S(2)}, u32[]{:S(2)}) %all-to-all-start.1) | async-done | bytes 1277984 | tf_op jit(solution)/shard_map/all_to_all | solution.py:320
  373.8 2.3 fusion.119
  376.2 5.9 %collective-permute-done.8 = bf16[1,4992,128]{2,1,0:T(8,128)(2,1)} collective-permute-done((bf16[1,4992,128]{2,1,0:T(8,128)(2,1)}, bf16[1,4992,128]{2,1,0:T(8,128)(2,1)}, u32[]{:S(2)}, u32[]{:S(2)}) %collective-permute-start.8) | collective-permute-done | bytes 1277984 | tf_op jit(solution)/shard_map/ppermute | solution.py:317
  383.7 4.0 collective-permute-done.7
  392.3 11.7 %collective-permute-done.10 = bf16[1,2496,128]{2,1,0:T(8,128)(2,1)S(1)} collective-permute-done((bf16[1,2496,128]{2,1,0:T(8,128)(2,1)S(1)}, bf16[1,2496,128]{2,1,0:T(8,128)(2,1)S(1)}, u32[]{:S(2)}, u32[]{:S(2)}) %collective-permute-start.10) | collective-permute-done | bytes 639008 | tf_op jit(solution)/shard_map/ppermute | solution.py:317
  408.1 4.5 all-to-all-start.2
  413.0 6.3 %collective-permute-done.11 = bf16[1,2496,128]{2,1,0:T(8,128)(2,1)} collective-permute-done((bf16[1,2496,128]{2,1,0:T(8,128)(2,1)}, bf16[1,2496,128]{2,1,0:T(8,128)(2,1)}, u32[]{:S(2)}, u32[]{:S(2)}) %collective-permute-start.11) | collective-permute-done | bytes 639008 | tf_op jit(solution)/shard_map/ppermute | solution.py:317
  420.9 5.2 collective-permute-done.12
  426.3 16.6 %all-to-all-done.2 = bf16[4,1248,128]{2,1,0:T(8,128)(2,1)} async-done(((bf16[4,1248,128]{2,1,0:T(8,128)(2,1)}), bf16[4,1248,128]{2,1,0:T(8,128)(2,1)}, u32[]{:S(2)}, u32[]{:S(2)}) %all-to-all-start.2) | async-done | bytes 1277984 | tf_op jit(solution)/shard_map/all_to_all | solution.py:320
  445.7 4.3 all-to-all-start.3
  450.5 29.8 %all-to-all-done.3 = bf16[4,1,1248,128]{3,2,1,0:T(8,128)(2,1)} async-done(((bf16[4,1,1248,128]{3,2,1,0:T(8,128)(2,1)}), bf16[4,1,1248,128]{3,2,1,0:T(8,128)(2,1)}, u32[]{:S(2)}, u32[]{:S(2)}) %all-to-all-start.3) | async-done | bytes 1277984 | tf_op jit(solution)/shard_map/all_to_all | solution.py:320
  482.5 4.9 join.1.high1
  489.1 11.9 %collective-permute-done.17 = bf16[1,2496,128]{2,1,0:T(8,128)(2,1)S(1)} collective-permute-done((bf16[1,2496,128]{2,1,0:T(8,128)(2,1)S(1)}, bf16[1,2496,128]{2,1,0:T(8,128)(2,1)S(1)}, u32[]{:S(2)}, u32[]{:S(2)}) %collective-permute-start.17) | collective-permute-done | bytes 639008 | tf_op jit(solution)/shard_map/ppermute | solution.py:317
  501.2 7.5 %collective-permute-start.20 = (bf16[4992,128]{1,0:T(8,128)(2,1)S(1)}, bf16[4992,128]{1,0:T(8,128)(2,1)}, u32[]{:S(2)}, u32[]{:S(2)}) collective-permute-start(bf16[4992,128]{1,0:T(8,128)(2,1)S(1)} %bitcast.219), channel_id=1, source_target_pairs={{1,0},{3,2},{5,4},{7,6},{9,8},{11,10},{13,12},{15,14},{17,16},{19,... | collective-permute-start | bytes 3833864 | tf_op jit(solution)/shard_map/ppermute | solution.py:531
  508.9 2.3 collective-permute-start.19
  513.0 27.5 %adam0.1 = (f32[39552,128]{1,0:T(8,128)}, f32[39552,128]{1,0:T(8,128)}, f32[39552,128]{1,0:T(8,128)}, f32[39552,128]{1,0:T(8,128)}, f32[8,128]{1,0:T(8,128)S(1)}) custom-call(s32[3]{0:T(128)S(1)} %pad_add_fusion.1.places, bf16[4992,128]{1,0:T(8,128)(2,1)S(1)} %bitcast.224, bf16[4992,128]{1,0:T(8,128)(2,1)S(1)} %bitcast.221, ...), custom_call_target="tpu_custom_call" | custom-call | flops 40894464 | bytes 66453504 | tf_op jit(solution)/shard_map/adam0/pallas_call | solution.py:511
  550.0 28.0 %adam1.1 = (f32[39552,128]{1,0:T(8,128)}, f32[39552,128]{1,0:T(8,128)}, f32[39552,128]{1,0:T(8,128)}, f32[39552,128]{1,0:T(8,128)}, f32[8,128]{1,0:T(8,128)}) custom-call(s32[3]{0:T(128)S(1)} %pad_add_fusion.places, bf16[4992,128]{1,0:T(8,128)(2,1)} %collective-permute-done.16.low0, ...), custom_call_target="tpu_custom_call", output_to_operand_aliasing={{0}: (9, {}), {1}: (10, {}), {2}: (11, {}), {3}: (12, {})} | custom-call | flops 40894464 | bytes 66453504 | tf_op jit(solution)/shard_map/adam1/pallas_call | solution.py:511
  (422 shorter events, 139.2 us)
Async XLA Ops:
  0.6 11.9 %copy-start = (bf16[6,256,768]{2,1,0:T(8,128)(2,1)S(1)}, bf16[6,256,768]{2,1,0:T(8,128)(2,1)}, u32[]{:S(2)}) copy-start(bf16[6,256,768]{2,1,0:T(8,128)(2,1)} %param.9) | copy-start | bytes 7077892
  0.7 7.9 %copy-start.108 = (s32[6]{0:T(128)S(1)}, s32[6]{0:T(128)}, u32[]{:S(2)}) copy-start(s32[6]{0:T(128)} %param.12) | copy-start | bytes 76
  0.7 7.9 %copy-start.88 = (bf16[6,768]{1,0:T(8,128)(2,1)S(1)}, bf16[6,768]{1,0:T(8,128)(2,1)}, u32[]{:S(2)}) copy-start(bf16[6,768]{1,0:T(8,128)(2,1)} %param.10) | copy-start | bytes 27652
  0.7 8.0 %copy-start.71 = (s32[6,64]{1,0:T(8,128)S(1)}, s32[6,64]{1,0:T(8,128)}, u32[]{:S(2)}) copy-start(s32[6,64]{1,0:T(8,128)} %param.11) | copy-start | bytes 4612
  8.4 15.8 %collective-permute-start = (bf16[39552,128]{1,0:T(8,128)(2,1)S(1)}, bf16[39552,128]{1,0:T(8,128)(2,1)}, u32[]{:S(2)}, u32[]{:S(2)}) collective-permute-start(bf16[39552,128]{1,0:T(8,128)(2,1)S(1)} %convert_element_type.319.refs_0_), channel_id=1, source_target_pairs={{0,1},{1,0},{2,3},{3,2},{4,5},{5,4},{6,7},{7,6},{8,9},{9,8},{10,11... | collective-permute-start | bytes 30375944 | tf_op jit(solution)/shard_map/ppermute | solution.py:341
  8.7 57.0 %copy-start.60 = (f32[6,1,768]{2,1,0:T(1,128)}, f32[6,1,768]{2,1,0:T(1,128)S(1)}, u32[]{:S(2)}) copy-start(f32[6,1,768]{2,1,0:T(1,128)S(1)} %broadcast_in_dim.32) | copy-start | bytes 55300
  14.2 34.6 %copy-start.11 = (f32[6,64,768]{2,1,0:T(8,128)S(1)}, f32[6,64,768]{2,1,0:T(8,128)}, u32[]{:S(2)}) copy-start(f32[6,64,768]{2,1,0:T(8,128)} %fusion.72) | copy-start | bytes 3538948
  43.8 9.7 %copy-start.86 = (f32[768]{0:T(1024)}, f32[768]{0:T(1024)S(1)}, u32[]{:S(2)}) copy-start(f32[768]{0:T(1024)S(1)} %reduce.4) | copy-start | bytes 9220
  44.5 23.3 %copy-start.78 = (f32[768]{0:T(1024)}, f32[768]{0:T(1024)S(1)}, u32[]{:S(2)}) copy-start(f32[768]{0:T(1024)S(1)} %reduce.7) | copy-start | bytes 9220
  45.9 7.6 %copy-start.89 = (f32[768]{0:T(1024)}, f32[768]{0:T(1024)S(1)}, u32[]{:S(2)}) copy-start(f32[768]{0:T(1024)S(1)} %reduce.5) | copy-start | bytes 9220
  46.6 21.2 %copy-start.91 = (f32[768]{0:T(1024)}, f32[768]{0:T(1024)S(1)}, u32[]{:S(2)}) copy-start(f32[768]{0:T(1024)S(1)} %reduce.8) | copy-start | bytes 9220
  48.8 16.9 %copy-start.62 = (f32[6,1,768]{2,1,0:T(1,128)}, f32[6,1,768]{2,1,0:T(1,128)S(1)}, u32[]{:S(2)}) copy-start(f32[6,1,768]{2,1,0:T(1,128)S(1)} %broadcast_in_dim.31) | copy-start | bytes 55300
  67.5 12.2 %copy-start.14 = (f32[6,66,768]{2,1,0:T(8,128)}, f32[6,66,768]{2,1,0:T(8,128)S(1)}, u32[]{:S(2)}) copy-start(f32[6,66,768]{2,1,0:T(8,128)S(1)} %get-tuple-element.249) | copy-start | bytes 3649540
  67.5 9.8 %copy-start.72 = (f32[6,66]{1,0:T(8,128)}, f32[6,66]{1,0:T(8,128)S(1)}, u32[]{:S(2)}) copy-start(f32[6,66]{1,0:T(8,128)S(1)} %broadcast_multiply_fusion.3) | copy-start | bytes 4756
  67.5 9.8 %slice-start.8 = ((s8[4718592]{0:T(1024)(128)(4,1)}), s8[4194304]{0:T(1024)(128)(4,1)S(1)}, s32[]{:S(2)}) async-start(s8[4718592]{0:T(1024)(128)(4,1)} %bitcast.315), calls=%async_computation.12 | async-start | bytes 8388608
  67.8 9.5 %copy-start.82 = (f32[6,66]{1,0:T(8,128)}, f32[6,66]{1,0:T(8,128)S(1)}, u32[]{:S(2)}) copy-start(f32[6,66]{1,0:T(8,128)S(1)} %multiply_reduce_fusion.15) | copy-start | bytes 4756
  67.8 9.5 %copy-start.76 = (f32[6,66]{1,0:T(8,128)}, f32[6,66]{1,0:T(8,128)S(1)}, u32[]{:S(2)}) copy-start(f32[6,66]{1,0:T(8,128)S(1)} %fusion.92) | copy-start | bytes 4756
  67.9 9.4 %slice-start.9 = ((s8[4718592]{0:T(1024)(128)(4,1)}), s8[524288]{0:T(1024)(128)(4,1)S(1)}, s32[]{:S(2)}) async-start(s8[4718592]{0:T(1024)(128)(4,1)} %bitcast.315), calls=%async_computation.13 | async-start | bytes 1048576
  83.8 18.5 %copy-start.7 = (f32[6,256,512]{2,1,0:T(8,128)}, f32[6,256,512]{2,1,0:T(8,128)S(1)}, u32[]{:S(2)}) copy-start(f32[6,256,512]{2,1,0:T(8,128)S(1)} %get-tuple-element.251) | copy-start | bytes 9437188
  104.8 18.7 %copy-start.97 = (bf16[2048,512]{1,0:T(8,128)(2,1)S(1)}, bf16[2048,512]{1,0:T(8,128)(2,1)}, u32[]{:S(2)}) copy-start(bf16[2048,512]{1,0:T(8,128)(2,1)} %get-tuple-element.124) | copy-start | bytes 6291460
  104.8 18.7 %copy-start.99 = (bf16[6,256,512]{2,1,0:T(8,128)(2,1)S(1)}, bf16[6,256,512]{2,1,0:T(8,128)(2,1)}, u32[]{:S(2)}) copy-start(bf16[6,256,512]{2,1,0:T(8,128)(2,1)} %param.13) | copy-start | bytes 4718596
  123.5 15.2 %slice-start.10 = ((s8[6291456]{0:T(1024)(128)(4,1)}), s8[2097152]{0:T(1024)(128)(4,1)S(1)}, s32[]{:S(2)}) async-start(s8[6291456]{0:T(1024)(128)(4,1)} %bitcast.325), calls=%async_computation.14 | async-start | bytes 4194304
  127.8 10.9 %slice-start.11 = ((s8[6291456]{0:T(1024)(128)(4,1)}), s8[4194304]{0:T(1024)(128)(4,1)S(1)}, s32[]{:S(2)}) async-start(s8[6291456]{0:T(1024)(128)(4,1)} %bitcast.325), calls=%async_computation.15 | async-start | bytes 8388608
  150.3 7.9 %copy-start.43 = (bf16[6,4,64,256]{3,2,1,0:T(8,128)(2,1)S(1)}, bf16[6,4,64,256]{3,2,1,0:T(8,128)(2,1)}, u32[]{:S(2)}) copy-start(bf16[6,4,64,256]{3,2,1,0:T(8,128)(2,1)} %copy-done.42) | copy-start | bytes 2359300
  150.3 11.9 %slice-start = ((s8[6291456]{0:T(1024)(128)(4,1)}), s8[2097152]{0:T(1024)(128)(4,1)S(1)}, s32[]{:S(2)}) async-start(s8[6291456]{0:T(1024)(128)(4,1)} %bitcast.225), calls=%async_computation.4 | async-start | bytes 4194304
  171.8 7.1 %copy-start.8 = (f32[6,256,512]{2,1,0:T(8,128)S(1)}, f32[6,256,512]{2,1,0:T(8,128)}, u32[]{:S(2)}) copy-start(f32[6,256,512]{2,1,0:T(8,128)} %copy-done.7) | copy-start | bytes 9437188
  202.7 15.4 %slice-start.6 = ((s8[4718592]{0:T(1024)(128)(4,1)}), s8[524288]{0:T(1024)(128)(4,1)S(1)}, s32[]{:S(2)}) async-start(s8[4718592]{0:T(1024)(128)(4,1)} %bitcast.313), calls=%async_computation.10 | async-start | bytes 1048576
  211.8 12.9 %collective-permute-start.1 = (bf16[19968,128]{1,0:T(8,128)(2,1)}, bf16[19968,128]{1,0:T(8,128)(2,1)}, u32[]{:S(2)}, u32[]{:S(2)}) collective-permute-start(bf16[19968,128]{1,0:T(8,128)(2,1)} %get-tuple-element.139), channel_id=1, source_target_pairs={{0,1},{1,0},{2,3},{3,2},{4,5},{5,4},{6,7},{7,6},{8,9},{9,8},{10,11... | collective-permute-start | bytes 15335432 | tf_op jit(solution)/shard_map/ppermute | solution.py:341
  224.6 16.0 %copy-start.35 = (bf16[768,3072]{1,0:T(8,128)(2,1)}, bf16[768,3072]{1,0:T(8,128)(2,1)S(1)}, u32[]{:S(2)}) copy-start(bf16[768,3072]{1,0:T(8,128)(2,1)S(1)} %bitcast_convert_fusion.refs_0_) | copy-start | bytes 14155780
  231.8 31.2 %collective-permute-start.3 = (bf16[1,4992,128]{2,1,0:T(8,128)(2,1)}, bf16[1,4992,128]{2,1,0:T(8,128)(2,1)}, u32[]{:S(2)}, u32[]{:S(2)}) collective-permute-start(bf16[1,4992,128]{2,1,0:T(8,128)(2,1)} %constant_dynamic-slice_fusion.6), channel_id=1, source_target_pairs={{0,4},{4,0},{2,6},{6,2},{8,12},{12,8},{10,14},{14,10},{16,20},{20,... | collective-permute-start | bytes 3833864 | tf_op jit(solution)/shard_map/ppermute | solution.py:317
  234.9 32.6 %copy-start.20 = (f32[6,66,768]{2,1,0:T(8,128)}, f32[6,66,768]{2,1,0:T(8,128)S(1)}, u32[]{:S(2)}) copy-start(f32[6,66,768]{2,1,0:T(8,128)S(1)} %add_add_fusion.9) | copy-start | bytes 3649540
  236.1 30.0 %collective-permute-start.2 = (bf16[1,4992,128]{2,1,0:T(8,128)(2,1)}, bf16[1,4992,128]{2,1,0:T(8,128)(2,1)S(1)}, u32[]{:S(2)}, u32[]{:S(2)}) collective-permute-start(bf16[1,4992,128]{2,1,0:T(8,128)(2,1)} %constant_dynamic-slice_fusion.7), channel_id=1, source_target_pairs={{0,2},{2,0},{4,6},{6,4},{8,10},{10,8},{12,14},{14,12},{16,18},{18,... | collective-permute-start | bytes 3833864 | tf_op jit(solution)/shard_map/ppermute | solution.py:317
  249.6 16.5 %copy-start.26 = (bf16[9984,128]{1,0:T(8,128)(2,1)S(1)}, bf16[9984,128]{1,0:T(8,128)(2,1)}, u32[]{:S(2)}) copy-start(bf16[9984,128]{1,0:T(8,128)(2,1)} %copy-done.25) | copy-start | bytes 7667716
  268.3 7.1 %copy-start.19 = (f32[6,12,66,66]{2,3,1,0:T(8,128)S(1)}, f32[6,12,66,66]{2,3,1,0:T(8,128)}, u32[]{:S(2)}) copy-start(f32[6,12,66,66]{2,3,1,0:T(8,128)} %copy-done.18) | copy-start | bytes 3763588
  272.9 15.5 %collective-permute-start.4 = (bf16[1,2496,128]{2,1,0:T(8,128)(2,1)}, bf16[1,2496,128]{2,1,0:T(8,128)(2,1)}, u32[]{:S(2)}, u32[]{:S(2)}) collective-permute-start(bf16[1,2496,128]{2,1,0:T(8,128)(2,1)} %constant_dynamic-slice_fusion.5), channel_id=1, source_target_pairs={{0,4},{4,0},{2,6},{6,2},{8,12},{12,8},{10,14},{14,10},{16,20},{20,... | collective-permute-start | bytes 1916936 | tf_op jit(solution)/shard_map/ppermute | solution.py:317
  274.1 16.6 %collective-permute-start.5 = (bf16[1,2496,128]{2,1,0:T(8,128)(2,1)S(1)}, bf16[1,2496,128]{2,1,0:T(8,128)(2,1)}, u32[]{:S(2)}, u32[]{:S(2)}) collective-permute-start(bf16[1,2496,128]{2,1,0:T(8,128)(2,1)S(1)} %constant_dynamic-slice_fusion.4), channel_id=1, source_target_pairs={{0,2},{2,0},{4,6},{6,4},{8,10},{10,8},{12,14},{14,12},{16,18},{18,... | collective-permute-start | bytes 1916936 | tf_op jit(solution)/shard_map/ppermute | solution.py:317
  282.5 10.6 %copy-start.24 = (bf16[6,66,768]{1,2,0:T(8,128)(2,1)S(1)}, bf16[6,66,768]{1,2,0:T(8,128)(2,1)}, u32[]{:S(2)}) copy-start(bf16[6,66,768]{1,2,0:T(8,128)(2,1)} %copy.133) | copy-start | bytes 1824772
  282.5 10.6 %copy-start.32 = (bf16[6,12,66,66]{2,3,1,0:T(8,128)(2,1)S(1)}, bf16[6,12,66,66]{2,3,1,0:T(8,128)(2,1)}, u32[]{:S(2)}) copy-start(bf16[6,12,66,66]{2,3,1,0:T(8,128)(2,1)} %multiply_convert_fusion.4) | copy-start | bytes 1881796
  301.1 34.7 %all-to-all-start = ((bf16[4,1248,128]{2,1,0:T(8,128)(2,1)}), bf16[4,1248,128]{2,1,0:T(8,128)(2,1)S(1)}, u32[]{:S(2)}, u32[]{:S(2)}) async-start(bf16[4,1248,128]{2,1,0:T(8,128)(2,1)} %pad_maximum_fusion.3), calls=%async_computation | async-start | bytes 2555904 | tf_op jit(solution)/shard_map/all_to_all | solution.py:320
  336.1 9.9 %collective-permute-start.6 = (bf16[19968,128]{1,0:T(8,128)(2,1)}, bf16[19968,128]{1,0:T(8,128)(2,1)}, u32[]{:S(2)}, u32[]{:S(2)}) collective-permute-start(bf16[19968,128]{1,0:T(8,128)(2,1)} %get-tuple-element.154), channel_id=1, source_target_pairs={{0,1},{1,0},{2,3},{3,2},{4,5},{5,4},{6,7},{7,6},{8,9},{9,8},{10,11... | collective-permute-start | bytes 15335432 | tf_op jit(solution)/shard_map/ppermute | solution.py:341
  338.8 35.1 %all-to-all-start.1 = ((bf16[4,1,1248,128]{3,2,1,0:T(8,128)(2,1)}), bf16[4,1,1248,128]{3,2,1,0:T(8,128)(2,1)}, u32[]{:S(2)}, u32[]{:S(2)}) async-start(bf16[4,1,1248,128]{3,2,1,0:T(8,128)(2,1)} %broadcast_in_dim.43), calls=%async_computation.1 | async-start | bytes 2555904 | tf_op jit(solution)/shard_map/all_to_all | solution.py:320
  352.5 29.6 %collective-permute-start.8 = (bf16[1,4992,128]{2,1,0:T(8,128)(2,1)}, bf16[1,4992,128]{2,1,0:T(8,128)(2,1)}, u32[]{:S(2)}, u32[]{:S(2)}) collective-permute-start(bf16[1,4992,128]{2,1,0:T(8,128)(2,1)} %constant_dynamic-slice_fusion.2), channel_id=1, source_target_pairs={{0,4},{4,0},{2,6},{6,2},{8,12},{12,8},{10,14},{14,10},{16,20},{20,... | collective-permute-start | bytes 3833864 | tf_op jit(solution)/shard_map/ppermute | solution.py:317
  358.4 29.3 %collective-permute-start.7 = (bf16[1,4992,128]{2,1,0:T(8,128)(2,1)}, bf16[1,4992,128]{2,1,0:T(8,128)(2,1)}, u32[]{:S(2)}, u32[]{:S(2)}) collective-permute-start(bf16[1,4992,128]{2,1,0:T(8,128)(2,1)} %constant_dynamic-slice_fusion.3), channel_id=1, source_target_pairs={{0,2},{2,0},{4,6},{6,4},{8,10},{10,8},{12,14},{14,12},{16,18},{18,... | collective-permute-start | bytes 3833864 | tf_op jit(solution)/shard_map/ppermute | solution.py:317
  373.8 8.2 %copy-start.29 = (bf16[9984,128]{1,0:T(8,128)(2,1)S(1)}, bf16[9984,128]{1,0:T(8,128)(2,1)}, u32[]{:S(2)}) copy-start(bf16[9984,128]{1,0:T(8,128)(2,1)} %copy-done.28) | copy-start | bytes 7667716
  389.4 14.5 %collective-permute-start.10 = (bf16[1,2496,128]{2,1,0:T(8,128)(2,1)S(1)}, bf16[1,2496,128]{2,1,0:T(8,128)(2,1)S(1)}, u32[]{:S(2)}, u32[]{:S(2)}) collective-permute-start(bf16[1,2496,128]{2,1,0:T(8,128)(2,1)S(1)} %constant_dynamic-slice_fusion), channel_id=1, source_target_pairs={{0,2},{2,0},{4,6},{6,4},{8,10},{10,8},{12,14},{14,12},{16,18},{18,... | collective-permute-start | bytes 1916936 | tf_op jit(solution)/shard_map/ppermute | solution.py:317
  390.8 14.2 %collective-permute-start.9 = (bf16[1,2496,128]{2,1,0:T(8,128)(2,1)S(1)}, bf16[1,2496,128]{2,1,0:T(8,128)(2,1)S(1)}, u32[]{:S(2)}, u32[]{:S(2)}) collective-permute-start(bf16[1,2496,128]{2,1,0:T(8,128)(2,1)S(1)} %constant_dynamic-slice_fusion.1), channel_id=1, source_target_pairs={{0,4},{4,0},{2,6},{6,2},{8,12},{12,8},{10,14},{14,10},{16,20},{20,... | collective-permute-start | bytes 1916936 | tf_op jit(solution)/shard_map/ppermute | solution.py:317
  405.2 14.2 %collective-permute-start.11 = (bf16[1,2496,128]{2,1,0:T(8,128)(2,1)}, bf16[1,2496,128]{2,1,0:T(8,128)(2,1)}, u32[]{:S(2)}, u32[]{:S(2)}) collective-permute-start(bf16[1,2496,128]{2,1,0:T(8,128)(2,1)} %bitcast.70), channel_id=1, source_target_pairs={{0,4},{4,0},{2,6},{6,2},{8,12},{12,8},{10,14},{14,10},{16,20},{20,... | collective-permute-start | bytes 1916936 | tf_op jit(solution)/shard_map/ppermute | solution.py:317
  408.1 34.8 %all-to-all-start.2 = ((bf16[4,1248,128]{2,1,0:T(8,128)(2,1)}), bf16[4,1248,128]{2,1,0:T(8,128)(2,1)}, u32[]{:S(2)}, u32[]{:S(2)}) async-start(bf16[4,1248,128]{2,1,0:T(8,128)(2,1)} %pad_maximum_fusion.4), calls=%async_computation.2 | async-start | bytes 2555904 | tf_op jit(solution)/shard_map/all_to_all | solution.py:320
  412.6 13.5 %collective-permute-start.12 = (bf16[1,2496,128]{2,1,0:T(8,128)(2,1)S(1)}, bf16[1,2496,128]{2,1,0:T(8,128)(2,1)S(1)}, u32[]{:S(2)}, u32[]{:S(2)}) collective-permute-start(bf16[1,2496,128]{2,1,0:T(8,128)(2,1)S(1)} %bitcast.271), channel_id=1, source_target_pairs={{0,2},{2,0},{4,6},{6,4},{8,10},{10,8},{12,14},{14,12},{16,18},{18,... | collective-permute-start | bytes 1916936 | tf_op jit(solution)/shard_map/ppermute | solution.py:317
  420.8 29.2 %copy-start.33 = (bf16[2,2496,128]{2,1,0:T(8,128)(2,1)}, bf16[2,2496,128]{2,1,0:T(8,128)(2,1)S(1)}, u32[]{:S(2)}) copy-start(bf16[2,2496,128]{2,1,0:T(8,128)(2,1)S(1)} %pad_maximum_fusion.5) | copy-start | bytes 3833860
  426.3 24.2 %copy-start.34 = (bf16[2,2496,128]{2,1,0:T(8,128)(2,1)}, bf16[2,2496,128]{2,1,0:T(8,128)(2,1)S(1)}, u32[]{:S(2)}) copy-start(bf16[2,2496,128]{2,1,0:T(8,128)(2,1)S(1)} %pad_maximum_fusion.6) | copy-start | bytes 3833860
  445.7 34.6 %all-to-all-start.3 = ((bf16[4,1,1248,128]{3,2,1,0:T(8,128)(2,1)}), bf16[4,1,1248,128]{3,2,1,0:T(8,128)(2,1)}, u32[]{:S(2)}, u32[]{:S(2)}) async-start(bf16[4,1,1248,128]{3,2,1,0:T(8,128)(2,1)} %broadcast_in_dim.44), calls=%async_computation.3 | async-start | bytes 2555904 | tf_op jit(solution)/shard_map/all_to_all | solution.py:320
  450.0 32.4 %collective-permute-start.13 = (bf16[4992,128]{1,0:T(8,128)(2,1)S(1)}, bf16[4992,128]{1,0:T(8,128)(2,1)}, u32[]{:S(2)}, u32[]{:S(2)}) collective-permute-start(bf16[4992,128]{1,0:T(8,128)(2,1)S(1)} %bitcast.247), channel_id=1, source_target_pairs={{0,2},{2,0},{4,6},{6,4},{8,10},{10,8},{12,14},{14,12},{16,18},{18,... | collective-permute-start | bytes 3833864 | tf_op jit(solution)/shard_map/ppermute | solution.py:317
  450.5 32.0 %collective-permute-start.14 = (bf16[4992,128]{1,0:T(8,128)(2,1)S(1)}, bf16[4992,128]{1,0:T(8,128)(2,1)}, u32[]{:S(2)}, u32[]{:S(2)}) collective-permute-start(bf16[4992,128]{1,0:T(8,128)(2,1)S(1)} %bitcast.249), channel_id=1, source_target_pairs={{0,4},{4,0},{2,6},{6,2},{8,12},{12,8},{10,14},{14,10},{16,20},{20,... | collective-permute-start | bytes 3833864 | tf_op jit(solution)/shard_map/ppermute | solution.py:317
  487.4 25.6 %collective-permute-start.21 = (bf16[19968,128]{1,0:T(8,128)(2,1)}, bf16[19968,128]{1,0:T(8,128)(2,1)}, u32[]{:S(2)}, u32[]{:S(2)}) collective-permute-start(bf16[19968,128]{1,0:T(8,128)(2,1)} %join.1.high1), channel_id=1, source_target_pairs={{0,1},{2,3},{4,5},{6,7},{8,9},{10,11},{12,13},{14,15},{16,17},{18,... | collective-permute-start | bytes 15335432 | tf_op jit(solution)/shard_map/ppermute | solution.py:531
  488.7 12.3 %collective-permute-start.17 = (bf16[1,2496,128]{2,1,0:T(8,128)(2,1)S(1)}, bf16[1,2496,128]{2,1,0:T(8,128)(2,1)S(1)}, u32[]{:S(2)}, u32[]{:S(2)}) collective-permute-start(bf16[1,2496,128]{2,1,0:T(8,128)(2,1)S(1)} %bitcast.275), channel_id=1, source_target_pairs={{0,2},{2,0},{4,6},{6,4},{8,10},{10,8},{12,14},{14,12},{16,18},{18,... | collective-permute-start | bytes 1916936 | tf_op jit(solution)/shard_map/ppermute | solution.py:317
  489.1 19.6 %collective-permute-start.15 = (bf16[1,2496,128]{2,1,0:T(8,128)(2,1)S(1)}, bf16[1,2496,128]{2,1,0:T(8,128)(2,1)S(1)}, u32[]{:S(2)}, u32[]{:S(2)}) collective-permute-start(bf16[1,2496,128]{2,1,0:T(8,128)(2,1)S(1)} %bitcast.273), channel_id=1, source_target_pairs={{0,4},{4,0},{2,6},{6,2},{8,12},{12,8},{10,14},{14,10},{16,20},{20,... | collective-permute-start | bytes 1916936 | tf_op jit(solution)/shard_map/ppermute | solution.py:317
  501.2 10.5 %collective-permute-start.20 = (bf16[4992,128]{1,0:T(8,128)(2,1)S(1)}, bf16[4992,128]{1,0:T(8,128)(2,1)}, u32[]{:S(2)}, u32[]{:S(2)}) collective-permute-start(bf16[4992,128]{1,0:T(8,128)(2,1)S(1)} %bitcast.219), channel_id=1, source_target_pairs={{1,0},{3,2},{5,4},{7,6},{9,8},{11,10},{13,12},{15,14},{17,16},{19,... | collective-permute-start | bytes 3833864 | tf_op jit(solution)/shard_map/ppermute | solution.py:531
  508.9 4.0 collective-permute-start.19
  511.3 29.1 %collective-permute-start.18 = (bf16[4992,128]{1,0:T(8,128)(2,1)S(1)}, bf16[4992,128]{1,0:T(8,128)(2,1)}, u32[]{:S(2)}, u32[]{:S(2)}) collective-permute-start(bf16[4992,128]{1,0:T(8,128)(2,1)S(1)} %bitcast.220), channel_id=1, source_target_pairs={{0,4},{4,0},{2,6},{6,2},{8,12},{12,8},{10,14},{14,10},{16,20},{20,... | collective-permute-start | bytes 3833864 | tf_op jit(solution)/shard_map/ppermute | solution.py:317
  511.3 29.1 %collective-permute-start.16 = (bf16[4992,128]{1,0:T(8,128)(2,1)S(1)}, bf16[4992,128]{1,0:T(8,128)(2,1)}, u32[]{:S(2)}, u32[]{:S(2)}) collective-permute-start(bf16[4992,128]{1,0:T(8,128)(2,1)S(1)} %bitcast.223), channel_id=1, source_target_pairs={{0,2},{2,0},{4,6},{6,4},{8,10},{10,8},{12,14},{14,12},{16,18},{18,... | collective-permute-start | bytes 3833864 | tf_op jit(solution)/shard_map/ppermute | solution.py:317
  540.4 4.1 collective-permute-start.22
  541.8 4.6 collective-permute-start.23
  550.0 28.0 %copy-start.1 = (bf16[6,256,768]{2,1,0:T(8,128)(2,1)S(1)}, bf16[6,256,768]{2,1,0:T(8,128)(2,1)}, u32[]{:S(2)}) copy-start(bf16[6,256,768]{2,1,0:T(8,128)(2,1)} %param.9) | copy-start | bytes 7077892
  (87 other events, 277.8 us)

commit v8 on v7

--- a/solution.py
+++ b/solution.py
@@ -844,10 +844,9 @@
         high = gather_second(high)
         low = scatter_last(low)
         low, high = tie((low, high))
-        high = gather_last(high)
+        high = joined(gather_last(high))
         low = gather_first(low)
         low, high = tie((low, high))
-        high = joined(high)
         high = (to_owner(high, 0), high)
         low = gather_second(low)
         early = (*low, *[to_owner(v, 1) for v in low])

time: 589 us -> 585 us (level)
    all_to_all x4, waiting for transfers between devices: 69.1 us -> 38.3 us  [exchange(): return lax.all_to_all(value, 'wide', 0, 0, axis_index_groups=self.groups)]
    ppermute x16, waiting for transfers between devices: 65.3 us -> 92.4 us  [swap(): return lax.ppermute(value, 'wide', pairs)]
  transfers between devices with their start and end apart: 28 -> 28, of which waited for: 18 -> 18; matrix products, arithmetic and copies ran while one was open for 12% -> 12% of each run, Pallas kernels for 7% -> 8%
where the time goes in v8:
time: 585 us; the launch traced here: 575 us
  waiting for transfers between devices  147 us (25%)
  matrix products  136 us (23%)
  Pallas kernels  110 us (19%)
  local copies, waits for them, and re-layouts  68.2 us (12%)
  other arithmetic  62.5 us (11%)
  starting transfers between devices  48.1 us (8%)
    ppermute x16, waiting for transfers between devices, swap(): return lax.ppermute(value, 'wide', pairs)  92.4 us
    pallas_call x2, Pallas kernels, adam_rows(): pl.pallas_call(kernel, out_shape=[jax.ShapeDtypeStruct(moment1.shape, jnp...  55.5 us
    all_to_all x4, waiting for transfers between devices, exchange(): return lax.all_to_all(value, 'wide', 0, 0, axis_index_groups=self.groups)  38.3 us
    pallas_call x4, Pallas kernels, pack_part(): pl.pallas_call(kernel, out_shape=[jax.ShapeDtypeStruct((middle - first, 1...  32.1 us
    dot_general x2, matrix products, block_forward(): jnp.einsum('ctd,df->ctf', second_in, weights_map[prefix + 'u'], preferred...  28.1 us
    convert_element_type x10, other arithmetic, added(): (first.astype(jnp.float32) + second.astype(jnp.float32)).astype(jnp.bfloa...  22.9 us
    pallas_call x1, Pallas kernels, unpack(): pl.pallas_call(kernel, out_shape=out_shape, in_specs=[pl.BlockSpec(memory...  18.1 us
    all_to_all x4, starting transfers between devices, exchange(): return lax.all_to_all(value, 'wide', 0, 0, axis_index_groups=self.groups)  16.9 us
  transfers between devices with their start and end apart: 28, of which 18 were waited for; matrix products, arithmetic and copies ran while one was open for 12% of the time, Pallas kernels for 8%

profile of v8, /device:TPU:1, one launch (start us, length us, event | category | flops | bytes accessed | tf_op | source)
XLA Modules:
  0.0 574.7 jit_solution(8987957532297089238)
XLA Ops:
  0.7 7.7 %convert_element_type.319.refs_0_ = bf16[39552,128]{1,0:T(8,128)(2,1)S(1)} convert(f32[39552,128]{1,0:T(8,128)} %param.14) | non-fusion elementwise | flops 5062656 | bytes 30375936 | tf_op jit(solution)/shard_map/convert_element_type | solution.py:535
  14.2 10.1 %collective-permute-done.refs_1_ = bf16[39552,128]{1,0:T(8,128)(2,1)} collective-permute-done((bf16[39552,128]{1,0:T(8,128)(2,1)S(1)}, bf16[39552,128]{1,0:T(8,128)(2,1)}, u32[]{:S(2)}, u32[]{:S(2)}) %collective-permute-start) | collective-permute-done | bytes 10125344 | tf_op jit(solution)/shard_map/ppermute | solution.py:341
  24.3 18.1 %unpack.1 = (f32[1,768]{1,0:T(1,128)}, f32[1,768]{1,0:T(1,128)}, f32[1,768]{1,0:T(1,128)}, bf16[768,2304]{1,0:T(8,128)(2,1)}, bf16[768,768]{1,0:T(8,128)(2,1)}, ...) custom-call(bf16[39552,128]{1,0:T(8,128)(2,1)} %copy-done.13, ...), custom_call_target="tpu_custom_call" | custom-call | tf_op jit(solution)/shard_map/unpack/pallas_call | solution.py:171
  49.5 4.0 convolution_convert_fusion
  56.4 2.6 copy.133
  67.9 9.4 %fusion.14 = (bf16[6,66,3072]{2,1,0:T(8,128)(2,1)}, bf16[6,66,3072]{2,1,0:T(8,128)(2,1)S(1)}) fusion(f32[3072]{0:T(1024)S(1)} %bitcast.317, bf16[768,3072]{1,0:T(8,128)(2,1)S(1)} %bitcast.312, f32[6,66,768]{2,1,0:T(8,128)S(1)} %get-tuple-element.243, f32[768]{0:T(1024)S(1)} %reduce.8, f32[768]{0:T(1024)S(1)} %reduce.7, f32[6,66]{1,0:T(8,128)S(1)} %fusion.92, ...), kind=kOutput, calls=%fused_computation.31 | convolution fusion | flops 1911444480 | bytes 10822752 | tf_op jit(solution)/shard_map/ctd,df->ctf/dot_general | solution.py:630
  77.4 2.3 fusion.17
  88.9 2.3 copy.94
  91.2 2.3 copy.93
  93.5 2.3 copy.92
  95.8 2.4 multiply_reduce_fusion.1
  104.8 18.7 %fusion.6 = (bf16[6,256,2048]{2,1,0:T(8,128)(2,1)S(1)}, bf16[6,256,2048]{2,1,0:T(8,128)(2,1)}) fusion(f32[2048]{0:T(1024)S(1)} %bitcast.318, bf16[512,2048]{1,0:T(8,128)(2,1)S(1)} %copy-done.98, f32[6,256,512]{2,1,0:T(8,128)S(1)} %get-tuple-element.249, f32[512]{0:T(512)S(1)} %bitcast.322, f32[512]{0:T(512)S(1)} %bitcast.296, f32[6,256]{1,0:T(8,128)S(1)} %fusion.90, ...), kind=kOutput, calls=%fused_computation.8 | convolution fusion | flops 3332112384 | bytes 17850368 | tf_op jit(solution)/shard_map/ctd,df->ctf/dot_general | solution.py:630
  123.6 4.3 convert_reduce_fusion
  127.8 4.7 fusion.107
  132.5 4.0 bitcast_convert_fusion.4.refs_0_
  138.7 4.8 bitcast_convert_fusion.3.refs_2_
  144.1 6.2 %convert_add_fusion = (f32[6,256,512]{2,1,0:T(8,128)}, bf16[6,256,512]{2,1,0:T(8,128)(2,1)}, f32[512]{0:T(512)}) fusion(bf16[6,256,512]{2,1,0:T(8,128)(2,1)S(1)} %copy-done.99, f32[6,256]{1,0:T(8,128)S(1)} %negate_multiply_fusion.1, f32[6,256]{1,0:T(8,128)S(1)} %multiply_multiply_fusion.3, f32[6,256,512]{2,1,0:T(8,128)S(1)} %get-tuple-element.249, ...), kind=kOutput, calls=%fused_computation.51 | convolution fusion | flops 3231448576 | bytes 21002240 | tf_op jit(solution)/shard_map/ctf,fd->ctd/dot_general | solution.py:636
  150.3 7.9 %pack62592.1 = (bf16[19968,128]{1,0:T(8,128)(2,1)}, bf16[19968,128]{1,0:T(8,128)(2,1)}) custom-call(bf16[512,2048]{1,0:T(8,128)(2,1)} %copy-done.47, f32[1,2048]{1,0:T(1,128)} %bitcast.291, bf16[2048,512]{1,0:T(8,128)(2,1)} %bitcast_convert_fusion.3.refs_2_, f32[1,512]{1,0:T(1,128)} %bitcast.306), custom_call_target="tpu_custom_call" | custom-call | tf_op jit(solution)/shard_map/pack62592/pallas_call | solution.py:273
  158.3 3.4 fusion.57.refs_10_
  171.8 2.4 copy.104
  174.2 2.3 copy.102
  178.9 4.4 bitcast_convert_fusion.6.refs_9_
  183.3 2.8 multiply_reduce_fusion.3
  196.7 4.3 bitcast_convert_fusion.1.refs_0_
  202.7 9.0 %pack39552.1 = (bf16[19968,128]{1,0:T(8,128)(2,1)}, bf16[19968,128]{1,0:T(8,128)(2,1)}) custom-call(bf16[3072,768]{1,0:T(8,128)(2,1)} %bitcast_convert_fusion.1.refs_0_, f32[1,768]{1,0:T(1,128)} %reshape.407.refs_1_, f32[1,768]{1,0:T(1,128)} %reshape.408.refs_2_, f32[1,768]{1,0:T(1,128)} %reshape.409.refs_3_, ...), custom_call_target="tpu_custom_call", output_to_operand_aliasing={{0}: (15, {}), {1}: (16, {})} | custom-call | tf_op jit(solution)/shard_map/pack39552/pallas_call | solution.py:273
  212.0 6.2 %convert_reduce_fusion.1 = (f32[3072]{0:T(1024)}, bf16[6,66,3072]{2,1,0:T(8,128)(2,1)S(1)}) fusion(bf16[6,66,3072]{2,1,0:T(8,128)(2,1)} %get-tuple-element.132, bf16[3072,768]{1,0:T(8,128)(2,1)} %get-tuple-element.104, f32[6,66,768]{2,1,0:T(8,128)S(1)} %get-tuple-element.131), kind=kOutput, calls=%fused_computation.32 | convolution fusion | flops 1874946048 | bytes 10813440 | tf_op jit(solution)/shard_map/ctd,fd->ctf/dot_general | solution.py:669
  218.2 2.5 fusion.108
  221.5 3.2 bitcast_convert_fusion.refs_0_
  224.7 5.2 add_convert_fusion.1
  231.8 2.6 collective-permute-start.3
  241.2 8.3 %pack18560.1 = (bf16[19968,128]{1,0:T(8,128)(2,1)}, bf16[19968,128]{1,0:T(8,128)(2,1)}) custom-call(bf16[768,3072]{1,0:T(8,128)(2,1)} %copy-done.35, f32[1,3072]{1,0:T(1,128)} %bitcast.290, bf16[512,768]{1,0:T(8,128)(2,1)} %slice.73.refs_2_), custom_call_target="tpu_custom_call" | custom-call | tf_op jit(solution)/shard_map/pack18560/pallas_call | solution.py:273
  249.6 13.4 %collective-permute-done.3 = bf16[1,4992,128]{2,1,0:T(8,128)(2,1)} collective-permute-done((bf16[1,4992,128]{2,1,0:T(8,128)(2,1)}, bf16[1,4992,128]{2,1,0:T(8,128)(2,1)}, u32[]{:S(2)}, u32[]{:S(2)}) %collective-permute-start.3) | collective-permute-done | bytes 1277984 | tf_op jit(solution)/shard_map/ppermute | solution.py:317
  263.0 3.1 add_convert_fusion.7
  277.2 5.3 multiply_convert_fusion.4
  282.5 5.9 %collective-permute-done.4 = bf16[1,2496,128]{2,1,0:T(8,128)(2,1)} collective-permute-done((bf16[1,2496,128]{2,1,0:T(8,128)(2,1)}, bf16[1,2496,128]{2,1,0:T(8,128)(2,1)}, u32[]{:S(2)}, u32[]{:S(2)}) %collective-permute-start.4) | collective-permute-done | bytes 639008 | tf_op jit(solution)/shard_map/ppermute | solution.py:317
  288.4 2.3 add_convert_fusion.14
  290.7 2.4 add_convert_fusion.13
  298.7 2.3 pad_maximum_fusion.3
  301.1 4.5 all-to-all-start
  305.6 4.4 fusion.109
  316.3 4.0 bitcast_convert_fusion.2.refs_3_
  320.3 6.8 %pack0.1 = (bf16[19968,128]{1,0:T(8,128)(2,1)}, bf16[19968,128]{1,0:T(8,128)(2,1)}) custom-call(f32[1,768]{1,0:T(1,128)} %reshape.424.refs_0_, f32[1,768]{1,0:T(1,128)} %reshape.425.refs_1_, f32[1,768]{1,0:T(1,128)} %reshape.426.refs_2_, bf16[768,2304]{1,0:T(8,128)(2,1)} %bitcast_convert_fusion.2.refs_3_, ...), custom_call_target="tpu_custom_call", output_to_operand_aliasing={{0}: (9, {}), {1}: (10, {})} | custom-call | tf_op jit(solution)/shard_map/pack0/pallas_call | solution.py:273
  327.2 8.6 %all-to-all-done = bf16[4,1248,128]{2,1,0:T(8,128)(2,1)S(1)} async-done(((bf16[4,1248,128]{2,1,0:T(8,128)(2,1)}), bf16[4,1248,128]{2,1,0:T(8,128)(2,1)S(1)}, u32[]{:S(2)}, u32[]{:S(2)}) %all-to-all-start) | async-done | bytes 1277984 | tf_op jit(solution)/shard_map/all_to_all | solution.py:320
  338.8 4.3 all-to-all-start.1
  343.1 2.9 collective-permute-done.6
  346.0 5.0 add_convert_fusion
  353.8 3.6 convolution_convert_fusion.1
  359.7 14.2 %all-to-all-done.1 = bf16[4,1,1248,128]{3,2,1,0:T(8,128)(2,1)} async-done(((bf16[4,1,1248,128]{3,2,1,0:T(8,128)(2,1)}), bf16[4,1,1248,128]{3,2,1,0:T(8,128)(2,1)}, u32[]{:S(2)}, u32[]{:S(2)}) %all-to-all-start.1) | async-done | bytes 1277984 | tf_op jit(solution)/shard_map/all_to_all | solution.py:320
  373.8 2.3 fusion.119
  376.2 5.9 %collective-permute-done.8 = bf16[1,4992,128]{2,1,0:T(8,128)(2,1)} collective-permute-done((bf16[1,4992,128]{2,1,0:T(8,128)(2,1)}, bf16[1,4992,128]{2,1,0:T(8,128)(2,1)}, u32[]{:S(2)}, u32[]{:S(2)}) %collective-permute-start.8) | collective-permute-done | bytes 1277984 | tf_op jit(solution)/shard_map/ppermute | solution.py:317
  383.7 4.0 collective-permute-done.7
  392.3 11.7 %collective-permute-done.10 = bf16[1,2496,128]{2,1,0:T(8,128)(2,1)S(1)} collective-permute-done((bf16[1,2496,128]{2,1,0:T(8,128)(2,1)S(1)}, bf16[1,2496,128]{2,1,0:T(8,128)(2,1)S(1)}, u32[]{:S(2)}, u32[]{:S(2)}) %collective-permute-start.10) | collective-permute-done | bytes 639008 | tf_op jit(solution)/shard_map/ppermute | solution.py:317
  408.1 3.8 all-to-all-start.2
  412.3 7.1 %collective-permute-done.11 = bf16[1,2496,128]{2,1,0:T(8,128)(2,1)} collective-permute-done((bf16[1,2496,128]{2,1,0:T(8,128)(2,1)}, bf16[1,2496,128]{2,1,0:T(8,128)(2,1)}, u32[]{:S(2)}, u32[]{:S(2)}) %collective-permute-start.11) | collective-permute-done | bytes 639008 | tf_op jit(solution)/shard_map/ppermute | solution.py:317
  420.9 4.4 collective-permute-done.12
  426.5 15.6 %all-to-all-done.2 = bf16[4,1248,128]{2,1,0:T(8,128)(2,1)S(1)} async-done(((bf16[4,1248,128]{2,1,0:T(8,128)(2,1)}), bf16[4,1248,128]{2,1,0:T(8,128)(2,1)S(1)}, u32[]{:S(2)}, u32[]{:S(2)}) %all-to-all-start.2) | async-done | bytes 1277984 | tf_op jit(solution)/shard_map/all_to_all | solution.py:320
  443.6 4.3 all-to-all-start.3
  448.4 28.0 %collective-permute-done.13.other1 = bf16[4992,128]{1,0:T(8,128)(2,1)S(1)} collective-permute-done((bf16[4992,128]{1,0:T(8,128)(2,1)S(1)}, bf16[4992,128]{1,0:T(8,128)(2,1)S(1)}, u32[]{:S(2)}, u32[]{:S(2)}) %collective-permute-start.13) | collective-permute-done | bytes 1277984 | tf_op jit(solution)/shard_map/ppermute | solution.py:317
  477.4 4.8 join.1.high1
  485.3 11.2 %collective-permute-done.17 = bf16[1,2496,128]{2,1,0:T(8,128)(2,1)S(1)} collective-permute-done((bf16[1,2496,128]{2,1,0:T(8,128)(2,1)S(1)}, bf16[1,2496,128]{2,1,0:T(8,128)(2,1)S(1)}, u32[]{:S(2)}, u32[]{:S(2)}) %collective-permute-start.17) | collective-permute-done | bytes 639008 | tf_op jit(solution)/shard_map/ppermute | solution.py:317
  496.7 8.2 %collective-permute-start.20 = (bf16[4992,128]{1,0:T(8,128)(2,1)S(1)}, bf16[4992,128]{1,0:T(8,128)(2,1)}, u32[]{:S(2)}, u32[]{:S(2)}) collective-permute-start(bf16[4992,128]{1,0:T(8,128)(2,1)S(1)} %bitcast.219), channel_id=1, source_target_pairs={{1,0},{3,2},{5,4},{7,6},{9,8},{11,10},{13,12},{15,14},{17,16},{19,... | collective-permute-start | bytes 3833864 | tf_op jit(solution)/shard_map/ppermute | solution.py:531
  505.1 2.3 collective-permute-start.19
  509.2 27.5 %adam0.1 = (f32[39552,128]{1,0:T(8,128)}, f32[39552,128]{1,0:T(8,128)}, f32[39552,128]{1,0:T(8,128)}, f32[39552,128]{1,0:T(8,128)}, f32[8,128]{1,0:T(8,128)S(1)}) custom-call(s32[3]{0:T(128)S(1)} %pad_add_fusion.1.places, bf16[4992,128]{1,0:T(8,128)(2,1)S(1)} %bitcast.224, bf16[4992,128]{1,0:T(8,128)(2,1)S(1)} %bitcast.221, ...), custom_call_target="tpu_custom_call" | custom-call | flops 40894464 | bytes 66453504 | tf_op jit(solution)/shard_map/adam0/pallas_call | solution.py:511
  546.2 28.0 %adam1.1 = (f32[39552,128]{1,0:T(8,128)}, f32[39552,128]{1,0:T(8,128)}, f32[39552,128]{1,0:T(8,128)}, f32[39552,128]{1,0:T(8,128)}, f32[8,128]{1,0:T(8,128)}) custom-call(s32[3]{0:T(128)S(1)} %pad_add_fusion.places, bf16[4992,128]{1,0:T(8,128)(2,1)} %collective-permute-done.16.low0, ...), custom_call_target="tpu_custom_call", output_to_operand_aliasing={{0}: (9, {}), {1}: (10, {}), {2}: (11, {}), {3}: (12, {})} | custom-call | flops 40894464 | bytes 66453504 | tf_op jit(solution)/shard_map/adam1/pallas_call | solution.py:511
  (422 shorter events, 139.2 us)
Async XLA Ops:
  0.6 11.9 %copy-start = (bf16[6,256,768]{2,1,0:T(8,128)(2,1)S(1)}, bf16[6,256,768]{2,1,0:T(8,128)(2,1)}, u32[]{:S(2)}) copy-start(bf16[6,256,768]{2,1,0:T(8,128)(2,1)} %param.9) | copy-start | bytes 7077892
  0.7 7.9 %copy-start.108 = (s32[6]{0:T(128)S(1)}, s32[6]{0:T(128)}, u32[]{:S(2)}) copy-start(s32[6]{0:T(128)} %param.12) | copy-start | bytes 76
  0.7 7.9 %copy-start.88 = (bf16[6,768]{1,0:T(8,128)(2,1)S(1)}, bf16[6,768]{1,0:T(8,128)(2,1)}, u32[]{:S(2)}) copy-start(bf16[6,768]{1,0:T(8,128)(2,1)} %param.10) | copy-start | bytes 27652
  0.7 8.0 %copy-start.71 = (s32[6,64]{1,0:T(8,128)S(1)}, s32[6,64]{1,0:T(8,128)}, u32[]{:S(2)}) copy-start(s32[6,64]{1,0:T(8,128)} %param.11) | copy-start | bytes 4612
  8.4 15.8 %collective-permute-start = (bf16[39552,128]{1,0:T(8,128)(2,1)S(1)}, bf16[39552,128]{1,0:T(8,128)(2,1)}, u32[]{:S(2)}, u32[]{:S(2)}) collective-permute-start(bf16[39552,128]{1,0:T(8,128)(2,1)S(1)} %convert_element_type.319.refs_0_), channel_id=1, source_target_pairs={{0,1},{1,0},{2,3},{3,2},{4,5},{5,4},{6,7},{7,6},{8,9},{9,8},{10,11... | collective-permute-start | bytes 30375944 | tf_op jit(solution)/shard_map/ppermute | solution.py:341
  8.7 57.0 %copy-start.60 = (f32[6,1,768]{2,1,0:T(1,128)}, f32[6,1,768]{2,1,0:T(1,128)S(1)}, u32[]{:S(2)}) copy-start(f32[6,1,768]{2,1,0:T(1,128)S(1)} %broadcast_in_dim.32) | copy-start | bytes 55300
  14.2 34.6 %copy-start.11 = (f32[6,64,768]{2,1,0:T(8,128)S(1)}, f32[6,64,768]{2,1,0:T(8,128)}, u32[]{:S(2)}) copy-start(f32[6,64,768]{2,1,0:T(8,128)} %fusion.72) | copy-start | bytes 3538948
  43.8 9.7 %copy-start.86 = (f32[768]{0:T(1024)}, f32[768]{0:T(1024)S(1)}, u32[]{:S(2)}) copy-start(f32[768]{0:T(1024)S(1)} %reduce.4) | copy-start | bytes 9220
  44.5 23.3 %copy-start.78 = (f32[768]{0:T(1024)}, f32[768]{0:T(1024)S(1)}, u32[]{:S(2)}) copy-start(f32[768]{0:T(1024)S(1)} %reduce.7) | copy-start | bytes 9220
  45.9 7.6 %copy-start.89 = (f32[768]{0:T(1024)}, f32[768]{0:T(1024)S(1)}, u32[]{:S(2)}) copy-start(f32[768]{0:T(1024)S(1)} %reduce.5) | copy-start | bytes 9220
  46.6 21.2 %copy-start.91 = (f32[768]{0:T(1024)}, f32[768]{0:T(1024)S(1)}, u32[]{:S(2)}) copy-start(f32[768]{0:T(1024)S(1)} %reduce.8) | copy-start | bytes 9220
  48.8 16.9 %copy-start.62 = (f32[6,1,768]{2,1,0:T(1,128)}, f32[6,1,768]{2,1,0:T(1,128)S(1)}, u32[]{:S(2)}) copy-start(f32[6,1,768]{2,1,0:T(1,128)S(1)} %broadcast_in_dim.31) | copy-start | bytes 55300
  67.5 12.2 %copy-start.14 = (f32[6,66,768]{2,1,0:T(8,128)}, f32[6,66,768]{2,1,0:T(8,128)S(1)}, u32[]{:S(2)}) copy-start(f32[6,66,768]{2,1,0:T(8,128)S(1)} %get-tuple-element.243) | copy-start | bytes 3649540
  67.5 9.8 %copy-start.72 = (f32[6,66]{1,0:T(8,128)}, f32[6,66]{1,0:T(8,128)S(1)}, u32[]{:S(2)}) copy-start(f32[6,66]{1,0:T(8,128)S(1)} %broadcast_multiply_fusion.3) | copy-start | bytes 4756
  67.5 9.8 %slice-start.8 = ((s8[4718592]{0:T(1024)(128)(4,1)}), s8[4194304]{0:T(1024)(128)(4,1)S(1)}, s32[]{:S(2)}) async-start(s8[4718592]{0:T(1024)(128)(4,1)} %bitcast.315), calls=%async_computation.12 | async-start | bytes 8388608
  67.8 9.5 %copy-start.82 = (f32[6,66]{1,0:T(8,128)}, f32[6,66]{1,0:T(8,128)S(1)}, u32[]{:S(2)}) copy-start(f32[6,66]{1,0:T(8,128)S(1)} %multiply_reduce_fusion.15) | copy-start | bytes 4756
  67.8 9.5 %copy-start.76 = (f32[6,66]{1,0:T(8,128)}, f32[6,66]{1,0:T(8,128)S(1)}, u32[]{:S(2)}) copy-start(f32[6,66]{1,0:T(8,128)S(1)} %fusion.92) | copy-start | bytes 4756
  67.9 9.4 %slice-start.9 = ((s8[4718592]{0:T(1024)(128)(4,1)}), s8[524288]{0:T(1024)(128)(4,1)S(1)}, s32[]{:S(2)}) async-start(s8[4718592]{0:T(1024)(128)(4,1)} %bitcast.315), calls=%async_computation.13 | async-start | bytes 1048576
  83.8 18.5 %copy-start.7 = (f32[6,256,512]{2,1,0:T(8,128)}, f32[6,256,512]{2,1,0:T(8,128)S(1)}, u32[]{:S(2)}) copy-start(f32[6,256,512]{2,1,0:T(8,128)S(1)} %get-tuple-element.245) | copy-start | bytes 9437188
  104.8 18.7 %copy-start.97 = (bf16[2048,512]{1,0:T(8,128)(2,1)S(1)}, bf16[2048,512]{1,0:T(8,128)(2,1)}, u32[]{:S(2)}) copy-start(bf16[2048,512]{1,0:T(8,128)(2,1)} %get-tuple-element.121) | copy-start | bytes 6291460
  104.8 18.7 %copy-start.99 = (bf16[6,256,512]{2,1,0:T(8,128)(2,1)S(1)}, bf16[6,256,512]{2,1,0:T(8,128)(2,1)}, u32[]{:S(2)}) copy-start(bf16[6,256,512]{2,1,0:T(8,128)(2,1)} %param.13) | copy-start | bytes 4718596
  123.5 15.2 %slice-start.10 = ((s8[6291456]{0:T(1024)(128)(4,1)}), s8[2097152]{0:T(1024)(128)(4,1)S(1)}, s32[]{:S(2)}) async-start(s8[6291456]{0:T(1024)(128)(4,1)} %bitcast.325), calls=%async_computation.14 | async-start | bytes 4194304
  127.8 10.9 %slice-start.11 = ((s8[6291456]{0:T(1024)(128)(4,1)}), s8[4194304]{0:T(1024)(128)(4,1)S(1)}, s32[]{:S(2)}) async-start(s8[6291456]{0:T(1024)(128)(4,1)} %bitcast.325), calls=%async_computation.15 | async-start | bytes 8388608
  136.5 7.0 %copy-start.47 = (bf16[512,2048]{1,0:T(8,128)(2,1)}, bf16[512,2048]{1,0:T(8,128)(2,1)S(1)}, u32[]{:S(2)}) copy-start(bf16[512,2048]{1,0:T(8,128)(2,1)S(1)} %bitcast_convert_fusion.4.refs_0_) | copy-start | bytes 6291460
  150.3 7.9 %copy-start.43 = (bf16[6,4,64,256]{3,2,1,0:T(8,128)(2,1)S(1)}, bf16[6,4,64,256]{3,2,1,0:T(8,128)(2,1)}, u32[]{:S(2)}) copy-start(bf16[6,4,64,256]{3,2,1,0:T(8,128)(2,1)} %copy-done.42) | copy-start | bytes 2359300
  150.3 11.9 %slice-start = ((s8[6291456]{0:T(1024)(128)(4,1)}), s8[2097152]{0:T(1024)(128)(4,1)S(1)}, s32[]{:S(2)}) async-start(s8[6291456]{0:T(1024)(128)(4,1)} %bitcast.225), calls=%async_computation.4 | async-start | bytes 4194304
  171.8 7.1 %copy-start.8 = (f32[6,256,512]{2,1,0:T(8,128)S(1)}, f32[6,256,512]{2,1,0:T(8,128)}, u32[]{:S(2)}) copy-start(f32[6,256,512]{2,1,0:T(8,128)} %copy-done.7) | copy-start | bytes 9437188
  202.7 15.4 %slice-start.6 = ((s8[4718592]{0:T(1024)(128)(4,1)}), s8[524288]{0:T(1024)(128)(4,1)S(1)}, s32[]{:S(2)}) async-start(s8[4718592]{0:T(1024)(128)(4,1)} %bitcast.313), calls=%async_computation.10 | async-start | bytes 1048576
  211.8 12.9 %collective-permute-start.1 = (bf16[19968,128]{1,0:T(8,128)(2,1)}, bf16[19968,128]{1,0:T(8,128)(2,1)}, u32[]{:S(2)}, u32[]{:S(2)}) collective-permute-start(bf16[19968,128]{1,0:T(8,128)(2,1)} %get-tuple-element.136), channel_id=1, source_target_pairs={{0,1},{1,0},{2,3},{3,2},{4,5},{5,4},{6,7},{7,6},{8,9},{9,8},{10,11... | collective-permute-start | bytes 15335432 | tf_op jit(solution)/shard_map/ppermute | solution.py:341
  224.6 15.9 %copy-start.35 = (bf16[768,3072]{1,0:T(8,128)(2,1)}, bf16[768,3072]{1,0:T(8,128)(2,1)S(1)}, u32[]{:S(2)}) copy-start(bf16[768,3072]{1,0:T(8,128)(2,1)S(1)} %bitcast_convert_fusion.refs_0_) | copy-start | bytes 14155780
  231.8 31.2 %collective-permute-start.3 = (bf16[1,4992,128]{2,1,0:T(8,128)(2,1)}, bf16[1,4992,128]{2,1,0:T(8,128)(2,1)}, u32[]{:S(2)}, u32[]{:S(2)}) collective-permute-start(bf16[1,4992,128]{2,1,0:T(8,128)(2,1)} %constant_dynamic-slice_fusion.6), channel_id=1, source_target_pairs={{0,4},{4,0},{2,6},{6,2},{8,12},{12,8},{10,14},{14,10},{16,20},{20,... | collective-permute-start | bytes 3833864 | tf_op jit(solution)/shard_map/ppermute | solution.py:317
  234.9 32.6 %copy-start.20 = (f32[6,66,768]{2,1,0:T(8,128)}, f32[6,66,768]{2,1,0:T(8,128)S(1)}, u32[]{:S(2)}) copy-start(f32[6,66,768]{2,1,0:T(8,128)S(1)} %add_add_fusion.9) | copy-start | bytes 3649540
  236.1 30.0 %collective-permute-start.2 = (bf16[1,4992,128]{2,1,0:T(8,128)(2,1)}, bf16[1,4992,128]{2,1,0:T(8,128)(2,1)S(1)}, u32[]{:S(2)}, u32[]{:S(2)}) collective-permute-start(bf16[1,4992,128]{2,1,0:T(8,128)(2,1)} %constant_dynamic-slice_fusion.7), channel_id=1, source_target_pairs={{0,2},{2,0},{4,6},{6,4},{8,10},{10,8},{12,14},{14,12},{16,18},{18,... | collective-permute-start | bytes 3833864 | tf_op jit(solution)/shard_map/ppermute | solution.py:317
  249.6 16.5 %copy-start.26 = (bf16[9984,128]{1,0:T(8,128)(2,1)S(1)}, bf16[9984,128]{1,0:T(8,128)(2,1)}, u32[]{:S(2)}) copy-start(bf16[9984,128]{1,0:T(8,128)(2,1)} %copy-done.25) | copy-start | bytes 7667716
  268.3 7.1 %copy-start.19 = (f32[6,12,66,66]{2,3,1,0:T(8,128)S(1)}, f32[6,12,66,66]{2,3,1,0:T(8,128)}, u32[]{:S(2)}) copy-start(f32[6,12,66,66]{2,3,1,0:T(8,128)} %copy-done.18) | copy-start | bytes 3763588
  272.9 15.5 %collective-permute-start.4 = (bf16[1,2496,128]{2,1,0:T(8,128)(2,1)}, bf16[1,2496,128]{2,1,0:T(8,128)(2,1)}, u32[]{:S(2)}, u32[]{:S(2)}) collective-permute-start(bf16[1,2496,128]{2,1,0:T(8,128)(2,1)} %constant_dynamic-slice_fusion.5), channel_id=1, source_target_pairs={{0,4},{4,0},{2,6},{6,2},{8,12},{12,8},{10,14},{14,10},{16,20},{20,... | collective-permute-start | bytes 1916936 | tf_op jit(solution)/shard_map/ppermute | solution.py:317
  274.1 16.6 %collective-permute-start.5 = (bf16[1,2496,128]{2,1,0:T(8,128)(2,1)S(1)}, bf16[1,2496,128]{2,1,0:T(8,128)(2,1)}, u32[]{:S(2)}, u32[]{:S(2)}) collective-permute-start(bf16[1,2496,128]{2,1,0:T(8,128)(2,1)S(1)} %constant_dynamic-slice_fusion.4), channel_id=1, source_target_pairs={{0,2},{2,0},{4,6},{6,4},{8,10},{10,8},{12,14},{14,12},{16,18},{18,... | collective-permute-start | bytes 1916936 | tf_op jit(solution)/shard_map/ppermute | solution.py:317
  282.5 10.6 %copy-start.24 = (bf16[6,66,768]{1,2,0:T(8,128)(2,1)S(1)}, bf16[6,66,768]{1,2,0:T(8,128)(2,1)}, u32[]{:S(2)}) copy-start(bf16[6,66,768]{1,2,0:T(8,128)(2,1)} %copy.133) | copy-start | bytes 1824772
  282.5 10.6 %copy-start.32 = (bf16[6,12,66,66]{2,3,1,0:T(8,128)(2,1)S(1)}, bf16[6,12,66,66]{2,3,1,0:T(8,128)(2,1)}, u32[]{:S(2)}) copy-start(bf16[6,12,66,66]{2,3,1,0:T(8,128)(2,1)} %multiply_convert_fusion.4) | copy-start | bytes 1881796
  301.1 34.7 %all-to-all-start = ((bf16[4,1248,128]{2,1,0:T(8,128)(2,1)}), bf16[4,1248,128]{2,1,0:T(8,128)(2,1)S(1)}, u32[]{:S(2)}, u32[]{:S(2)}) async-start(bf16[4,1248,128]{2,1,0:T(8,128)(2,1)} %pad_maximum_fusion.3), calls=%async_computation | async-start | bytes 2555904 | tf_op jit(solution)/shard_map/all_to_all | solution.py:320
  336.1 9.9 %collective-permute-start.6 = (bf16[19968,128]{1,0:T(8,128)(2,1)}, bf16[19968,128]{1,0:T(8,128)(2,1)}, u32[]{:S(2)}, u32[]{:S(2)}) collective-permute-start(bf16[19968,128]{1,0:T(8,128)(2,1)} %get-tuple-element.151), channel_id=1, source_target_pairs={{0,1},{1,0},{2,3},{3,2},{4,5},{5,4},{6,7},{7,6},{8,9},{9,8},{10,11... | collective-permute-start | bytes 15335432 | tf_op jit(solution)/shard_map/ppermute | solution.py:341
  338.8 35.1 %all-to-all-start.1 = ((bf16[4,1,1248,128]{3,2,1,0:T(8,128)(2,1)}), bf16[4,1,1248,128]{3,2,1,0:T(8,128)(2,1)}, u32[]{:S(2)}, u32[]{:S(2)}) async-start(bf16[4,1,1248,128]{3,2,1,0:T(8,128)(2,1)} %broadcast_in_dim.43), calls=%async_computation.1 | async-start | bytes 2555904 | tf_op jit(solution)/shard_map/all_to_all | solution.py:320
  352.5 29.6 %collective-permute-start.8 = (bf16[1,4992,128]{2,1,0:T(8,128)(2,1)}, bf16[1,4992,128]{2,1,0:T(8,128)(2,1)}, u32[]{:S(2)}, u32[]{:S(2)}) collective-permute-start(bf16[1,4992,128]{2,1,0:T(8,128)(2,1)} %constant_dynamic-slice_fusion.2), channel_id=1, source_target_pairs={{0,4},{4,0},{2,6},{6,2},{8,12},{12,8},{10,14},{14,10},{16,20},{20,... | collective-permute-start | bytes 3833864 | tf_op jit(solution)/shard_map/ppermute | solution.py:317
  358.4 29.3 %collective-permute-start.7 = (bf16[1,4992,128]{2,1,0:T(8,128)(2,1)}, bf16[1,4992,128]{2,1,0:T(8,128)(2,1)}, u32[]{:S(2)}, u32[]{:S(2)}) collective-permute-start(bf16[1,4992,128]{2,1,0:T(8,128)(2,1)} %constant_dynamic-slice_fusion.3), channel_id=1, source_target_pairs={{0,2},{2,0},{4,6},{6,4},{8,10},{10,8},{12,14},{14,12},{16,18},{18,... | collective-permute-start | bytes 3833864 | tf_op jit(solution)/shard_map/ppermute | solution.py:317
  373.8 8.2 %copy-start.29 = (bf16[9984,128]{1,0:T(8,128)(2,1)S(1)}, bf16[9984,128]{1,0:T(8,128)(2,1)}, u32[]{:S(2)}) copy-start(bf16[9984,128]{1,0:T(8,128)(2,1)} %copy-done.28) | copy-start | bytes 7667716
  389.4 14.5 %collective-permute-start.10 = (bf16[1,2496,128]{2,1,0:T(8,128)(2,1)S(1)}, bf16[1,2496,128]{2,1,0:T(8,128)(2,1)S(1)}, u32[]{:S(2)}, u32[]{:S(2)}) collective-permute-start(bf16[1,2496,128]{2,1,0:T(8,128)(2,1)S(1)} %constant_dynamic-slice_fusion), channel_id=1, source_target_pairs={{0,2},{2,0},{4,6},{6,4},{8,10},{10,8},{12,14},{14,12},{16,18},{18,... | collective-permute-start | bytes 1916936 | tf_op jit(solution)/shard_map/ppermute | solution.py:317
  390.8 14.2 %collective-permute-start.9 = (bf16[1,2496,128]{2,1,0:T(8,128)(2,1)S(1)}, bf16[1,2496,128]{2,1,0:T(8,128)(2,1)S(1)}, u32[]{:S(2)}, u32[]{:S(2)}) collective-permute-start(bf16[1,2496,128]{2,1,0:T(8,128)(2,1)S(1)} %constant_dynamic-slice_fusion.1), channel_id=1, source_target_pairs={{0,4},{4,0},{2,6},{6,2},{8,12},{12,8},{10,14},{14,10},{16,20},{20,... | collective-permute-start | bytes 1916936 | tf_op jit(solution)/shard_map/ppermute | solution.py:317
  405.2 14.2 %collective-permute-start.11 = (bf16[1,2496,128]{2,1,0:T(8,128)(2,1)}, bf16[1,2496,128]{2,1,0:T(8,128)(2,1)}, u32[]{:S(2)}, u32[]{:S(2)}) collective-permute-start(bf16[1,2496,128]{2,1,0:T(8,128)(2,1)} %bitcast.70), channel_id=1, source_target_pairs={{0,4},{4,0},{2,6},{6,2},{8,12},{12,8},{10,14},{14,10},{16,20},{20,... | collective-permute-start | bytes 1916936 | tf_op jit(solution)/shard_map/ppermute | solution.py:317
  408.1 34.0 %all-to-all-start.2 = ((bf16[4,1248,128]{2,1,0:T(8,128)(2,1)}), bf16[4,1248,128]{2,1,0:T(8,128)(2,1)S(1)}, u32[]{:S(2)}, u32[]{:S(2)}) async-start(bf16[4,1248,128]{2,1,0:T(8,128)(2,1)} %pad_maximum_fusion.4), calls=%async_computation.2 | async-start | bytes 2555904 | tf_op jit(solution)/shard_map/all_to_all | solution.py:320
  411.9 13.4 %collective-permute-start.12 = (bf16[1,2496,128]{2,1,0:T(8,128)(2,1)S(1)}, bf16[1,2496,128]{2,1,0:T(8,128)(2,1)S(1)}, u32[]{:S(2)}, u32[]{:S(2)}) collective-permute-start(bf16[1,2496,128]{2,1,0:T(8,128)(2,1)S(1)} %bitcast.271), channel_id=1, source_target_pairs={{0,2},{2,0},{4,6},{6,4},{8,10},{10,8},{12,14},{14,12},{16,18},{18,... | collective-permute-start | bytes 1916936 | tf_op jit(solution)/shard_map/ppermute | solution.py:317
  420.8 27.1 %copy-start.33 = (bf16[2,2496,128]{2,1,0:T(8,128)(2,1)}, bf16[2,2496,128]{2,1,0:T(8,128)(2,1)S(1)}, u32[]{:S(2)}) copy-start(bf16[2,2496,128]{2,1,0:T(8,128)(2,1)S(1)} %pad_maximum_fusion.5) | copy-start | bytes 3833860
  443.6 38.6 %all-to-all-start.3 = ((bf16[4,1,1248,128]{3,2,1,0:T(8,128)(2,1)}), bf16[4,1,1248,128]{3,2,1,0:T(8,128)(2,1)}, u32[]{:S(2)}, u32[]{:S(2)}) async-start(bf16[4,1,1248,128]{3,2,1,0:T(8,128)(2,1)} %broadcast_in_dim.44), calls=%async_computation.3 | async-start | bytes 2555904 | tf_op jit(solution)/shard_map/all_to_all | solution.py:320
  447.9 28.4 %collective-permute-start.13 = (bf16[4992,128]{1,0:T(8,128)(2,1)S(1)}, bf16[4992,128]{1,0:T(8,128)(2,1)S(1)}, u32[]{:S(2)}, u32[]{:S(2)}) collective-permute-start(bf16[4992,128]{1,0:T(8,128)(2,1)S(1)} %bitcast.247), channel_id=1, source_target_pairs={{0,2},{2,0},{4,6},{6,4},{8,10},{10,8},{12,14},{14,12},{16,18},{18,... | collective-permute-start | bytes 3833864 | tf_op jit(solution)/shard_map/ppermute | solution.py:317
  448.3 29.0 %collective-permute-start.14 = (bf16[4992,128]{1,0:T(8,128)(2,1)S(1)}, bf16[4992,128]{1,0:T(8,128)(2,1)}, u32[]{:S(2)}, u32[]{:S(2)}) collective-permute-start(bf16[4992,128]{1,0:T(8,128)(2,1)S(1)} %bitcast.250), channel_id=1, source_target_pairs={{0,4},{4,0},{2,6},{6,2},{8,12},{12,8},{10,14},{14,10},{16,20},{20,... | collective-permute-start | bytes 3833864 | tf_op jit(solution)/shard_map/ppermute | solution.py:317
  483.6 25.6 %collective-permute-start.21 = (bf16[19968,128]{1,0:T(8,128)(2,1)}, bf16[19968,128]{1,0:T(8,128)(2,1)}, u32[]{:S(2)}, u32[]{:S(2)}) collective-permute-start(bf16[19968,128]{1,0:T(8,128)(2,1)} %join.1.high1), channel_id=1, source_target_pairs={{0,1},{2,3},{4,5},{6,7},{8,9},{10,11},{12,13},{14,15},{16,17},{18,... | collective-permute-start | bytes 15335432 | tf_op jit(solution)/shard_map/ppermute | solution.py:531
  484.9 11.6 %collective-permute-start.17 = (bf16[1,2496,128]{2,1,0:T(8,128)(2,1)S(1)}, bf16[1,2496,128]{2,1,0:T(8,128)(2,1)S(1)}, u32[]{:S(2)}, u32[]{:S(2)}) collective-permute-start(bf16[1,2496,128]{2,1,0:T(8,128)(2,1)S(1)} %bitcast.275), channel_id=1, source_target_pairs={{0,2},{2,0},{4,6},{6,4},{8,10},{10,8},{12,14},{14,12},{16,18},{18,... | collective-permute-start | bytes 1916936 | tf_op jit(solution)/shard_map/ppermute | solution.py:317
  485.3 19.6 %collective-permute-start.15 = (bf16[1,2496,128]{2,1,0:T(8,128)(2,1)S(1)}, bf16[1,2496,128]{2,1,0:T(8,128)(2,1)S(1)}, u32[]{:S(2)}, u32[]{:S(2)}) collective-permute-start(bf16[1,2496,128]{2,1,0:T(8,128)(2,1)S(1)} %bitcast.273), channel_id=1, source_target_pairs={{0,4},{4,0},{2,6},{6,2},{8,12},{12,8},{10,14},{14,10},{16,20},{20,... | collective-permute-start | bytes 1916936 | tf_op jit(solution)/shard_map/ppermute | solution.py:317
  496.7 11.3 %collective-permute-start.20 = (bf16[4992,128]{1,0:T(8,128)(2,1)S(1)}, bf16[4992,128]{1,0:T(8,128)(2,1)}, u32[]{:S(2)}, u32[]{:S(2)}) collective-permute-start(bf16[4992,128]{1,0:T(8,128)(2,1)S(1)} %bitcast.219), channel_id=1, source_target_pairs={{1,0},{3,2},{5,4},{7,6},{9,8},{11,10},{13,12},{15,14},{17,16},{19,... | collective-permute-start | bytes 3833864 | tf_op jit(solution)/shard_map/ppermute | solution.py:531
  505.1 4.0 collective-permute-start.19
  507.5 29.1 %collective-permute-start.18 = (bf16[4992,128]{1,0:T(8,128)(2,1)S(1)}, bf16[4992,128]{1,0:T(8,128)(2,1)}, u32[]{:S(2)}, u32[]{:S(2)}) collective-permute-start(bf16[4992,128]{1,0:T(8,128)(2,1)S(1)} %bitcast.220), channel_id=1, source_target_pairs={{0,4},{4,0},{2,6},{6,2},{8,12},{12,8},{10,14},{14,10},{16,20},{20,... | collective-permute-start | bytes 3833864 | tf_op jit(solution)/shard_map/ppermute | solution.py:317
  507.5 29.1 %collective-permute-start.16 = (bf16[4992,128]{1,0:T(8,128)(2,1)S(1)}, bf16[4992,128]{1,0:T(8,128)(2,1)}, u32[]{:S(2)}, u32[]{:S(2)}) collective-permute-start(bf16[4992,128]{1,0:T(8,128)(2,1)S(1)} %bitcast.223), channel_id=1, source_target_pairs={{0,2},{2,0},{4,6},{6,4},{8,10},{10,8},{12,14},{14,12},{16,18},{18,... | collective-permute-start | bytes 3833864 | tf_op jit(solution)/shard_map/ppermute | solution.py:317
  536.6 4.1 collective-permute-start.22
  538.0 4.6 collective-permute-start.23
  546.2 28.0 %copy-start.1 = (bf16[6,256,768]{2,1,0:T(8,128)(2,1)S(1)}, bf16[6,256,768]{2,1,0:T(8,128)(2,1)}, u32[]{:S(2)}) copy-start(bf16[6,256,768]{2,1,0:T(8,128)(2,1)} %param.9) | copy-start | bytes 7077892
  (87 other events, 272.8 us)
